TPU v7x, 32 devices: a whole 2x2x4 slice. The times are simulated.
32 devices in a mesh: groups: 2 (over x), wide: 8 (over z, y), narrow: 2 (over core).
Axes of the slice: x: 2, y: 2, z: 4, core: 2. Of those that a mesh axis runs over, the one named last changes fastest.
Arguments:
- features: bfloat16 [64, 16, 128, 256], P(('groups', 'wide'), 'narrow'), parts along dimension 0, may hold values from -6 to 6
- tile_ids: int32 [64, 16, 3], P(('groups', 'wide'), 'narrow'), parts along dimension 0, may hold values from 0 to 15
- tiles: bfloat16 [16, 128, 128], replicated, may hold values from -0.25 to 0.25
- w_first: bfloat16 [256, 256], replicated, may hold values from -0.375 to 0.375
- w_second: bfloat16 [256, 256], replicated, may hold values from -0.375 to 0.375
- readout: bfloat16 [256], replicated, may hold values from -0.375 to 0.375
- target: float32 [64, 16, 128], P(('groups', 'wide'), 'narrow'), parts along dimension 0, may hold values from -6 to 6
Outputs:
- pred: float32 [64, 16, 128], P(('groups', 'wide'), 'narrow'), parts along dimension 0
- grad_first: float32 [512, 256], P(('groups', 'wide', 'narrow')), parts along dimension 0
- grad_second: float32 [512, 256], P(('groups', 'wide', 'narrow')), parts along dimension 0
- grad_readout: float32 [512], P('groups'), parts along dimension 0
There are 2 independent parts, one for each index of `groups`. A program takes and returns all parts, laid end to end along the dimension named above; an argument that names none is the same for every part. Nothing has to cross between parts.
All inputs are finite; a program needn't handle non-finite values.
Results may differ from a plain program's by a relative error of at most 0.0049.
Values may be sent and summed in bfloat16 or wider, within the bound.
No kernel may reach another device: no remote copies, remote signals or barrier semaphores. Data moves between devices by JAX's collectives and lax.ppermute only.
A program may use at most 128 MiB of HBM per device.

v0:
```python
import jax
import jax.numpy as jnp
from jax import lax
from jax.sharding import PartitionSpec as P


def extended(cells, sides, width):
    for axis, dim in sides:
        count = lax.axis_size(axis)
        ends = count - 1
        head = lax.slice_in_dim(cells, 0, width, axis=dim)
        tail = lax.slice_in_dim(cells, cells.shape[dim] - width, cells.shape[dim], axis=dim)
        cells = jnp.concatenate(
            [
                lax.ppermute(tail, axis, [(i, (i + 1) % count) for i in range(ends)]),
                cells,
                lax.ppermute(head, axis, [((i + 1) % count, i) for i in range(ends)]),
            ],
            axis=dim,
        )
    return cells


def shifted(block, axis, distance):
    devices = range(lax.axis_size(axis))
    route = [(i - distance, i) for i in devices if i - distance in devices]
    return lax.ppermute(block, axis, route)


def apply_operator(padded, ids_pad, tiles, offset):
    nx = padded.shape[0] - 2
    ny = padded.shape[1] - 2
    centre_ids = ids_pad[offset + 1 : offset + 1 + nx, offset + 1 : offset + 1 + ny]
    west_ids = ids_pad[offset : offset + nx, offset + 1 : offset + 1 + ny, 1]
    south_ids = ids_pad[offset + 1 : offset + 1 + nx, offset : offset + ny, 2]
    centre = padded[1:-1, 1:-1]
    selfs = jnp.take(tiles, centre_ids[..., 0], axis=0)
    total = jnp.einsum("xynm,xymh->xynh", selfs, centre, preferred_element_type=jnp.float32)
    total = total + jnp.einsum("xymn,xymh->xynh", selfs, centre, preferred_element_type=jnp.float32)
    east = jnp.take(tiles, centre_ids[..., 1], axis=0)
    total = total + jnp.einsum(
        "xynm,xymh->xynh", east, padded[2:, 1:-1], preferred_element_type=jnp.float32
    )
    west = jnp.take(tiles, west_ids, axis=0)
    total = total + jnp.einsum(
        "xymn,xymh->xynh", west, padded[:-2, 1:-1], preferred_element_type=jnp.float32
    )
    north = jnp.take(tiles, centre_ids[..., 2], axis=0)
    total = total + jnp.einsum(
        "xynm,xymh->xynh", north, padded[1:-1, 2:], preferred_element_type=jnp.float32
    )
    south = jnp.take(tiles, south_ids, axis=0)
    total = total + jnp.einsum(
        "xymn,xymh->xynh", south, padded[1:-1, :-2], preferred_element_type=jnp.float32
    )
    return total


def edge_rim(field):
    return extended(field, (("wide", 0), ("narrow", 1)), 1)


def column_term(matrix, grads):
    return lax.dot_general(
        matrix, grads, (((0,), (0,)), ((), ())), preferred_element_type=jnp.float32
    )


def per_device(features, tile_ids, tiles, w_first, w_second, readout, target):
    bx = features.shape[0]
    by = features.shape[1]
    width = features.shape[3]
    west_rim = shifted(tile_ids[bx - 1, :, 1], "wide", 1)
    south_rim = shifted(tile_ids[:, by - 1, 2], "narrow", 1)
    ids_pad = jnp.zeros((bx + 2, by + 2, 3), jnp.int32)
    ids_pad = ids_pad.at[1 : 1 + bx, 1 : 1 + by].set(tile_ids)
    ids_pad = ids_pad.at[0, 1 : 1 + by, 1].set(west_rim)
    ids_pad = ids_pad.at[1 : 1 + bx, 0, 2].set(south_rim)
    id_off = 0
    m_one = apply_operator(edge_rim(features), ids_pad, tiles, id_off).astype(jnp.bfloat16)
    z_one = jnp.einsum("xynh,hk->xynk", m_one, w_first, preferred_element_type=jnp.float32)
    x_one = (features.astype(jnp.float32) + jnp.tanh(z_one)).astype(jnp.bfloat16)
    m_two = apply_operator(edge_rim(x_one), ids_pad, tiles, id_off).astype(jnp.bfloat16)
    z_two = jnp.einsum("xynh,hk->xynk", m_two, w_second, preferred_element_type=jnp.float32)
    x_two = (x_one.astype(jnp.float32) + jnp.tanh(z_two)).astype(jnp.bfloat16)
    readf = readout.astype(jnp.float32)
    pred = jnp.einsum("xynh,h->xyn", x_two, readout, preferred_element_type=jnp.float32)
    nodes = bx * by * features.shape[2] * lax.axis_size("wide") * lax.axis_size("narrow")
    scale = jnp.sqrt(jnp.float32(width) / jnp.float32(nodes))
    grad_pred = (pred - target) * scale
    local_readout = jnp.einsum("xynh,xyn->h", x_two.astype(jnp.float32), grad_pred)
    grad_readout = lax.psum(local_readout, ("wide", "narrow"))
    grad_x_two = grad_pred[..., None] * readf
    tanh_two = jnp.tanh(z_two)
    grad_z_two = (grad_x_two * (1.0 - tanh_two * tanh_two)).astype(jnp.bfloat16)
    m_two_flat = m_two.reshape(-1, width)
    m_one_flat = m_one.reshape(-1, width)
    gz_two_flat = grad_z_two.reshape(-1, width)
    grad_second = lax.psum_scatter(
        column_term(m_two_flat, gz_two_flat), ("wide", "narrow"), scatter_dimension=0, tiled=True
    )
    grad_m_two = jnp.einsum(
        "xynk,hk->xynh", grad_z_two, w_second, preferred_element_type=jnp.float32
    ).astype(jnp.bfloat16)
    grad_pad = extended(grad_m_two, (("wide", 0), ("narrow", 1)), 1)
    grad_x_one = grad_x_two + apply_operator(grad_pad, ids_pad, tiles, id_off)
    tanh_one = jnp.tanh(z_one)
    grad_z_one = (grad_x_one * (1.0 - tanh_one * tanh_one)).astype(jnp.bfloat16)
    gz_one_flat = grad_z_one.reshape(-1, width)
    grad_first = lax.psum_scatter(
        column_term(m_one_flat, gz_one_flat), ("wide", "narrow"), scatter_dimension=0, tiled=True
    )
    return (pred, grad_first, grad_second, grad_readout)


def solution(mesh):
    in_specs = (
        P(("groups", "wide"), "narrow", None, None),
        P(("groups", "wide"), "narrow", None),
        P(),
        P(),
        P(),
        P(),
        P(("groups", "wide"), "narrow", None),
    )
    out_specs = (
        P(("groups", "wide"), "narrow", None),
        P(("groups", "wide", "narrow"), None),
        P(("groups", "wide", "narrow"), None),
        P("groups"),
    )
    return jax.shard_map(
        per_device, mesh=mesh, in_specs=in_specs, out_specs=out_specs, check_vma=False
    )
```

profile of v0, /device:TPU:0, one launch (start us, length us, event | category | flops | bytes accessed | tf_op | source)
XLA Modules:
  0.0 255.8 jit_solution(11594053089742596315)
XLA Ops:
  8.0 4.9 %collective-permute-start = (s32[8]{0:T(128)S(1)}, s32[8]{0:T(128)S(1)}, u32[]{:S(2)}, u32[]{:S(2)}) collective-permute-start(s32[8]{0:T(128)S(1)} %slice_bitcast_fusion.5), channel_id=1, source_target_pairs={{0,2},{2,4},{4,6},{6,8},{8,10},{10,12},{12,14},{1,3},{3,5},{5,7},{... | collective-permute-start | bytes 104 | tf_op jit(solution)/shard_map/ppermute | solution.py:27
  15.2 2.3 fusion.94
  17.5 3.4 %collective-permute-start.3 = (bf16[1,8,128,256]{3,2,1,0:T(8,128)(2,1)}, bf16[1,8,128,256]{3,2,1,0:T(8,128)(2,1)S(1)}, u32[]{:S(2)}, u32[]{:S(2)}) collective-permute-start(bf16[1,8,128,256]{3,2,1,0:T(8,128)(2,1)} %get-tuple-element.52), channel_id=1, source_target_pairs={{0,2},{2,4},{4,6},{6,8},{8,10},{10,12},{12,14},{1,3},{3,5},{5,7},{... | collective-permute-start | bytes 1572872 | tf_op jit(solution)/shard_map/ppermute | solution.py:15
  28.8 4.0 %fusion.46 = f32[4,8,128,256]{3,2,1,0:T(8,128)} fusion(bf16[4,8,128,256]{3,2,1,0:T(8,128)(2,1)S(1)} %copy-done.2, bf16[4,8,128,128]{2,3,1,0:T(8,128)(2,1)} %copy.13, pred[4,8]{1,0:T(4,128)(4,1)S(1)} %get-tuple-element.57), kind=kOutput, calls=%fused_computation.83 | convolution fusion | flops 268959744 | bytes 7340064 | tf_op jit(solution)/shard_map/xymn,xymh->xynh/dot_general | solution.py:39
  36.2 2.3 copy.15
  41.8 2.3 copy.16
  44.1 4.4 %fusion.47 = f32[4,8,128,256]{3,2,1,0:T(8,128)} fusion(bf16[4,8,128,256]{3,2,1,0:T(8,128)(2,1)S(1)} %copy-done.2, bf16[4,8,128,128]{2,3,1,0:T(8,128)(2,1)} %copy.13, pred[4,8]{1,0:T(4,128)(4,1)S(1)} %get-tuple-element.57), kind=kOutput, calls=%fused_computation.84 | convolution fusion | flops 268959744 | bytes 7340064 | tf_op jit(solution)/shard_map/xynm,xymh->xynh/dot_general | solution.py:38
  51.2 3.1 %collective-permute-start.5 = (bf16[6,1,128,256]{3,2,1,0:T(8,128)(2,1)S(1)}, bf16[6,1,128,256]{3,2,1,0:T(8,128)(2,1)S(1)}, u32[]{:S(2)}, u32[]{:S(2)}) collective-permute-start(bf16[6,1,128,256]{3,2,1,0:T(8,128)(2,1)S(1)} %get-tuple-element.45), channel_id=1, source_target_pairs={{0,1},{2,3},{4,5},{6,7},{8,9},{10,11},{12,13},{14,15},{16,17},{18,... | collective-permute-start | bytes 1179656 | tf_op jit(solution)/shard_map/ppermute | solution.py:15
  57.5 2.9 %fusion.21 = f32[4,8,128,256]{3,2,1,0:T(8,128)} fusion(bf16[6,1,128,256]{3,2,1,0:T(8,128)(2,1)S(1)} %collective-permute-done.4, bf16[6,8,128,256]{3,2,1,0:T(8,128)(2,1)S(1)} %constant_dynamic-update-slice_fusion, bf16[4,8,128,128]{3,2,1,0:T(8,128)(2,1)S(1)} %bitcast.88, pred[4,8]{1,0:T(4,128)(4,1)S(1)} %get-tuple-element.54), kind=kOutput, calls=%fused_computation.50 | convolution fusion | flops 270008320 | bytes 8781856 | tf_op jit(solution)/shard_map/xynm,xymh->xynh/dot_general | solution.py:49
  61.5 7.3 %add_convert_fusion.3 = bf16[4,8,128,256]{3,2,1,0:T(8,128)(2,1)} fusion(f32[4,8,128,256]{3,2,1,0:T(8,128)} %fusion.21, f32[4,8,128,256]{3,2,1,0:T(8,128)S(1)} %fusion.23, f32[4,8,128,256]{3,2,1,0:T(8,128)S(1)} %fusion.25, f32[4,8,128,256]{3,2,1,0:T(8,128)} %fusion.47, f32[4,8,128,256]{3,2,1,0:T(8,128)S(1)} %copy-done.13, ...), kind=kOutput, calls=%fused_computation.13 | convolution fusion | flops 276299776 | bytes 27656224 | tf_op jit(solution)/shard_map/xymn,xymh->xynh/dot_general | solution.py:53
  68.8 4.4 %add_convert_fusion.2 = (bf16[4,8,128,256]{3,2,1,0:T(8,128)(2,1)S(1)}, f32[4,8,128,256]{3,2,1,0:T(8,128)}) fusion(bf16[4,8,128,256]{3,2,1,0:T(8,128)(2,1)S(1)} %copy-done.3, bf16[4,8,128,256]{3,2,1,0:T(8,128)(2,1)} %add_convert_fusion.3, bf16[256,256]{1,0:T(8,128)(2,1)S(1)} %copy-done.19), kind=kOutput, calls=%fused_computation.12 | convolution fusion | flops 540016640 | bytes 10616832 | tf_op jit(solution)/shard_map/xynh,hk->xynk/dot_general | solution.py:81
  74.7 5.2 %collective-permute-start.7 = (bf16[1,8,128,256]{3,2,1,0:T(8,128)(2,1)S(1)}, bf16[1,8,128,256]{3,2,1,0:T(8,128)(2,1)S(1)}, u32[]{:S(2)}, u32[]{:S(2)}) collective-permute-start(bf16[1,8,128,256]{3,2,1,0:T(8,128)(2,1)S(1)} %get-tuple-element.49), channel_id=1, source_target_pairs={{0,2},{2,4},{4,6},{6,8},{8,10},{10,12},{12,14},{1,3},{3,5},{5,7},{... | collective-permute-start | bytes 1572872 | tf_op jit(solution)/shard_map/ppermute | solution.py:15
  80.7 3.2 %fusion.45 = f32[4,8,128,256]{3,2,1,0:T(8,128)} fusion(bf16[4,8,128,256]{3,2,1,0:T(8,128)(2,1)S(1)} %get-tuple-element.63, bf16[4,8,128,128]{2,3,1,0:T(8,128)(2,1)S(1)} %copy-done.6, pred[4,8]{1,0:T(4,128)(4,1)S(1)} %get-tuple-element.57), kind=kOutput, calls=%fused_computation.82 | convolution fusion | flops 268959744 | bytes 7340064 | tf_op jit(solution)/shard_map/xynm,xymh->xynh/dot_general | solution.py:38
  83.9 5.4 %collective-permute-done.6 = bf16[1,8,128,256]{3,2,1,0:T(8,128)(2,1)S(1)} collective-permute-done((bf16[1,8,128,256]{3,2,1,0:T(8,128)(2,1)S(1)}, bf16[1,8,128,256]{3,2,1,0:T(8,128)(2,1)S(1)}, u32[]{:S(2)}, u32[]{:S(2)}) %collective-permute-start.6) | collective-permute-done | bytes 524320 | tf_op jit(solution)/shard_map/ppermute | solution.py:17
  89.4 11.4 %collective-permute-done.7 = bf16[1,8,128,256]{3,2,1,0:T(8,128)(2,1)S(1)} collective-permute-done((bf16[1,8,128,256]{3,2,1,0:T(8,128)(2,1)S(1)}, bf16[1,8,128,256]{3,2,1,0:T(8,128)(2,1)S(1)}, u32[]{:S(2)}, u32[]{:S(2)}) %collective-permute-start.7) | collective-permute-done | bytes 524320 | tf_op jit(solution)/shard_map/ppermute | solution.py:15
  102.1 3.3 %collective-permute-start.9 = (bf16[6,1,128,256]{3,2,1,0:T(8,128)(2,1)S(1)}, bf16[6,1,128,256]{3,2,1,0:T(8,128)(2,1)S(1)}, u32[]{:S(2)}, u32[]{:S(2)}) collective-permute-start(bf16[6,1,128,256]{3,2,1,0:T(8,128)(2,1)S(1)} %get-tuple-element.43), channel_id=1, source_target_pairs={{0,1},{2,3},{4,5},{6,7},{8,9},{10,11},{12,13},{14,15},{16,17},{18,... | collective-permute-start | bytes 1179656 | tf_op jit(solution)/shard_map/ppermute | solution.py:15
  107.4 2.8 %fusion.13 = f32[4,8,128,256]{3,2,1,0:T(8,128)} fusion(bf16[6,1,128,256]{3,2,1,0:T(8,128)(2,1)S(1)} %collective-permute-done.8, bf16[1,8,128,256]{3,2,1,0:T(8,128)(2,1)S(1)} %collective-permute-done.6, bf16[4,8,128,256]{3,2,1,0:T(8,128)(2,1)S(1)} %get-tuple-element.63, bf16[1,8,128,256]{3,2,1,0:T(8,128)(2,1)S(1)} %collective-permute-done.7, ...), kind=kOutput, calls=%fused_computation.36 | convolution fusion | flops 272105472 | bytes 8781856 | tf_op jit(solution)/shard_map/xynm,xymh->xynh/dot_general | solution.py:49
  110.2 4.7 %add_convert_fusion.1 = bf16[4,8,128,256]{3,2,1,0:T(8,128)(2,1)S(1)} fusion(f32[4,8,128,256]{3,2,1,0:T(8,128)} %fusion.13, f32[4,8,128,256]{3,2,1,0:T(8,128)S(1)} %fusion.15, f32[4,8,128,256]{3,2,1,0:T(8,128)S(1)} %fusion.17, f32[4,8,128,256]{3,2,1,0:T(8,128)} %fusion.45, f32[4,8,128,256]{3,2,1,0:T(8,128)S(1)} %fusion.44, ...), kind=kOutput, calls=%fused_computation.11 | convolution fusion | flops 278396928 | bytes 27656224 | tf_op jit(solution)/shard_map/xymn,xymh->xynh/dot_general | solution.py:53
  117.6 2.3 convolution_bitcast_fusion
  119.9 3.2 %convolution_convert_fusion = bf16[4,8,128,256]{3,2,1,0:T(8,128)(2,1)S(1)} fusion(bf16[256,256]{1,0:T(8,128)(2,1)S(1)} %copy-done.20, f32[4,8,128,256]{3,2,1,0:T(8,128)} %copy-done.8, f32[256]{0:T(256)S(1)} %copy-done.33, f32[4,8,128]{2,1,0:T(8,128)S(1)} %subtract_multiply_fusion), kind=kOutput, calls=%fused_computation.58 | convolution fusion | flops 543162368 | bytes 6439936 | tf_op jit(solution)/shard_map/xynk,hk->xynh/dot_general | solution.py:102
  125.6 5.0 %collective-permute-start.11 = (bf16[1,8,128,256]{3,2,1,0:T(8,128)(2,1)}, bf16[1,8,128,256]{3,2,1,0:T(8,128)(2,1)S(1)}, u32[]{:S(2)}, u32[]{:S(2)}) collective-permute-start(bf16[1,8,128,256]{3,2,1,0:T(8,128)(2,1)} %get-tuple-element.47), channel_id=1, source_target_pairs={{0,2},{2,4},{4,6},{6,8},{8,10},{10,12},{12,14},{1,3},{3,5},{5,7},{... | collective-permute-start | bytes 1572872 | tf_op jit(solution)/shard_map/ppermute | solution.py:15
  130.7 2.7 %fusion.42 = f32[4,8,128,256]{3,2,1,0:T(8,128)} fusion(bf16[4,8,128,256]{3,2,1,0:T(8,128)(2,1)S(1)} %convolution_convert_fusion, bf16[4,8,128,128]{2,3,1,0:T(8,128)(2,1)S(1)} %copy-done.7, pred[4,8]{1,0:T(4,128)(4,1)S(1)} %copy-done.22), kind=kOutput, calls=%fused_computation.79 | convolution fusion | flops 268959744 | bytes 7340064 | tf_op jit(solution)/shard_map/xymn,xymh->xynh/dot_general | solution.py:39
  133.5 5.3 %fusion.43 = f32[4,8,128,256]{3,2,1,0:T(8,128)} fusion(bf16[4,8,128,256]{3,2,1,0:T(8,128)(2,1)} %copy-done.4, bf16[4,8,128,128]{2,3,1,0:T(8,128)(2,1)} %copy.13, pred[4,8]{1,0:T(4,128)(4,1)S(1)} %copy-done.22), kind=kOutput, calls=%fused_computation.80 | convolution fusion | flops 268959744 | bytes 7340064 | tf_op jit(solution)/shard_map/xynm,xymh->xynh/dot_general | solution.py:38
  140.3 11.5 %collective-permute-done.11 = bf16[1,8,128,256]{3,2,1,0:T(8,128)(2,1)S(1)} collective-permute-done((bf16[1,8,128,256]{3,2,1,0:T(8,128)(2,1)}, bf16[1,8,128,256]{3,2,1,0:T(8,128)(2,1)S(1)}, u32[]{:S(2)}, u32[]{:S(2)}) %collective-permute-start.11) | collective-permute-done | bytes 524320 | tf_op jit(solution)/shard_map/ppermute | solution.py:15
  153.2 3.4 %collective-permute-start.13 = (bf16[6,1,128,256]{3,2,1,0:T(8,128)(2,1)S(1)}, bf16[6,1,128,256]{3,2,1,0:T(8,128)(2,1)S(1)}, u32[]{:S(2)}, u32[]{:S(2)}) collective-permute-start(bf16[6,1,128,256]{3,2,1,0:T(8,128)(2,1)S(1)} %get-tuple-element.41), channel_id=1, source_target_pairs={{0,1},{2,3},{4,5},{6,7},{8,9},{10,11},{12,13},{14,15},{16,17},{18,... | collective-permute-start | bytes 1179656 | tf_op jit(solution)/shard_map/ppermute | solution.py:15
  156.7 2.8 %fusion.9 = f32[4,8,128,256]{3,2,1,0:T(8,128)} fusion(bf16[1,8,128,256]{3,2,1,0:T(8,128)(2,1)S(1)} %collective-permute-done.10, bf16[4,8,128,256]{3,2,1,0:T(8,128)(2,1)S(1)} %copy-done.5, bf16[4,8,128,128]{3,2,1,0:T(8,128)(2,1)S(1)} %bitcast.87, pred[4,8]{1,0:T(4,128)(4,1)S(1)} %copy-done.26), kind=kOutput, calls=%fused_computation.28 | convolution fusion | flops 270008320 | bytes 7864352 | tf_op jit(solution)/shard_map/xynm,xymh->xynh/dot_general | solution.py:41
  159.5 2.8 %fusion.7 = f32[4,8,128,256]{3,2,1,0:T(8,128)} fusion(bf16[4,8,128,256]{3,2,1,0:T(8,128)(2,1)S(1)} %copy-done.5, bf16[1,8,128,256]{3,2,1,0:T(8,128)(2,1)S(1)} %collective-permute-done.11, bf16[4,8,128,128]{2,3,1,0:T(8,128)(2,1)S(1)} %copy-done.10, pred[4,8]{1,0:T(4,128)(4,1)S(1)} %copy-done.24), kind=kOutput, calls=%fused_computation.25 | convolution fusion | flops 270008320 | bytes 7864352 | tf_op jit(solution)/shard_map/xymn,xymh->xynh/dot_general | solution.py:45
  162.3 2.9 %fusion.5 = f32[4,8,128,256]{3,2,1,0:T(8,128)} fusion(bf16[6,1,128,256]{3,2,1,0:T(8,128)(2,1)S(1)} %collective-permute-done.12, bf16[1,8,128,256]{3,2,1,0:T(8,128)(2,1)S(1)} %collective-permute-done.10, bf16[4,8,128,256]{3,2,1,0:T(8,128)(2,1)S(1)} %copy-done.5, bf16[1,8,128,256]{3,2,1,0:T(8,128)(2,1)S(1)} %collective-permute-done.11, ...), kind=kOutput, calls=%fused_computation.20 | convolution fusion | flops 272105472 | bytes 8781856 | tf_op jit(solution)/shard_map/xynm,xymh->xynh/dot_general | solution.py:49
  165.1 13.3 %fusion.28 = f32[256,256]{1,0:T(8,128)} fusion(bf16[4,8,128,256]{3,2,1,0:T(8,128)(2,1)} %add_convert_fusion.3, f32[4,8,128,256]{3,2,1,0:T(8,128)} %fusion.5, f32[4,8,128,256]{3,2,1,0:T(8,128)} %fusion.7, f32[4,8,128,256]{3,2,1,0:T(8,128)} %fusion.9, f32[4,8,128,256]{3,2,1,0:T(8,128)} %fusion.43, f32[4,8,128,256]{3,2,1,0:T(8,128)} %fusion.42, ...), kind=kOutput, calls=%fused_computation.60 | convolution fusion | flops 820510720 | bytes 32130080 | tf_op jit(solution)/shard_map/dot_general | solution.py:64
  178.5 2.9 %fusion.90 = f32[1,256,1,1]{1,0,3,2:T(1,128)S(1)} fusion(f32[4,8,128,1]{2,3,1,0:T(1,128)S(1)} %bitcast.94, bf16[4,8,128,256]{3,2,1,0:T(8,128)(2,1)S(1)} %get-tuple-element.63, f32[4,8,128,256]{3,2,1,0:T(8,128)} %copy-done.8), kind=kOutput, calls=%fused_computation.155 | convolution fusion | flops 5242880 | bytes 6308864 | tf_op jit(solution)/shard_map/xynh,xyn->h/dot_general | solution.py:91
  181.4 31.6 %psum.7 = f32[256]{0:T(256)} all-reduce(f32[256]{0:T(256)S(1)} %bitcast.97), channel_id=1, replica_groups=mesh['groups'=2,'wide'=8,'narrow'=2] {'wide','narrow'}, use_global_device_ids=true, to_apply=%region_2.4 | all-reduce | flops 256 | bytes 2048 | tf_op jit(solution)/shard_map/psum | solution.py:92
  213.0 35.9 %reduce-scatter.3.cloned.1.call-done = f32[16,256]{1,0:T(8,128)} async-done(((f32[256,256]{1,0:T(8,128)}), f32[16,256]{1,0:T(8,128)}) %reduce-scatter.3.cloned.1.call-update) | async-done | bytes 16400 | tf_op jit(solution)/shard_map/reduce_scatter | solution.py:110
  (135 shorter events, 38.5 us)
Async XLA Ops:
  7.2 17.6 %copy-start = (bf16[16,128,128]{2,1,0:T(8,128)(2,1)S(1)}, bf16[16,128,128]{2,1,0:T(8,128)(2,1)}, u32[]{:S(2)}) copy-start(bf16[16,128,128]{2,1,0:T(8,128)(2,1)} %param.17) | copy-start | bytes 1572868
  7.2 16.2 %copy-start.31 = (s32[4,8,3]{1,0,2:T(4,128)S(1)}, s32[4,8,3]{1,0,2:T(4,128)}, u32[]{:S(2)}) copy-start(s32[4,8,3]{1,0,2:T(4,128)} %param.16) | copy-start | bytes 1156
  7.2 15.0 %copy-start.35 = (bf16[256]{0:T(256)(128)(2,1)S(1)}, bf16[256]{0:T(256)(128)(2,1)}, u32[]{:S(2)}) copy-start(bf16[256]{0:T(256)(128)(2,1)} %param.20) | copy-start | bytes 1540
  7.2 205.8 %reduce-scatter.5.cloned.1.call-start = ((), (), s32[]{:S(2)}) async-start(), calls=%async_computation.3 | async-start | bytes 278528 | tf_op jit(solution)/shard_map/reduce_scatter | solution.py:99
  8.0 15.6 %collective-permute-start = (s32[8]{0:T(128)S(1)}, s32[8]{0:T(128)S(1)}, u32[]{:S(2)}, u32[]{:S(2)}) collective-permute-start(s32[8]{0:T(128)S(1)} %slice_bitcast_fusion.5), channel_id=1, source_target_pairs={{0,2},{2,4},{4,6},{6,8},{8,10},{10,12},{12,14},{1,3},{3,5},{5,7},{... | collective-permute-start | bytes 104 | tf_op jit(solution)/shard_map/ppermute | solution.py:27
  13.7 9.7 %collective-permute-start.1 = (s32[4]{0:T(128)S(1)}, s32[4]{0:T(128)S(1)}, u32[]{:S(2)}, u32[]{:S(2)}) collective-permute-start(s32[4]{0:T(128)S(1)} %slice_reduce_fusion), channel_id=1, source_target_pairs={{0,1},{2,3},{4,5},{6,7},{8,9},{10,11},{12,13},{14,15},{16,17},{18,... | collective-permute-start | bytes 56 | tf_op jit(solution)/shard_map/ppermute | solution.py:27
  17.5 31.0 %collective-permute-start.3 = (bf16[1,8,128,256]{3,2,1,0:T(8,128)(2,1)}, bf16[1,8,128,256]{3,2,1,0:T(8,128)(2,1)S(1)}, u32[]{:S(2)}, u32[]{:S(2)}) collective-permute-start(bf16[1,8,128,256]{3,2,1,0:T(8,128)(2,1)} %get-tuple-element.52), channel_id=1, source_target_pairs={{0,2},{2,4},{4,6},{6,8},{8,10},{10,12},{12,14},{1,3},{3,5},{5,7},{... | collective-permute-start | bytes 1572872 | tf_op jit(solution)/shard_map/ppermute | solution.py:15
  20.9 27.8 %collective-permute-start.2 = (bf16[1,8,128,256]{3,2,1,0:T(8,128)(2,1)}, bf16[1,8,128,256]{3,2,1,0:T(8,128)(2,1)}, u32[]{:S(2)}, u32[]{:S(2)}) collective-permute-start(bf16[1,8,128,256]{3,2,1,0:T(8,128)(2,1)} %get-tuple-element.51), channel_id=1, source_target_pairs={{2,0},{4,2},{6,4},{8,6},{10,8},{12,10},{14,12},{3,1},{5,3},{7,5},{... | collective-permute-start | bytes 1572872 | tf_op jit(solution)/shard_map/ppermute | solution.py:17
  24.5 56.1 %copy-start.21 = (pred[4,8]{1,0:T(4,128)(4,1)}, pred[4,8]{1,0:T(4,128)(4,1)S(1)}, u32[]{:S(2)}) copy-start(pred[4,8]{1,0:T(4,128)(4,1)S(1)} %get-tuple-element.57) | copy-start | bytes 100
  24.5 80.9 %copy-start.25 = (pred[4,8]{1,0:T(4,128)(4,1)}, pred[4,8]{1,0:T(4,128)(4,1)S(1)}, u32[]{:S(2)}) copy-start(pred[4,8]{1,0:T(4,128)(4,1)S(1)} %get-tuple-element.56) | copy-start | bytes 100
  24.5 81.7 %copy-start.23 = (pred[4,8]{1,0:T(4,128)(4,1)}, pred[4,8]{1,0:T(4,128)(4,1)S(1)}, u32[]{:S(2)}) copy-start(pred[4,8]{1,0:T(4,128)(4,1)S(1)} %get-tuple-element.55) | copy-start | bytes 100
  24.5 82.5 %copy-start.29 = (pred[4,8]{1,0:T(4,128)(4,1)}, pred[4,8]{1,0:T(4,128)(4,1)S(1)}, u32[]{:S(2)}) copy-start(pred[4,8]{1,0:T(4,128)(4,1)S(1)} %get-tuple-element.54) | copy-start | bytes 100
  49.9 7.6 %copy-start.14 = (bf16[6,8,128,256]{3,2,1,0:T(8,128)(2,1)}, bf16[6,8,128,256]{3,2,1,0:T(8,128)(2,1)S(1)}, u32[]{:S(2)}) copy-start(bf16[6,8,128,256]{3,2,1,0:T(8,128)(2,1)S(1)} %constant_dynamic-update-slice_fusion) | copy-start | bytes 9437188
  49.9 7.5 %collective-permute-start.4 = (bf16[6,1,128,256]{3,2,1,0:T(8,128)(2,1)S(1)}, bf16[6,1,128,256]{3,2,1,0:T(8,128)(2,1)S(1)}, u32[]{:S(2)}, u32[]{:S(2)}) collective-permute-start(bf16[6,1,128,256]{3,2,1,0:T(8,128)(2,1)S(1)} %get-tuple-element.46), channel_id=1, source_target_pairs={{1,0},{3,2},{5,4},{7,6},{9,8},{11,10},{13,12},{15,14},{17,16},{19,... | collective-permute-start | bytes 1179656 | tf_op jit(solution)/shard_map/ppermute | solution.py:17
  51.2 9.2 %collective-permute-start.5 = (bf16[6,1,128,256]{3,2,1,0:T(8,128)(2,1)S(1)}, bf16[6,1,128,256]{3,2,1,0:T(8,128)(2,1)S(1)}, u32[]{:S(2)}, u32[]{:S(2)}) collective-permute-start(bf16[6,1,128,256]{3,2,1,0:T(8,128)(2,1)S(1)} %get-tuple-element.45), channel_id=1, source_target_pairs={{0,1},{2,3},{4,5},{6,7},{8,9},{10,11},{12,13},{14,15},{16,17},{18,... | collective-permute-start | bytes 1179656 | tf_op jit(solution)/shard_map/ppermute | solution.py:15
  61.5 7.3 %copy-start.19 = (bf16[256,256]{1,0:T(8,128)(2,1)S(1)}, bf16[256,256]{1,0:T(8,128)(2,1)}, u32[]{:S(2)}) copy-start(bf16[256,256]{1,0:T(8,128)(2,1)} %param.18) | copy-start | bytes 393220
  73.2 16.1 %collective-permute-start.6 = (bf16[1,8,128,256]{3,2,1,0:T(8,128)(2,1)S(1)}, bf16[1,8,128,256]{3,2,1,0:T(8,128)(2,1)S(1)}, u32[]{:S(2)}, u32[]{:S(2)}) collective-permute-start(bf16[1,8,128,256]{3,2,1,0:T(8,128)(2,1)S(1)} %get-tuple-element.50), channel_id=1, source_target_pairs={{2,0},{4,2},{6,4},{8,6},{10,8},{12,10},{14,12},{3,1},{5,3},{7,5},{... | collective-permute-start | bytes 1572872 | tf_op jit(solution)/shard_map/ppermute | solution.py:17
  74.7 26.1 %collective-permute-start.7 = (bf16[1,8,128,256]{3,2,1,0:T(8,128)(2,1)S(1)}, bf16[1,8,128,256]{3,2,1,0:T(8,128)(2,1)S(1)}, u32[]{:S(2)}, u32[]{:S(2)}) collective-permute-start(bf16[1,8,128,256]{3,2,1,0:T(8,128)(2,1)S(1)} %get-tuple-element.49), channel_id=1, source_target_pairs={{0,2},{2,4},{4,6},{6,8},{8,10},{10,12},{12,14},{1,3},{3,5},{5,7},{... | collective-permute-start | bytes 1572872 | tf_op jit(solution)/shard_map/ppermute | solution.py:15
  100.8 6.2 %collective-permute-start.8 = (bf16[6,1,128,256]{3,2,1,0:T(8,128)(2,1)S(1)}, bf16[6,1,128,256]{3,2,1,0:T(8,128)(2,1)S(1)}, u32[]{:S(2)}, u32[]{:S(2)}) collective-permute-start(bf16[6,1,128,256]{3,2,1,0:T(8,128)(2,1)S(1)} %get-tuple-element.44), channel_id=1, source_target_pairs={{1,0},{3,2},{5,4},{7,6},{9,8},{11,10},{13,12},{15,14},{17,16},{19,... | collective-permute-start | bytes 1179656 | tf_op jit(solution)/shard_map/ppermute | solution.py:17
  102.1 8.1 %collective-permute-start.9 = (bf16[6,1,128,256]{3,2,1,0:T(8,128)(2,1)S(1)}, bf16[6,1,128,256]{3,2,1,0:T(8,128)(2,1)S(1)}, u32[]{:S(2)}, u32[]{:S(2)}) collective-permute-start(bf16[6,1,128,256]{3,2,1,0:T(8,128)(2,1)S(1)} %get-tuple-element.43), channel_id=1, source_target_pairs={{0,1},{2,3},{4,5},{6,7},{8,9},{10,11},{12,13},{14,15},{16,17},{18,... | collective-permute-start | bytes 1179656 | tf_op jit(solution)/shard_map/ppermute | solution.py:15
  123.1 7.6 %copy-start.4 = (bf16[4,8,128,256]{3,2,1,0:T(8,128)(2,1)}, bf16[4,8,128,256]{3,2,1,0:T(8,128)(2,1)S(1)}, u32[]{:S(2)}) copy-start(bf16[4,8,128,256]{3,2,1,0:T(8,128)(2,1)S(1)} %convolution_convert_fusion) | copy-start | bytes 6291460
  123.1 7.6 %copy-start.7 = (bf16[4,8,128,128]{2,3,1,0:T(8,128)(2,1)S(1)}, bf16[4,8,128,128]{2,3,1,0:T(8,128)(2,1)}, u32[]{:S(2)}) copy-start(bf16[4,8,128,128]{2,3,1,0:T(8,128)(2,1)} %copy.13) | copy-start | bytes 3145732
  123.1 7.6 %copy-start.22 = (pred[4,8]{1,0:T(4,128)(4,1)S(1)}, pred[4,8]{1,0:T(4,128)(4,1)}, u32[]{:S(2)}) copy-start(pred[4,8]{1,0:T(4,128)(4,1)} %copy-done.21) | copy-start | bytes 100
  124.2 16.2 %collective-permute-start.10 = (bf16[1,8,128,256]{3,2,1,0:T(8,128)(2,1)}, bf16[1,8,128,256]{3,2,1,0:T(8,128)(2,1)S(1)}, u32[]{:S(2)}, u32[]{:S(2)}) collective-permute-start(bf16[1,8,128,256]{3,2,1,0:T(8,128)(2,1)} %get-tuple-element.48), channel_id=1, source_target_pairs={{2,0},{4,2},{6,4},{8,6},{10,8},{12,10},{14,12},{3,1},{5,3},{7,5},{... | collective-permute-start | bytes 1572872 | tf_op jit(solution)/shard_map/ppermute | solution.py:17
  125.6 26.2 %collective-permute-start.11 = (bf16[1,8,128,256]{3,2,1,0:T(8,128)(2,1)}, bf16[1,8,128,256]{3,2,1,0:T(8,128)(2,1)S(1)}, u32[]{:S(2)}, u32[]{:S(2)}) collective-permute-start(bf16[1,8,128,256]{3,2,1,0:T(8,128)(2,1)} %get-tuple-element.47), channel_id=1, source_target_pairs={{0,2},{2,4},{4,6},{6,8},{8,10},{10,12},{12,14},{1,3},{3,5},{5,7},{... | collective-permute-start | bytes 1572872 | tf_op jit(solution)/shard_map/ppermute | solution.py:15
  133.4 115.5 %reduce-scatter.3.cloned.1.call-start = ((), (), s32[]{:S(2)}) async-start(), calls=%async_computation.2 | async-start | bytes 278528 | tf_op jit(solution)/shard_map/reduce_scatter | solution.py:110
  133.4 18.4 %copy-start.5 = (bf16[4,8,128,256]{3,2,1,0:T(8,128)(2,1)S(1)}, bf16[4,8,128,256]{3,2,1,0:T(8,128)(2,1)}, u32[]{:S(2)}) copy-start(bf16[4,8,128,256]{3,2,1,0:T(8,128)(2,1)} %copy-done.4) | copy-start | bytes 6291460
  138.7 18.0 %copy-start.12 = (bf16[32,128,128]{2,1,0:T(8,128)(2,1)S(1)}, bf16[32,128,128]{2,1,0:T(8,128)(2,1)}, u32[]{:S(2)}) copy-start(bf16[32,128,128]{2,1,0:T(8,128)(2,1)} %gather_fusion.1) | copy-start | bytes 3145732
  138.7 18.0 %copy-start.26 = (pred[4,8]{1,0:T(4,128)(4,1)S(1)}, pred[4,8]{1,0:T(4,128)(4,1)}, u32[]{:S(2)}) copy-start(pred[4,8]{1,0:T(4,128)(4,1)} %copy-done.25) | copy-start | bytes 100
  151.9 10.3 %collective-permute-start.12 = (bf16[6,1,128,256]{3,2,1,0:T(8,128)(2,1)S(1)}, bf16[6,1,128,256]{3,2,1,0:T(8,128)(2,1)S(1)}, u32[]{:S(2)}, u32[]{:S(2)}) collective-permute-start(bf16[6,1,128,256]{3,2,1,0:T(8,128)(2,1)S(1)} %get-tuple-element.42), channel_id=1, source_target_pairs={{1,0},{3,2},{5,4},{7,6},{9,8},{11,10},{13,12},{15,14},{17,16},{19,... | collective-permute-start | bytes 1179656 | tf_op jit(solution)/shard_map/ppermute | solution.py:17
  153.2 11.9 %collective-permute-start.13 = (bf16[6,1,128,256]{3,2,1,0:T(8,128)(2,1)S(1)}, bf16[6,1,128,256]{3,2,1,0:T(8,128)(2,1)S(1)}, u32[]{:S(2)}, u32[]{:S(2)}) collective-permute-start(bf16[6,1,128,256]{3,2,1,0:T(8,128)(2,1)S(1)} %get-tuple-element.41), channel_id=1, source_target_pairs={{0,1},{2,3},{4,5},{6,7},{8,9},{10,11},{12,13},{14,15},{16,17},{18,... | collective-permute-start | bytes 1179656 | tf_op jit(solution)/shard_map/ppermute | solution.py:15
  178.5 70.4 %copy-start.1 = (bf16[16,128,128]{2,1,0:T(8,128)(2,1)S(1)}, bf16[16,128,128]{2,1,0:T(8,128)(2,1)}, u32[]{:S(2)}) copy-start(bf16[16,128,128]{2,1,0:T(8,128)(2,1)} %param.17) | copy-start | bytes 1572868
  (20 other events, 70.9 us)
Sparse Core Ops, SparseCore 0:
  133.5 56.8 reduce-scatter.4
  194.5 54.3 reduce-scatter.2
where the time goes:
time: 257 us; the launch traced here: 256 us
  matrix products  78 us (30%)
  waiting for transfers between devices  65.9 us (26%)
  starting transfers between devices  37.9 us (15%)
  blocking collectives  31.6 us (12%)
  local copies, waits for them, and re-layouts  26.4 us (10%)
  between operations  14.6 us (6%)
    reduce_scatter x1, waiting for transfers between devices, per_device(): lax.psum_scatter(column_term(m_one_flat, gz_one_flat), ('wide', 'narrow')...  35.9 us
    psum x1, blocking collectives, per_device(): grad_readout = lax.psum(local_readout, ('wide', 'narrow'))  31.6 us
    ppermute x6, starting transfers between devices, extended(): lax.ppermute(tail, axis, [(i, (i + 1) % count) for i in range(ends)])  23.5 us
    ppermute x6, waiting for transfers between devices, extended(): lax.ppermute(tail, axis, [(i, (i + 1) % count) for i in range(ends)])  22.9 us
    dot_general x2, matrix products, column_term(): lax.dot_general(matrix, grads, (((0,), (0,)), ((), ())), preferred_elemen...  15.6 us
    dot_general x3, matrix products, apply_operator(): jnp.einsum('xynm,xymh->xynh', selfs, centre, preferred_element_type=jnp.f...  12.9 us
    dot_general x2, matrix products, apply_operator(): jnp.einsum('xymn,xymh->xynh', south, padded[1:-1, :-2], preferred_element...  12 us
    dot_general x3, matrix products, apply_operator(): jnp.einsum('xynm,xymh->xynh', north, padded[1:-1, 2:], preferred_element_...  8.55 us
  transfers between devices with their start and end apart: 16, of which 5 were waited for; matrix products, arithmetic and copies ran while one was open for 30% of the time, Pallas kernels for 0%

commit v1 on v0

v1 whole, which is shorter than its diff:
```python
import functools

import jax
import jax.numpy as jnp
import numpy as np
from jax import lax
from jax.experimental import pallas as pl
from jax.experimental.pallas import tpu as pltpu
from jax.sharding import PartitionSpec as P

F32 = jnp.float32
BF16 = jnp.bfloat16
AXES = ("wide", "narrow")
VMEM_LIMIT = 40 * 1024 * 1024
ANY = pl.BlockSpec(memory_space=pl.ANY)
VMEM = pl.BlockSpec(memory_space=pltpu.VMEM)
SMEM = pl.BlockSpec(memory_space=pltpu.SMEM)

SELF, EAST, WEST, NORTH, SOUTH, FLAGS = 0, 1, 2, 3, 4, 5


def routes(wide):
    depth = wide // 2

    def at(z, y, c):
        return (2 * z + y) * 2 + c

    every = [(z, y, c) for z in range(depth) for y in range(2) for c in range(2)]
    swap = [(at(z, c, y), at(z, y, c)) for z, y, c in every if y != c]
    first_side = [(at(z, c, 1 - y), at(z, y, c)) for z, y, c in every]
    inner = [(at(z, y, 1 - c), at(z, y, c)) for z, y, c in every]
    outer = [(at(z - 1, y, 1), at(z, y, 0)) for z, y, c in every if c == 0 and z > 0]
    outer += [(at(z + 1, y, 0), at(z, y, 1)) for z, y, c in every if c == 1 and z + 1 < depth]
    side = [(at(z, 1 - y, c), at(z, y, c)) for z, y, c in every]
    above = [(at(z, 0, y), at(z, y, 1)) for z, y, c in every if c == 1]
    above += [(at(z - 1, 1, y), at(z, y, 0)) for z, y, c in every if c == 0 and z > 0]
    left = [(at(z, c, 0), at(z, y, c)) for z, y, c in every if y == 1]
    return swap, first_side, inner, outer, side, above, left


def block_product(table, field, tiles, turned, row, col, rows, cols):
    at = row * cols + col
    step = rows * cols
    own = table[SELF * step + at]
    lhs = jnp.concatenate(
        [
            tiles[own],
            turned[own],
            tiles[table[EAST * step + at]],
            turned[table[WEST * step + at]],
            tiles[table[NORTH * step + at]],
            turned[table[SOUTH * step + at]],
        ],
        axis=1,
    )
    centre = field[row + 1, col + 1]
    rhs = jnp.concatenate(
        [
            centre,
            centre,
            field[row + 2, col + 1],
            field[row, col + 1],
            field[row + 1, col + 2],
            field[row + 1, col],
        ],
        axis=0,
    )
    return lax.dot_general(lhs, rhs, (((1,), (0,)), ((), ())), preferred_element_type=F32)


def rim_copies(table, field, inner, outer, side, sems, rows, cols):
    base = FLAGS * rows * cols
    low, right = table[base + 1], table[base + 2]
    bottom, end = rows + 1, cols + 1
    zero_col = jnp.where(right == 0, 0, end)
    side_col = jnp.where(right == 0, end, 0)
    for row in range(1, rows + 1):
        field[row, zero_col] = jnp.zeros(field.shape[2:], field.dtype)
    return [
        pltpu.make_async_copy(inner, field.at[jnp.where(low == 0, bottom, 0), pl.ds(1, cols)], sems.at[0]),
        pltpu.make_async_copy(outer, field.at[jnp.where(low == 0, 0, bottom), pl.ds(1, cols)], sems.at[1]),
        pltpu.make_async_copy(side, field.at[pl.ds(1, rows), side_col], sems.at[2]),
    ]


def edge_copies(table, done, inner, outer, side, sems, rows, cols):
    base = FLAGS * rows * cols
    low, right = table[base + 1], table[base + 2]
    return [
        pltpu.make_async_copy(done.at[jnp.where(low == 0, rows - 1, 0)], inner, sems.at[3]),
        pltpu.make_async_copy(done.at[jnp.where(low == 0, 0, rows - 1)], outer, sems.at[4]),
        pltpu.make_async_copy(done.at[:, jnp.where(right == 0, cols - 1, 0)], side, sems.at[5]),
    ]


def first_kernel(rows, cols, table, own, ends, middle, inner, outer, side, tiles, turned, weight,
                 x_out, m_out, inner_out, outer_out, side_out, field, x_new, m_new, sems):
    nodes, width = own.shape[2], own.shape[3]
    moving = table[FLAGS * rows * cols]
    inside = pl.ds(1, cols)
    copies = rim_copies(table, field, inner, outer, side, sems, rows, cols)
    for copy in copies:
        copy.start()

    @pl.when(moving == 0)
    def _():
        copy = pltpu.make_async_copy(own, field.at[pl.ds(1, rows), inside], sems.at[6])
        copy.start()
        copy.wait()

    @pl.when(moving != 0)
    def _():
        parts = [
            pltpu.make_async_copy(ends.at[0], field.at[1, inside], sems.at[6]),
            pltpu.make_async_copy(ends.at[1], field.at[rows, inside], sems.at[7]),
            pltpu.make_async_copy(middle, field.at[pl.ds(2, rows - 2), inside], sems.at[8]),
        ]
        for part in parts:
            part.start()
        for part in parts:
            part.wait()

    for copy in copies:
        copy.wait()

    def one_row(row, carry):
        for col in range(cols):
            m_new[row, col] = block_product(table, field, tiles, turned, row, col, rows, cols).astype(BF16)
        for col in range(0, cols, 2):
            m_part = m_new[row, pl.ds(col, 2)].reshape(2 * nodes, width)
            z = jnp.dot(m_part, weight[...], preferred_element_type=F32)
            base = field[row + 1, pl.ds(1 + col, 2)].reshape(2 * nodes, width)
            x_new[row, pl.ds(col, 2)] = (base.astype(F32) + jnp.tanh(z)).astype(BF16).reshape(2, nodes, width)
        return carry

    lax.fori_loop(0, rows, one_row, 0)
    outs = edge_copies(table, x_new, inner_out, outer_out, side_out, sems, rows, cols)
    outs += [
        pltpu.make_async_copy(x_new, x_out, sems.at[0]),
        pltpu.make_async_copy(m_new, m_out, sems.at[1]),
    ]
    for copy in outs:
        copy.start()
    for copy in outs:
        copy.wait()


def second_kernel(rows, cols, scale, table, x_own, inner, outer, side, tiles, turned, weight, readout,
                  spread, target, g_out, inner_out, outer_out, side_out, pred_out, second_out, readout_out,
                  field, g_new, m_row, gz_row, sems):
    nodes, width = x_own.shape[2], x_own.shape[3]
    copies = rim_copies(table, field, inner, outer, side, sems, rows, cols)
    copies.append(pltpu.make_async_copy(x_own, field.at[pl.ds(1, rows), pl.ds(1, cols)], sems.at[6]))
    for copy in copies:
        copy.start()
    for copy in copies:
        copy.wait()
    readf = readout[...]
    lanes = lax.broadcasted_iota(jnp.int32, (nodes, 128), 1)
    second_out[...] = jnp.zeros_like(second_out)
    readout_out[...] = jnp.zeros_like(readout_out)

    def one_row(row, carry):
        goal = target[row].T
        seen = jnp.zeros((nodes, 128), F32)
        for col in range(cols):
            m_row[col] = block_product(table, field, tiles, turned, row, col, rows, cols).astype(BF16)
        for col in range(cols):
            z = jnp.dot(m_row[col], weight[...], preferred_element_type=F32)
            t = jnp.tanh(z)
            x = (field[row + 1, col + 1].astype(F32) + t).astype(BF16)
            pred = jnp.dot(x, spread[...], preferred_element_type=F32)
            seen = jnp.where(lanes == col, pred, seen)
            gp = (pred[:, 0:1] - goal[:, col : col + 1]) * scale
            part = x.astype(F32) * gp
            readout_out[...] += part.reshape(nodes // 8, 8, width).sum(axis=0)
            gz = (gp * readf * (1.0 - t * t)).astype(BF16)
            gz_row[col] = gz
            g_new[row, col] = lax.dot_general(
                gz, weight[...], (((1,), (1,)), ((), ())), preferred_element_type=F32
            ).astype(BF16)
        second_out[...] += lax.dot_general(
            m_row[...].reshape(cols * nodes, width), gz_row[...].reshape(cols * nodes, width),
            (((0,), (0,)), ((), ())), preferred_element_type=F32,
        )
        pred_out[row] = seen.T[0:cols]
        return carry

    lax.fori_loop(0, rows, one_row, 0)
    outs = edge_copies(table, g_new, inner_out, outer_out, side_out, sems, rows, cols)
    outs.append(pltpu.make_async_copy(g_new, g_out, sems.at[0]))
    for copy in outs:
        copy.start()
    for copy in outs:
        copy.wait()


def third_kernel(rows, cols, scale, table, g_own, inner, outer, side, tiles, turned, m_own, weight, readout,
                 pred, target, first_out, field, m_in, gz_row, sems):
    nodes, width = g_own.shape[2], g_own.shape[3]
    copies = rim_copies(table, field, inner, outer, side, sems, rows, cols)
    copies.append(pltpu.make_async_copy(g_own, field.at[pl.ds(1, rows), pl.ds(1, cols)], sems.at[6]))
    copies.append(pltpu.make_async_copy(m_own, m_in, sems.at[7]))
    for copy in copies:
        copy.start()
    for copy in copies:
        copy.wait()
    readf = readout[...]
    first_out[...] = jnp.zeros_like(first_out)

    def one_row(row, carry):
        gp_all = ((pred[row] - target[row]) * scale).T
        for col in range(cols):
            gx = gp_all[:, col : col + 1] * readf
            gx = gx + block_product(table, field, tiles, turned, row, col, rows, cols)
            t = jnp.tanh(jnp.dot(m_in[row, col], weight[...], preferred_element_type=F32))
            gz_row[col] = (gx * (1.0 - t * t)).astype(BF16)
        first_out[...] += lax.dot_general(
            m_in[row].reshape(cols * nodes, width), gz_row[...].reshape(cols * nodes, width),
            (((0,), (0,)), ((), ())), preferred_element_type=F32,
        )
        return carry

    lax.fori_loop(0, rows, one_row, 0)


def sum_shares(slots, extra, count):
    place = lax.axis_index(AXES)
    bit = 1
    while bit < count:
        route = [(i, i ^ bit) for i in range(count)]
        mine = (place // bit) % 2
        pairs = slots.reshape(slots.shape[0] // 2, 2, *slots.shape[1:])
        keep = lax.dynamic_index_in_dim(pairs, mine, 1, keepdims=False)
        send = lax.dynamic_index_in_dim(pairs, 1 - mine, 1, keepdims=False)
        load = jnp.concatenate([send.reshape(-1, send.shape[-1]), extra], axis=0)
        got = lax.ppermute(load, AXES, route)
        cut = load.shape[0] - extra.shape[0]
        slots = keep + got[:cut].reshape(keep.shape)
        extra = extra + got[cut:]
        bit *= 2
    return slots[0], extra


def per_device(features, tile_ids, tiles, w_first, w_second, readout, target):
    rows, cols, nodes, width = features.shape
    wide, narrow = lax.axis_size("wide"), lax.axis_size("narrow")
    count = wide * narrow
    swap, first_side, inner_way, outer_way, side_way, above_way, left_way = routes(wide)
    y = lax.axis_index("wide") % 2
    c = lax.axis_index("narrow")
    moving = (y != c).astype(jnp.int32)
    scale = float(np.sqrt(np.float32(width) / np.float32(rows * cols * nodes * count)))

    def send(value, way):
        return lax.ppermute(value, AXES, way)

    def edges(inner, outer, side):
        return send(inner, inner_way), send(outer, outer_way), send(side, side_way)

    ends = send(jnp.concatenate([features[0:1], features[rows - 1 : rows]], axis=0), swap)
    side = send(jnp.where(c == 1, features[:, 0], features[:, cols - 1]), first_side)
    middle = send(features[1 : rows - 1], swap)
    ids_swap = send(tile_ids, swap)
    above_ids = send(tile_ids[rows - 1, :, 1], above_way)
    left_ids = send(tile_ids[:, cols - 1, 2], left_way)
    goal_swap = send(target, swap)

    ids = jnp.where(moving == 1, ids_swap, tile_ids)
    goal = jnp.where(moving == 1, goal_swap, target)
    west = jnp.concatenate([above_ids[None], ids[: rows - 1, :, 1]], axis=0)
    south = jnp.concatenate([left_ids[:, None], ids[:, : cols - 1, 2]], axis=1)
    table = jnp.concatenate(
        [
            jnp.stack([ids[:, :, 0], ids[:, :, 1], west, ids[:, :, 2], south]).reshape(-1),
            jnp.stack([moving, c, y]).astype(jnp.int32),
        ]
    )
    turned = jnp.swapaxes(tiles, 1, 2)
    readf = readout.astype(F32)[None]
    spread = jnp.broadcast_to(readout[:, None], (width, 128))

    top = jnp.where(moving == 1, ends[0], features[0])
    low = jnp.where(moving == 1, ends[1], features[rows - 1])
    inner = send(jnp.where(c == 0, low, top), inner_way)
    outer = send(jnp.where(c == 0, top, low), outer_way)

    patch = jax.ShapeDtypeStruct(features.shape, BF16)
    line = jax.ShapeDtypeStruct((cols, nodes, width), BF16)
    column = jax.ShapeDtypeStruct((rows, nodes, width), BF16)
    square = jax.ShapeDtypeStruct((width, width), F32)
    rim = pltpu.VMEM((rows + 2, cols + 2, nodes, width), BF16)
    whole = pltpu.VMEM(features.shape, BF16)
    strip = pltpu.VMEM((cols, nodes, width), BF16)
    sems = pltpu.SemaphoreType.DMA((9,))
    params = pltpu.CompilerParams(vmem_limit_bytes=VMEM_LIMIT)
    product = 2 * rows * cols * nodes * width * (6 * nodes)
    dense = 2 * rows * cols * nodes * width * width
    moved = features.size * 2

    x_one, m_one, inner_s, outer_s, side_s = pl.pallas_call(
        functools.partial(first_kernel, rows, cols),
        out_shape=(patch, patch, line, line, column),
        in_specs=[SMEM] + [ANY] * 6 + [VMEM] * 3,
        out_specs=(ANY,) * 5,
        scratch_shapes=[rim, whole, whole, sems],
        compiler_params=params,
        cost_estimate=pl.CostEstimate(flops=product + dense, bytes_accessed=4 * moved, transcendentals=features.size),
        name="layer_one",
    )(table, features, ends, middle, inner, outer, side, tiles, turned, w_first)

    inner, outer, side = edges(inner_s, outer_s, side_s)
    g_two, inner_s, outer_s, side_s, pred, second, readout_part = pl.pallas_call(
        functools.partial(second_kernel, rows, cols, scale),
        out_shape=(patch, line, line, column, jax.ShapeDtypeStruct(target.shape, F32), square,
                   jax.ShapeDtypeStruct((8, width), F32)),
        in_specs=[SMEM] + [ANY] * 4 + [VMEM] * 6,
        out_specs=(ANY,) * 4 + (VMEM,) * 3,
        scratch_shapes=[rim, whole, strip, strip, sems],
        compiler_params=params,
        cost_estimate=pl.CostEstimate(flops=product + 3 * dense, bytes_accessed=3 * moved, transcendentals=features.size),
        name="layer_two",
    )(table, x_one, inner, outer, side, tiles, turned, w_second, readf, spread, goal)

    inner, outer, side = edges(inner_s, outer_s, side_s)
    first = pl.pallas_call(
        functools.partial(third_kernel, rows, cols, scale),
        out_shape=square,
        in_specs=[SMEM] + [ANY] * 4 + [VMEM] * 2 + [ANY] + [VMEM] * 4,
        out_specs=VMEM,
        scratch_shapes=[rim, whole, strip, sems],
        compiler_params=params,
        cost_estimate=pl.CostEstimate(flops=product + 2 * dense, bytes_accessed=3 * moved, transcendentals=features.size),
        name="layer_one_back",
    )(table, g_two, inner, outer, side, tiles, turned, m_one, w_first, readf, pred, goal)

    share = width // count
    slots = jnp.concatenate([first.reshape(count, share, width), second.reshape(count, share, width)], axis=1)
    mine, extra = sum_shares(slots, readout_part, count)
    pred = jnp.where(moving == 1, send(pred, swap), pred)
    return pred, mine[:share], mine[share:], extra.sum(axis=0)


def solution(mesh):
    in_specs = (
        P(("groups", "wide"), "narrow", None, None),
        P(("groups", "wide"), "narrow", None),
        P(),
        P(),
        P(),
        P(),
        P(("groups", "wide"), "narrow", None),
    )
    out_specs = (
        P(("groups", "wide"), "narrow", None),
        P(("groups", "wide", "narrow"), None),
        P(("groups", "wide", "narrow"), None),
        P("groups"),
    )
    return jax.shard_map(
        per_device, mesh=mesh, in_specs=in_specs, out_specs=out_specs, check_vma=False
    )
```

time: 257 us -> 117 us (0.46)
  matrix products: 78 us -> 0 us
  waiting for transfers between devices: 65.9 us -> 20 us
  blocking collectives: 31.6 us -> 0 us
  Pallas kernels: 0 us -> 20.9 us
  starting transfers between devices: 37.9 us -> 52.1 us
  between operations: 14.6 us -> 1.05 us
  local copies, waits for them, and re-layouts: 26.4 us -> 16 us
  other arithmetic: 1.37 us -> 5.81 us
    dot_general x24 -> x0, matrix products: 78 us -> none  [the longest x2 15.6 us: column_term(): lax.dot_general(matrix, grads, (((0,), (0,)), ((), ())), preferred_elemen...]
    reduce_scatter x2 -> x0, waiting for transfers between devices: 35.9 us -> none  [the longest x1 35.9 us: per_device(): lax.psum_scatter(column_term(m_one_flat, gz_one_flat), ('wide', 'narrow')...]
    psum x1 -> x0, blocking collectives: 31.6 us -> none  [per_device(): grad_readout = lax.psum(local_readout, ('wide', 'narrow'))]
    pallas_call x0 -> x3, Pallas kernels: none -> 20.9 us  [the longest x1 10 us: per_device(): pl.pallas_call(functools.partial(second_kernel, rows, cols, scale), out_s...]
    gather x8 -> x0, local copies, waits for them, and re-layouts: 15.1 us -> none  [the longest x2 3.93 us: apply_operator(): west = jnp.take(tiles, west_ids, axis=0)]
    ppermute x14 -> x20, starting transfers between devices: 37.8 us -> 52.1 us  [the longest x16 42.8 us: send(): return lax.ppermute(value, AXES, way)]
    ppermute x14 -> x20, waiting for transfers between devices: 30 us -> 20 us  [the longest x16 10.1 us: send(): return lax.ppermute(value, AXES, way)]
    unnamed x75 -> x36, local copies, waits for them, and re-layouts: 4 us -> 10.1 us
  transfers between devices with their start and end apart: 16 -> 20, of which waited for: 5 -> 6; matrix products, arithmetic and copies ran while one was open for 30% -> 11% of each run, Pallas kernels for 0% -> 0%
where the time goes in v1:
time: 117 us; the launch traced here: 116 us
  starting transfers between devices  52.1 us (45%)
  Pallas kernels  20.9 us (18%)
  waiting for transfers between devices  20 us (17%)
  local copies, waits for them, and re-layouts  16 us (14%)
  other arithmetic  5.81 us (5%)
    ppermute x16, starting transfers between devices, send(): return lax.ppermute(value, AXES, way)  42.8 us
    unnamed x36, local copies, waits for them, and re-layouts  10.1 us
    ppermute x16, waiting for transfers between devices, send(): return lax.ppermute(value, AXES, way)  10.1 us
    pallas_call x1, Pallas kernels, per_device(): pl.pallas_call(functools.partial(second_kernel, rows, cols, scale), out_s...  10 us
    ppermute x4, waiting for transfers between devices, sum_shares(): got = lax.ppermute(load, AXES, route)  9.92 us
    ppermute x4, starting transfers between devices, sum_shares(): got = lax.ppermute(load, AXES, route)  9.35 us
    pallas_call x1, Pallas kernels, per_device(): pl.pallas_call(functools.partial(third_kernel, rows, cols, scale), out_sh...  5.66 us
    pallas_call x1, Pallas kernels, per_device(): pl.pallas_call(functools.partial(first_kernel, rows, cols), out_shape=(pa...  5.2 us
  transfers between devices with their start and end apart: 20, of which 6 were waited for; matrix products, arithmetic and copies ran while one was open for 11% of the time, Pallas kernels for 0%

profile of v1, /device:TPU:0, one launch (start us, length us, event | category | flops | bytes accessed | tf_op | source)
XLA Modules:
  0.0 115.9 jit_solution(8690131609019823901)
XLA Ops:
  0.6 1.2 %collective-permute-start = (s32[4,8,3]{1,0,2:T(4,128)}, s32[4,8,3]{1,0,2:T(4,128)}, u32[]{:S(2)}, u32[]{:S(2)}) collective-permute-start(s32[4,8,3]{1,0,2:T(4,128)} %param.8), channel_id=1, source_target_pairs={{2,1},{1,2},{6,5},{5,6},{10,9},{9,10},{14,13},{13,14},{18,17},{17,... | collective-permute-start | bytes 1160 | tf_op jit(solution)/shard_map/ppermute | solution.py:256
  1.9 1.2 %slice_bitcast_fusion.7 = s32[8]{0:T(128)} fusion(s32[4,8,3]{1,0,2:T(4,128)} %param.8), kind=kLoop, calls=%fused_computation.50 | loop fusion | bytes 64 | tf_op jit(solution)/shard_map/squeeze | solution.py:265
  3.1 6.2 %collective-permute-start.1 = (s32[8]{0:T(128)}, s32[8]{0:T(128)}, u32[]{:S(2)}, u32[]{:S(2)}) collective-permute-start(s32[8]{0:T(128)} %slice_bitcast_fusion.7), channel_id=1, source_target_pairs={{0,1},{1,3},{4,5},{5,7},{8,9},{9,11},{12,13},{13,15},{2,4},{3,6},{... | collective-permute-start | bytes 104 | tf_op jit(solution)/shard_map/ppermute | solution.py:256
  10.2 2.8 %collective-permute-start.2 = (s32[4]{0:T(128)S(1)}, s32[4]{0:T(128)S(1)}, u32[]{:S(2)}, u32[]{:S(2)}) collective-permute-start(s32[4]{0:T(128)S(1)} %slice_reduce_fusion), channel_id=1, source_target_pairs={{0,2},{2,3},{4,6},{6,7},{8,10},{10,11},{12,14},{14,15},{16,18},{18... | collective-permute-start | bytes 56 | tf_op jit(solution)/shard_map/ppermute | solution.py:256
  12.9 1.3 %fusion.5 = (bf16[1,8,128,256]{3,2,1,0:T(8,128)(2,1)S(1)}, bf16[1,8,128,256]{3,2,1,0:T(8,128)(2,1)S(1)}) fusion(bf16[4,8,128,256]{3,2,1,0:T(8,128)(2,1)} %own.1), kind=kLoop, calls=%fused_computation.51 | loop fusion | bytes 2097152 | tf_op jit(solution)/shard_map/slice | solution.py:261
  16.9 1.5 %collective-permute-start.7 = (bf16[4,128,256]{2,1,0:T(8,128)(2,1)}, bf16[4,128,256]{2,1,0:T(8,128)(2,1)S(1)}, u32[]{:S(2)}, u32[]{:S(2)}) collective-permute-start(bf16[4,128,256]{2,1,0:T(8,128)(2,1)} %fusion.2), channel_id=1, source_target_pairs={{1,0},{3,1},{0,2},{2,3},{5,4},{7,5},{4,6},{6,7},{9,8},{11,9},{8,10... | collective-permute-start | bytes 786440 | tf_op jit(solution)/shard_map/ppermute | solution.py:256
  19.4 2.1 %copy.20 = bf16[16,128,128]{1,2,0:T(8,128)(2,1)} copy(bf16[16,128,128]{2,1,0:T(8,128)(2,1)} %tiles.5) | data formatting | bytes 1048576 | tf_op args[2]
  21.5 1.6 %collective-permute-start.4 = (bf16[2,8,128,256]{3,2,1,0:T(8,128)(2,1)}, bf16[2,8,128,256]{3,2,1,0:T(8,128)(2,1)}, u32[]{:S(2)}, u32[]{:S(2)}) collective-permute-start(bf16[2,8,128,256]{3,2,1,0:T(8,128)(2,1)} %slice.89), channel_id=1, source_target_pairs={{2,1},{1,2},{6,5},{5,6},{10,9},{9,10},{14,13},{13,14},{18,17},{17,... | collective-permute-start | bytes 3145736 | tf_op jit(solution)/shard_map/ppermute | solution.py:256
  24.4 9.9 %collective-permute-start.5 = (bf16[8,128,256]{2,1,0:T(8,128)(2,1)}, bf16[8,128,256]{2,1,0:T(8,128)(2,1)}, u32[]{:S(2)}, u32[]{:S(2)}) collective-permute-start(bf16[8,128,256]{2,1,0:T(8,128)(2,1)} %get-tuple-element.29), channel_id=1, source_target_pairs={{1,0},{0,1},{3,2},{2,3},{5,4},{4,5},{7,6},{6,7},{9,8},{8,9},{11,10... | collective-permute-start | bytes 1572872 | tf_op jit(solution)/shard_map/ppermute | solution.py:256
  34.4 1.5 %collective-permute-start.6 = (bf16[8,128,256]{2,1,0:T(8,128)(2,1)}, bf16[8,128,256]{2,1,0:T(8,128)(2,1)}, u32[]{:S(2)}, u32[]{:S(2)}) collective-permute-start(bf16[8,128,256]{2,1,0:T(8,128)(2,1)} %get-tuple-element.28), channel_id=1, source_target_pairs={{1,4},{3,6},{5,8},{7,10},{9,12},{11,14},{4,1},{6,3},{8,5},{10,7},{... | collective-permute-start | bytes 1572872 | tf_op jit(solution)/shard_map/ppermute | solution.py:256
  40.1 5.2 %layer_one.1 = (bf16[4,8,128,256]{3,2,1,0:T(8,128)(2,1)S(1)}, bf16[4,8,128,256]{3,2,1,0:T(8,128)(2,1)S(1)}, bf16[8,128,256]{2,1,0:T(8,128)(2,1)S(1)}, bf16[8,128...) custom-call(s32[163]{0:T(256)S(1)} %pad_add_fusion.table, bf16[4,8,128,256]{3,2,1,0:T(8,128)(2,1)S(1)} %copy-done, ...), custom_call_target="tpu_custom_call" | custom-call | flops 2147483648 | bytes 8388608 | tf_op jit(solution)/shard_map/layer_one/pallas_call | solution.py:301
  45.4 1.3 %copy-done.9 = bf16[4,8,128,256]{3,2,1,0:T(8,128)(2,1)} copy-done((bf16[4,8,128,256]{3,2,1,0:T(8,128)(2,1)}, bf16[4,8,128,256]{3,2,1,0:T(8,128)(2,1)S(1)}, u32[]{:S(2)}) %copy-start.9) | copy-done | bytes 2097176
  46.7 7.5 %collective-permute-start.8 = (bf16[8,128,256]{2,1,0:T(8,128)(2,1)S(1)}, bf16[8,128,256]{2,1,0:T(8,128)(2,1)S(1)}, u32[]{:S(2)}, u32[]{:S(2)}) collective-permute-start(bf16[8,128,256]{2,1,0:T(8,128)(2,1)S(1)} %get-tuple-element.17), channel_id=1, source_target_pairs={{1,0},{0,1},{3,2},{2,3},{5,4},{4,5},{7,6},{6,7},{9,8},{8,9},{11,10... | collective-permute-start | bytes 1572872 | tf_op jit(solution)/shard_map/ppermute | solution.py:256
  54.9 1.8 %collective-permute-start.10 = (bf16[4,128,256]{2,1,0:T(8,128)(2,1)S(1)}, bf16[4,128,256]{2,1,0:T(8,128)(2,1)S(1)}, u32[]{:S(2)}, u32[]{:S(2)}) collective-permute-start(bf16[4,128,256]{2,1,0:T(8,128)(2,1)S(1)} %get-tuple-element.19), channel_id=1, source_target_pairs={{2,0},{3,1},{0,2},{1,3},{6,4},{7,5},{4,6},{5,7},{10,8},{11,9},{8,1... | collective-permute-start | bytes 786440 | tf_op jit(solution)/shard_map/ppermute | solution.py:256
  57.4 4.6 %collective-permute-done.10.side = bf16[4,128,256]{2,1,0:T(8,128)(2,1)S(1)} collective-permute-done((bf16[4,128,256]{2,1,0:T(8,128)(2,1)S(1)}, bf16[4,128,256]{2,1,0:T(8,128)(2,1)S(1)}, u32[]{:S(2)}, u32[]{:S(2)}) %collective-permute-start.10) | collective-permute-done | bytes 262176 | tf_op jit(solution)/shard_map/ppermute | solution.py:256
  62.2 10.0 %layer_two.1 = (bf16[4,8,128,256]{3,2,1,0:T(8,128)(2,1)S(1)}, bf16[8,128,256]{2,1,0:T(8,128)(2,1)S(1)}, bf16[8,128,256]{2,1,0:T(8,128)(2,1)S(1)}, bf16[4,128,256...) custom-call(s32[163]{0:T(256)S(1)} %pad_add_fusion.table, ...), custom_call_target="tpu_custom_call" | custom-call | flops 3221225472 | bytes 6291456 | tf_op jit(solution)/shard_map/layer_two/pallas_call | solution.py:313
  72.2 1.3 %copy-done.11 = bf16[4,8,128,256]{3,2,1,0:T(8,128)(2,1)} copy-done((bf16[4,8,128,256]{3,2,1,0:T(8,128)(2,1)}, bf16[4,8,128,256]{3,2,1,0:T(8,128)(2,1)S(1)}, u32[]{:S(2)}) %copy-start.11) | copy-done | bytes 2097176
  73.6 2.7 %collective-permute-start.13 = (bf16[8,128,256]{2,1,0:T(8,128)(2,1)S(1)}, bf16[8,128,256]{2,1,0:T(8,128)(2,1)S(1)}, u32[]{:S(2)}, u32[]{:S(2)}) collective-permute-start(bf16[8,128,256]{2,1,0:T(8,128)(2,1)S(1)} %get-tuple-element.22), channel_id=1, source_target_pairs={{1,0},{0,1},{3,2},{2,3},{5,4},{4,5},{7,6},{6,7},{9,8},{8,9},{11,10... | collective-permute-start | bytes 1572872 | tf_op jit(solution)/shard_map/ppermute | solution.py:256
  76.3 1.5 %collective-permute-start.14 = (bf16[8,128,256]{2,1,0:T(8,128)(2,1)S(1)}, bf16[8,128,256]{2,1,0:T(8,128)(2,1)}, u32[]{:S(2)}, u32[]{:S(2)}) collective-permute-start(bf16[8,128,256]{2,1,0:T(8,128)(2,1)S(1)} %get-tuple-element.23), channel_id=1, source_target_pairs={{1,4},{3,6},{5,8},{7,10},{9,12},{11,14},{4,1},{6,3},{8,5},{10,7},{... | collective-permute-start | bytes 1572872 | tf_op jit(solution)/shard_map/ppermute | solution.py:256
  77.8 1.7 %collective-permute-start.15 = (bf16[4,128,256]{2,1,0:T(8,128)(2,1)S(1)}, bf16[4,128,256]{2,1,0:T(8,128)(2,1)}, u32[]{:S(2)}, u32[]{:S(2)}) collective-permute-start(bf16[4,128,256]{2,1,0:T(8,128)(2,1)S(1)} %get-tuple-element.24), channel_id=1, source_target_pairs={{2,0},{3,1},{0,2},{1,3},{6,4},{7,5},{4,6},{5,7},{10,8},{11,9},{8,1... | collective-permute-start | bytes 786440 | tf_op jit(solution)/shard_map/ppermute | solution.py:256
  79.5 5.4 %collective-permute-done.15.side = bf16[4,128,256]{2,1,0:T(8,128)(2,1)} collective-permute-done((bf16[4,128,256]{2,1,0:T(8,128)(2,1)S(1)}, bf16[4,128,256]{2,1,0:T(8,128)(2,1)}, u32[]{:S(2)}, u32[]{:S(2)}) %collective-permute-start.15) | collective-permute-done | bytes 262176 | tf_op jit(solution)/shard_map/ppermute | solution.py:256
  84.9 1.6 %copy-done.10 = bf16[4,8,128,256]{3,2,1,0:T(8,128)(2,1)S(1)} copy-done((bf16[4,8,128,256]{3,2,1,0:T(8,128)(2,1)S(1)}, bf16[4,8,128,256]{3,2,1,0:T(8,128)(2,1)}, u32[]{:S(2)}) %copy-start.10) | copy-done | bytes 2097176
  86.5 1.6 %copy-done.12 = bf16[4,8,128,256]{3,2,1,0:T(8,128)(2,1)S(1)} copy-done((bf16[4,8,128,256]{3,2,1,0:T(8,128)(2,1)S(1)}, bf16[4,8,128,256]{3,2,1,0:T(8,128)(2,1)}, u32[]{:S(2)}) %copy-start.12) | copy-done | bytes 2097176
  88.1 5.7 %layer_one_back.1 = f32[256,256]{1,0:T(8,128)S(1)} custom-call(s32[163]{0:T(256)S(1)} %pad_add_fusion.table, bf16[4,8,128,256]{3,2,1,0:T(8,128)(2,1)S(1)} %copy-done.12, bf16[8,128,256]{2,1,0:T(8,128)(2,1)S(1)} %collective-permute-done.13.inner, bf16[8,128,256]{2,1,0:T(8,128)(2,1)} %collective-permute-done.14.outer, ...), custom_call_target="tpu_custom_call" | custom-call | flops 2684354560 | bytes 6291456 | tf_op jit(solution)/shard_map/layer_one_back/pallas_call | solution.py:326
  93.9 2.7 %collective-permute-start.16 = (f32[264,256]{1,0:T(8,128)S(1)}, f32[264,256]{1,0:T(8,128)S(1)}, u32[]{:S(2)}, u32[]{:S(2)}) collective-permute-start(f32[264,256]{1,0:T(8,128)S(1)} %pad_maximum_fusion.1), channel_id=1, source_target_pairs={{0,1},{1,0},{2,3},{3,2},{4,5},{5,4},{6,7},{7,6},{8,9},{9,8},{10,11... | collective-permute-start | bytes 811016 | tf_op jit(solution)/shard_map/ppermute | solution.py:237
  96.6 1.2 %collective-permute-done.16 = f32[264,256]{1,0:T(8,128)S(1)} collective-permute-done((f32[264,256]{1,0:T(8,128)S(1)}, f32[264,256]{1,0:T(8,128)S(1)}, u32[]{:S(2)}, u32[]{:S(2)}) %collective-permute-start.16) | collective-permute-done | bytes 270368 | tf_op jit(solution)/shard_map/ppermute | solution.py:237
  97.9 2.0 %collective-permute-start.17 = (f32[136,256]{1,0:T(8,128)S(1)}, f32[136,256]{1,0:T(8,128)S(1)}, u32[]{:S(2)}, u32[]{:S(2)}) collective-permute-start(f32[136,256]{1,0:T(8,128)S(1)} %pad_maximum_fusion.2), channel_id=1, source_target_pairs={{0,2},{1,3},{2,0},{3,1},{4,6},{5,7},{6,4},{7,5},{8,10},{9,11},{10,... | collective-permute-start | bytes 417800 | tf_op jit(solution)/shard_map/ppermute | solution.py:237
  99.9 4.2 %collective-permute-done.17 = f32[136,256]{1,0:T(8,128)S(1)} collective-permute-done((f32[136,256]{1,0:T(8,128)S(1)}, f32[136,256]{1,0:T(8,128)S(1)}, u32[]{:S(2)}, u32[]{:S(2)}) %collective-permute-start.17) | collective-permute-done | bytes 139296 | tf_op jit(solution)/shard_map/ppermute | solution.py:237
  104.2 2.3 %collective-permute-start.18 = (f32[72,256]{1,0:T(8,128)S(1)}, f32[72,256]{1,0:T(8,128)S(1)}, u32[]{:S(2)}, u32[]{:S(2)}) collective-permute-start(f32[72,256]{1,0:T(8,128)S(1)} %pad_maximum_fusion.3), channel_id=1, source_target_pairs={{0,4},{1,5},{2,6},{3,7},{4,0},{5,1},{6,2},{7,3},{8,12},{9,13},{10,... | collective-permute-start | bytes 221192 | tf_op jit(solution)/shard_map/ppermute | solution.py:237
  107.2 1.7 %collective-permute-done.18 = f32[72,256]{1,0:T(8,128)S(1)} collective-permute-done((f32[72,256]{1,0:T(8,128)S(1)}, f32[72,256]{1,0:T(8,128)S(1)}, u32[]{:S(2)}, u32[]{:S(2)}) %collective-permute-start.18) | collective-permute-done | bytes 73760 | tf_op jit(solution)/shard_map/ppermute | solution.py:237
  108.9 2.3 %collective-permute-start.19 = (f32[40,256]{1,0:T(8,128)S(1)}, f32[40,256]{1,0:T(8,128)S(1)}, u32[]{:S(2)}, u32[]{:S(2)}) collective-permute-start(f32[40,256]{1,0:T(8,128)S(1)} %pad_maximum_fusion.4), channel_id=1, source_target_pairs={{0,8},{1,9},{2,10},{3,11},{4,12},{5,13},{6,14},{7,15},{8,0},{9,1},... | collective-permute-start | bytes 122888 | tf_op jit(solution)/shard_map/ppermute | solution.py:237
  111.8 2.9 %collective-permute-done.19 = f32[40,256]{1,0:T(8,128)S(1)} collective-permute-done((f32[40,256]{1,0:T(8,128)S(1)}, f32[40,256]{1,0:T(8,128)S(1)}, u32[]{:S(2)}, u32[]{:S(2)}) %collective-permute-start.19) | collective-permute-done | bytes 40992 | tf_op jit(solution)/shard_map/ppermute | solution.py:237
  (86 shorter events, 14.3 us)
Async XLA Ops:
  0.6 22.6 %collective-permute-start = (s32[4,8,3]{1,0,2:T(4,128)}, s32[4,8,3]{1,0,2:T(4,128)}, u32[]{:S(2)}, u32[]{:S(2)}) collective-permute-start(s32[4,8,3]{1,0,2:T(4,128)} %param.8), channel_id=1, source_target_pairs={{2,1},{1,2},{6,5},{5,6},{10,9},{9,10},{14,13},{13,14},{18,17},{17,... | collective-permute-start | bytes 1160 | tf_op jit(solution)/shard_map/ppermute | solution.py:256
  3.1 32.7 %collective-permute-start.1 = (s32[8]{0:T(128)}, s32[8]{0:T(128)}, u32[]{:S(2)}, u32[]{:S(2)}) collective-permute-start(s32[8]{0:T(128)} %slice_bitcast_fusion.7), channel_id=1, source_target_pairs={{0,1},{1,3},{4,5},{5,7},{8,9},{9,11},{12,13},{13,15},{2,4},{3,6},{... | collective-permute-start | bytes 104 | tf_op jit(solution)/shard_map/ppermute | solution.py:256
  10.2 6.0 %copy-start = (bf16[4,8,128,256]{3,2,1,0:T(8,128)(2,1)S(1)}, bf16[4,8,128,256]{3,2,1,0:T(8,128)(2,1)}, u32[]{:S(2)}) copy-start(bf16[4,8,128,256]{3,2,1,0:T(8,128)(2,1)} %own.1) | copy-start | bytes 6291460
  10.2 11.4 %collective-permute-start.2 = (s32[4]{0:T(128)S(1)}, s32[4]{0:T(128)S(1)}, u32[]{:S(2)}, u32[]{:S(2)}) collective-permute-start(s32[4]{0:T(128)S(1)} %slice_reduce_fusion), channel_id=1, source_target_pairs={{0,2},{2,3},{4,6},{6,7},{8,10},{10,11},{12,14},{14,15},{16,18},{18... | collective-permute-start | bytes 56 | tf_op jit(solution)/shard_map/ppermute | solution.py:256
  15.3 8.0 %copy-start.14 = (s32[4,8,3]{1,0,2:T(4,128)S(1)}, s32[4,8,3]{1,0,2:T(4,128)}, u32[]{:S(2)}) copy-start(s32[4,8,3]{1,0,2:T(4,128)} %param.8) | copy-start | bytes 1156
  15.3 8.0 %collective-permute-start.3 = (bf16[2,8,128,256]{3,2,1,0:T(8,128)(2,1)}, bf16[2,8,128,256]{3,2,1,0:T(8,128)(2,1)S(1)}, u32[]{:S(2)}, u32[]{:S(2)}) collective-permute-start(bf16[2,8,128,256]{3,2,1,0:T(8,128)(2,1)} %pad_maximum_fusion), channel_id=1, source_target_pairs={{2,1},{1,2},{6,5},{5,6},{10,9},{9,10},{14,13},{13,14},{18,17},{17,... | collective-permute-start | bytes 3145736 | tf_op jit(solution)/shard_map/ppermute | solution.py:256
  16.9 21.1 %collective-permute-start.7 = (bf16[4,128,256]{2,1,0:T(8,128)(2,1)}, bf16[4,128,256]{2,1,0:T(8,128)(2,1)S(1)}, u32[]{:S(2)}, u32[]{:S(2)}) collective-permute-start(bf16[4,128,256]{2,1,0:T(8,128)(2,1)} %fusion.2), channel_id=1, source_target_pairs={{1,0},{3,1},{0,2},{2,3},{5,4},{7,5},{4,6},{6,7},{9,8},{11,9},{8,10... | collective-permute-start | bytes 786440 | tf_op jit(solution)/shard_map/ppermute | solution.py:256
  19.4 18.6 %copy-start.8 = (bf16[256,256]{1,0:T(8,128)(2,1)S(1)}, bf16[256,256]{1,0:T(8,128)(2,1)}, u32[]{:S(2)}) copy-start(bf16[256,256]{1,0:T(8,128)(2,1)} %weight.5) | copy-start | bytes 393220
  21.5 16.5 %collective-permute-start.4 = (bf16[2,8,128,256]{3,2,1,0:T(8,128)(2,1)}, bf16[2,8,128,256]{3,2,1,0:T(8,128)(2,1)}, u32[]{:S(2)}, u32[]{:S(2)}) collective-permute-start(bf16[2,8,128,256]{3,2,1,0:T(8,128)(2,1)} %slice.89), channel_id=1, source_target_pairs={{2,1},{1,2},{6,5},{5,6},{10,9},{9,10},{14,13},{13,14},{18,17},{17,... | collective-permute-start | bytes 3145736 | tf_op jit(solution)/shard_map/ppermute | solution.py:256
  24.4 13.6 %collective-permute-start.5 = (bf16[8,128,256]{2,1,0:T(8,128)(2,1)}, bf16[8,128,256]{2,1,0:T(8,128)(2,1)}, u32[]{:S(2)}, u32[]{:S(2)}) collective-permute-start(bf16[8,128,256]{2,1,0:T(8,128)(2,1)} %get-tuple-element.29), channel_id=1, source_target_pairs={{1,0},{0,1},{3,2},{2,3},{5,4},{4,5},{7,6},{6,7},{9,8},{8,9},{11,10... | collective-permute-start | bytes 1572872 | tf_op jit(solution)/shard_map/ppermute | solution.py:256
  34.4 3.7 %collective-permute-start.6 = (bf16[8,128,256]{2,1,0:T(8,128)(2,1)}, bf16[8,128,256]{2,1,0:T(8,128)(2,1)}, u32[]{:S(2)}, u32[]{:S(2)}) collective-permute-start(bf16[8,128,256]{2,1,0:T(8,128)(2,1)} %get-tuple-element.28), channel_id=1, source_target_pairs={{1,4},{3,6},{5,8},{7,10},{9,12},{11,14},{4,1},{6,3},{8,5},{10,7},{... | collective-permute-start | bytes 1572872 | tf_op jit(solution)/shard_map/ppermute | solution.py:256
  40.1 16.6 %copy-start.13 = (f32[4,8,128]{2,1,0:T(8,128)S(1)}, f32[4,8,128]{2,1,0:T(8,128)}, u32[]{:S(2)}) copy-start(f32[4,8,128]{2,1,0:T(8,128)} %param.13) | copy-start | bytes 49156
  40.1 17.2 %copy-start.15 = (bf16[256]{0:T(256)(128)(2,1)S(1)}, bf16[256]{0:T(256)(128)(2,1)}, u32[]{:S(2)}) copy-start(bf16[256]{0:T(256)(128)(2,1)} %param.12) | copy-start | bytes 1540
  40.1 22.0 %copy-start.2 = (bf16[16,128,128]{2,1,0:T(8,128)(2,1)S(1)}, bf16[16,128,128]{2,1,0:T(8,128)(2,1)}, u32[]{:S(2)}) copy-start(bf16[16,128,128]{2,1,0:T(8,128)(2,1)} %tiles.5) | copy-start | bytes 1572868
  40.1 22.0 %copy-start.5 = (bf16[16,128,128]{1,2,0:T(8,128)(2,1)S(1)}, bf16[16,128,128]{1,2,0:T(8,128)(2,1)}, u32[]{:S(2)}) copy-start(bf16[16,128,128]{1,2,0:T(8,128)(2,1)} %copy.20) | copy-start | bytes 1572868
  40.1 22.0 %copy-start.7 = (bf16[256,256]{1,0:T(8,128)(2,1)S(1)}, bf16[256,256]{1,0:T(8,128)(2,1)}, u32[]{:S(2)}) copy-start(bf16[256,256]{1,0:T(8,128)(2,1)} %weight.4) | copy-start | bytes 393220
  46.7 15.3 %collective-permute-start.8 = (bf16[8,128,256]{2,1,0:T(8,128)(2,1)S(1)}, bf16[8,128,256]{2,1,0:T(8,128)(2,1)S(1)}, u32[]{:S(2)}, u32[]{:S(2)}) collective-permute-start(bf16[8,128,256]{2,1,0:T(8,128)(2,1)S(1)} %get-tuple-element.17), channel_id=1, source_target_pairs={{1,0},{0,1},{3,2},{2,3},{5,4},{4,5},{7,6},{6,7},{9,8},{8,9},{11,10... | collective-permute-start | bytes 1572872 | tf_op jit(solution)/shard_map/ppermute | solution.py:256
  54.2 7.8 %collective-permute-start.9 = (bf16[8,128,256]{2,1,0:T(8,128)(2,1)S(1)}, bf16[8,128,256]{2,1,0:T(8,128)(2,1)S(1)}, u32[]{:S(2)}, u32[]{:S(2)}) collective-permute-start(bf16[8,128,256]{2,1,0:T(8,128)(2,1)S(1)} %get-tuple-element.18), channel_id=1, source_target_pairs={{1,4},{3,6},{5,8},{7,10},{9,12},{11,14},{4,1},{6,3},{8,5},{10,7},{... | collective-permute-start | bytes 1572872 | tf_op jit(solution)/shard_map/ppermute | solution.py:256
  54.9 7.1 %collective-permute-start.10 = (bf16[4,128,256]{2,1,0:T(8,128)(2,1)S(1)}, bf16[4,128,256]{2,1,0:T(8,128)(2,1)S(1)}, u32[]{:S(2)}, u32[]{:S(2)}) collective-permute-start(bf16[4,128,256]{2,1,0:T(8,128)(2,1)S(1)} %get-tuple-element.19), channel_id=1, source_target_pairs={{2,0},{3,1},{0,2},{1,3},{6,4},{7,5},{4,6},{5,7},{10,8},{11,9},{8,1... | collective-permute-start | bytes 786440 | tf_op jit(solution)/shard_map/ppermute | solution.py:256
  56.7 0.7 collective-permute-start.11
  62.2 22.8 %copy-start.3 = (bf16[16,128,128]{2,1,0:T(8,128)(2,1)S(1)}, bf16[16,128,128]{2,1,0:T(8,128)(2,1)}, u32[]{:S(2)}) copy-start(bf16[16,128,128]{2,1,0:T(8,128)(2,1)} %tiles.5) | copy-start | bytes 1572868
  62.2 22.8 %copy-start.6 = (bf16[16,128,128]{1,2,0:T(8,128)(2,1)S(1)}, bf16[16,128,128]{1,2,0:T(8,128)(2,1)}, u32[]{:S(2)}) copy-start(bf16[16,128,128]{1,2,0:T(8,128)(2,1)} %copy.20) | copy-start | bytes 1572868
  73.6 11.3 %collective-permute-start.13 = (bf16[8,128,256]{2,1,0:T(8,128)(2,1)S(1)}, bf16[8,128,256]{2,1,0:T(8,128)(2,1)S(1)}, u32[]{:S(2)}, u32[]{:S(2)}) collective-permute-start(bf16[8,128,256]{2,1,0:T(8,128)(2,1)S(1)} %get-tuple-element.22), channel_id=1, source_target_pairs={{1,0},{0,1},{3,2},{2,3},{5,4},{4,5},{7,6},{6,7},{9,8},{8,9},{11,10... | collective-permute-start | bytes 1572872 | tf_op jit(solution)/shard_map/ppermute | solution.py:256
  76.3 8.6 %collective-permute-start.14 = (bf16[8,128,256]{2,1,0:T(8,128)(2,1)S(1)}, bf16[8,128,256]{2,1,0:T(8,128)(2,1)}, u32[]{:S(2)}, u32[]{:S(2)}) collective-permute-start(bf16[8,128,256]{2,1,0:T(8,128)(2,1)S(1)} %get-tuple-element.23), channel_id=1, source_target_pairs={{1,4},{3,6},{5,8},{7,10},{9,12},{11,14},{4,1},{6,3},{8,5},{10,7},{... | collective-permute-start | bytes 1572872 | tf_op jit(solution)/shard_map/ppermute | solution.py:256
  77.8 7.1 %collective-permute-start.15 = (bf16[4,128,256]{2,1,0:T(8,128)(2,1)S(1)}, bf16[4,128,256]{2,1,0:T(8,128)(2,1)}, u32[]{:S(2)}, u32[]{:S(2)}) collective-permute-start(bf16[4,128,256]{2,1,0:T(8,128)(2,1)S(1)} %get-tuple-element.24), channel_id=1, source_target_pairs={{2,0},{3,1},{0,2},{1,3},{6,4},{7,5},{4,6},{5,7},{10,8},{11,9},{8,1... | collective-permute-start | bytes 786440 | tf_op jit(solution)/shard_map/ppermute | solution.py:256
  84.9 1.6 %copy-start.10 = (bf16[4,8,128,256]{3,2,1,0:T(8,128)(2,1)S(1)}, bf16[4,8,128,256]{3,2,1,0:T(8,128)(2,1)}, u32[]{:S(2)}) copy-start(bf16[4,8,128,256]{3,2,1,0:T(8,128)(2,1)} %copy-done.9) | copy-start | bytes 6291460
  86.5 1.6 %copy-start.12 = (bf16[4,8,128,256]{3,2,1,0:T(8,128)(2,1)S(1)}, bf16[4,8,128,256]{3,2,1,0:T(8,128)(2,1)}, u32[]{:S(2)}) copy-start(bf16[4,8,128,256]{3,2,1,0:T(8,128)(2,1)} %copy-done.11) | copy-start | bytes 6291460
  93.9 3.9 %collective-permute-start.16 = (f32[264,256]{1,0:T(8,128)S(1)}, f32[264,256]{1,0:T(8,128)S(1)}, u32[]{:S(2)}, u32[]{:S(2)}) collective-permute-start(f32[264,256]{1,0:T(8,128)S(1)} %pad_maximum_fusion.1), channel_id=1, source_target_pairs={{0,1},{1,0},{2,3},{3,2},{4,5},{5,4},{6,7},{7,6},{8,9},{9,8},{10,11... | collective-permute-start | bytes 811016 | tf_op jit(solution)/shard_map/ppermute | solution.py:237
  97.9 6.2 %collective-permute-start.17 = (f32[136,256]{1,0:T(8,128)S(1)}, f32[136,256]{1,0:T(8,128)S(1)}, u32[]{:S(2)}, u32[]{:S(2)}) collective-permute-start(f32[136,256]{1,0:T(8,128)S(1)} %pad_maximum_fusion.2), channel_id=1, source_target_pairs={{0,2},{1,3},{2,0},{3,1},{4,6},{5,7},{6,4},{7,5},{8,10},{9,11},{10,... | collective-permute-start | bytes 417800 | tf_op jit(solution)/shard_map/ppermute | solution.py:237
  104.2 4.7 %collective-permute-start.18 = (f32[72,256]{1,0:T(8,128)S(1)}, f32[72,256]{1,0:T(8,128)S(1)}, u32[]{:S(2)}, u32[]{:S(2)}) collective-permute-start(f32[72,256]{1,0:T(8,128)S(1)} %pad_maximum_fusion.3), channel_id=1, source_target_pairs={{0,4},{1,5},{2,6},{3,7},{4,0},{5,1},{6,2},{7,3},{8,12},{9,13},{10,... | collective-permute-start | bytes 221192 | tf_op jit(solution)/shard_map/ppermute | solution.py:237
  106.5 4.7 %collective-permute-start.12 = (f32[4,8,128]{2,1,0:T(8,128)S(1)}, f32[4,8,128]{2,1,0:T(8,128)S(1)}, u32[]{:S(2)}, u32[]{:S(2)}) collective-permute-start(f32[4,8,128]{2,1,0:T(8,128)S(1)} %get-tuple-element.20.pred), channel_id=1, source_target_pairs={{2,1},{1,2},{6,5},{5,6},{10,9},{9,10},{14,13},{13,14},{18,17},{17,... | collective-permute-start | bytes 49160 | tf_op jit(solution)/shard_map/ppermute | solution.py:256
  108.9 5.8 %collective-permute-start.19 = (f32[40,256]{1,0:T(8,128)S(1)}, f32[40,256]{1,0:T(8,128)S(1)}, u32[]{:S(2)}, u32[]{:S(2)}) collective-permute-start(f32[40,256]{1,0:T(8,128)S(1)} %pad_maximum_fusion.4), channel_id=1, source_target_pairs={{0,8},{1,9},{2,10},{3,11},{4,12},{5,13},{6,14},{7,15},{8,0},{9,1},... | collective-permute-start | bytes 122888 | tf_op jit(solution)/shard_map/ppermute | solution.py:237
  (4 other events, 4.8 us)

commit v2 on v1

--- a/solution.py
+++ b/solution.py
@@ -11,9 +11,11 @@
 F32 = jnp.float32
 BF16 = jnp.bfloat16
 AXES = ("wide", "narrow")
-VMEM_LIMIT = 40 * 1024 * 1024
+VMEM_LIMIT = 20 * 1024 * 1024
+BIG_VMEM = 60 * 1024 * 1024
 ANY = pl.BlockSpec(memory_space=pl.ANY)
 VMEM = pl.BlockSpec(memory_space=pltpu.VMEM)
+HBM = pl.BlockSpec(memory_space=pltpu.HBM)
 SMEM = pl.BlockSpec(memory_space=pltpu.SMEM)
 
 SELF, EAST, WEST, NORTH, SOUTH, FLAGS = 0, 1, 2, 3, 4, 5
@@ -91,6 +93,36 @@
         pltpu.make_async_copy(done.at[jnp.where(low == 0, 0, rows - 1)], outer, sems.at[4]),
         pltpu.make_async_copy(done.at[:, jnp.where(right == 0, cols - 1, 0)], side, sems.at[5]),
     ]
+
+
+def pack_kernel(rows, cols, flags, own, ends, side, sems):
+    copies = [
+        pltpu.make_async_copy(own.at[0], ends.at[0], sems.at[0]),
+        pltpu.make_async_copy(own.at[rows - 1], ends.at[1], sems.at[1]),
+        pltpu.make_async_copy(own.at[:, jnp.where(flags[1] == 1, 0, cols - 1)], side, sems.at[2]),
+    ]
+    for copy in copies:
+        copy.start()
+    for copy in copies:
+        copy.wait()
+
+
+def middle_kernel(rows, own, after, middle, sem):
+    copy = pltpu.make_async_copy(own.at[pl.ds(1, rows - 2)], middle, sem)
+    copy.start()
+    copy.wait()
+
+
+def turn_kernel(tiles, plain, turned, sem):
+    copy = pltpu.make_async_copy(tiles, plain, sem)
+    copy.start()
+    copy.wait()
+
+    def one_tile(tile, carry):
+        turned[tile] = plain[tile].T
+        return carry
+
+    lax.fori_loop(0, tiles.shape[0], one_tile, 0)
 
 
 def first_kernel(rows, cols, table, own, ends, middle, inner, outer, side, tiles, turned, weight,
@@ -195,8 +227,33 @@
         copy.wait()
 
 
+def spread_shares(parts, extra, digit, outs):
+    size = parts.shape[1]
+    for k, out in enumerate(outs):
+        for group in range(parts.shape[0] // 4):
+            out[group * size : (group + 1) * size] = parts[4 * group + jnp.bitwise_xor(digit, k)]
+        out[out.shape[0] - 8 :] = extra
+
+
+def fold_kernel(base, flags, keep, one, two, three, *refs):
+    digit = lax.rem(flags[3] // base, 4)
+    parts = refs[-1]
+    count, size, width = parts.shape
+    total = keep[...] + one[...] + two[...] + three[...]
+    parts[...] = total[: count * size].reshape(count, size, width)
+    spread_shares(parts, total[count * size :], digit, refs[:-1])
+
+
+def last_fold_kernel(keep, one, two, three, first, second, readout):
+    share = first.shape[0]
+    total = keep[...] + one[...] + two[...] + three[...]
+    first[...] = total[:share]
+    second[...] = total[share : 2 * share]
+    readout[...] = total[2 * share :].sum(axis=0, keepdims=True)
+
+
 def third_kernel(rows, cols, scale, table, g_own, inner, outer, side, tiles, turned, m_own, weight, readout,
-                 pred, target, first_out, field, m_in, gz_row, sems):
+                 pred, target, second, extra, keep, one, two, three, first_out, parts, field, m_in, gz_row, sems):
     nodes, width = g_own.shape[2], g_own.shape[3]
     copies = rim_copies(table, field, inner, outer, side, sems, rows, cols)
     copies.append(pltpu.make_async_copy(g_own, field.at[pl.ds(1, rows), pl.ds(1, cols)], sems.at[6]))
@@ -222,24 +279,45 @@
         return carry
 
     lax.fori_loop(0, rows, one_row, 0)
-
-
-def sum_shares(slots, extra, count):
-    place = lax.axis_index(AXES)
-    bit = 1
-    while bit < count:
-        route = [(i, i ^ bit) for i in range(count)]
-        mine = (place // bit) % 2
-        pairs = slots.reshape(slots.shape[0] // 2, 2, *slots.shape[1:])
-        keep = lax.dynamic_index_in_dim(pairs, mine, 1, keepdims=False)
-        send = lax.dynamic_index_in_dim(pairs, 1 - mine, 1, keepdims=False)
-        load = jnp.concatenate([send.reshape(-1, send.shape[-1]), extra], axis=0)
-        got = lax.ppermute(load, AXES, route)
-        cut = load.shape[0] - extra.shape[0]
-        slots = keep + got[:cut].reshape(keep.shape)
-        extra = extra + got[cut:]
-        bit *= 2
-    return slots[0], extra
+    count, size, _ = parts.shape
+    parts[:, : size // 2] = first_out[...].reshape(count, size // 2, width)
+    parts[:, size // 2 :] = second[...].reshape(count, size // 2, width)
+    digit = lax.rem(table[FLAGS * rows * cols + 3], 4)
+    spread_shares(parts, extra[...], digit, (keep, one, two, three))
+
+
+def shares_shape(groups, size, width):
+    return (jax.ShapeDtypeStruct((groups * size + 8, width), F32),) * 4
+
+
+def sum_shares(flags, outs, count, share, width, params):
+    base, groups = 1, count // 4
+    while True:
+        got = [
+            lax.ppermute(outs[k], AXES, [(i, i ^ (k * base)) for i in range(count)]) for k in (1, 2, 3)
+        ]
+        if groups == 1:
+            break
+        base *= 4
+        outs = pl.pallas_call(
+            functools.partial(fold_kernel, base),
+            out_shape=shares_shape(groups // 4, 2 * share, width),
+            in_specs=[SMEM] + [VMEM] * 4,
+            out_specs=(VMEM,) * 4,
+            scratch_shapes=[pltpu.VMEM((groups, 2 * share, width), F32)],
+            compiler_params=params,
+            name="fold",
+        )(flags, outs[0], *got)
+        groups //= 4
+    small = jax.ShapeDtypeStruct((share, width), F32)
+    return pl.pallas_call(
+        last_fold_kernel,
+        out_shape=(small, small, jax.ShapeDtypeStruct((1, width), F32)),
+        in_specs=[VMEM] * 4,
+        out_specs=(VMEM,) * 3,
+        compiler_params=params,
+        name="last_fold",
+    )(outs[0], *got)
 
 
 def per_device(features, tile_ids, tiles, w_first, w_second, readout, target):
@@ -258,9 +336,33 @@
     def edges(inner, outer, side):
         return send(inner, inner_way), send(outer, outer_way), send(side, side_way)
 
-    ends = send(jnp.concatenate([features[0:1], features[rows - 1 : rows]], axis=0), swap)
-    side = send(jnp.where(c == 1, features[:, 0], features[:, cols - 1]), first_side)
-    middle = send(features[1 : rows - 1], swap)
+    params = pltpu.CompilerParams(vmem_limit_bytes=VMEM_LIMIT)
+    patch = jax.ShapeDtypeStruct(features.shape, BF16)
+    line = jax.ShapeDtypeStruct((cols, nodes, width), BF16)
+    column = jax.ShapeDtypeStruct((rows, nodes, width), BF16)
+    flags = jnp.stack([moving, c, y, lax.axis_index(AXES)]).astype(jnp.int32)
+    ends_s, side_s = pl.pallas_call(
+        functools.partial(pack_kernel, rows, cols),
+        out_shape=(jax.ShapeDtypeStruct((2, cols, nodes, width), BF16), column),
+        in_specs=[SMEM, HBM],
+        out_specs=(HBM,) * 2,
+        scratch_shapes=[pltpu.SemaphoreType.DMA((3,))],
+        compiler_params=pltpu.CompilerParams(vmem_limit_bytes=BIG_VMEM),
+        name="pack",
+    )(flags, features)
+    ends = send(ends_s, swap)
+    side = send(side_s, first_side)
+    middle_s = pl.pallas_call(
+        functools.partial(middle_kernel, rows),
+        out_shape=jax.ShapeDtypeStruct((rows - 2, cols, nodes, width), BF16),
+        in_specs=[HBM, HBM],
+        out_specs=HBM,
+        scratch_shapes=[pltpu.SemaphoreType.DMA],
+        compiler_params=params,
+        name="pack_middle",
+    )(features, side)
+    middle = send(middle_s, swap)
+    tile_ids, target, tiles, _ = lax.optimization_barrier((tile_ids, target, tiles, middle_s))
     ids_swap = send(tile_ids, swap)
     above_ids = send(tile_ids[rows - 1, :, 1], above_way)
     left_ids = send(tile_ids[:, cols - 1, 2], left_way)
@@ -273,10 +375,18 @@
     table = jnp.concatenate(
         [
             jnp.stack([ids[:, :, 0], ids[:, :, 1], west, ids[:, :, 2], south]).reshape(-1),
-            jnp.stack([moving, c, y]).astype(jnp.int32),
+            flags,
         ]
     )
-    turned = jnp.swapaxes(tiles, 1, 2)
+    tiles, turned = pl.pallas_call(
+        turn_kernel,
+        out_shape=(jax.ShapeDtypeStruct(tiles.shape, BF16),) * 2,
+        in_specs=[HBM],
+        out_specs=(VMEM,) * 2,
+        scratch_shapes=[pltpu.SemaphoreType.DMA],
+        compiler_params=params,
+        name="turn",
+    )(tiles)
     readf = readout.astype(F32)[None]
     spread = jnp.broadcast_to(readout[:, None], (width, 128))
 
@@ -285,15 +395,11 @@
     inner = send(jnp.where(c == 0, low, top), inner_way)
     outer = send(jnp.where(c == 0, top, low), outer_way)
 
-    patch = jax.ShapeDtypeStruct(features.shape, BF16)
-    line = jax.ShapeDtypeStruct((cols, nodes, width), BF16)
-    column = jax.ShapeDtypeStruct((rows, nodes, width), BF16)
     square = jax.ShapeDtypeStruct((width, width), F32)
     rim = pltpu.VMEM((rows + 2, cols + 2, nodes, width), BF16)
     whole = pltpu.VMEM(features.shape, BF16)
     strip = pltpu.VMEM((cols, nodes, width), BF16)
     sems = pltpu.SemaphoreType.DMA((9,))
-    params = pltpu.CompilerParams(vmem_limit_bytes=VMEM_LIMIT)
     product = 2 * rows * cols * nodes * width * (6 * nodes)
     dense = 2 * rows * cols * nodes * width * width
     moved = features.size * 2
@@ -323,22 +429,21 @@
     )(table, x_one, inner, outer, side, tiles, turned, w_second, readf, spread, goal)
 
     inner, outer, side = edges(inner_s, outer_s, side_s)
-    first = pl.pallas_call(
+    pred_out = jnp.where(moving == 1, send(pred, swap), pred)
+    pred_out, side = lax.optimization_barrier((pred_out, side))
+    share = width // count
+    outs = pl.pallas_call(
         functools.partial(third_kernel, rows, cols, scale),
-        out_shape=square,
-        in_specs=[SMEM] + [ANY] * 4 + [VMEM] * 2 + [ANY] + [VMEM] * 4,
-        out_specs=VMEM,
-        scratch_shapes=[rim, whole, strip, sems],
+        out_shape=shares_shape(count // 4, 2 * share, width),
+        in_specs=[SMEM] + [ANY] * 4 + [VMEM] * 2 + [ANY] + [VMEM] * 6,
+        out_specs=(VMEM,) * 4,
+        scratch_shapes=[pltpu.VMEM((width, width), F32), pltpu.VMEM((count, 2 * share, width), F32), rim, whole, strip, sems],
         compiler_params=params,
         cost_estimate=pl.CostEstimate(flops=product + 2 * dense, bytes_accessed=3 * moved, transcendentals=features.size),
         name="layer_one_back",
-    )(table, g_two, inner, outer, side, tiles, turned, m_one, w_first, readf, pred, goal)
-
-    share = width // count
-    slots = jnp.concatenate([first.reshape(count, share, width), second.reshape(count, share, width)], axis=1)
-    mine, extra = sum_shares(slots, readout_part, count)
-    pred = jnp.where(moving == 1, send(pred, swap), pred)
-    return pred, mine[:share], mine[share:], extra.sum(axis=0)
+    )(table, g_two, inner, outer, side, tiles, turned, m_one, w_first, readf, pred, goal, second, readout_part)
+    first, second, extra = sum_shares(flags, outs, count, share, width, params)
+    return pred_out, first, second, extra[0]
 
 
 def solution(mesh):

time: 117 us -> 151 us (1.29)
  Pallas kernels: 20.9 us -> 65.1 us
  local copies, waits for them, and re-layouts: 16 us -> 6.05 us
  other arithmetic: 5.81 us -> 3.13 us
  waiting for transfers between devices: 20 us -> 22.6 us
    pallas_call x0 -> x5, Pallas kernels: none -> 45 us  [the longest x1 41.6 us: per_device(): pl.pallas_call(functools.partial(pack_kernel, rows, cols), out_shape=(jax...]
    unnamed x36 -> x31, local copies, waits for them, and re-layouts: 10.1 us -> 3.74 us
    ppermute x16, starting transfers between devices: 42.8 us -> 39.4 us  [send(): return lax.ppermute(value, AXES, way)]
    ppermute x4 -> x6, starting transfers between devices: 9.35 us -> 12.7 us  [sum_shares(): lax.ppermute(outs[k], AXES, [(i, i ^ k * base) for i in range(count)])]
    slice x6 -> x0, local copies, waits for them, and re-layouts: 2.96 us -> none  [the longest x1 1.27 us: per_device(): features[0:1]]
    ppermute x16, waiting for transfers between devices: 10.1 us -> 12.5 us  [send(): return lax.ppermute(value, AXES, way)]
    concatenate x7 -> x0, other arithmetic: 1.93 us -> none  [the longest x1 1.09 us: per_device(): jnp.concatenate([features[0:1], features[rows - 1:rows]], axis=0)]
    ppermute x4 -> x6, waiting for transfers between devices: 9.92 us -> 10.1 us  [sum_shares(): lax.ppermute(outs[k], AXES, [(i, i ^ k * base) for i in range(count)])]
  transfers between devices with their start and end apart: 20 -> 22, of which waited for: 6 -> 7; matrix products, arithmetic and copies ran while one was open for 11% -> 3% of each run, Pallas kernels for 0% -> 1%
where the time goes in v2:
time: 151 us; the launch traced here: 150 us
  Pallas kernels  65.1 us (43%)
  starting transfers between devices  52.1 us (35%)
  waiting for transfers between devices  22.6 us (15%)
  local copies, waits for them, and re-layouts  6.05 us (4%)
  other arithmetic  3.13 us (2%)
    pallas_call x1, Pallas kernels, per_device(): pl.pallas_call(functools.partial(pack_kernel, rows, cols), out_shape=(jax...  41.6 us
    ppermute x16, starting transfers between devices, send(): return lax.ppermute(value, AXES, way)  39.4 us
    ppermute x6, starting transfers between devices, sum_shares(): lax.ppermute(outs[k], AXES, [(i, i ^ k * base) for i in range(count)])  12.7 us
    ppermute x16, waiting for transfers between devices, send(): return lax.ppermute(value, AXES, way)  12.5 us
    ppermute x6, waiting for transfers between devices, sum_shares(): lax.ppermute(outs[k], AXES, [(i, i ^ k * base) for i in range(count)])  10.1 us
    pallas_call x1, Pallas kernels, per_device(): pl.pallas_call(functools.partial(second_kernel, rows, cols, scale), out_s...  10 us
    pallas_call x1, Pallas kernels, per_device(): pl.pallas_call(functools.partial(first_kernel, rows, cols), out_shape=(pa...  5.2 us
    pallas_call x1, Pallas kernels, per_device(): pl.pallas_call(functools.partial(third_kernel, rows, cols, scale), out_sh...  4.89 us
  transfers between devices with their start and end apart: 22, of which 7 were waited for; matrix products, arithmetic and copies ran while one was open for 3% of the time, Pallas kernels for 1%

profile of v2, /device:TPU:0, one launch (start us, length us, event | category | flops | bytes accessed | tf_op | source)
XLA Modules:
  0.0 150.0 jit_solution(17590100305754716396)
XLA Ops:
  1.3 41.6 %pack.1 = (bf16[2,8,128,256]{3,2,1,0:T(8,128)(2,1)}, bf16[4,128,256]{2,1,0:T(8,128)(2,1)}) custom-call(s32[4]{0:T(128)} %pad_add_fusion.flags, bf16[4,8,128,256]{3,2,1,0:T(8,128)(2,1)} %own.5), custom_call_target="tpu_custom_call" | custom-call | tf_op jit(solution)/shard_map/pack/pallas_call | solution.py:344
  42.9 3.0 %collective-permute-start = (bf16[4,128,256]{2,1,0:T(8,128)(2,1)}, bf16[4,128,256]{2,1,0:T(8,128)(2,1)S(1)}, u32[]{:S(2)}, u32[]{:S(2)}) collective-permute-start(bf16[4,128,256]{2,1,0:T(8,128)(2,1)} %get-tuple-element.36), channel_id=1, source_target_pairs={{1,0},{3,1},{0,2},{2,3},{5,4},{7,5},{4,6},{6,7},{9,8},{11,9},{8,10... | collective-permute-start | bytes 786440 | tf_op jit(solution)/shard_map/ppermute | solution.py:334
  46.6 4.9 %collective-permute-done.after.side = bf16[4,128,256]{2,1,0:T(8,128)(2,1)S(1)} collective-permute-done((bf16[4,128,256]{2,1,0:T(8,128)(2,1)}, bf16[4,128,256]{2,1,0:T(8,128)(2,1)S(1)}, u32[]{:S(2)}, u32[]{:S(2)}) %collective-permute-start) | collective-permute-done | bytes 262176 | tf_op jit(solution)/shard_map/ppermute | solution.py:334
  51.5 1.0 pack_middle.1
  53.2 1.2 collective-permute-start.1
  54.5 1.6 %collective-permute-start.5 = (bf16[2,8,128,256]{3,2,1,0:T(8,128)(2,1)}, bf16[2,8,128,256]{3,2,1,0:T(8,128)(2,1)}, u32[]{:S(2)}, u32[]{:S(2)}) collective-permute-start(bf16[2,8,128,256]{3,2,1,0:T(8,128)(2,1)} %pack_middle.1), channel_id=1, source_target_pairs={{2,1},{1,2},{6,5},{5,6},{10,9},{9,10},{14,13},{13,14},{18,17},{17,... | collective-permute-start | bytes 3145736 | tf_op jit(solution)/shard_map/ppermute | solution.py:334
  56.1 5.9 %collective-permute-start.2 = (s32[8]{0:T(128)}, s32[8]{0:T(128)}, u32[]{:S(2)}, u32[]{:S(2)}) collective-permute-start(s32[8]{0:T(128)} %slice_bitcast_fusion.5), channel_id=1, source_target_pairs={{0,1},{1,3},{4,5},{5,7},{8,9},{9,11},{12,13},{13,15},{2,4},{3,6},{... | collective-permute-start | bytes 104 | tf_op jit(solution)/shard_map/ppermute | solution.py:334
  62.0 2.9 %collective-permute-start.3 = (s32[4]{0:T(128)S(1)}, s32[4]{0:T(128)S(1)}, u32[]{:S(2)}, u32[]{:S(2)}) collective-permute-start(s32[4]{0:T(128)S(1)} %slice_reduce_fusion), channel_id=1, source_target_pairs={{0,2},{2,3},{4,6},{6,7},{8,10},{10,11},{12,14},{14,15},{16,18},{18... | collective-permute-start | bytes 56 | tf_op jit(solution)/shard_map/ppermute | solution.py:334
  65.0 1.2 turn.1
  66.1 0.8 copy-done.3
  66.9 0.8 copy-done.6
  68.6 1.2 select_bitcast_fusion
  69.7 1.5 collective-permute-start.7
  71.2 5.4 %collective-permute-start.6 = (bf16[8,128,256]{2,1,0:T(8,128)(2,1)}, bf16[8,128,256]{2,1,0:T(8,128)(2,1)}, u32[]{:S(2)}, u32[]{:S(2)}) collective-permute-start(bf16[8,128,256]{2,1,0:T(8,128)(2,1)} %get-tuple-element.69), channel_id=1, source_target_pairs={{1,0},{0,1},{3,2},{2,3},{5,4},{4,5},{7,6},{6,7},{9,8},{8,9},{11,10... | collective-permute-start | bytes 1572872 | tf_op jit(solution)/shard_map/ppermute | solution.py:334
  78.5 1.0 copy-done.4
  79.5 1.0 copy-done.7
  80.6 5.2 %layer_one.1 = (bf16[4,8,128,256]{3,2,1,0:T(8,128)(2,1)S(1)}, bf16[4,8,128,256]{3,2,1,0:T(8,128)(2,1)S(1)}, bf16[8,128,256]{2,1,0:T(8,128)(2,1)S(1)}, bf16[8,128...) custom-call(s32[164]{0:T(256)S(1)} %concatenate.12.table, bf16[4,8,128,256]{3,2,1,0:T(8,128)(2,1)S(1)} %copy-done, ...), custom_call_target="tpu_custom_call" | custom-call | flops 2147483648 | bytes 8388608 | tf_op jit(solution)/shard_map/layer_one/pallas_call | solution.py:407
  85.8 7.4 %collective-permute-start.8 = (bf16[8,128,256]{2,1,0:T(8,128)(2,1)S(1)}, bf16[8,128,256]{2,1,0:T(8,128)(2,1)S(1)}, u32[]{:S(2)}, u32[]{:S(2)}) collective-permute-start(bf16[8,128,256]{2,1,0:T(8,128)(2,1)S(1)} %get-tuple-element.43), channel_id=1, source_target_pairs={{1,0},{0,1},{3,2},{2,3},{5,4},{4,5},{7,6},{6,7},{9,8},{8,9},{11,10... | collective-permute-start | bytes 1572872 | tf_op jit(solution)/shard_map/ppermute | solution.py:334
  93.8 2.1 %collective-permute-start.10 = (bf16[4,128,256]{2,1,0:T(8,128)(2,1)S(1)}, bf16[4,128,256]{2,1,0:T(8,128)(2,1)S(1)}, u32[]{:S(2)}, u32[]{:S(2)}) collective-permute-start(bf16[4,128,256]{2,1,0:T(8,128)(2,1)S(1)} %get-tuple-element.45), channel_id=1, source_target_pairs={{2,0},{3,1},{0,2},{1,3},{6,4},{7,5},{4,6},{5,7},{10,8},{11,9},{8,1... | collective-permute-start | bytes 786440 | tf_op jit(solution)/shard_map/ppermute | solution.py:334
  96.7 4.2 %collective-permute-done.10.side = bf16[4,128,256]{2,1,0:T(8,128)(2,1)S(1)} collective-permute-done((bf16[4,128,256]{2,1,0:T(8,128)(2,1)S(1)}, bf16[4,128,256]{2,1,0:T(8,128)(2,1)S(1)}, u32[]{:S(2)}, u32[]{:S(2)}) %collective-permute-start.10) | collective-permute-done | bytes 262176 | tf_op jit(solution)/shard_map/ppermute | solution.py:334
  101.0 10.0 %layer_two.1 = (bf16[4,8,128,256]{3,2,1,0:T(8,128)(2,1)S(1)}, bf16[8,128,256]{2,1,0:T(8,128)(2,1)S(1)}, bf16[8,128,256]{2,1,0:T(8,128)(2,1)S(1)}, bf16[4,128,256...) custom-call(s32[164]{0:T(256)S(1)} %concatenate.12.table, ...), custom_call_target="tpu_custom_call" | custom-call | flops 3221225472 | bytes 6291456 | tf_op jit(solution)/shard_map/layer_two/pallas_call | solution.py:419
  111.0 2.9 %collective-permute-start.14 = (bf16[8,128,256]{2,1,0:T(8,128)(2,1)S(1)}, bf16[8,128,256]{2,1,0:T(8,128)(2,1)S(1)}, u32[]{:S(2)}, u32[]{:S(2)}) collective-permute-start(bf16[8,128,256]{2,1,0:T(8,128)(2,1)S(1)} %get-tuple-element.51), channel_id=1, source_target_pairs={{1,0},{0,1},{3,2},{2,3},{5,4},{4,5},{7,6},{6,7},{9,8},{8,9},{11,10... | collective-permute-start | bytes 1572872 | tf_op jit(solution)/shard_map/ppermute | solution.py:334
  114.6 2.1 %collective-permute-start.13 = (bf16[4,128,256]{2,1,0:T(8,128)(2,1)S(1)}, bf16[4,128,256]{2,1,0:T(8,128)(2,1)S(1)}, u32[]{:S(2)}, u32[]{:S(2)}) collective-permute-start(bf16[4,128,256]{2,1,0:T(8,128)(2,1)S(1)} %get-tuple-element.48), channel_id=1, source_target_pairs={{2,0},{3,1},{0,2},{1,3},{6,4},{7,5},{4,6},{5,7},{10,8},{11,9},{8,1... | collective-permute-start | bytes 786440 | tf_op jit(solution)/shard_map/ppermute | solution.py:334
  118.0 3.1 %collective-permute-done.13.side = bf16[4,128,256]{2,1,0:T(8,128)(2,1)S(1)} collective-permute-done((bf16[4,128,256]{2,1,0:T(8,128)(2,1)S(1)}, bf16[4,128,256]{2,1,0:T(8,128)(2,1)S(1)}, u32[]{:S(2)}, u32[]{:S(2)}) %collective-permute-start.13) | collective-permute-done | bytes 262176 | tf_op jit(solution)/shard_map/ppermute | solution.py:334
  121.1 4.9 %layer_one_back.1 = (f32[136,256]{1,0:T(8,128)S(1)}, f32[136,256]{1,0:T(8,128)S(1)}, f32[136,256]{1,0:T(8,128)S(1)}, f32[136,256]{1,0:T(8,128)S(1)}) custom-call(s32[164]{0:T(256)S(1)} %concatenate.12.table, bf16[4,8,128,256]{3,2,1,0:T(8,128)(2,1)S(1)} %get-tuple-element.50.g_own, bf16[8,128,256]{2,1,0:T(8,128)(2,1)S(1)} %collective-permute-done.14.inner, ...), custom_call_target="tpu_custom_call" | custom-call | flops 2684354560 | bytes 6291456 | tf_op jit(solution)/shard_map/layer_one_back/pallas_call | solution.py:435
  126.0 5.0 %collective-permute-start.16 = (f32[136,256]{1,0:T(8,128)S(1)}, f32[136,256]{1,0:T(8,128)S(1)}, u32[]{:S(2)}, u32[]{:S(2)}) collective-permute-start(f32[136,256]{1,0:T(8,128)S(1)} %get-tuple-element.58), channel_id=1, source_target_pairs={{0,1},{1,0},{2,3},{3,2},{4,5},{5,4},{6,7},{7,6},{8,9},{9,8},{10,11... | collective-permute-start | bytes 417800 | tf_op jit(solution)/shard_map/ppermute | solution.py:297
  131.0 1.4 collective-permute-start.17
  132.4 5.1 %collective-permute-done.17.two = f32[136,256]{1,0:T(8,128)S(1)} collective-permute-done((f32[136,256]{1,0:T(8,128)S(1)}, f32[136,256]{1,0:T(8,128)S(1)}, u32[]{:S(2)}, u32[]{:S(2)}) %collective-permute-start.17) | collective-permute-done | bytes 139296 | tf_op jit(solution)/shard_map/ppermute | solution.py:297
  137.5 1.2 collective-permute-done.18.three
  139.3 3.9 %collective-permute-start.19 = (f32[40,256]{1,0:T(8,128)S(1)}, f32[40,256]{1,0:T(8,128)S(1)}, u32[]{:S(2)}, u32[]{:S(2)}) collective-permute-start(f32[40,256]{1,0:T(8,128)S(1)} %get-tuple-element.62), channel_id=1, source_target_pairs={{0,4},{1,5},{2,6},{3,7},{4,0},{5,1},{6,2},{7,3},{8,12},{9,13},{10,... | collective-permute-start | bytes 122888 | tf_op jit(solution)/shard_map/ppermute | solution.py:297
  143.2 2.4 %collective-permute-start.21 = (f32[40,256]{1,0:T(8,128)S(1)}, f32[40,256]{1,0:T(8,128)S(1)}, u32[]{:S(2)}, u32[]{:S(2)}) collective-permute-start(f32[40,256]{1,0:T(8,128)S(1)} %get-tuple-element.64), channel_id=1, source_target_pairs={{0,12},{1,13},{2,14},{3,15},{4,8},{5,9},{6,10},{7,11},{8,4},{9,5},... | collective-permute-start | bytes 122888 | tf_op jit(solution)/shard_map/ppermute | solution.py:297
  145.6 3.7 %collective-permute-done.20.two = f32[40,256]{1,0:T(8,128)S(1)} collective-permute-done((f32[40,256]{1,0:T(8,128)S(1)}, f32[40,256]{1,0:T(8,128)S(1)}, u32[]{:S(2)}, u32[]{:S(2)}) %collective-permute-start.20) | collective-permute-done | bytes 40992 | tf_op jit(solution)/shard_map/ppermute | solution.py:297
  (67 shorter events, 9.4 us)
Async XLA Ops:
  0.6 50.9 %copy-start = (bf16[4,8,128,256]{3,2,1,0:T(8,128)(2,1)S(1)}, bf16[4,8,128,256]{3,2,1,0:T(8,128)(2,1)}, u32[]{:S(2)}) copy-start(bf16[4,8,128,256]{3,2,1,0:T(8,128)(2,1)} %own.5) | copy-start | bytes 6291460
  42.9 9.6 %copy-start.12 = (s32[4,8,3]{1,0,2:T(4,128)S(1)}, s32[4,8,3]{1,0,2:T(4,128)}, u32[]{:S(2)}) copy-start(s32[4,8,3]{1,0,2:T(4,128)} %param.8) | copy-start | bytes 1156
  42.9 8.6 %collective-permute-start = (bf16[4,128,256]{2,1,0:T(8,128)(2,1)}, bf16[4,128,256]{2,1,0:T(8,128)(2,1)S(1)}, u32[]{:S(2)}, u32[]{:S(2)}) collective-permute-start(bf16[4,128,256]{2,1,0:T(8,128)(2,1)} %get-tuple-element.36), channel_id=1, source_target_pairs={{1,0},{3,1},{0,2},{2,3},{5,4},{7,5},{4,6},{6,7},{9,8},{11,9},{8,10... | collective-permute-start | bytes 786440 | tf_op jit(solution)/shard_map/ppermute | solution.py:334
  45.9 22.7 %collective-permute-start.4 = (bf16[2,8,128,256]{3,2,1,0:T(8,128)(2,1)}, bf16[2,8,128,256]{3,2,1,0:T(8,128)(2,1)S(1)}, u32[]{:S(2)}, u32[]{:S(2)}) collective-permute-start(bf16[2,8,128,256]{3,2,1,0:T(8,128)(2,1)} %get-tuple-element.38), channel_id=1, source_target_pairs={{2,1},{1,2},{6,5},{5,6},{10,9},{9,10},{14,13},{13,14},{18,17},{17,... | collective-permute-start | bytes 3145736 | tf_op jit(solution)/shard_map/ppermute | solution.py:334
  46.6 18.3 %copy-start.1 = (bf16[16,128,128]{2,1,0:T(8,128)(2,1)S(1)}, bf16[16,128,128]{2,1,0:T(8,128)(2,1)}, u32[]{:S(2)}) copy-start(bf16[16,128,128]{2,1,0:T(8,128)(2,1)} %tiles) | copy-start | bytes 1572868
  52.5 25.9 %copy-start.10 = (bf16[256,256]{1,0:T(8,128)(2,1)S(1)}, bf16[256,256]{1,0:T(8,128)(2,1)}, u32[]{:S(2)}) copy-start(bf16[256,256]{1,0:T(8,128)(2,1)} %weight.5) | copy-start | bytes 393220
  53.2 14.6 %collective-permute-start.1 = (s32[4,8,3]{1,0,2:T(4,128)S(1)}, s32[4,8,3]{1,0,2:T(4,128)}, u32[]{:S(2)}, u32[]{:S(2)}) collective-permute-start(s32[4,8,3]{1,0,2:T(4,128)S(1)} %copy-done.12), channel_id=1, source_target_pairs={{2,1},{1,2},{6,5},{5,6},{10,9},{9,10},{14,13},{13,14},{18,17},{17,... | collective-permute-start | bytes 1160 | tf_op jit(solution)/shard_map/ppermute | solution.py:334
  54.5 23.6 %collective-permute-start.5 = (bf16[2,8,128,256]{3,2,1,0:T(8,128)(2,1)}, bf16[2,8,128,256]{3,2,1,0:T(8,128)(2,1)}, u32[]{:S(2)}, u32[]{:S(2)}) collective-permute-start(bf16[2,8,128,256]{3,2,1,0:T(8,128)(2,1)} %pack_middle.1), channel_id=1, source_target_pairs={{2,1},{1,2},{6,5},{5,6},{10,9},{9,10},{14,13},{13,14},{18,17},{17,... | collective-permute-start | bytes 3145736 | tf_op jit(solution)/shard_map/ppermute | solution.py:334
  56.1 11.8 %collective-permute-start.2 = (s32[8]{0:T(128)}, s32[8]{0:T(128)}, u32[]{:S(2)}, u32[]{:S(2)}) collective-permute-start(s32[8]{0:T(128)} %slice_bitcast_fusion.5), channel_id=1, source_target_pairs={{0,1},{1,3},{4,5},{5,7},{8,9},{9,11},{12,13},{13,15},{2,4},{3,6},{... | collective-permute-start | bytes 104 | tf_op jit(solution)/shard_map/ppermute | solution.py:334
  62.0 5.7 %collective-permute-start.3 = (s32[4]{0:T(128)S(1)}, s32[4]{0:T(128)S(1)}, u32[]{:S(2)}, u32[]{:S(2)}) collective-permute-start(s32[4]{0:T(128)S(1)} %slice_reduce_fusion), channel_id=1, source_target_pairs={{0,2},{2,3},{4,6},{6,7},{8,10},{10,11},{12,14},{14,15},{16,18},{18... | collective-permute-start | bytes 56 | tf_op jit(solution)/shard_map/ppermute | solution.py:334
  69.7 8.4 %collective-permute-start.7 = (bf16[8,128,256]{2,1,0:T(8,128)(2,1)}, bf16[8,128,256]{2,1,0:T(8,128)(2,1)}, u32[]{:S(2)}, u32[]{:S(2)}) collective-permute-start(bf16[8,128,256]{2,1,0:T(8,128)(2,1)} %get-tuple-element.68), channel_id=1, source_target_pairs={{1,4},{3,6},{5,8},{7,10},{9,12},{11,14},{4,1},{6,3},{8,5},{10,7},{... | collective-permute-start | bytes 1572872 | tf_op jit(solution)/shard_map/ppermute | solution.py:334
  71.2 7.3 %collective-permute-start.6 = (bf16[8,128,256]{2,1,0:T(8,128)(2,1)}, bf16[8,128,256]{2,1,0:T(8,128)(2,1)}, u32[]{:S(2)}, u32[]{:S(2)}) collective-permute-start(bf16[8,128,256]{2,1,0:T(8,128)(2,1)} %get-tuple-element.69), channel_id=1, source_target_pairs={{1,0},{0,1},{3,2},{2,3},{5,4},{4,5},{7,6},{6,7},{9,8},{8,9},{11,10... | collective-permute-start | bytes 1572872 | tf_op jit(solution)/shard_map/ppermute | solution.py:334
  80.5 15.5 %copy-start.11 = (f32[4,8,128]{2,1,0:T(8,128)S(1)}, f32[4,8,128]{2,1,0:T(8,128)}, u32[]{:S(2)}) copy-start(f32[4,8,128]{2,1,0:T(8,128)} %param.13) | copy-start | bytes 49156
  80.5 16.1 %copy-start.13 = (bf16[256]{0:T(256)(128)(2,1)S(1)}, bf16[256]{0:T(256)(128)(2,1)}, u32[]{:S(2)}) copy-start(bf16[256]{0:T(256)(128)(2,1)} %param.12) | copy-start | bytes 1540
  80.5 20.5 %copy-start.5 = (bf16[16,128,128]{2,1,0:T(8,128)(2,1)S(1)}, bf16[16,128,128]{2,1,0:T(8,128)(2,1)}, u32[]{:S(2)}) copy-start(bf16[16,128,128]{2,1,0:T(8,128)(2,1)} %copy-done.3) | copy-start | bytes 1572868
  80.5 20.5 %copy-start.8 = (bf16[16,128,128]{2,1,0:T(8,128)(2,1)S(1)}, bf16[16,128,128]{2,1,0:T(8,128)(2,1)}, u32[]{:S(2)}) copy-start(bf16[16,128,128]{2,1,0:T(8,128)(2,1)} %copy-done.6) | copy-start | bytes 1572868
  80.5 20.5 %copy-start.9 = (bf16[256,256]{1,0:T(8,128)(2,1)S(1)}, bf16[256,256]{1,0:T(8,128)(2,1)}, u32[]{:S(2)}) copy-start(bf16[256,256]{1,0:T(8,128)(2,1)} %weight.4) | copy-start | bytes 393220
  85.8 15.1 %collective-permute-start.8 = (bf16[8,128,256]{2,1,0:T(8,128)(2,1)S(1)}, bf16[8,128,256]{2,1,0:T(8,128)(2,1)S(1)}, u32[]{:S(2)}, u32[]{:S(2)}) collective-permute-start(bf16[8,128,256]{2,1,0:T(8,128)(2,1)S(1)} %get-tuple-element.43), channel_id=1, source_target_pairs={{1,0},{0,1},{3,2},{2,3},{5,4},{4,5},{7,6},{6,7},{9,8},{8,9},{11,10... | collective-permute-start | bytes 1572872 | tf_op jit(solution)/shard_map/ppermute | solution.py:334
  93.2 7.7 %collective-permute-start.9 = (bf16[8,128,256]{2,1,0:T(8,128)(2,1)S(1)}, bf16[8,128,256]{2,1,0:T(8,128)(2,1)S(1)}, u32[]{:S(2)}, u32[]{:S(2)}) collective-permute-start(bf16[8,128,256]{2,1,0:T(8,128)(2,1)S(1)} %get-tuple-element.44), channel_id=1, source_target_pairs={{1,4},{3,6},{5,8},{7,10},{9,12},{11,14},{4,1},{6,3},{8,5},{10,7},{... | collective-permute-start | bytes 1572872 | tf_op jit(solution)/shard_map/ppermute | solution.py:334
  93.8 7.0 %collective-permute-start.10 = (bf16[4,128,256]{2,1,0:T(8,128)(2,1)S(1)}, bf16[4,128,256]{2,1,0:T(8,128)(2,1)S(1)}, u32[]{:S(2)}, u32[]{:S(2)}) collective-permute-start(bf16[4,128,256]{2,1,0:T(8,128)(2,1)S(1)} %get-tuple-element.45), channel_id=1, source_target_pairs={{2,0},{3,1},{0,2},{1,3},{6,4},{7,5},{4,6},{5,7},{10,8},{11,9},{8,1... | collective-permute-start | bytes 786440 | tf_op jit(solution)/shard_map/ppermute | solution.py:334
  96.0 0.7 collective-permute-start.11
  111.0 10.0 %collective-permute-start.14 = (bf16[8,128,256]{2,1,0:T(8,128)(2,1)S(1)}, bf16[8,128,256]{2,1,0:T(8,128)(2,1)S(1)}, u32[]{:S(2)}, u32[]{:S(2)}) collective-permute-start(bf16[8,128,256]{2,1,0:T(8,128)(2,1)S(1)} %get-tuple-element.51), channel_id=1, source_target_pairs={{1,0},{0,1},{3,2},{2,3},{5,4},{4,5},{7,6},{6,7},{9,8},{8,9},{11,10... | collective-permute-start | bytes 1572872 | tf_op jit(solution)/shard_map/ppermute | solution.py:334
  113.9 7.2 %collective-permute-start.15 = (bf16[8,128,256]{2,1,0:T(8,128)(2,1)S(1)}, bf16[8,128,256]{2,1,0:T(8,128)(2,1)S(1)}, u32[]{:S(2)}, u32[]{:S(2)}) collective-permute-start(bf16[8,128,256]{2,1,0:T(8,128)(2,1)S(1)} %get-tuple-element.52), channel_id=1, source_target_pairs={{1,4},{3,6},{5,8},{7,10},{9,12},{11,14},{4,1},{6,3},{8,5},{10,7},{... | collective-permute-start | bytes 1572872 | tf_op jit(solution)/shard_map/ppermute | solution.py:334
  114.6 6.5 %collective-permute-start.13 = (bf16[4,128,256]{2,1,0:T(8,128)(2,1)S(1)}, bf16[4,128,256]{2,1,0:T(8,128)(2,1)S(1)}, u32[]{:S(2)}, u32[]{:S(2)}) collective-permute-start(bf16[4,128,256]{2,1,0:T(8,128)(2,1)S(1)} %get-tuple-element.48), channel_id=1, source_target_pairs={{2,0},{3,1},{0,2},{1,3},{6,4},{7,5},{4,6},{5,7},{10,8},{11,9},{8,1... | collective-permute-start | bytes 786440 | tf_op jit(solution)/shard_map/ppermute | solution.py:334
  116.7 0.7 collective-permute-start.12
  121.1 17.6 %copy-start.2 = (s32[4]{0:T(128)S(1)}, s32[4]{0:T(128)}, u32[]{:S(2)}) copy-start(s32[4]{0:T(128)} %pad_add_fusion.flags) | copy-start | bytes 52
  126.0 6.4 %collective-permute-start.16 = (f32[136,256]{1,0:T(8,128)S(1)}, f32[136,256]{1,0:T(8,128)S(1)}, u32[]{:S(2)}, u32[]{:S(2)}) collective-permute-start(f32[136,256]{1,0:T(8,128)S(1)} %get-tuple-element.58), channel_id=1, source_target_pairs={{0,1},{1,0},{2,3},{3,2},{4,5},{5,4},{6,7},{7,6},{8,9},{9,8},{10,11... | collective-permute-start | bytes 417800 | tf_op jit(solution)/shard_map/ppermute | solution.py:297
  131.0 6.5 %collective-permute-start.17 = (f32[136,256]{1,0:T(8,128)S(1)}, f32[136,256]{1,0:T(8,128)S(1)}, u32[]{:S(2)}, u32[]{:S(2)}) collective-permute-start(f32[136,256]{1,0:T(8,128)S(1)} %get-tuple-element.59), channel_id=1, source_target_pairs={{0,2},{1,3},{2,0},{3,1},{4,6},{5,7},{6,4},{7,5},{8,10},{9,11},{10,... | collective-permute-start | bytes 417800 | tf_op jit(solution)/shard_map/ppermute | solution.py:297
  132.3 6.4 %collective-permute-start.18 = (f32[136,256]{1,0:T(8,128)S(1)}, f32[136,256]{1,0:T(8,128)S(1)}, u32[]{:S(2)}, u32[]{:S(2)}) collective-permute-start(f32[136,256]{1,0:T(8,128)S(1)} %get-tuple-element.60), channel_id=1, source_target_pairs={{0,3},{1,2},{2,1},{3,0},{4,7},{5,6},{6,5},{7,4},{8,11},{9,10},{10,... | collective-permute-start | bytes 417800 | tf_op jit(solution)/shard_map/ppermute | solution.py:297
  139.3 6.3 %collective-permute-start.19 = (f32[40,256]{1,0:T(8,128)S(1)}, f32[40,256]{1,0:T(8,128)S(1)}, u32[]{:S(2)}, u32[]{:S(2)}) collective-permute-start(f32[40,256]{1,0:T(8,128)S(1)} %get-tuple-element.62), channel_id=1, source_target_pairs={{0,4},{1,5},{2,6},{3,7},{4,0},{5,1},{6,2},{7,3},{8,12},{9,13},{10,... | collective-permute-start | bytes 122888 | tf_op jit(solution)/shard_map/ppermute | solution.py:297
  143.2 6.2 %collective-permute-start.20 = (f32[40,256]{1,0:T(8,128)S(1)}, f32[40,256]{1,0:T(8,128)S(1)}, u32[]{:S(2)}, u32[]{:S(2)}) collective-permute-start(f32[40,256]{1,0:T(8,128)S(1)} %get-tuple-element.63), channel_id=1, source_target_pairs={{0,8},{1,9},{2,10},{3,11},{4,12},{5,13},{6,14},{7,15},{8,0},{9,1},... | collective-permute-start | bytes 122888 | tf_op jit(solution)/shard_map/ppermute | solution.py:297
  143.2 6.2 %collective-permute-start.21 = (f32[40,256]{1,0:T(8,128)S(1)}, f32[40,256]{1,0:T(8,128)S(1)}, u32[]{:S(2)}, u32[]{:S(2)}) collective-permute-start(f32[40,256]{1,0:T(8,128)S(1)} %get-tuple-element.64), channel_id=1, source_target_pairs={{0,12},{1,13},{2,14},{3,15},{4,8},{5,9},{6,10},{7,11},{8,4},{9,5},... | collective-permute-start | bytes 122888 | tf_op jit(solution)/shard_map/ppermute | solution.py:297
  (4 other events, 3.7 us)

commit v3 on v2

v3 whole, which is shorter than its diff:
```python
import functools

import jax
import jax.numpy as jnp
import numpy as np
from jax import lax
from jax.experimental import pallas as pl
from jax.experimental.pallas import tpu as pltpu
from jax.sharding import PartitionSpec as P

F32 = jnp.float32
BF16 = jnp.bfloat16
AXES = ("wide", "narrow")
VMEM_LIMIT = 16 * 1024 * 1024
ANY = pl.BlockSpec(memory_space=pl.ANY)
VMEM = pl.BlockSpec(memory_space=pltpu.VMEM)
SMEM = pl.BlockSpec(memory_space=pltpu.SMEM)

SELF, EAST, WEST, NORTH, SOUTH = 0, 1, 2, 3, 4
TAIL = 16


def routes(wide):
    depth = wide // 2

    def at(z, y, c):
        return (2 * z + y) * 2 + c

    every = [(z, y, c) for z in range(depth) for y in range(2) for c in range(2)]
    swap = [(at(z, c, y), at(z, y, c)) for z, y, c in every if y != c]
    first_side = [(at(z, c, 1 - y), at(z, y, c)) for z, y, c in every]
    inner = [(at(z, y, 1 - c), at(z, y, c)) for z, y, c in every]
    outer = [(at(z - 1, y, 1), at(z, y, 0)) for z, y, c in every if c == 0 and z > 0]
    outer += [(at(z + 1, y, 0), at(z, y, 1)) for z, y, c in every if c == 1 and z + 1 < depth]
    side = [(at(z, 1 - y, c), at(z, y, c)) for z, y, c in every]
    return swap, first_side, inner, outer, side


def place():
    half = lax.axis_index("narrow")
    side = lax.rem(lax.axis_index("wide"), 2)
    return half, side, half != side


def start_all(pairs, sems, first=0):
    copies = [pltpu.make_async_copy(a, b, sems.at[first + i]) for i, (a, b) in enumerate(pairs)]
    for copy in copies:
        copy.start()
    return copies


def wait_all(copies):
    for copy in copies:
        copy.wait()


def block_product(table, field, tiles, turned, row, col, nodes, rows, cols):
    at = row * cols + col
    step = rows * cols

    def block(r, c):
        return field[r, c * nodes : (c + 1) * nodes]

    lhs = jnp.concatenate(
        [
            tiles[table[SELF * step + at]],
            turned[table[SELF * step + at]],
            tiles[table[EAST * step + at]],
            turned[table[WEST * step + at]],
            tiles[table[NORTH * step + at]],
            turned[table[SOUTH * step + at]],
        ],
        axis=1,
    )
    centre = block(row + 1, col + 1)
    rhs = jnp.concatenate(
        [
            centre,
            centre,
            block(row + 2, col + 1),
            block(row, col + 1),
            block(row + 1, col + 2),
            block(row + 1, col),
        ],
        axis=0,
    )
    return jnp.dot(lhs, rhs, preferred_element_type=F32)


def rim_pairs(field, inner, outer, side, nodes, rows, cols):
    half, right, _ = place()
    zero_col = pl.multiple_of(jnp.where(right == 0, 0, (cols + 1) * nodes), nodes)
    side_col = pl.multiple_of(jnp.where(right == 0, (cols + 1) * nodes, 0), nodes)
    inside = pl.ds(nodes, cols * nodes)
    line = pl.ds(0, cols * nodes)
    for row in range(1, rows + 1):
        field[row, pl.ds(zero_col, nodes)] = jnp.zeros((nodes, field.shape[2]), field.dtype)
    pairs = [
        (inner.at[line], field.at[jnp.where(half == 0, rows + 1, 0), inside]),
        (outer.at[line], field.at[jnp.where(half == 0, 0, rows + 1), inside]),
    ]
    for row in range(rows):
        pairs.append((side.at[pl.ds(row * nodes, nodes)], field.at[row + 1, pl.ds(side_col, nodes)]))
    return pairs


def edge_pairs(done, inner, outer, side, nodes, rows, cols):
    half, right, _ = place()
    col = pl.multiple_of(jnp.where(right == 0, (cols - 1) * nodes, 0), nodes)
    pairs = [
        (done.at[jnp.where(half == 0, rows - 1, 0)], inner),
        (done.at[jnp.where(half == 0, 0, rows - 1)], outer),
    ]
    for row in range(rows):
        pairs.append((done.at[row, pl.ds(col, nodes)], side.at[pl.ds(row * nodes, nodes)]))
    return pairs


def pack_kernel(nodes, cols, ids, own, ends, side, numbers, ids_in, wide_ids, sems):
    rows, line = own.shape[0], own.shape[1]
    ids_copy = start_all([(ids, ids_in)], sems, 2 + rows)
    half, _, _ = place()
    col = pl.multiple_of(jnp.where(half == 1, 0, (cols - 1) * nodes), nodes)
    pairs = [(own.at[0], ends.at[pl.ds(0, line)]), (own.at[rows - 1], ends.at[pl.ds(line, line)])]
    for row in range(rows):
        pairs.append((own.at[row, pl.ds(col, nodes)], side.at[pl.ds(row * nodes, nodes)]))
    copies = start_all(pairs, sems)
    wait_all(ids_copy)
    wide_ids[...] = jnp.zeros_like(wide_ids)
    for kind in range(3):
        wide_ids[kind * rows : (kind + 1) * rows, 0:cols] = ids_in[kind].astype(F32)
    tail = wide_ids[...].astype(BF16)
    numbers[...] = tail
    ends[2 * line :] = tail
    side[rows * nodes :] = tail
    wait_all(copies)


def middle_kernel(own, after, middle, sems):
    wait_all(start_all([(own.at[pl.ds(1, own.shape[0] - 2)], middle)], sems))


def turn_kernel(tiles, turned, plain, sems):
    wait_all(start_all([(tiles, plain)], sems))

    def one_tile(tile, carry):
        turned[tile] = plain[tile].T
        return carry

    lax.fori_loop(0, tiles.shape[0], one_tile, 0)


def pick_kernel(numbers, own, ends, after, inner, outer, sems):
    rows, line = own.shape[0], own.shape[1]
    half, _, moved = place()
    whole = pl.ds(0, line)
    tail = pl.ds(line, TAIL)

    @pl.when(moved)
    def _():
        near = pl.multiple_of(jnp.where(half == 0, line, 0), line)
        far = pl.multiple_of(jnp.where(half == 0, 0, line), line)
        wait_all(start_all([
            (ends.at[pl.ds(near, line)], inner.at[whole]),
            (ends.at[pl.ds(far, line)], outer.at[whole]),
            (ends.at[pl.ds(2 * line, TAIL)], inner.at[tail]),
            (ends.at[pl.ds(2 * line, TAIL)], outer.at[tail]),
        ], sems))

    @pl.when(jnp.logical_not(moved))
    def _():
        copies = start_all([
            (own.at[jnp.where(half == 0, rows - 1, 0)], inner.at[whole]),
            (own.at[jnp.where(half == 0, 0, rows - 1)], outer.at[whole]),
        ], sems)
        inner[line:] = numbers[...]
        outer[line:] = numbers[...]
        wait_all(copies)


def first_kernel(nodes, cols, numbers, own, ends, middle, inner, outer, side, tiles_in, turned_in, weight_in,
                 table, x_out, m_out, inner_out, outer_out, side_out,
                 field, x_new, m_new, tiles, turned, weight, heads, heads_int, marks, sems):
    rows, line, width = own.shape
    step = rows * cols
    half, _, moved = place()
    inside = pl.ds(nodes, line)

    def main_pairs(flag):
        if flag:
            pairs = [
                (ends.at[pl.ds(2 * line, TAIL)], heads.at[0]),
                (ends.at[pl.ds(0, line)], field.at[1, inside]),
                (ends.at[pl.ds(line, line)], field.at[rows, inside]),
                (middle, field.at[pl.ds(2, rows - 2), inside]),
            ]
        else:
            pairs = [(numbers, heads.at[0]), (own, field.at[pl.ds(1, rows), inside])]
        return pairs

    def above_pairs(flag):
        return [((inner if flag else outer).at[pl.ds(line, TAIL)], heads.at[1])]

    def either(flag, build, first):
        @pl.when(flag)
        def _():
            start_all(build(True), sems, first)

        @pl.when(jnp.logical_not(flag))
        def _():
            start_all(build(False), sems, first)

    def either_wait(flag, build, first, low, high):
        def some(value):
            for i, (a, b) in list(enumerate(build(value)))[low:high]:
                pltpu.make_async_copy(a, b, sems.at[first + i]).wait()

        @pl.when(flag)
        def _():
            some(True)

        @pl.when(jnp.logical_not(flag))
        def _():
            some(False)

    either(moved, main_pairs, 0)
    either(half == 1, above_pairs, 4)
    left = start_all([(side.at[pl.ds(rows * nodes, TAIL)], heads.at[2])], sems, 5)
    rest = start_all(
        [(tiles_in, tiles), (turned_in, turned), (weight_in, weight)]
        + rim_pairs(field, inner, outer, side, nodes, rows, cols),
        sems,
        6,
    )
    either_wait(moved, main_pairs, 0, 0, 1)
    either_wait(half == 1, above_pairs, 4, 0, 1)
    wait_all(left)
    heads_int[...] = heads[:, :, 0:128].astype(F32).astype(jnp.int32)
    wait_all(start_all([(heads_int, marks)], sems, 5))

    def fill(at, carry):
        row, col = at // cols, lax.rem(at, cols)
        last = rows - 1
        up = jnp.where(row == 0, marks[1, rows + last, col], marks[0, rows + jnp.maximum(row - 1, 0), col])
        back = jnp.where(
            col == 0, marks[2, 2 * rows + row, cols - 1], marks[0, 2 * rows + row, jnp.maximum(col - 1, 0)]
        )
        table[SELF * step + at] = marks[0, row, col]
        table[EAST * step + at] = marks[0, rows + row, col]
        table[WEST * step + at] = up
        table[NORTH * step + at] = marks[0, 2 * rows + row, col]
        table[SOUTH * step + at] = back
        return carry

    lax.fori_loop(0, step, fill, 0)
    wait_all(rest)
    either_wait(moved, main_pairs, 0, 1, None)

    def one_row(row, carry):
        for col in range(cols):
            m_new[row, col * nodes : (col + 1) * nodes] = block_product(
                table, field, tiles, turned, row, col, nodes, rows, cols
            ).astype(BF16)
        for part in range(0, line, 2 * nodes):
            z = jnp.dot(m_new[row, part : part + 2 * nodes], weight[...], preferred_element_type=F32)
            base = field[row + 1, nodes + part : 3 * nodes + part]
            x_new[row, part : part + 2 * nodes] = (base.astype(F32) + jnp.tanh(z)).astype(BF16)
        return carry

    lax.fori_loop(0, rows, one_row, 0)
    wait_all(start_all(
        edge_pairs(x_new, inner_out, outer_out, side_out, nodes, rows, cols) + [(x_new, x_out), (m_new, m_out)], sems
    ))


def second_kernel(nodes, cols, scale, table, x_own, inner, outer, side, tiles_in, turned_in, weight_in, readout,
                  spread, target, target_swap, g_out, inner_out, outer_out, side_out, pred_out, second_out, readout_out, goals,
                  field, g_new, m_row, gz_row, tiles, turned, weight, sems):
    rows, line, width = x_own.shape
    wait_all(start_all(
        [(x_own, field.at[pl.ds(1, rows), pl.ds(nodes, line)]), (tiles_in, tiles), (turned_in, turned), (weight_in, weight)]
        + rim_pairs(field, inner, outer, side, nodes, rows, cols),
        sems,
    ))
    readf = readout[...]
    moved = place()[2]

    @pl.when(moved)
    def _():
        goals[...] = target_swap[...]

    @pl.when(jnp.logical_not(moved))
    def _():
        goals[...] = target[...]

    lanes = lax.broadcasted_iota(jnp.int32, (nodes, 128), 1)
    second_out[...] = jnp.zeros_like(second_out)
    readout_out[...] = jnp.zeros_like(readout_out)

    def one_row(row, carry):
        goal = goals[row].T
        seen = jnp.zeros((nodes, 128), F32)
        for col in range(cols):
            m_row[col * nodes : (col + 1) * nodes] = block_product(
                table, field, tiles, turned, row, col, nodes, rows, cols
            ).astype(BF16)
        for col in range(cols):
            here = slice(col * nodes, (col + 1) * nodes)
            z = jnp.dot(m_row[here], weight[...], preferred_element_type=F32)
            t = jnp.tanh(z)
            x = (field[row + 1, (col + 1) * nodes : (col + 2) * nodes].astype(F32) + t).astype(BF16)
            pred = jnp.dot(x, spread[...], preferred_element_type=F32)
            seen = jnp.where(lanes == col, pred, seen)
            gp = (pred[:, 0:1] - goal[:, col : col + 1]) * scale
            part = x.astype(F32) * gp
            readout_out[...] += part.reshape(nodes // 8, 8, width).sum(axis=0)
            gz = (gp * readf * (1.0 - t * t)).astype(BF16)
            gz_row[here] = gz
            g_new[row, here] = lax.dot_general(
                gz, weight[...], (((1,), (1,)), ((), ())), preferred_element_type=F32
            ).astype(BF16)
        second_out[...] += lax.dot_general(
            m_row[...], gz_row[...], (((0,), (0,)), ((), ())), preferred_element_type=F32
        )
        pred_out[row] = seen.T[0:cols]
        return carry

    lax.fori_loop(0, rows, one_row, 0)
    wait_all(start_all(
        edge_pairs(g_new, inner_out, outer_out, side_out, nodes, rows, cols) + [(g_new, g_out)], sems
    ))


def spread_shares(parts, extra, digit, outs):
    size = parts.shape[1]
    for k, out in enumerate(outs):
        for group in range(parts.shape[0] // 4):
            out[group * size : (group + 1) * size] = parts[4 * group + jnp.bitwise_xor(digit, k)]
        out[out.shape[0] - 8 :] = extra


def fold_kernel(base, keep, one, two, three, *refs):
    digit = lax.rem(lax.axis_index(AXES) // base, 4)
    parts = refs[-1]
    count, size, width = parts.shape
    total = keep[...] + one[...] + two[...] + three[...]
    parts[...] = total[: count * size].reshape(count, size, width)
    spread_shares(parts, total[count * size :], digit, refs[:-1])


def last_fold_kernel(keep, one, two, three, first, second, readout):
    share = first.shape[0]
    total = keep[...] + one[...] + two[...] + three[...]
    first[...] = total[:share]
    second[...] = total[share : 2 * share]
    readout[...] = total[2 * share :].sum(axis=0, keepdims=True)


def third_kernel(nodes, cols, scale, table, g_own, inner, outer, side, tiles_in, turned_in, m_own, weight_in, readout,
                 pred, pred_swap, target, second, extra, keep, one, two, three, pred_out,
                 first_out, parts, field, m_in, gz_row, tiles, turned, weight, sems):
    rows, line, width = g_own.shape
    wait_all(start_all(
        [
            (g_own, field.at[pl.ds(1, rows), pl.ds(nodes, line)]),
            (m_own, m_in),
            (tiles_in, tiles),
            (turned_in, turned),
            (weight_in, weight),
        ]
        + rim_pairs(field, inner, outer, side, nodes, rows, cols),
        sems,
    ))
    readf = readout[...]
    moved = place()[2]

    @pl.when(moved)
    def _():
        pred_out[...] = pred_swap[...]

    @pl.when(jnp.logical_not(moved))
    def _():
        pred_out[...] = pred[...]

    first_out[...] = jnp.zeros_like(first_out)

    def one_row(row, carry):
        gp_all = ((pred[row] - target[row]) * scale).T
        for col in range(cols):
            here = slice(col * nodes, (col + 1) * nodes)
            gx = gp_all[:, col : col + 1] * readf
            gx = gx + block_product(table, field, tiles, turned, row, col, nodes, rows, cols)
            t = jnp.tanh(jnp.dot(m_in[row, here], weight[...], preferred_element_type=F32))
            gz_row[here] = (gx * (1.0 - t * t)).astype(BF16)
        first_out[...] += lax.dot_general(
            m_in[row], gz_row[...], (((0,), (0,)), ((), ())), preferred_element_type=F32
        )
        return carry

    lax.fori_loop(0, rows, one_row, 0)
    count, size, _ = parts.shape
    parts[:, : size // 2] = first_out[...].reshape(count, size // 2, width)
    parts[:, size // 2 :] = second[...].reshape(count, size // 2, width)
    spread_shares(parts, extra[...], lax.rem(lax.axis_index(AXES), 4), (keep, one, two, three))


def shares_shape(groups, size, width):
    return (jax.ShapeDtypeStruct((groups * size + 8, width), F32),) * 4


def sum_shares(outs, count, share, width, params):
    base, groups = 1, count // 4
    while True:
        got = [
            lax.ppermute(outs[k], AXES, [(i, i ^ (k * base)) for i in range(count)]) for k in (1, 2, 3)
        ]
        if groups == 1:
            break
        base *= 4
        outs = pl.pallas_call(
            functools.partial(fold_kernel, base),
            out_shape=shares_shape(groups // 4, 2 * share, width),
            in_specs=[VMEM] * 4,
            out_specs=(VMEM,) * 4,
            scratch_shapes=[pltpu.VMEM((groups, 2 * share, width), F32)],
            compiler_params=params,
            name="fold",
        )(outs[0], *got)
        groups //= 4
    small = jax.ShapeDtypeStruct((share, width), F32)
    return pl.pallas_call(
        last_fold_kernel,
        out_shape=(small, small, jax.ShapeDtypeStruct((1, width), F32)),
        in_specs=[VMEM] * 4,
        out_specs=(VMEM,) * 3,
        compiler_params=params,
        name="last_fold",
    )(outs[0], *got)


def per_device(features, tile_ids, tiles, w_first, w_second, readout, target):
    rows, cols, nodes, width = features.shape
    wide, narrow = lax.axis_size("wide"), lax.axis_size("narrow")
    count = wide * narrow
    line, step = cols * nodes, rows * cols
    swap, first_side, inner_way, outer_way, side_way = routes(wide)
    scale = float(np.sqrt(np.float32(width) / np.float32(rows * line * count)))
    params = pltpu.CompilerParams(vmem_limit_bytes=VMEM_LIMIT)

    def send(value, way):
        return lax.ppermute(value, AXES, way)

    def edges(inner, outer, side):
        return send(inner, inner_way), send(outer, outer_way), send(side, side_way)

    def bf(*shape):
        return jax.ShapeDtypeStruct(shape, BF16)

    def sems(number):
        return pltpu.SemaphoreType.DMA((number,))

    features = features.reshape(rows, line, width)
    ends_s, side_s, numbers = pl.pallas_call(
        functools.partial(pack_kernel, nodes, cols),
        out_shape=(bf(2 * line + TAIL, width), bf(rows * nodes + TAIL, width), bf(TAIL, width)),
        in_specs=[ANY, ANY],
        out_specs=(VMEM,) * 3,
        scratch_shapes=[pltpu.VMEM((3, rows, cols), jnp.int32), pltpu.VMEM((TAIL, width), F32), sems(3 + rows)],
        compiler_params=params,
        name="pack",
    )(jnp.transpose(tile_ids, (2, 0, 1)), features)
    ends = send(ends_s, swap)
    side = send(side_s, first_side)
    middle_s = pl.pallas_call(
        middle_kernel,
        out_shape=bf(rows - 2, line, width),
        in_specs=[ANY, ANY],
        out_specs=VMEM,
        scratch_shapes=[sems(1)],
        compiler_params=params,
        name="pack_middle",
    )(features, side_s)
    middle = send(middle_s, swap)
    target, tiles, _ = lax.optimization_barrier((target, tiles, middle_s))
    goal_swap = send(target, swap)
    turned = pl.pallas_call(
        turn_kernel,
        out_shape=bf(*tiles.shape),
        in_specs=[ANY],
        out_specs=VMEM,
        scratch_shapes=[pltpu.VMEM(tiles.shape, BF16), sems(1)],
        compiler_params=params,
        name="turn",
    )(tiles)
    readf = readout.astype(F32)[None]
    spread = jnp.broadcast_to(readout[:, None], (width, 128))

    inner_s, outer_s = pl.pallas_call(
        pick_kernel,
        out_shape=(bf(line + TAIL, width),) * 2,
        in_specs=[VMEM, ANY, ANY, ANY],
        out_specs=(VMEM,) * 2,
        scratch_shapes=[sems(4)],
        compiler_params=params,
        name="pick",
    )(numbers, features, ends, side)
    outer, inner = send(outer_s, outer_way), send(inner_s, inner_way)

    patch = bf(rows, line, width)
    edge_shapes = (bf(line, width), bf(line, width), bf(rows * nodes, width))
    square = jax.ShapeDtypeStruct((width, width), F32)
    rim = pltpu.VMEM((rows + 2, line + 2 * nodes, width), BF16)
    whole = pltpu.VMEM((rows, line, width), BF16)
    strip = pltpu.VMEM((line, width), BF16)
    loads = [pltpu.VMEM(tiles.shape, BF16), pltpu.VMEM(tiles.shape, BF16), pltpu.VMEM((width, width), BF16)]
    product = 2 * rows * line * width * 6 * nodes
    dense = 2 * rows * line * width * width
    moves = 2 * rows * line * width

    def cost(denses, passes):
        return pl.CostEstimate(
            flops=product + denses * dense, bytes_accessed=passes * moves, transcendentals=rows * line * width
        )

    table, x_one, m_one, inner_s, outer_s, side_s = pl.pallas_call(
        functools.partial(first_kernel, nodes, cols),
        out_shape=(jax.ShapeDtypeStruct((5 * step,), jnp.int32), patch, patch) + edge_shapes,
        in_specs=[ANY] * 10,
        out_specs=(SMEM,) + (ANY,) * 5,
        scratch_shapes=[rim, whole, whole]
        + loads
        + [
            pltpu.VMEM((3, TAIL, width), BF16),
            pltpu.VMEM((3, TAIL, 128), jnp.int32),
            pltpu.SMEM((3, TAIL, 128), jnp.int32),
            sems(11 + rows),
        ],
        compiler_params=params,
        cost_estimate=cost(1, 4),
        name="layer_one",
    )(numbers, features, ends, middle, inner, outer, side, tiles, turned, w_first)

    inner, outer, side = edges(inner_s, outer_s, side_s)
    g_two, inner_s, outer_s, side_s, pred, second, readout_part, goal = pl.pallas_call(
        functools.partial(second_kernel, nodes, cols, scale),
        out_shape=(patch,) + edge_shapes
        + (
            jax.ShapeDtypeStruct(target.shape, F32),
            square,
            jax.ShapeDtypeStruct((8, width), F32),
            jax.ShapeDtypeStruct(target.shape, F32),
        ),
        in_specs=[SMEM] + [ANY] * 7 + [VMEM] * 4,
        out_specs=(ANY,) * 4 + (VMEM,) * 4,
        scratch_shapes=[rim, whole, strip, strip] + loads + [sems(6 + rows)],
        compiler_params=params,
        cost_estimate=cost(3, 3),
        name="layer_two",
    )(table, x_one, inner, outer, side, tiles, turned, w_second, readf, spread, target, goal_swap)

    inner, outer, side = edges(inner_s, outer_s, side_s)
    pred_swap = send(pred, swap)
    share = width // count
    *outs, pred_out = pl.pallas_call(
        functools.partial(third_kernel, nodes, cols, scale),
        out_shape=shares_shape(count // 4, 2 * share, width) + (jax.ShapeDtypeStruct(target.shape, F32),),
        in_specs=[SMEM] + [ANY] * 8 + [VMEM] * 6,
        out_specs=(VMEM,) * 5,
        scratch_shapes=[pltpu.VMEM((width, width), F32), pltpu.VMEM((count, 2 * share, width), F32), rim, whole, strip]
        + loads
        + [sems(7 + rows)],
        compiler_params=params,
        cost_estimate=cost(2, 3),
        name="layer_one_back",
    )(table, g_two, inner, outer, side, tiles, turned, m_one, w_first, readf, pred, pred_swap, goal, second, readout_part)
    first, second, extra = sum_shares(outs, count, share, width, params)
    return pred_out, first, second, extra[0]


def solution(mesh):
    in_specs = (
        P(("groups", "wide"), "narrow", None, None),
        P(("groups", "wide"), "narrow", None),
        P(),
        P(),
        P(),
        P(),
        P(("groups", "wide"), "narrow", None),
    )
    out_specs = (
        P(("groups", "wide"), "narrow", None),
        P(("groups", "wide", "narrow"), None),
        P(("groups", "wide", "narrow"), None),
        P("groups"),
    )
    return jax.shard_map(
        per_device, mesh=mesh, in_specs=in_specs, out_specs=out_specs, check_vma=False
    )
```

time: 151 us -> 101 us (0.67)
  Pallas kernels: 65.1 us -> 26.4 us
  starting transfers between devices: 52.1 us -> 44.5 us
  local copies, waits for them, and re-layouts: 6.05 us -> 2.62 us
  other arithmetic: 3.13 us -> 0.01 us
  waiting for transfers between devices: 22.6 us -> 25.7 us
    pallas_call x6 -> x7, Pallas kernels: 63.9 us -> 25.7 us  [the longest x1 11 us: per_device(): pl.pallas_call(functools.partial(second_kernel, nodes, cols, scale), out_...]
    ppermute x16 -> x13, starting transfers between devices: 39.4 us -> 32.4 us  [send(): return lax.ppermute(value, AXES, way)]
    ppermute x16 -> x13, waiting for transfers between devices: 12.5 us -> 15.4 us  [send(): return lax.ppermute(value, AXES, way)]
    select_n x4 -> x0, other arithmetic: 1.78 us -> none  [the longest x1 1.15 us: per_device(): outer = send(jnp.where(c == 0, top, low), outer_way)]
    unnamed x31 -> x16, local copies, waits for them, and re-layouts: 3.74 us -> 2.53 us
  transfers between devices with their start and end apart: 22 -> 19, of which waited for: 7 -> 7; matrix products, arithmetic and copies ran while one was open for 3% -> 0% of each run, Pallas kernels for 1% -> 1%
where the time goes in v3:
time: 101 us; the launch traced here: 100 us
  starting transfers between devices  44.5 us (44%)
  Pallas kernels  26.4 us (26%)
  waiting for transfers between devices  25.7 us (25%)
  local copies, waits for them, and re-layouts  2.62 us (3%)
    ppermute x13, starting transfers between devices, send(): return lax.ppermute(value, AXES, way)  32.4 us
    ppermute x13, waiting for transfers between devices, send(): return lax.ppermute(value, AXES, way)  15.4 us
    ppermute x6, starting transfers between devices, sum_shares(): lax.ppermute(outs[k], AXES, [(i, i ^ k * base) for i in range(count)])  12.1 us
    pallas_call x1, Pallas kernels, per_device(): pl.pallas_call(functools.partial(second_kernel, nodes, cols, scale), out_...  11 us
    ppermute x6, waiting for transfers between devices, sum_shares(): lax.ppermute(outs[k], AXES, [(i, i ^ k * base) for i in range(count)])  10.3 us
    pallas_call x1, Pallas kernels, per_device(): pl.pallas_call(functools.partial(first_kernel, nodes, cols), out_shape=(j...  7.1 us
    pallas_call x1, Pallas kernels, per_device(): pl.pallas_call(functools.partial(third_kernel, nodes, cols, scale), out_s...  5.76 us
    unnamed x16, local copies, waits for them, and re-layouts  2.53 us
  transfers between devices with their start and end apart: 19, of which 7 were waited for; matrix products, arithmetic and copies ran while one was open for 0% of the time, Pallas kernels for 1%

profile of v3, /device:TPU:0, one launch (start us, length us, event | category | flops | bytes accessed | tf_op | source)
XLA Modules:
  0.0 100.2 jit_solution(2397503275368022576)
XLA Ops:
  0.6 1.6 %copy-done = bf16[4,8,128,256]{3,2,1,0:T(8,128)(2,1)S(1)} copy-done((bf16[4,8,128,256]{3,2,1,0:T(8,128)(2,1)S(1)}, bf16[4,8,128,256]{3,2,1,0:T(8,128)(2,1)}, u32[]{:S(2)}) %copy-start) | copy-done | bytes 2097176
  2.2 0.7 copy-done.3
  3.4 0.9 collective-permute-start
  4.6 0.9 collective-permute-start.1
  5.5 6.9 %collective-permute-start.2 = (bf16[528,256]{1,0:T(8,128)(2,1)S(1)}, bf16[528,256]{1,0:T(8,128)(2,1)S(1)}, u32[]{:S(2)}, u32[]{:S(2)}) collective-permute-start(bf16[528,256]{1,0:T(8,128)(2,1)S(1)} %get-tuple-element.39.after), channel_id=1, source_target_pairs={{1,0},{3,1},{0,2},{2,3},{5,4},{7,5},{4,6},{6,7},{9,8},{11,9},{8,10... | collective-permute-start | bytes 811016 | tf_op jit(solution)/shard_map/ppermute | solution.py:451
  12.4 6.9 %collective-permute-done.2.after.side = bf16[528,256]{1,0:T(8,128)(2,1)S(1)} collective-permute-done((bf16[528,256]{1,0:T(8,128)(2,1)S(1)}, bf16[528,256]{1,0:T(8,128)(2,1)S(1)}, u32[]{:S(2)}, u32[]{:S(2)}) %collective-permute-start.2) | collective-permute-done | bytes 270368 | tf_op jit(solution)/shard_map/ppermute | solution.py:451
  19.4 4.8 %collective-permute-start.3 = (bf16[1040,256]{1,0:T(8,128)(2,1)S(1)}, bf16[1040,256]{1,0:T(8,128)(2,1)S(1)}, u32[]{:S(2)}, u32[]{:S(2)}) collective-permute-start(bf16[1040,256]{1,0:T(8,128)(2,1)S(1)} %get-tuple-element.40), channel_id=1, source_target_pairs={{1,0},{0,1},{3,2},{2,3},{5,4},{4,5},{7,6},{6,7},{9,8},{8,9},{11,10... | collective-permute-start | bytes 1597448 | tf_op jit(solution)/shard_map/ppermute | solution.py:451
  24.2 0.7 collective-permute-start.4
  24.9 1.2 %turn.1.turned_in = bf16[16,128,128]{2,1,0:T(8,128)(2,1)S(1)} custom-call(bf16[16,128,128]{2,1,0:T(8,128)(2,1)S(1)} %copy-done.2), custom_call_target="tpu_custom_call" | custom-call | tf_op jit(solution)/shard_map/turn/pallas_call | solution.py:486
  26.2 7.1 %layer_one.1 = (s32[160]{0:T(256)S(1)}, bf16[4,1024,256]{2,1,0:T(8,128)(2,1)S(1)}, bf16[4,1024,256]{2,1,0:T(8,128)(2,1)S(1)}, bf16[1024,256]{1,0:T(8,128)(2,1)S(...) custom-call(bf16[16,256]{1,0:T(8,128)(2,1)S(1)} %get-tuple-element.37.numbers, ...), custom_call_target="tpu_custom_call" | custom-call | flops 2147483648 | bytes 8388608 | tf_op jit(solution)/shard_map/layer_one/pallas_call | solution.py:525
  33.3 9.1 %collective-permute-start.5 = (bf16[1024,256]{1,0:T(8,128)(2,1)S(1)}, bf16[1024,256]{1,0:T(8,128)(2,1)S(1)}, u32[]{:S(2)}, u32[]{:S(2)}) collective-permute-start(bf16[1024,256]{1,0:T(8,128)(2,1)S(1)} %get-tuple-element.45), channel_id=1, source_target_pairs={{1,0},{0,1},{3,2},{2,3},{5,4},{4,5},{7,6},{6,7},{9,8},{8,9},{11,10... | collective-permute-start | bytes 1572872 | tf_op jit(solution)/shard_map/ppermute | solution.py:451
  42.4 0.7 collective-permute-start.6
  43.1 1.8 %collective-permute-start.7 = (bf16[512,256]{1,0:T(8,128)(2,1)S(1)}, bf16[512,256]{1,0:T(8,128)(2,1)S(1)}, u32[]{:S(2)}, u32[]{:S(2)}) collective-permute-start(bf16[512,256]{1,0:T(8,128)(2,1)S(1)} %get-tuple-element.47), channel_id=1, source_target_pairs={{2,0},{3,1},{0,2},{1,3},{6,4},{7,5},{4,6},{5,7},{10,8},{11,9},{8,1... | collective-permute-start | bytes 786440 | tf_op jit(solution)/shard_map/ppermute | solution.py:451
  44.9 0.7 collective-permute-start.8
  45.6 4.8 %collective-permute-done.7.side = bf16[512,256]{1,0:T(8,128)(2,1)S(1)} collective-permute-done((bf16[512,256]{1,0:T(8,128)(2,1)S(1)}, bf16[512,256]{1,0:T(8,128)(2,1)S(1)}, u32[]{:S(2)}, u32[]{:S(2)}) %collective-permute-start.7) | collective-permute-done | bytes 262176 | tf_op jit(solution)/shard_map/ppermute | solution.py:451
  50.5 11.0 %layer_two.1 = (bf16[4,1024,256]{2,1,0:T(8,128)(2,1)S(1)}, bf16[1024,256]{1,0:T(8,128)(2,1)S(1)}, bf16[1024,256]{1,0:T(8,128)(2,1)S(1)}, bf16[512,256]{1,0:T(8,1...) custom-call(s32[160]{0:T(256)S(1)} %get-tuple-element.43.table, ...), custom_call_target="tpu_custom_call" | custom-call | flops 3221225472 | bytes 6291456 | tf_op jit(solution)/shard_map/layer_two/pallas_call | solution.py:544
  61.5 2.6 %collective-permute-start.9 = (bf16[1024,256]{1,0:T(8,128)(2,1)S(1)}, bf16[1024,256]{1,0:T(8,128)(2,1)S(1)}, u32[]{:S(2)}, u32[]{:S(2)}) collective-permute-start(bf16[1024,256]{1,0:T(8,128)(2,1)S(1)} %get-tuple-element.50), channel_id=1, source_target_pairs={{1,0},{0,1},{3,2},{2,3},{5,4},{4,5},{7,6},{6,7},{9,8},{8,9},{11,10... | collective-permute-start | bytes 1572872 | tf_op jit(solution)/shard_map/ppermute | solution.py:451
  64.1 0.7 collective-permute-start.10
  64.8 2.2 %collective-permute-start.11 = (bf16[512,256]{1,0:T(8,128)(2,1)S(1)}, bf16[512,256]{1,0:T(8,128)(2,1)S(1)}, u32[]{:S(2)}, u32[]{:S(2)}) collective-permute-start(bf16[512,256]{1,0:T(8,128)(2,1)S(1)} %get-tuple-element.52), channel_id=1, source_target_pairs={{2,0},{3,1},{0,2},{1,3},{6,4},{7,5},{4,6},{5,7},{10,8},{11,9},{8,1... | collective-permute-start | bytes 786440 | tf_op jit(solution)/shard_map/ppermute | solution.py:451
  67.0 0.7 collective-permute-start.12
  67.7 3.7 %collective-permute-done.11.side = bf16[512,256]{1,0:T(8,128)(2,1)S(1)} collective-permute-done((bf16[512,256]{1,0:T(8,128)(2,1)S(1)}, bf16[512,256]{1,0:T(8,128)(2,1)S(1)}, u32[]{:S(2)}, u32[]{:S(2)}) %collective-permute-start.11) | collective-permute-done | bytes 262176 | tf_op jit(solution)/shard_map/ppermute | solution.py:451
  71.4 5.8 %layer_one_back.1 = (f32[136,256]{1,0:T(8,128)S(1)}, f32[136,256]{1,0:T(8,128)S(1)}, f32[136,256]{1,0:T(8,128)S(1)}, f32[136,256]{1,0:T(8,128)S(1)}, f32[4,8,128]{2,1,0:T(8,128)}) custom-call(s32[160]{0:T(256)S(1)} %get-tuple-element.43.table, bf16[4,1024,256]{2,1,0:T(8,128)(2,1)S(1)} %get-tuple-element.49.g_own, ...), custom_call_target="tpu_custom_call" | custom-call | flops 2684354560 | bytes 6291456 | tf_op jit(solution)/shard_map/layer_one_back/pallas_call | solution.py:564
  77.1 4.3 %collective-permute-start.13 = (f32[136,256]{1,0:T(8,128)S(1)}, f32[136,256]{1,0:T(8,128)S(1)}, u32[]{:S(2)}, u32[]{:S(2)}) collective-permute-start(f32[136,256]{1,0:T(8,128)S(1)} %get-tuple-element.60), channel_id=1, source_target_pairs={{0,1},{1,0},{2,3},{3,2},{4,5},{5,4},{6,7},{7,6},{8,9},{9,8},{10,11... | collective-permute-start | bytes 417800 | tf_op jit(solution)/shard_map/ppermute | solution.py:415
  81.5 2.0 %collective-permute-start.14 = (f32[136,256]{1,0:T(8,128)S(1)}, f32[136,256]{1,0:T(8,128)S(1)}, u32[]{:S(2)}, u32[]{:S(2)}) collective-permute-start(f32[136,256]{1,0:T(8,128)S(1)} %get-tuple-element.61), channel_id=1, source_target_pairs={{0,2},{1,3},{2,0},{3,1},{4,6},{5,7},{6,4},{7,5},{8,10},{9,11},{10,... | collective-permute-start | bytes 417800 | tf_op jit(solution)/shard_map/ppermute | solution.py:415
  83.5 4.5 %collective-permute-done.14.two = f32[136,256]{1,0:T(8,128)S(1)} collective-permute-done((f32[136,256]{1,0:T(8,128)S(1)}, f32[136,256]{1,0:T(8,128)S(1)}, u32[]{:S(2)}, u32[]{:S(2)}) %collective-permute-start.14) | collective-permute-done | bytes 139296 | tf_op jit(solution)/shard_map/ppermute | solution.py:415
  88.0 1.8 %collective-permute-done.15.three = f32[136,256]{1,0:T(8,128)S(1)} collective-permute-done((f32[136,256]{1,0:T(8,128)S(1)}, f32[136,256]{1,0:T(8,128)S(1)}, u32[]{:S(2)}, u32[]{:S(2)}) %collective-permute-start.15) | collective-permute-done | bytes 139296 | tf_op jit(solution)/shard_map/ppermute | solution.py:415
  89.8 3.3 %collective-permute-start.16 = (f32[40,256]{1,0:T(8,128)S(1)}, f32[40,256]{1,0:T(8,128)S(1)}, u32[]{:S(2)}, u32[]{:S(2)}) collective-permute-start(f32[40,256]{1,0:T(8,128)S(1)} %get-tuple-element.64), channel_id=1, source_target_pairs={{0,4},{1,5},{2,6},{3,7},{4,0},{5,1},{6,2},{7,3},{8,12},{9,13},{10,... | collective-permute-start | bytes 122888 | tf_op jit(solution)/shard_map/ppermute | solution.py:415
  93.1 0.5 collective-permute-start.17
  93.6 1.9 %collective-permute-start.18 = (f32[40,256]{1,0:T(8,128)S(1)}, f32[40,256]{1,0:T(8,128)S(1)}, u32[]{:S(2)}, u32[]{:S(2)}) collective-permute-start(f32[40,256]{1,0:T(8,128)S(1)} %get-tuple-element.66), channel_id=1, source_target_pairs={{0,12},{1,13},{2,14},{3,15},{4,8},{5,9},{6,10},{7,11},{8,4},{9,5},... | collective-permute-start | bytes 122888 | tf_op jit(solution)/shard_map/ppermute | solution.py:415
  95.6 3.3 %collective-permute-done.17.two = f32[40,256]{1,0:T(8,128)S(1)} collective-permute-done((f32[40,256]{1,0:T(8,128)S(1)}, f32[40,256]{1,0:T(8,128)S(1)}, u32[]{:S(2)}, u32[]{:S(2)}) %collective-permute-start.17) | collective-permute-done | bytes 40992 | tf_op jit(solution)/shard_map/ppermute | solution.py:415
  98.9 0.6 collective-permute-done.18.three
  99.5 0.6 last_fold.1
  (33 shorter events, 1.1 us)
Async XLA Ops:
  0.6 1.6 %copy-start = (bf16[4,8,128,256]{3,2,1,0:T(8,128)(2,1)S(1)}, bf16[4,8,128,256]{3,2,1,0:T(8,128)(2,1)}, u32[]{:S(2)}) copy-start(bf16[4,8,128,256]{3,2,1,0:T(8,128)(2,1)} %param.7) | copy-start | bytes 6291460
  2.2 0.7 copy-start.3
  2.9 1.6 %copy-start.1 = (bf16[4,8,128,256]{3,2,1,0:T(8,128)(2,1)S(1)}, bf16[4,8,128,256]{3,2,1,0:T(8,128)(2,1)}, u32[]{:S(2)}) copy-start(bf16[4,8,128,256]{3,2,1,0:T(8,128)(2,1)} %param.7) | copy-start | bytes 6291460
  3.4 15.9 %collective-permute-start = (bf16[2064,256]{1,0:T(8,128)(2,1)S(1)}, bf16[2064,256]{1,0:T(8,128)(2,1)S(1)}, u32[]{:S(2)}, u32[]{:S(2)}) collective-permute-start(bf16[2064,256]{1,0:T(8,128)(2,1)S(1)} %get-tuple-element.38), channel_id=1, source_target_pairs={{2,1},{1,2},{6,5},{5,6},{10,9},{9,10},{14,13},{13,14},{18,17},{17,... | collective-permute-start | bytes 3170312 | tf_op jit(solution)/shard_map/ppermute | solution.py:451
  4.6 20.3 %copy-start.2 = (bf16[16,128,128]{2,1,0:T(8,128)(2,1)S(1)}, bf16[16,128,128]{2,1,0:T(8,128)(2,1)}, u32[]{:S(2)}) copy-start(bf16[16,128,128]{2,1,0:T(8,128)(2,1)} %tiles_in.2) | copy-start | bytes 1572868
  4.6 21.5 %collective-permute-start.1 = (bf16[2,1024,256]{2,1,0:T(8,128)(2,1)S(1)}, bf16[2,1024,256]{2,1,0:T(8,128)(2,1)S(1)}, u32[]{:S(2)}, u32[]{:S(2)}) collective-permute-start(bf16[2,1024,256]{2,1,0:T(8,128)(2,1)S(1)} %pack_middle.1), channel_id=1, source_target_pairs={{2,1},{1,2},{6,5},{5,6},{10,9},{9,10},{14,13},{13,14},{18,17},{17,... | collective-permute-start | bytes 3145736 | tf_op jit(solution)/shard_map/ppermute | solution.py:451
  5.5 13.8 %collective-permute-start.2 = (bf16[528,256]{1,0:T(8,128)(2,1)S(1)}, bf16[528,256]{1,0:T(8,128)(2,1)S(1)}, u32[]{:S(2)}, u32[]{:S(2)}) collective-permute-start(bf16[528,256]{1,0:T(8,128)(2,1)S(1)} %get-tuple-element.39.after), channel_id=1, source_target_pairs={{1,0},{3,1},{0,2},{2,3},{5,4},{7,5},{4,6},{6,7},{9,8},{11,9},{8,10... | collective-permute-start | bytes 811016 | tf_op jit(solution)/shard_map/ppermute | solution.py:451
  19.3 6.9 %copy-start.5 = (bf16[256,256]{1,0:T(8,128)(2,1)S(1)}, bf16[256,256]{1,0:T(8,128)(2,1)}, u32[]{:S(2)}) copy-start(bf16[256,256]{1,0:T(8,128)(2,1)} %weight_in.5) | copy-start | bytes 393220
  19.4 6.7 %collective-permute-start.3 = (bf16[1040,256]{1,0:T(8,128)(2,1)S(1)}, bf16[1040,256]{1,0:T(8,128)(2,1)S(1)}, u32[]{:S(2)}, u32[]{:S(2)}) collective-permute-start(bf16[1040,256]{1,0:T(8,128)(2,1)S(1)} %get-tuple-element.40), channel_id=1, source_target_pairs={{1,0},{0,1},{3,2},{2,3},{5,4},{4,5},{7,6},{6,7},{9,8},{8,9},{11,10... | collective-permute-start | bytes 1597448 | tf_op jit(solution)/shard_map/ppermute | solution.py:451
  24.2 1.9 %collective-permute-start.4 = (bf16[1040,256]{1,0:T(8,128)(2,1)S(1)}, bf16[1040,256]{1,0:T(8,128)(2,1)S(1)}, u32[]{:S(2)}, u32[]{:S(2)}) collective-permute-start(bf16[1040,256]{1,0:T(8,128)(2,1)S(1)} %get-tuple-element.41), channel_id=1, source_target_pairs={{1,4},{3,6},{5,8},{7,10},{9,12},{11,14},{4,1},{6,3},{8,5},{10,7},{... | collective-permute-start | bytes 1597448 | tf_op jit(solution)/shard_map/ppermute | solution.py:451
  26.1 18.8 %copy-start.6 = (f32[4,8,128]{2,1,0:T(8,128)S(1)}, f32[4,8,128]{2,1,0:T(8,128)}, u32[]{:S(2)}) copy-start(f32[4,8,128]{2,1,0:T(8,128)} %target) | copy-start | bytes 49156
  26.1 19.4 %copy-start.7 = (bf16[256]{0:T(256)(128)(2,1)S(1)}, bf16[256]{0:T(256)(128)(2,1)}, u32[]{:S(2)}) copy-start(bf16[256]{0:T(256)(128)(2,1)} %param.12) | copy-start | bytes 1540
  26.1 24.3 %copy-start.4 = (bf16[256,256]{1,0:T(8,128)(2,1)S(1)}, bf16[256,256]{1,0:T(8,128)(2,1)}, u32[]{:S(2)}) copy-start(bf16[256,256]{1,0:T(8,128)(2,1)} %weight_in.4) | copy-start | bytes 393220
  33.3 17.1 %collective-permute-start.5 = (bf16[1024,256]{1,0:T(8,128)(2,1)S(1)}, bf16[1024,256]{1,0:T(8,128)(2,1)S(1)}, u32[]{:S(2)}, u32[]{:S(2)}) collective-permute-start(bf16[1024,256]{1,0:T(8,128)(2,1)S(1)} %get-tuple-element.45), channel_id=1, source_target_pairs={{1,0},{0,1},{3,2},{2,3},{5,4},{4,5},{7,6},{6,7},{9,8},{8,9},{11,10... | collective-permute-start | bytes 1572872 | tf_op jit(solution)/shard_map/ppermute | solution.py:451
  42.4 7.9 %collective-permute-start.6 = (bf16[1024,256]{1,0:T(8,128)(2,1)S(1)}, bf16[1024,256]{1,0:T(8,128)(2,1)S(1)}, u32[]{:S(2)}, u32[]{:S(2)}) collective-permute-start(bf16[1024,256]{1,0:T(8,128)(2,1)S(1)} %get-tuple-element.46), channel_id=1, source_target_pairs={{1,4},{3,6},{5,8},{7,10},{9,12},{11,14},{4,1},{6,3},{8,5},{10,7},{... | collective-permute-start | bytes 1572872 | tf_op jit(solution)/shard_map/ppermute | solution.py:451
  43.1 7.2 %collective-permute-start.7 = (bf16[512,256]{1,0:T(8,128)(2,1)S(1)}, bf16[512,256]{1,0:T(8,128)(2,1)S(1)}, u32[]{:S(2)}, u32[]{:S(2)}) collective-permute-start(bf16[512,256]{1,0:T(8,128)(2,1)S(1)} %get-tuple-element.47), channel_id=1, source_target_pairs={{2,0},{3,1},{0,2},{1,3},{6,4},{7,5},{4,6},{5,7},{10,8},{11,9},{8,1... | collective-permute-start | bytes 786440 | tf_op jit(solution)/shard_map/ppermute | solution.py:451
  44.9 0.7 collective-permute-start.8
  61.5 9.9 %collective-permute-start.9 = (bf16[1024,256]{1,0:T(8,128)(2,1)S(1)}, bf16[1024,256]{1,0:T(8,128)(2,1)S(1)}, u32[]{:S(2)}, u32[]{:S(2)}) collective-permute-start(bf16[1024,256]{1,0:T(8,128)(2,1)S(1)} %get-tuple-element.50), channel_id=1, source_target_pairs={{1,0},{0,1},{3,2},{2,3},{5,4},{4,5},{7,6},{6,7},{9,8},{8,9},{11,10... | collective-permute-start | bytes 1572872 | tf_op jit(solution)/shard_map/ppermute | solution.py:451
  64.1 7.2 %collective-permute-start.10 = (bf16[1024,256]{1,0:T(8,128)(2,1)S(1)}, bf16[1024,256]{1,0:T(8,128)(2,1)S(1)}, u32[]{:S(2)}, u32[]{:S(2)}) collective-permute-start(bf16[1024,256]{1,0:T(8,128)(2,1)S(1)} %get-tuple-element.51), channel_id=1, source_target_pairs={{1,4},{3,6},{5,8},{7,10},{9,12},{11,14},{4,1},{6,3},{8,5},{10,7},{... | collective-permute-start | bytes 1572872 | tf_op jit(solution)/shard_map/ppermute | solution.py:451
  64.8 6.5 %collective-permute-start.11 = (bf16[512,256]{1,0:T(8,128)(2,1)S(1)}, bf16[512,256]{1,0:T(8,128)(2,1)S(1)}, u32[]{:S(2)}, u32[]{:S(2)}) collective-permute-start(bf16[512,256]{1,0:T(8,128)(2,1)S(1)} %get-tuple-element.52), channel_id=1, source_target_pairs={{2,0},{3,1},{0,2},{1,3},{6,4},{7,5},{4,6},{5,7},{10,8},{11,9},{8,1... | collective-permute-start | bytes 786440 | tf_op jit(solution)/shard_map/ppermute | solution.py:451
  67.0 0.7 collective-permute-start.12
  77.1 6.3 %collective-permute-start.13 = (f32[136,256]{1,0:T(8,128)S(1)}, f32[136,256]{1,0:T(8,128)S(1)}, u32[]{:S(2)}, u32[]{:S(2)}) collective-permute-start(f32[136,256]{1,0:T(8,128)S(1)} %get-tuple-element.60), channel_id=1, source_target_pairs={{0,1},{1,0},{2,3},{3,2},{4,5},{5,4},{6,7},{7,6},{8,9},{9,8},{10,11... | collective-permute-start | bytes 417800 | tf_op jit(solution)/shard_map/ppermute | solution.py:415
  81.5 6.5 %collective-permute-start.14 = (f32[136,256]{1,0:T(8,128)S(1)}, f32[136,256]{1,0:T(8,128)S(1)}, u32[]{:S(2)}, u32[]{:S(2)}) collective-permute-start(f32[136,256]{1,0:T(8,128)S(1)} %get-tuple-element.61), channel_id=1, source_target_pairs={{0,2},{1,3},{2,0},{3,1},{4,6},{5,7},{6,4},{7,5},{8,10},{9,11},{10,... | collective-permute-start | bytes 417800 | tf_op jit(solution)/shard_map/ppermute | solution.py:415
  83.5 6.3 %collective-permute-start.15 = (f32[136,256]{1,0:T(8,128)S(1)}, f32[136,256]{1,0:T(8,128)S(1)}, u32[]{:S(2)}, u32[]{:S(2)}) collective-permute-start(f32[136,256]{1,0:T(8,128)S(1)} %get-tuple-element.62), channel_id=1, source_target_pairs={{0,3},{1,2},{2,1},{3,0},{4,7},{5,6},{6,5},{7,4},{8,11},{9,10},{10,... | collective-permute-start | bytes 417800 | tf_op jit(solution)/shard_map/ppermute | solution.py:415
  89.8 5.8 %collective-permute-start.16 = (f32[40,256]{1,0:T(8,128)S(1)}, f32[40,256]{1,0:T(8,128)S(1)}, u32[]{:S(2)}, u32[]{:S(2)}) collective-permute-start(f32[40,256]{1,0:T(8,128)S(1)} %get-tuple-element.64), channel_id=1, source_target_pairs={{0,4},{1,5},{2,6},{3,7},{4,0},{5,1},{6,2},{7,3},{8,12},{9,13},{10,... | collective-permute-start | bytes 122888 | tf_op jit(solution)/shard_map/ppermute | solution.py:415
  93.1 5.8 %collective-permute-start.17 = (f32[40,256]{1,0:T(8,128)S(1)}, f32[40,256]{1,0:T(8,128)S(1)}, u32[]{:S(2)}, u32[]{:S(2)}) collective-permute-start(f32[40,256]{1,0:T(8,128)S(1)} %get-tuple-element.65), channel_id=1, source_target_pairs={{0,8},{1,9},{2,10},{3,11},{4,12},{5,13},{6,14},{7,15},{8,0},{9,1},... | collective-permute-start | bytes 122888 | tf_op jit(solution)/shard_map/ppermute | solution.py:415
  93.6 5.9 %collective-permute-start.18 = (f32[40,256]{1,0:T(8,128)S(1)}, f32[40,256]{1,0:T(8,128)S(1)}, u32[]{:S(2)}, u32[]{:S(2)}) collective-permute-start(f32[40,256]{1,0:T(8,128)S(1)} %get-tuple-element.66), channel_id=1, source_target_pairs={{0,12},{1,13},{2,14},{3,15},{4,8},{5,9},{6,10},{7,11},{8,4},{9,5},... | collective-permute-start | bytes 122888 | tf_op jit(solution)/shard_map/ppermute | solution.py:415

commit v4 on v3

--- a/solution.py
+++ b/solution.py
@@ -54,12 +54,17 @@
         copy.wait()
 
 
-def block_product(table, field, tiles, turned, row, col, nodes, rows, cols):
+def at_block(col, nodes):
+    return pl.ds(col * nodes if isinstance(col, int) else pl.multiple_of(col * nodes, nodes), nodes)
+
+
+def block_product(table, field, tiles, turned, row, col, shape):
+    nodes, rows, cols = shape
     at = row * cols + col
     step = rows * cols
 
     def block(r, c):
-        return field[r, c * nodes : (c + 1) * nodes]
+        return field[r, at_block(c, nodes)]
 
     lhs = jnp.concatenate(
         [
@@ -87,7 +92,132 @@
     return jnp.dot(lhs, rhs, preferred_element_type=F32)
 
 
-def rim_pairs(field, inner, outer, side, nodes, rows, cols):
+def edge_blocks(shape, body):
+    _, rows, cols = shape
+
+    def one_row(i, carry):
+        for col in range(0, cols, 2):
+            body(i * (rows - 1), [col, col + 1])
+        return carry
+
+    lax.fori_loop(0, 2, one_row, 0)
+    _, right, _ = place()
+    for row in range(1, rows - 1):
+        body(row, [jnp.where(right == 0, cols - 1, 0)])
+
+
+def inner_blocks(shape, body):
+    _, rows, cols = shape
+    _, right, _ = place()
+
+    def one_row(row, carry):
+        for col in range(0, cols - 1, 2):
+            body(row, [right + c for c in range(col, min(col + 2, cols - 1))])
+        return carry
+
+    lax.fori_loop(1, rows - 1, one_row, 0)
+
+
+def group(cols, nodes):
+    start = cols[0] * nodes
+    return pl.ds(start if isinstance(start, int) else pl.multiple_of(start, nodes), len(cols) * nodes)
+
+
+def group_in_field(cols, nodes):
+    return group([cols[0] + 1] + cols[1:], nodes)
+
+
+def forward_one(shape, table, field, tiles, turned, weight, x_field, m_all):
+    nodes = shape[0]
+
+    def body(row, cols):
+        for col in cols:
+            m_all[row, at_block(col, nodes)] = block_product(table, field, tiles, turned, row, col, shape).astype(BF16)
+        z = jnp.dot(m_all[row, group(cols, nodes)], weight[...], preferred_element_type=F32)
+        inside = group_in_field(cols, nodes)
+        x_field[row + 1, inside] = (field[row + 1, inside].astype(F32) + jnp.tanh(z)).astype(BF16)
+
+    return body
+
+
+def residual_columns(seen, goal, scale):
+    gp = (seen - goal) * scale
+    column = jnp.broadcast_to(gp, (gp.shape[1], gp.shape[1])).T
+    return jnp.concatenate([column, column], axis=1)
+
+
+def through_two(shape, scale, table, field, tiles, turned, weight, readout, goals, m_all, gz_all, g_field, preds, sums):
+    nodes = shape[0]
+    eight = jnp.broadcast_to(readout[...], (8, readout.shape[1]))
+    readf = readout[...].astype(F32)
+
+    def body(row, cols):
+        for col in cols:
+            m_all[row, at_block(col, nodes)] = block_product(table, field, tiles, turned, row, col, shape).astype(BF16)
+        here, inside = group(cols, nodes), group_in_field(cols, nodes)
+        t = jnp.tanh(jnp.dot(m_all[row, here], weight[...], preferred_element_type=F32))
+        x = (field[row + 1, inside].astype(F32) + t).astype(BF16)
+        seen = lax.dot_general(eight, x, (((1,), (1,)), ((), ())), preferred_element_type=F32)[0:1]
+        parts = []
+        for k, col in enumerate(cols):
+            one = seen[:, k * nodes : (k + 1) * nodes]
+            preds[row, pl.ds(col, 1)] = one
+            parts.append(residual_columns(one, goals[row, pl.ds(col, 1)], scale))
+        gp = jnp.concatenate(parts, axis=0) if len(parts) > 1 else parts[0]
+        sums[...] += (x.astype(F32) * gp).reshape(gp.shape[0] // 8, 8, gp.shape[1]).sum(axis=0)
+        gz = (gp * readf * (1.0 - t * t)).astype(BF16)
+        gz_all[row, here] = gz
+        g_field[row + 1, inside] = lax.dot_general(
+            gz, weight[...], (((1,), (1,)), ((), ())), preferred_element_type=F32
+        ).astype(BF16)
+
+    return body
+
+
+def back_one(shape, scale, table, field, tiles, turned, weight, readout, goals, preds, m_all, gz_all):
+    nodes = shape[0]
+    readf = readout[...].astype(F32)
+
+    def body(row, cols):
+        here = group(cols, nodes)
+        t = jnp.tanh(jnp.dot(m_all[row, here], weight[...], preferred_element_type=F32))
+        for k, col in enumerate(cols):
+            gp = residual_columns(preds[row, pl.ds(col, 1)], goals[row, pl.ds(col, 1)], scale)
+            gx = gp * readf + block_product(table, field, tiles, turned, row, col, shape)
+            tk = t[k * nodes : (k + 1) * nodes]
+            gz_all[row, at_block(col, nodes)] = (gx * (1.0 - tk * tk)).astype(BF16)
+
+    return body
+
+
+def over_nodes(left, right):
+    return lax.dot_general(left, right, (((0,), (0,)), ((), ())), preferred_element_type=F32)
+
+
+def zero_rim(field, shape):
+    nodes, rows, cols = shape
+    field[0] = jnp.zeros(field.shape[1:], field.dtype)
+    field[rows + 1] = jnp.zeros(field.shape[1:], field.dtype)
+    for row in range(1, rows + 1):
+        for col in (0, cols + 1):
+            field[row, at_block(col, nodes)] = jnp.zeros((nodes, field.shape[2]), field.dtype)
+
+
+def edge_pairs(field, inner, outer, side, shape):
+    nodes, rows, cols = shape
+    half, right, _ = place()
+    inside = pl.ds(nodes, cols * nodes)
+    pairs = [
+        (field.at[jnp.where(half == 0, rows, 1), inside], inner),
+        (field.at[jnp.where(half == 0, 1, rows), inside], outer),
+    ]
+    for row in range(rows):
+        pairs.append((field.at[row + 1, at_block(jnp.where(right == 0, cols, 1), nodes)], side.at[at_block(row, nodes)]))
+    return pairs
+
+
+def rim_pairs(field, inner, outer, side, shape):
+    nodes, rows, cols = shape
     half, right, _ = place()
     zero_col = pl.multiple_of(jnp.where(right == 0, 0, (cols + 1) * nodes), nodes)
     side_col = pl.multiple_of(jnp.where(right == 0, (cols + 1) * nodes, 0), nodes)
@@ -101,18 +231,6 @@
     ]
     for row in range(rows):
         pairs.append((side.at[pl.ds(row * nodes, nodes)], field.at[row + 1, pl.ds(side_col, nodes)]))
-    return pairs
-
-
-def edge_pairs(done, inner, outer, side, nodes, rows, cols):
-    half, right, _ = place()
-    col = pl.multiple_of(jnp.where(right == 0, (cols - 1) * nodes, 0), nodes)
-    pairs = [
-        (done.at[jnp.where(half == 0, rows - 1, 0)], inner),
-        (done.at[jnp.where(half == 0, 0, rows - 1)], outer),
-    ]
-    for row in range(rows):
-        pairs.append((done.at[row, pl.ds(col, nodes)], side.at[pl.ds(row * nodes, nodes)]))
     return pairs
 
 
@@ -140,8 +258,8 @@
     wait_all(start_all([(own.at[pl.ds(1, own.shape[0] - 2)], middle)], sems))
 
 
-def turn_kernel(tiles, turned, plain, sems):
-    wait_all(start_all([(tiles, plain)], sems))
+def prepare_kernel(tiles, first, second, plain, turned, first_in, second_in, sems):
+    wait_all(start_all([(tiles, plain), (first, first_in), (second, second_in)], sems))
 
     def one_tile(tile, carry):
         turned[tile] = plain[tile].T
@@ -150,7 +268,7 @@
     lax.fori_loop(0, tiles.shape[0], one_tile, 0)
 
 
-def pick_kernel(numbers, own, ends, after, inner, outer, sems):
+def pick_kernel(numbers, own, ends, after, later, inner, outer, sems):
     rows, line = own.shape[0], own.shape[1]
     half, _, moved = place()
     whole = pl.ds(0, line)
@@ -178,10 +296,10 @@
         wait_all(copies)
 
 
-def first_kernel(nodes, cols, numbers, own, ends, middle, inner, outer, side, tiles_in, turned_in, weight_in,
-                 table, x_out, m_out, inner_out, outer_out, side_out,
-                 field, x_new, m_new, tiles, turned, weight, heads, heads_int, marks, sems):
-    rows, line, width = own.shape
+def first_edge_kernel(shape, numbers, own, ends, middle, inner, outer, side, tiles, turned, weight,
+                      table, field, x_field, m_all, inner_out, outer_out, side_out, heads, heads_int, marks, sems):
+    nodes, rows, cols = shape
+    line = cols * nodes
     step = rows * cols
     half, _, moved = place()
     inside = pl.ds(nodes, line)
@@ -227,8 +345,7 @@
     either(half == 1, above_pairs, 4)
     left = start_all([(side.at[pl.ds(rows * nodes, TAIL)], heads.at[2])], sems, 5)
     rest = start_all(
-        [(tiles_in, tiles), (turned_in, turned), (weight_in, weight)]
-        + rim_pairs(field, inner, outer, side, nodes, rows, cols),
+        rim_pairs(field, inner, outer, side, shape),
         sems,
         6,
     )
@@ -253,37 +370,17 @@
         return carry
 
     lax.fori_loop(0, step, fill, 0)
+    zero_rim(x_field, shape)
     wait_all(rest)
     either_wait(moved, main_pairs, 0, 1, None)
 
-    def one_row(row, carry):
-        for col in range(cols):
-            m_new[row, col * nodes : (col + 1) * nodes] = block_product(
-                table, field, tiles, turned, row, col, nodes, rows, cols
-            ).astype(BF16)
-        for part in range(0, line, 2 * nodes):
-            z = jnp.dot(m_new[row, part : part + 2 * nodes], weight[...], preferred_element_type=F32)
-            base = field[row + 1, nodes + part : 3 * nodes + part]
-            x_new[row, part : part + 2 * nodes] = (base.astype(F32) + jnp.tanh(z)).astype(BF16)
-        return carry
-
-    lax.fori_loop(0, rows, one_row, 0)
-    wait_all(start_all(
-        edge_pairs(x_new, inner_out, outer_out, side_out, nodes, rows, cols) + [(x_new, x_out), (m_new, m_out)], sems
-    ))
-
-
-def second_kernel(nodes, cols, scale, table, x_own, inner, outer, side, tiles_in, turned_in, weight_in, readout,
-                  spread, target, target_swap, g_out, inner_out, outer_out, side_out, pred_out, second_out, readout_out, goals,
-                  field, g_new, m_row, gz_row, tiles, turned, weight, sems):
-    rows, line, width = x_own.shape
-    wait_all(start_all(
-        [(x_own, field.at[pl.ds(1, rows), pl.ds(nodes, line)]), (tiles_in, tiles), (turned_in, turned), (weight_in, weight)]
-        + rim_pairs(field, inner, outer, side, nodes, rows, cols),
-        sems,
-    ))
-    readf = readout[...]
-    moved = place()[2]
+    edge_blocks(shape, forward_one(shape, table, field, tiles, turned, weight, x_field, m_all))
+    wait_all(start_all(edge_pairs(x_field, inner_out, outer_out, side_out, shape), sems))
+
+
+def middle_compute_kernel(shape, scale, table, field, tiles, turned, weight_one, weight_two, readout, target,
+                          target_swap, x_in, m_in, x_field, m_one, m_two, gz_two, g_field, preds, goals, sums):
+    _, _, moved = place()
 
     @pl.when(moved)
     def _():
@@ -293,42 +390,72 @@
     def _():
         goals[...] = target[...]
 
-    lanes = lax.broadcasted_iota(jnp.int32, (nodes, 128), 1)
+    zero_rim(g_field, shape)
+    sums[...] = jnp.zeros_like(sums)
+    inner_blocks(shape, forward_one(shape, table, field, tiles, turned, weight_one, x_field, m_one))
+    inner_blocks(shape, through_two(
+        shape, scale, table, x_field, tiles, turned, weight_two, readout, goals, m_two, gz_two, g_field, preds, sums
+    ))
+
+
+def second_edge_kernel(shape, scale, table, inner, outer, side, tiles, turned, weight, readout, goals,
+                       x_in, m_in, gz_in, g_in, preds_in, sums_in,
+                       x_field, m_two, gz_two, g_field, preds, sums, inner_out, outer_out, side_out, sems):
+    wait_all(start_all(rim_pairs(x_field, inner, outer, side, shape), sems))
+    edge_blocks(shape, through_two(
+        shape, scale, table, x_field, tiles, turned, weight, readout, goals, m_two, gz_two, g_field, preds, sums
+    ))
+    wait_all(start_all(edge_pairs(g_field, inner_out, outer_out, side_out, shape), sems))
+
+
+def back_inner_kernel(shape, scale, table, g_field, tiles, turned, weight, readout, goals, preds, m_one, m_two, gz_two,
+                      gz_one, first_out, second_out):
+    nodes, rows, cols = shape
+    _, right, _ = place()
+    inner_blocks(shape, back_one(shape, scale, table, g_field, tiles, turned, weight, readout, goals, preds, m_one, gz_one))
+    part = pl.ds(pl.multiple_of(right * nodes, nodes), (cols - 1) * nodes)
+    first_out[...] = jnp.zeros_like(first_out)
     second_out[...] = jnp.zeros_like(second_out)
-    readout_out[...] = jnp.zeros_like(readout_out)
 
     def one_row(row, carry):
-        goal = goals[row].T
-        seen = jnp.zeros((nodes, 128), F32)
-        for col in range(cols):
-            m_row[col * nodes : (col + 1) * nodes] = block_product(
-                table, field, tiles, turned, row, col, nodes, rows, cols
-            ).astype(BF16)
-        for col in range(cols):
-            here = slice(col * nodes, (col + 1) * nodes)
-            z = jnp.dot(m_row[here], weight[...], preferred_element_type=F32)
-            t = jnp.tanh(z)
-            x = (field[row + 1, (col + 1) * nodes : (col + 2) * nodes].astype(F32) + t).astype(BF16)
-            pred = jnp.dot(x, spread[...], preferred_element_type=F32)
-            seen = jnp.where(lanes == col, pred, seen)
-            gp = (pred[:, 0:1] - goal[:, col : col + 1]) * scale
-            part = x.astype(F32) * gp
-            readout_out[...] += part.reshape(nodes // 8, 8, width).sum(axis=0)
-            gz = (gp * readf * (1.0 - t * t)).astype(BF16)
-            gz_row[here] = gz
-            g_new[row, here] = lax.dot_general(
-                gz, weight[...], (((1,), (1,)), ((), ())), preferred_element_type=F32
-            ).astype(BF16)
-        second_out[...] += lax.dot_general(
-            m_row[...], gz_row[...], (((0,), (0,)), ((), ())), preferred_element_type=F32
-        )
-        pred_out[row] = seen.T[0:cols]
+        first_out[...] += over_nodes(m_one[row, part], gz_one[row, part])
         return carry
 
-    lax.fori_loop(0, rows, one_row, 0)
-    wait_all(start_all(
-        edge_pairs(g_new, inner_out, outer_out, side_out, nodes, rows, cols) + [(g_new, g_out)], sems
-    ))
+    def each_row(row, carry):
+        second_out[...] += over_nodes(m_two[row], gz_two[row])
+        return carry
+
+    lax.fori_loop(1, rows - 1, one_row, 0)
+    lax.fori_loop(0, rows, each_row, 0)
+
+
+def back_edge_kernel(shape, scale, table, inner, outer, side, tiles, turned, weight, readout, goals, preds, preds_swap,
+                     m_one, first_in, second, sums, g_in, gz_in, g_field, gz_one, keep, one, two, three, pred_out,
+                     first_out, parts, sems):
+    nodes, rows, cols = shape
+    _, right, moved = place()
+    copies = start_all(rim_pairs(g_field, inner, outer, side, shape), sems)
+
+    @pl.when(moved)
+    def _():
+        pred_out[...] = preds_swap[...]
+
+    @pl.when(jnp.logical_not(moved))
+    def _():
+        pred_out[...] = preds[...]
+
+    wait_all(copies)
+    edge_blocks(shape, back_one(shape, scale, table, g_field, tiles, turned, weight, readout, goals, preds, m_one, gz_one))
+    first_out[...] = first_in[...]
+    for row in (0, rows - 1):
+        first_out[...] += over_nodes(m_one[row], gz_one[row])
+    beside = at_block(jnp.where(right == 0, cols - 1, 0), nodes)
+    for row in range(1, rows - 1):
+        first_out[...] += over_nodes(m_one[row, beside], gz_one[row, beside])
+    count, size, width = parts.shape
+    parts[:, : size // 2] = first_out[...].reshape(count, size // 2, width)
+    parts[:, size // 2 :] = second[...].reshape(count, size // 2, width)
+    spread_shares(parts, sums[...], lax.rem(lax.axis_index(AXES), 4), (keep, one, two, three))
 
 
 def spread_shares(parts, extra, digit, outs):
@@ -354,54 +481,6 @@
     first[...] = total[:share]
     second[...] = total[share : 2 * share]
     readout[...] = total[2 * share :].sum(axis=0, keepdims=True)
-
-
-def third_kernel(nodes, cols, scale, table, g_own, inner, outer, side, tiles_in, turned_in, m_own, weight_in, readout,
-                 pred, pred_swap, target, second, extra, keep, one, two, three, pred_out,
-                 first_out, parts, field, m_in, gz_row, tiles, turned, weight, sems):
-    rows, line, width = g_own.shape
-    wait_all(start_all(
-        [
-            (g_own, field.at[pl.ds(1, rows), pl.ds(nodes, line)]),
-            (m_own, m_in),
-            (tiles_in, tiles),
-            (turned_in, turned),
-            (weight_in, weight),
-        ]
-        + rim_pairs(field, inner, outer, side, nodes, rows, cols),
-        sems,
-    ))
-    readf = readout[...]
-    moved = place()[2]
-
-    @pl.when(moved)
-    def _():
-        pred_out[...] = pred_swap[...]
-
-    @pl.when(jnp.logical_not(moved))
-    def _():
-        pred_out[...] = pred[...]
-
-    first_out[...] = jnp.zeros_like(first_out)
-
-    def one_row(row, carry):
-        gp_all = ((pred[row] - target[row]) * scale).T
-        for col in range(cols):
-            here = slice(col * nodes, (col + 1) * nodes)
-            gx = gp_all[:, col : col + 1] * readf
-            gx = gx + block_product(table, field, tiles, turned, row, col, nodes, rows, cols)
-            t = jnp.tanh(jnp.dot(m_in[row, here], weight[...], preferred_element_type=F32))
-            gz_row[here] = (gx * (1.0 - t * t)).astype(BF16)
-        first_out[...] += lax.dot_general(
-            m_in[row], gz_row[...], (((0,), (0,)), ((), ())), preferred_element_type=F32
-        )
-        return carry
-
-    lax.fori_loop(0, rows, one_row, 0)
-    count, size, _ = parts.shape
-    parts[:, : size // 2] = first_out[...].reshape(count, size // 2, width)
-    parts[:, size // 2 :] = second[...].reshape(count, size // 2, width)
-    spread_shares(parts, extra[...], lax.rem(lax.axis_index(AXES), 4), (keep, one, two, three))
 
 
 def shares_shape(groups, size, width):
@@ -481,98 +560,111 @@
         name="pack_middle",
     )(features, side_s)
     middle = send(middle_s, swap)
-    target, tiles, _ = lax.optimization_barrier((target, tiles, middle_s))
+    target, tiles, w_first, w_second, _ = lax.optimization_barrier((target, tiles, w_first, w_second, middle_s))
     goal_swap = send(target, swap)
-    turned = pl.pallas_call(
-        turn_kernel,
-        out_shape=bf(*tiles.shape),
-        in_specs=[ANY],
-        out_specs=VMEM,
-        scratch_shapes=[pltpu.VMEM(tiles.shape, BF16), sems(1)],
-        compiler_params=params,
-        name="turn",
-    )(tiles)
-    readf = readout.astype(F32)[None]
-    spread = jnp.broadcast_to(readout[:, None], (width, 128))
+    tiles, turned, w_first, w_second = pl.pallas_call(
+        prepare_kernel,
+        out_shape=(bf(*tiles.shape), bf(*tiles.shape), bf(width, width), bf(width, width)),
+        in_specs=[ANY] * 3,
+        out_specs=(VMEM,) * 4,
+        scratch_shapes=[sems(3)],
+        compiler_params=params,
+        name="prepare",
+    )(tiles, w_first, w_second)
+    readout = readout[None]
 
     inner_s, outer_s = pl.pallas_call(
         pick_kernel,
         out_shape=(bf(line + TAIL, width),) * 2,
-        in_specs=[VMEM, ANY, ANY, ANY],
+        in_specs=[VMEM, ANY, ANY, ANY, ANY],
         out_specs=(VMEM,) * 2,
         scratch_shapes=[sems(4)],
         compiler_params=params,
         name="pick",
-    )(numbers, features, ends, side)
+    )(numbers, features, ends, side, goal_swap)
     outer, inner = send(outer_s, outer_way), send(inner_s, inner_way)
 
-    patch = bf(rows, line, width)
+    shape = (nodes, rows, cols)
+    patch, padded = bf(rows, line, width), bf(rows + 2, line + 2 * nodes, width)
     edge_shapes = (bf(line, width), bf(line, width), bf(rows * nodes, width))
     square = jax.ShapeDtypeStruct((width, width), F32)
-    rim = pltpu.VMEM((rows + 2, line + 2 * nodes, width), BF16)
-    whole = pltpu.VMEM((rows, line, width), BF16)
-    strip = pltpu.VMEM((line, width), BF16)
-    loads = [pltpu.VMEM(tiles.shape, BF16), pltpu.VMEM(tiles.shape, BF16), pltpu.VMEM((width, width), BF16)]
-    product = 2 * rows * line * width * 6 * nodes
-    dense = 2 * rows * line * width * width
-    moves = 2 * rows * line * width
-
-    def cost(denses, passes):
+    sums_shape = jax.ShapeDtypeStruct((8, width), F32)
+    goal_shape = jax.ShapeDtypeStruct(target.shape, F32)
+    block = nodes * width
+    edge, inside = 2 * cols + rows - 2, (rows - 2) * (cols - 1)
+
+    def cost(products, denses):
         return pl.CostEstimate(
-            flops=product + denses * dense, bytes_accessed=passes * moves, transcendentals=rows * line * width
+            flops=2 * block * (products * 6 * nodes + denses * width),
+            bytes_accessed=4 * block * (products + denses),
+            transcendentals=block * products,
         )
 
-    table, x_one, m_one, inner_s, outer_s, side_s = pl.pallas_call(
-        functools.partial(first_kernel, nodes, cols),
-        out_shape=(jax.ShapeDtypeStruct((5 * step,), jnp.int32), patch, patch) + edge_shapes,
-        in_specs=[ANY] * 10,
-        out_specs=(SMEM,) + (ANY,) * 5,
-        scratch_shapes=[rim, whole, whole]
-        + loads
-        + [
+    table, f_field, x_field, m_one, inner_s, outer_s, side_s = pl.pallas_call(
+        functools.partial(first_edge_kernel, shape),
+        out_shape=(jax.ShapeDtypeStruct((5 * step,), jnp.int32), padded, padded, patch) + edge_shapes,
+        in_specs=[ANY] * 7 + [VMEM] * 3,
+        out_specs=(SMEM,) + (VMEM,) * 6,
+        scratch_shapes=[
             pltpu.VMEM((3, TAIL, width), BF16),
             pltpu.VMEM((3, TAIL, 128), jnp.int32),
             pltpu.SMEM((3, TAIL, 128), jnp.int32),
-            sems(11 + rows),
+            sems(8 + rows),
         ],
         compiler_params=params,
-        cost_estimate=cost(1, 4),
-        name="layer_one",
+        cost_estimate=cost(edge, edge),
+        name="first_edge",
     )(numbers, features, ends, middle, inner, outer, side, tiles, turned, w_first)
 
     inner, outer, side = edges(inner_s, outer_s, side_s)
-    g_two, inner_s, outer_s, side_s, pred, second, readout_part, goal = pl.pallas_call(
-        functools.partial(second_kernel, nodes, cols, scale),
-        out_shape=(patch,) + edge_shapes
-        + (
-            jax.ShapeDtypeStruct(target.shape, F32),
-            square,
-            jax.ShapeDtypeStruct((8, width), F32),
-            jax.ShapeDtypeStruct(target.shape, F32),
-        ),
-        in_specs=[SMEM] + [ANY] * 7 + [VMEM] * 4,
-        out_specs=(ANY,) * 4 + (VMEM,) * 4,
-        scratch_shapes=[rim, whole, strip, strip] + loads + [sems(6 + rows)],
-        compiler_params=params,
-        cost_estimate=cost(3, 3),
-        name="layer_two",
-    )(table, x_one, inner, outer, side, tiles, turned, w_second, readf, spread, target, goal_swap)
+    x_field, m_one, m_two, gz_two, g_field, preds, goals, sums = pl.pallas_call(
+        functools.partial(middle_compute_kernel, shape, scale),
+        out_shape=(padded, patch, patch, patch, padded, goal_shape, goal_shape, sums_shape),
+        in_specs=[SMEM] + [VMEM] * 10,
+        out_specs=(VMEM,) * 8,
+        input_output_aliases={9: 0, 10: 1},
+        compiler_params=params,
+        cost_estimate=cost(2 * inside, 3 * inside),
+        name="inner_forward",
+    )(table, f_field, tiles, turned, w_first, w_second, readout, target, goal_swap, x_field, m_one)
+
+    x_field, m_two, gz_two, g_field, preds, sums, inner_s, outer_s, side_s = pl.pallas_call(
+        functools.partial(second_edge_kernel, shape, scale),
+        out_shape=(padded, patch, patch, padded, goal_shape, sums_shape) + edge_shapes,
+        in_specs=[SMEM] + [ANY] * 3 + [VMEM] * 11,
+        out_specs=(VMEM,) * 9,
+        input_output_aliases={9 + i: i for i in range(6)},
+        scratch_shapes=[sems(2 + rows)],
+        compiler_params=params,
+        cost_estimate=cost(edge, 2 * edge),
+        name="second_edge",
+    )(table, inner, outer, side, tiles, turned, w_second, readout, goals, x_field, m_two, gz_two, g_field, preds, sums)
 
     inner, outer, side = edges(inner_s, outer_s, side_s)
-    pred_swap = send(pred, swap)
+    preds_swap = send(preds, swap)
+    gz_one, first, second = pl.pallas_call(
+        functools.partial(back_inner_kernel, shape, scale),
+        out_shape=(patch, square, square),
+        in_specs=[SMEM] + [VMEM] * 10,
+        out_specs=(VMEM,) * 3,
+        compiler_params=params,
+        cost_estimate=cost(inside, 2 * inside + rows * cols),
+        name="back_inner",
+    )(table, g_field, tiles, turned, w_first, readout, goals, preds, m_one, m_two, gz_two)
+
     share = width // count
-    *outs, pred_out = pl.pallas_call(
-        functools.partial(third_kernel, nodes, cols, scale),
-        out_shape=shares_shape(count // 4, 2 * share, width) + (jax.ShapeDtypeStruct(target.shape, F32),),
-        in_specs=[SMEM] + [ANY] * 8 + [VMEM] * 6,
-        out_specs=(VMEM,) * 5,
-        scratch_shapes=[pltpu.VMEM((width, width), F32), pltpu.VMEM((count, 2 * share, width), F32), rim, whole, strip]
-        + loads
-        + [sems(7 + rows)],
-        compiler_params=params,
-        cost_estimate=cost(2, 3),
-        name="layer_one_back",
-    )(table, g_two, inner, outer, side, tiles, turned, m_one, w_first, readf, pred, pred_swap, goal, second, readout_part)
+    _, _, *outs, pred_out = pl.pallas_call(
+        functools.partial(back_edge_kernel, shape, scale),
+        out_shape=(padded, patch) + shares_shape(count // 4, 2 * share, width) + (goal_shape,),
+        in_specs=[SMEM] + [ANY] * 3 + [VMEM] * 13,
+        out_specs=(VMEM,) * 7,
+        input_output_aliases={15: 0, 16: 1},
+        scratch_shapes=[pltpu.VMEM((width, width), F32), pltpu.VMEM((count, 2 * share, width), F32), sems(2 + rows)],
+        compiler_params=params,
+        cost_estimate=cost(edge, 2 * edge),
+        name="back_edge",
+    )(table, inner, outer, side, tiles, turned, w_first, readout, goals, preds, preds_swap, m_one, first, second, sums,
+      g_field, gz_one)
     first, second, extra = sum_shares(outs, count, share, width, params)
     return pred_out, first, second, extra[0]
 

time: 101 us -> 107 us (1.059)
  Pallas kernels: 26.4 us -> 33.6 us
  waiting for transfers between devices: 25.7 us -> 18.9 us
  starting transfers between devices: 44.5 us -> 51.1 us
    ppermute x13, starting transfers between devices: 32.4 us -> 41.7 us  [send(): return lax.ppermute(value, AXES, way)]
    pallas_call x4 -> x6, Pallas kernels: 25.1 us -> 32.2 us  [the longest x1 8.2 us: per_device(): pl.pallas_call(functools.partial(middle_compute_kernel, shape, scale), ou...]
    ppermute x13, waiting for transfers between devices: 15.4 us -> 8.45 us  [send(): return lax.ppermute(value, AXES, way)]
    ppermute x6, starting transfers between devices: 12.1 us -> 9.37 us  [sum_shares(): lax.ppermute(outs[k], AXES, [(i, i ^ k * base) for i in range(count)])]
  transfers between devices with their start and end apart: 19 -> 19, of which waited for: 7 -> 6; matrix products, arithmetic and copies ran while one was open for 0% -> 0% of each run, Pallas kernels for 1% -> 13%
where the time goes in v4:
time: 107 us
  starting transfers between devices  51.1 us (48%)
  Pallas kernels  33.6 us (31%)
  waiting for transfers between devices  18.9 us (18%)
  local copies, waits for them, and re-layouts  2.52 us (2%)
    ppermute x13, starting transfers between devices, send(): return lax.ppermute(value, AXES, way)  41.7 us
    ppermute x6, waiting for transfers between devices, sum_shares(): lax.ppermute(outs[k], AXES, [(i, i ^ k * base) for i in range(count)])  10.5 us
    ppermute x6, starting transfers between devices, sum_shares(): lax.ppermute(outs[k], AXES, [(i, i ^ k * base) for i in range(count)])  9.37 us
    ppermute x13, waiting for transfers between devices, send(): return lax.ppermute(value, AXES, way)  8.45 us
    pallas_call x1, Pallas kernels, per_device(): pl.pallas_call(functools.partial(middle_compute_kernel, shape, scale), ou...  8.2 us
    pallas_call x1, Pallas kernels, per_device(): pl.pallas_call(functools.partial(second_edge_kernel, shape, scale), out_s...  8.16 us
    pallas_call x1, Pallas kernels, per_device(): pl.pallas_call(functools.partial(first_edge_kernel, shape), out_shape=(ja...  6.6 us
    pallas_call x1, Pallas kernels, per_device(): pl.pallas_call(functools.partial(back_inner_kernel, shape, scale), out_sh...  4.04 us
  transfers between devices with their start and end apart: 19, of which 6 were waited for; matrix products, arithmetic and copies ran while one was open for 0% of the time, Pallas kernels for 13%

profile of v4, /device:TPU:0, one launch (start us, length us, event | category | flops | bytes accessed | tf_op | source)
XLA Modules:
  0.0 107.0 jit_solution(14250621929714471067)
XLA Ops:
  0.6 1.6 %copy-done = bf16[4,8,128,256]{3,2,1,0:T(8,128)(2,1)S(1)} copy-done((bf16[4,8,128,256]{3,2,1,0:T(8,128)(2,1)S(1)}, bf16[4,8,128,256]{3,2,1,0:T(8,128)(2,1)}, u32[]{:S(2)}) %copy-start) | copy-done | bytes 2097176
  2.2 0.7 copy-done.6
  3.4 0.9 collective-permute-start
  4.6 0.9 collective-permute-start.1
  5.5 6.9 %collective-permute-start.2 = (bf16[528,256]{1,0:T(8,128)(2,1)S(1)}, bf16[528,256]{1,0:T(8,128)(2,1)S(1)}, u32[]{:S(2)}, u32[]{:S(2)}) collective-permute-start(bf16[528,256]{1,0:T(8,128)(2,1)S(1)} %get-tuple-element.57.after), channel_id=1, source_target_pairs={{1,0},{3,1},{0,2},{2,3},{5,4},{7,5},{4,6},{6,7},{9,8},{11,9},{8,10... | collective-permute-start | bytes 811016 | tf_op jit(solution)/shard_map/ppermute | solution.py:530
  12.4 0.7 collective-permute-start.3
  13.1 6.3 %collective-permute-done.2.after.side = bf16[528,256]{1,0:T(8,128)(2,1)S(1)} collective-permute-done((bf16[528,256]{1,0:T(8,128)(2,1)S(1)}, bf16[528,256]{1,0:T(8,128)(2,1)S(1)}, u32[]{:S(2)}, u32[]{:S(2)}) %collective-permute-start.2) | collective-permute-done | bytes 270368 | tf_op jit(solution)/shard_map/ppermute | solution.py:530
  19.5 16.2 %collective-permute-start.4 = (bf16[1040,256]{1,0:T(8,128)(2,1)S(1)}, bf16[1040,256]{1,0:T(8,128)(2,1)S(1)}, u32[]{:S(2)}, u32[]{:S(2)}) collective-permute-start(bf16[1040,256]{1,0:T(8,128)(2,1)S(1)} %get-tuple-element.59), channel_id=1, source_target_pairs={{1,0},{0,1},{3,2},{2,3},{5,4},{4,5},{7,6},{6,7},{9,8},{8,9},{11,10... | collective-permute-start | bytes 1597448 | tf_op jit(solution)/shard_map/ppermute | solution.py:530
  35.6 0.7 collective-permute-start.5
  36.4 1.5 %prepare.1 = (bf16[16,128,128]{2,1,0:T(8,128)(2,1)S(1)}, bf16[16,128,128]{2,1,0:T(8,128)(2,1)S(1)}, bf16[256,256]{1,0:T(8,128)(2,1)S(1)}, bf16[256,256]{1,0:T(8,128)(2,1)S(1)}) custom-call(bf16[16,128,128]{2,1,0:T(8,128)(2,1)S(1)} %copy-done.2, bf16[256,256]{1,0:T(8,128)(2,1)S(1)} %copy-done.3, bf16[256,256]{1,0:T(8,128)(2,1)S(1)} %copy-done.4), custom_call_target="tpu_custom_call" | custom-call | tf_op jit(solution)/shard_map/prepare/pallas_call | solution.py:565
  37.9 6.6 %first_edge.1 = (s32[160]{0:T(256)S(1)}, bf16[6,1280,256]{2,1,0:T(8,128)(2,1)S(1)}, bf16[6,1280,256]{2,1,0:T(8,128)(2,1)S(1)}, bf16[4,1024,256]{2,1,0:T(8,128)(2...) custom-call(bf16[16,256]{1,0:T(8,128)(2,1)S(1)} %get-tuple-element.55.numbers, ...), custom_call_target="tpu_custom_call" | custom-call | flops 1207959552 | bytes 4718592 | tf_op jit(solution)/shard_map/first_edge/pallas_call | solution.py:603
  44.6 8.3 %collective-permute-start.6 = (bf16[1024,256]{1,0:T(8,128)(2,1)S(1)}, bf16[1024,256]{1,0:T(8,128)(2,1)S(1)}, u32[]{:S(2)}, u32[]{:S(2)}) collective-permute-start(bf16[1024,256]{1,0:T(8,128)(2,1)S(1)} %get-tuple-element.68), channel_id=1, source_target_pairs={{1,0},{0,1},{3,2},{2,3},{5,4},{4,5},{7,6},{6,7},{9,8},{8,9},{11,10... | collective-permute-start | bytes 1572872 | tf_op jit(solution)/shard_map/ppermute | solution.py:530
  52.9 0.7 collective-permute-start.7
  53.6 2.2 %collective-permute-start.8 = (bf16[512,256]{1,0:T(8,128)(2,1)S(1)}, bf16[512,256]{1,0:T(8,128)(2,1)S(1)}, u32[]{:S(2)}, u32[]{:S(2)}) collective-permute-start(bf16[512,256]{1,0:T(8,128)(2,1)S(1)} %get-tuple-element.70), channel_id=1, source_target_pairs={{2,0},{3,1},{0,2},{1,3},{6,4},{7,5},{4,6},{5,7},{10,8},{11,9},{8,1... | collective-permute-start | bytes 786440 | tf_op jit(solution)/shard_map/ppermute | solution.py:530
  55.7 8.2 %inner_forward.1 = (bf16[6,1280,256]{2,1,0:T(8,128)(2,1)S(1)}, bf16[4,1024,256]{2,1,0:T(8,128)(2,1)S(1)}, bf16[4,1024,256]{2,1,0:T(8,128)(2,1)S(1)}, bf16[4,1024...) custom-call(s32[160]{0:T(256)S(1)} %get-tuple-element.67.table, ...), custom_call_target="tpu_custom_call", output_to_operand_aliasing={{0}: (9, {}), {1}: (10, {})} | custom-call | flops 2113929216 | bytes 9175040 | tf_op jit(solution)/shard_map/inner_forward/pallas_call | solution.py:620
  64.0 8.2 %second_edge.1 = (bf16[6,1280,256]{2,1,0:T(8,128)(2,1)S(1)}, bf16[4,1024,256]{2,1,0:T(8,128)(2,1)S(1)}, bf16[4,1024,256]{2,1,0:T(8,128)(2,1)S(1)}, bf16[6,1280,2...) custom-call(s32[160]{0:T(256)S(1)} %get-tuple-element.67.table, ...), custom_call_target="tpu_custom_call", output_to_operand_aliasing={{0}: (9, {}), {1}: (10, {}), {2}: (11, {}), {3}: (12, {}), ... | custom-call | flops 1509949440 | bytes 7077888 | tf_op jit(solution)/shard_map/second_edge/pallas_call | solution.py:631
  72.1 2.7 %collective-permute-start.9 = (bf16[1024,256]{1,0:T(8,128)(2,1)S(1)}, bf16[1024,256]{1,0:T(8,128)(2,1)S(1)}, u32[]{:S(2)}, u32[]{:S(2)}) collective-permute-start(bf16[1024,256]{1,0:T(8,128)(2,1)S(1)} %get-tuple-element.82), channel_id=1, source_target_pairs={{1,0},{0,1},{3,2},{2,3},{5,4},{4,5},{7,6},{6,7},{9,8},{8,9},{11,10... | collective-permute-start | bytes 1572872 | tf_op jit(solution)/shard_map/ppermute | solution.py:530
  74.8 0.7 collective-permute-start.10
  75.9 0.7 collective-permute-start.12
  76.6 4.0 %back_inner.1 = (bf16[4,1024,256]{2,1,0:T(8,128)(2,1)S(1)}, f32[256,256]{1,0:T(8,128)S(1)}, f32[256,256]{1,0:T(8,128)S(1)}) custom-call(s32[160]{0:T(256)S(1)} %get-tuple-element.67.table, bf16[6,1280,256]{2,1,0:T(8,128)(2,1)S(1)} %get-tuple-element.87.g_field.g_in, bf16[16,128,128]{2,1,0:T(8,128)(2,1)S(1)} %get-tuple-element.64.tiles, ...), custom_call_target="tpu_custom_call" | custom-call | flops 1711276032 | bytes 9699328 | tf_op jit(solution)/shard_map/back_inner/pallas_call | solution.py:645
  80.6 2.1 %collective-permute-done.11.side = bf16[512,256]{1,0:T(8,128)(2,1)S(1)} collective-permute-done((bf16[512,256]{1,0:T(8,128)(2,1)S(1)}, bf16[512,256]{1,0:T(8,128)(2,1)S(1)}, u32[]{:S(2)}, u32[]{:S(2)}) %collective-permute-start.11) | collective-permute-done | bytes 262176 | tf_op jit(solution)/shard_map/ppermute | solution.py:530
  82.8 3.7 %back_edge.1 = (bf16[6,1280,256]{2,1,0:T(8,128)(2,1)S(1)}, bf16[4,1024,256]{2,1,0:T(8,128)(2,1)S(1)}, f32[136,256]{1,0:T(8,128)S(1)}, f32[136,256]{1,0:T(8,128)S...) custom-call(s32[160]{0:T(256)S(1)} %get-tuple-element.67.table, ...), custom_call_target="tpu_custom_call", output_to_operand_aliasing={{0}: (15, {}), {1}: (16, {})} | custom-call | flops 1509949440 | bytes 7077888 | tf_op jit(solution)/shard_map/back_edge/pallas_call | solution.py:656
  86.5 2.6 %collective-permute-start.13 = (f32[136,256]{1,0:T(8,128)S(1)}, f32[136,256]{1,0:T(8,128)S(1)}, u32[]{:S(2)}, u32[]{:S(2)}) collective-permute-start(f32[136,256]{1,0:T(8,128)S(1)} %get-tuple-element.96), channel_id=1, source_target_pairs={{0,1},{1,0},{2,3},{3,2},{4,5},{5,4},{6,7},{7,6},{8,9},{9,8},{10,11... | collective-permute-start | bytes 417800 | tf_op jit(solution)/shard_map/ppermute | solution.py:494
  89.1 0.9 collective-permute-start.14
  90.0 0.5 collective-permute-start.15
  90.6 5.1 %collective-permute-done.14.two = f32[136,256]{1,0:T(8,128)S(1)} collective-permute-done((f32[136,256]{1,0:T(8,128)S(1)}, f32[136,256]{1,0:T(8,128)S(1)}, u32[]{:S(2)}, u32[]{:S(2)}) %collective-permute-start.14) | collective-permute-done | bytes 139296 | tf_op jit(solution)/shard_map/ppermute | solution.py:494
  95.7 1.2 %collective-permute-done.15.three = f32[136,256]{1,0:T(8,128)S(1)} collective-permute-done((f32[136,256]{1,0:T(8,128)S(1)}, f32[136,256]{1,0:T(8,128)S(1)}, u32[]{:S(2)}, u32[]{:S(2)}) %collective-permute-start.15) | collective-permute-done | bytes 139296 | tf_op jit(solution)/shard_map/ppermute | solution.py:494
  96.9 2.9 %collective-permute-start.16 = (f32[40,256]{1,0:T(8,128)S(1)}, f32[40,256]{1,0:T(8,128)S(1)}, u32[]{:S(2)}, u32[]{:S(2)}) collective-permute-start(f32[40,256]{1,0:T(8,128)S(1)} %get-tuple-element.100), channel_id=1, source_target_pairs={{0,4},{1,5},{2,6},{3,7},{4,0},{5,1},{6,2},{7,3},{8,12},{9,13},{10,... | collective-permute-start | bytes 122888 | tf_op jit(solution)/shard_map/ppermute | solution.py:494
  99.8 0.7 collective-permute-start.17
  100.5 1.7 %collective-permute-start.18 = (f32[40,256]{1,0:T(8,128)S(1)}, f32[40,256]{1,0:T(8,128)S(1)}, u32[]{:S(2)}, u32[]{:S(2)}) collective-permute-start(f32[40,256]{1,0:T(8,128)S(1)} %get-tuple-element.102), channel_id=1, source_target_pairs={{0,12},{1,13},{2,14},{3,15},{4,8},{5,9},{6,10},{7,11},{8,4},{9,5},... | collective-permute-start | bytes 122888 | tf_op jit(solution)/shard_map/ppermute | solution.py:494
  102.2 3.7 %collective-permute-done.17.two = f32[40,256]{1,0:T(8,128)S(1)} collective-permute-done((f32[40,256]{1,0:T(8,128)S(1)}, f32[40,256]{1,0:T(8,128)S(1)}, u32[]{:S(2)}, u32[]{:S(2)}) %collective-permute-start.17) | collective-permute-done | bytes 40992 | tf_op jit(solution)/shard_map/ppermute | solution.py:494
  106.4 0.6 last_fold.1
  (34 shorter events, 1.9 us)
Async XLA Ops:
  0.6 1.6 %copy-start = (bf16[4,8,128,256]{3,2,1,0:T(8,128)(2,1)S(1)}, bf16[4,8,128,256]{3,2,1,0:T(8,128)(2,1)}, u32[]{:S(2)}) copy-start(bf16[4,8,128,256]{3,2,1,0:T(8,128)(2,1)} %param.7) | copy-start | bytes 6291460
  2.2 0.7 copy-start.6
  2.9 1.6 %copy-start.1 = (bf16[4,8,128,256]{3,2,1,0:T(8,128)(2,1)S(1)}, bf16[4,8,128,256]{3,2,1,0:T(8,128)(2,1)}, u32[]{:S(2)}) copy-start(bf16[4,8,128,256]{3,2,1,0:T(8,128)(2,1)} %param.7) | copy-start | bytes 6291460
  3.4 9.0 %copy-start.5 = (f32[4,8,128]{2,1,0:T(8,128)S(1)}, f32[4,8,128]{2,1,0:T(8,128)}, u32[]{:S(2)}) copy-start(f32[4,8,128]{2,1,0:T(8,128)} %target) | copy-start | bytes 49156
  3.4 15.9 %collective-permute-start = (bf16[2064,256]{1,0:T(8,128)(2,1)S(1)}, bf16[2064,256]{1,0:T(8,128)(2,1)S(1)}, u32[]{:S(2)}, u32[]{:S(2)}) collective-permute-start(bf16[2064,256]{1,0:T(8,128)(2,1)S(1)} %get-tuple-element.56), channel_id=1, source_target_pairs={{2,1},{1,2},{6,5},{5,6},{10,9},{9,10},{14,13},{13,14},{18,17},{17,... | collective-permute-start | bytes 3170312 | tf_op jit(solution)/shard_map/ppermute | solution.py:530
  4.6 31.7 %copy-start.2 = (bf16[16,128,128]{2,1,0:T(8,128)(2,1)S(1)}, bf16[16,128,128]{2,1,0:T(8,128)(2,1)}, u32[]{:S(2)}) copy-start(bf16[16,128,128]{2,1,0:T(8,128)(2,1)} %tiles) | copy-start | bytes 1572868
  4.6 31.7 %copy-start.3 = (bf16[256,256]{1,0:T(8,128)(2,1)S(1)}, bf16[256,256]{1,0:T(8,128)(2,1)}, u32[]{:S(2)}) copy-start(bf16[256,256]{1,0:T(8,128)(2,1)} %first) | copy-start | bytes 393220
  4.6 31.7 %copy-start.4 = (bf16[256,256]{1,0:T(8,128)(2,1)S(1)}, bf16[256,256]{1,0:T(8,128)(2,1)}, u32[]{:S(2)}) copy-start(bf16[256,256]{1,0:T(8,128)(2,1)} %second) | copy-start | bytes 393220
  4.6 33.3 %collective-permute-start.1 = (bf16[2,1024,256]{2,1,0:T(8,128)(2,1)S(1)}, bf16[2,1024,256]{2,1,0:T(8,128)(2,1)S(1)}, u32[]{:S(2)}, u32[]{:S(2)}) collective-permute-start(bf16[2,1024,256]{2,1,0:T(8,128)(2,1)S(1)} %pack_middle.1), channel_id=1, source_target_pairs={{2,1},{1,2},{6,5},{5,6},{10,9},{9,10},{14,13},{13,14},{18,17},{17,... | collective-permute-start | bytes 3145736 | tf_op jit(solution)/shard_map/ppermute | solution.py:530
  5.5 13.8 %collective-permute-start.2 = (bf16[528,256]{1,0:T(8,128)(2,1)S(1)}, bf16[528,256]{1,0:T(8,128)(2,1)S(1)}, u32[]{:S(2)}, u32[]{:S(2)}) collective-permute-start(bf16[528,256]{1,0:T(8,128)(2,1)S(1)} %get-tuple-element.57.after), channel_id=1, source_target_pairs={{1,0},{3,1},{0,2},{2,3},{5,4},{7,5},{4,6},{6,7},{9,8},{11,9},{8,10... | collective-permute-start | bytes 811016 | tf_op jit(solution)/shard_map/ppermute | solution.py:530
  12.4 0.7 collective-permute-start.3
  19.5 18.5 %collective-permute-start.4 = (bf16[1040,256]{1,0:T(8,128)(2,1)S(1)}, bf16[1040,256]{1,0:T(8,128)(2,1)S(1)}, u32[]{:S(2)}, u32[]{:S(2)}) collective-permute-start(bf16[1040,256]{1,0:T(8,128)(2,1)S(1)} %get-tuple-element.59), channel_id=1, source_target_pairs={{1,0},{0,1},{3,2},{2,3},{5,4},{4,5},{7,6},{6,7},{9,8},{8,9},{11,10... | collective-permute-start | bytes 1597448 | tf_op jit(solution)/shard_map/ppermute | solution.py:530
  35.6 2.3 %collective-permute-start.5 = (bf16[1040,256]{1,0:T(8,128)(2,1)S(1)}, bf16[1040,256]{1,0:T(8,128)(2,1)S(1)}, u32[]{:S(2)}, u32[]{:S(2)}) collective-permute-start(bf16[1040,256]{1,0:T(8,128)(2,1)S(1)} %get-tuple-element.60), channel_id=1, source_target_pairs={{1,4},{3,6},{5,8},{7,10},{9,12},{11,14},{4,1},{6,3},{8,5},{10,7},{... | collective-permute-start | bytes 1597448 | tf_op jit(solution)/shard_map/ppermute | solution.py:530
  37.9 17.8 %copy-start.7 = (bf16[256]{0:T(256)(128)(2,1)S(1)}, bf16[256]{0:T(256)(128)(2,1)}, u32[]{:S(2)}) copy-start(bf16[256]{0:T(256)(128)(2,1)} %param.12) | copy-start | bytes 1540
  44.6 19.4 %collective-permute-start.6 = (bf16[1024,256]{1,0:T(8,128)(2,1)S(1)}, bf16[1024,256]{1,0:T(8,128)(2,1)S(1)}, u32[]{:S(2)}, u32[]{:S(2)}) collective-permute-start(bf16[1024,256]{1,0:T(8,128)(2,1)S(1)} %get-tuple-element.68), channel_id=1, source_target_pairs={{1,0},{0,1},{3,2},{2,3},{5,4},{4,5},{7,6},{6,7},{9,8},{8,9},{11,10... | collective-permute-start | bytes 1572872 | tf_op jit(solution)/shard_map/ppermute | solution.py:530
  52.9 11.1 %collective-permute-start.7 = (bf16[1024,256]{1,0:T(8,128)(2,1)S(1)}, bf16[1024,256]{1,0:T(8,128)(2,1)S(1)}, u32[]{:S(2)}, u32[]{:S(2)}) collective-permute-start(bf16[1024,256]{1,0:T(8,128)(2,1)S(1)} %get-tuple-element.69), channel_id=1, source_target_pairs={{1,4},{3,6},{5,8},{7,10},{9,12},{11,14},{4,1},{6,3},{8,5},{10,7},{... | collective-permute-start | bytes 1572872 | tf_op jit(solution)/shard_map/ppermute | solution.py:530
  53.6 10.4 %collective-permute-start.8 = (bf16[512,256]{1,0:T(8,128)(2,1)S(1)}, bf16[512,256]{1,0:T(8,128)(2,1)S(1)}, u32[]{:S(2)}, u32[]{:S(2)}) collective-permute-start(bf16[512,256]{1,0:T(8,128)(2,1)S(1)} %get-tuple-element.70), channel_id=1, source_target_pairs={{2,0},{3,1},{0,2},{1,3},{6,4},{7,5},{4,6},{5,7},{10,8},{11,9},{8,1... | collective-permute-start | bytes 786440 | tf_op jit(solution)/shard_map/ppermute | solution.py:530
  72.1 10.6 %collective-permute-start.9 = (bf16[1024,256]{1,0:T(8,128)(2,1)S(1)}, bf16[1024,256]{1,0:T(8,128)(2,1)S(1)}, u32[]{:S(2)}, u32[]{:S(2)}) collective-permute-start(bf16[1024,256]{1,0:T(8,128)(2,1)S(1)} %get-tuple-element.82), channel_id=1, source_target_pairs={{1,0},{0,1},{3,2},{2,3},{5,4},{4,5},{7,6},{6,7},{9,8},{8,9},{11,10... | collective-permute-start | bytes 1572872 | tf_op jit(solution)/shard_map/ppermute | solution.py:530
  74.8 7.9 %collective-permute-start.10 = (bf16[1024,256]{1,0:T(8,128)(2,1)S(1)}, bf16[1024,256]{1,0:T(8,128)(2,1)S(1)}, u32[]{:S(2)}, u32[]{:S(2)}) collective-permute-start(bf16[1024,256]{1,0:T(8,128)(2,1)S(1)} %get-tuple-element.83), channel_id=1, source_target_pairs={{1,4},{3,6},{5,8},{7,10},{9,12},{11,14},{4,1},{6,3},{8,5},{10,7},{... | collective-permute-start | bytes 1572872 | tf_op jit(solution)/shard_map/ppermute | solution.py:530
  75.5 7.2 %collective-permute-start.11 = (bf16[512,256]{1,0:T(8,128)(2,1)S(1)}, bf16[512,256]{1,0:T(8,128)(2,1)S(1)}, u32[]{:S(2)}, u32[]{:S(2)}) collective-permute-start(bf16[512,256]{1,0:T(8,128)(2,1)S(1)} %get-tuple-element.84), channel_id=1, source_target_pairs={{2,0},{3,1},{0,2},{1,3},{6,4},{7,5},{4,6},{5,7},{10,8},{11,9},{8,1... | collective-permute-start | bytes 786440 | tf_op jit(solution)/shard_map/ppermute | solution.py:530
  75.9 4.7 %collective-permute-start.12 = (f32[4,8,128]{2,1,0:T(8,128)S(1)}, f32[4,8,128]{2,1,0:T(8,128)S(1)}, u32[]{:S(2)}, u32[]{:S(2)}) collective-permute-start(f32[4,8,128]{2,1,0:T(8,128)S(1)} %get-tuple-element.85.preds), channel_id=1, source_target_pairs={{2,1},{1,2},{6,5},{5,6},{10,9},{9,10},{14,13},{13,14},{18,17},{17,... | collective-permute-start | bytes 49160 | tf_op jit(solution)/shard_map/ppermute | solution.py:530
  86.5 4.1 %collective-permute-start.13 = (f32[136,256]{1,0:T(8,128)S(1)}, f32[136,256]{1,0:T(8,128)S(1)}, u32[]{:S(2)}, u32[]{:S(2)}) collective-permute-start(f32[136,256]{1,0:T(8,128)S(1)} %get-tuple-element.96), channel_id=1, source_target_pairs={{0,1},{1,0},{2,3},{3,2},{4,5},{5,4},{6,7},{7,6},{8,9},{9,8},{10,11... | collective-permute-start | bytes 417800 | tf_op jit(solution)/shard_map/ppermute | solution.py:494
  89.1 6.5 %collective-permute-start.14 = (f32[136,256]{1,0:T(8,128)S(1)}, f32[136,256]{1,0:T(8,128)S(1)}, u32[]{:S(2)}, u32[]{:S(2)}) collective-permute-start(f32[136,256]{1,0:T(8,128)S(1)} %get-tuple-element.97), channel_id=1, source_target_pairs={{0,2},{1,3},{2,0},{3,1},{4,6},{5,7},{6,4},{7,5},{8,10},{9,11},{10,... | collective-permute-start | bytes 417800 | tf_op jit(solution)/shard_map/ppermute | solution.py:494
  90.0 6.9 %collective-permute-start.15 = (f32[136,256]{1,0:T(8,128)S(1)}, f32[136,256]{1,0:T(8,128)S(1)}, u32[]{:S(2)}, u32[]{:S(2)}) collective-permute-start(f32[136,256]{1,0:T(8,128)S(1)} %get-tuple-element.98), channel_id=1, source_target_pairs={{0,3},{1,2},{2,1},{3,0},{4,7},{5,6},{6,5},{7,4},{8,11},{9,10},{10,... | collective-permute-start | bytes 417800 | tf_op jit(solution)/shard_map/ppermute | solution.py:494
  96.9 5.3 %collective-permute-start.16 = (f32[40,256]{1,0:T(8,128)S(1)}, f32[40,256]{1,0:T(8,128)S(1)}, u32[]{:S(2)}, u32[]{:S(2)}) collective-permute-start(f32[40,256]{1,0:T(8,128)S(1)} %get-tuple-element.100), channel_id=1, source_target_pairs={{0,4},{1,5},{2,6},{3,7},{4,0},{5,1},{6,2},{7,3},{8,12},{9,13},{10,... | collective-permute-start | bytes 122888 | tf_op jit(solution)/shard_map/ppermute | solution.py:494
  99.8 6.1 %collective-permute-start.17 = (f32[40,256]{1,0:T(8,128)S(1)}, f32[40,256]{1,0:T(8,128)S(1)}, u32[]{:S(2)}, u32[]{:S(2)}) collective-permute-start(f32[40,256]{1,0:T(8,128)S(1)} %get-tuple-element.101), channel_id=1, source_target_pairs={{0,8},{1,9},{2,10},{3,11},{4,12},{5,13},{6,14},{7,15},{8,0},{9,1},... | collective-permute-start | bytes 122888 | tf_op jit(solution)/shard_map/ppermute | solution.py:494
  100.5 5.9 %collective-permute-start.18 = (f32[40,256]{1,0:T(8,128)S(1)}, f32[40,256]{1,0:T(8,128)S(1)}, u32[]{:S(2)}, u32[]{:S(2)}) collective-permute-start(f32[40,256]{1,0:T(8,128)S(1)} %get-tuple-element.102), channel_id=1, source_target_pairs={{0,12},{1,13},{2,14},{3,15},{4,8},{5,9},{6,10},{7,11},{8,4},{9,5},... | collective-permute-start | bytes 122888 | tf_op jit(solution)/shard_map/ppermute | solution.py:494

commit v5 on v4

--- a/solution.py
+++ b/solution.py
@@ -92,16 +92,18 @@
     return jnp.dot(lhs, rhs, preferred_element_type=F32)
 
 
-def edge_blocks(shape, body):
+def edge_blocks(shape, body, after_row=None):
     _, rows, cols = shape
+    half, right, _ = place()
 
     def one_row(i, carry):
         for col in range(0, cols, 2):
-            body(i * (rows - 1), [col, col + 1])
+            body(jnp.where(half == i, 0, rows - 1), [col, col + 1])
+        if after_row is not None:
+            after_row(i)
         return carry
 
     lax.fori_loop(0, 2, one_row, 0)
-    _, right, _ = place()
     for row in range(1, rows - 1):
         body(row, [jnp.where(right == 0, cols - 1, 0)])
 
@@ -127,13 +129,18 @@
     return group([cols[0] + 1] + cols[1:], nodes)
 
 
+def messages(table, field, tiles, turned, row, cols, shape):
+    parts = [block_product(table, field, tiles, turned, row, col, shape).astype(BF16) for col in cols]
+    return jnp.concatenate(parts, axis=0) if len(parts) > 1 else parts[0]
+
+
 def forward_one(shape, table, field, tiles, turned, weight, x_field, m_all):
     nodes = shape[0]
 
     def body(row, cols):
-        for col in cols:
-            m_all[row, at_block(col, nodes)] = block_product(table, field, tiles, turned, row, col, shape).astype(BF16)
-        z = jnp.dot(m_all[row, group(cols, nodes)], weight[...], preferred_element_type=F32)
+        m = messages(table, field, tiles, turned, row, cols, shape)
+        m_all[row, group(cols, nodes)] = m
+        z = jnp.dot(m, weight[...], preferred_element_type=F32)
         inside = group_in_field(cols, nodes)
         x_field[row + 1, inside] = (field[row + 1, inside].astype(F32) + jnp.tanh(z)).astype(BF16)
 
@@ -146,30 +153,27 @@
     return jnp.concatenate([column, column], axis=1)
 
 
-def through_two(shape, scale, table, field, tiles, turned, weight, readout, goals, m_all, gz_all, g_field, preds, sums):
+def through_two(shape, scale, table, field, tiles, turned, weight, weight_turned, readout, spread, goals, m_all, gz_all, g_field, preds, sums):
     nodes = shape[0]
-    eight = jnp.broadcast_to(readout[...], (8, readout.shape[1]))
     readf = readout[...].astype(F32)
 
     def body(row, cols):
-        for col in cols:
-            m_all[row, at_block(col, nodes)] = block_product(table, field, tiles, turned, row, col, shape).astype(BF16)
+        m = messages(table, field, tiles, turned, row, cols, shape)
         here, inside = group(cols, nodes), group_in_field(cols, nodes)
-        t = jnp.tanh(jnp.dot(m_all[row, here], weight[...], preferred_element_type=F32))
+        m_all[row, here] = m
+        t = jnp.tanh(jnp.dot(m, weight[...], preferred_element_type=F32))
         x = (field[row + 1, inside].astype(F32) + t).astype(BF16)
-        seen = lax.dot_general(eight, x, (((1,), (1,)), ((), ())), preferred_element_type=F32)[0:1]
+        seen = jnp.dot(x, spread[...], preferred_element_type=F32)
         parts = []
         for k, col in enumerate(cols):
-            one = seen[:, k * nodes : (k + 1) * nodes]
+            one = seen[k * nodes : (k + 1) * nodes].T[0:1]
             preds[row, pl.ds(col, 1)] = one
             parts.append(residual_columns(one, goals[row, pl.ds(col, 1)], scale))
         gp = jnp.concatenate(parts, axis=0) if len(parts) > 1 else parts[0]
         sums[...] += (x.astype(F32) * gp).reshape(gp.shape[0] // 8, 8, gp.shape[1]).sum(axis=0)
         gz = (gp * readf * (1.0 - t * t)).astype(BF16)
         gz_all[row, here] = gz
-        g_field[row + 1, inside] = lax.dot_general(
-            gz, weight[...], (((1,), (1,)), ((), ())), preferred_element_type=F32
-        ).astype(BF16)
+        g_field[row + 1, inside] = jnp.dot(gz, weight_turned[...], preferred_element_type=F32).astype(BF16)
 
     return body
 
@@ -203,17 +207,30 @@
             field[row, at_block(col, nodes)] = jnp.zeros((nodes, field.shape[2]), field.dtype)
 
 
-def edge_pairs(field, inner, outer, side, shape):
+def send_edges(field, outer, inner, side, shape, sems, body):
     nodes, rows, cols = shape
     half, right, _ = place()
     inside = pl.ds(nodes, cols * nodes)
-    pairs = [
-        (field.at[jnp.where(half == 0, rows, 1), inside], inner),
-        (field.at[jnp.where(half == 0, 1, rows), inside], outer),
+    lines = [
+        pltpu.make_async_copy(field.at[jnp.where(half == i, 1, rows), inside], line, sems.at[i])
+        for i, line in enumerate((outer, inner))
     ]
-    for row in range(rows):
-        pairs.append((field.at[row + 1, at_block(jnp.where(right == 0, cols, 1), nodes)], side.at[at_block(row, nodes)]))
-    return pairs
+
+    def after_row(i):
+        @pl.when(i == 0)
+        def _():
+            lines[0].start()
+
+        @pl.when(i == 1)
+        def _():
+            lines[1].start()
+
+    edge_blocks(shape, body, after_row)
+    beside = [
+        (field.at[row + 1, at_block(jnp.where(right == 0, cols, 1), nodes)], side.at[at_block(row, nodes)])
+        for row in range(rows)
+    ]
+    wait_all(lines + start_all(beside, sems, 2))
 
 
 def rim_pairs(field, inner, outer, side, shape):
@@ -258,8 +275,10 @@
     wait_all(start_all([(own.at[pl.ds(1, own.shape[0] - 2)], middle)], sems))
 
 
-def prepare_kernel(tiles, first, second, plain, turned, first_in, second_in, sems):
+def prepare_kernel(tiles, first, second, plain, turned, first_in, second_in, second_turned, sems):
     wait_all(start_all([(tiles, plain), (first, first_in), (second, second_in)], sems))
+
+    second_turned[...] = second_in[...].T
 
     def one_tile(tile, carry):
         turned[tile] = plain[tile].T
@@ -268,7 +287,7 @@
     lax.fori_loop(0, tiles.shape[0], one_tile, 0)
 
 
-def pick_kernel(numbers, own, ends, after, later, inner, outer, sems):
+def pick_kernel(numbers, own, ends, after, outer, inner, sems):
     rows, line = own.shape[0], own.shape[1]
     half, _, moved = place()
     whole = pl.ds(0, line)
@@ -296,8 +315,8 @@
         wait_all(copies)
 
 
-def first_edge_kernel(shape, numbers, own, ends, middle, inner, outer, side, tiles, turned, weight,
-                      table, field, x_field, m_all, inner_out, outer_out, side_out, heads, heads_int, marks, sems):
+def first_edge_kernel(shape, numbers, own, ends, middle, outer, inner, side, later, tiles, turned, weight,
+                      table, field, x_field, m_all, outer_out, inner_out, side_out, heads, heads_int, marks, sems):
     nodes, rows, cols = shape
     line = cols * nodes
     step = rows * cols
@@ -374,11 +393,11 @@
     wait_all(rest)
     either_wait(moved, main_pairs, 0, 1, None)
 
-    edge_blocks(shape, forward_one(shape, table, field, tiles, turned, weight, x_field, m_all))
-    wait_all(start_all(edge_pairs(x_field, inner_out, outer_out, side_out, shape), sems))
-
-
-def middle_compute_kernel(shape, scale, table, field, tiles, turned, weight_one, weight_two, readout, target,
+    body = forward_one(shape, table, field, tiles, turned, weight, x_field, m_all)
+    send_edges(x_field, outer_out, inner_out, side_out, shape, sems, body)
+
+
+def middle_compute_kernel(shape, scale, table, field, tiles, turned, weight_one, weight_two, two_turned, readout, spread, target,
                           target_swap, x_in, m_in, x_field, m_one, m_two, gz_two, g_field, preds, goals, sums):
     _, _, moved = place()
 
@@ -394,18 +413,19 @@
     sums[...] = jnp.zeros_like(sums)
     inner_blocks(shape, forward_one(shape, table, field, tiles, turned, weight_one, x_field, m_one))
     inner_blocks(shape, through_two(
-        shape, scale, table, x_field, tiles, turned, weight_two, readout, goals, m_two, gz_two, g_field, preds, sums
+        shape, scale, table, x_field, tiles, turned, weight_two, two_turned, readout, spread, goals, m_two, gz_two, g_field, preds, sums
     ))
 
 
-def second_edge_kernel(shape, scale, table, inner, outer, side, tiles, turned, weight, readout, goals,
+def second_edge_kernel(shape, scale, table, outer, inner, side, tiles, turned, weight, weight_turned, readout, spread, goals,
                        x_in, m_in, gz_in, g_in, preds_in, sums_in,
-                       x_field, m_two, gz_two, g_field, preds, sums, inner_out, outer_out, side_out, sems):
+                       x_field, m_two, gz_two, g_field, preds, sums, outer_out, inner_out, side_out, sems):
     wait_all(start_all(rim_pairs(x_field, inner, outer, side, shape), sems))
-    edge_blocks(shape, through_two(
-        shape, scale, table, x_field, tiles, turned, weight, readout, goals, m_two, gz_two, g_field, preds, sums
-    ))
-    wait_all(start_all(edge_pairs(g_field, inner_out, outer_out, side_out, shape), sems))
+    body = through_two(
+        shape, scale, table, x_field, tiles, turned, weight, weight_turned, readout, spread, goals, m_two, gz_two,
+        g_field, preds, sums,
+    )
+    send_edges(g_field, outer_out, inner_out, side_out, shape, sems, body)
 
 
 def back_inner_kernel(shape, scale, table, g_field, tiles, turned, weight, readout, goals, preds, m_one, m_two, gz_two,
@@ -429,7 +449,7 @@
     lax.fori_loop(0, rows, each_row, 0)
 
 
-def back_edge_kernel(shape, scale, table, inner, outer, side, tiles, turned, weight, readout, goals, preds, preds_swap,
+def back_edge_kernel(shape, scale, table, outer, inner, side, tiles, turned, weight, readout, goals, preds, preds_swap,
                      m_one, first_in, second, sums, g_in, gz_in, g_field, gz_one, keep, one, two, three, pred_out,
                      first_out, parts, sems):
     nodes, rows, cols = shape
@@ -529,8 +549,8 @@
     def send(value, way):
         return lax.ppermute(value, AXES, way)
 
-    def edges(inner, outer, side):
-        return send(inner, inner_way), send(outer, outer_way), send(side, side_way)
+    def edges(outer, inner, side):
+        return send(outer, outer_way), send(inner, inner_way), send(side, side_way)
 
     def bf(*shape):
         return jax.ShapeDtypeStruct(shape, BF16)
@@ -560,29 +580,31 @@
         name="pack_middle",
     )(features, side_s)
     middle = send(middle_s, swap)
-    target, tiles, w_first, w_second, _ = lax.optimization_barrier((target, tiles, w_first, w_second, middle_s))
-    goal_swap = send(target, swap)
-    tiles, turned, w_first, w_second = pl.pallas_call(
+    tiles, w_first, w_second, _ = lax.optimization_barrier((tiles, w_first, w_second, middle_s))
+    tiles, turned, w_first, w_second, w_turned = pl.pallas_call(
         prepare_kernel,
-        out_shape=(bf(*tiles.shape), bf(*tiles.shape), bf(width, width), bf(width, width)),
+        out_shape=(bf(*tiles.shape), bf(*tiles.shape)) + (bf(width, width),) * 3,
         in_specs=[ANY] * 3,
-        out_specs=(VMEM,) * 4,
+        out_specs=(VMEM,) * 5,
         scratch_shapes=[sems(3)],
         compiler_params=params,
         name="prepare",
     )(tiles, w_first, w_second)
+    spread = jnp.broadcast_to(readout[:, None], (width, 128))
     readout = readout[None]
 
-    inner_s, outer_s = pl.pallas_call(
+    outer_s, inner_s = pl.pallas_call(
         pick_kernel,
         out_shape=(bf(line + TAIL, width),) * 2,
-        in_specs=[VMEM, ANY, ANY, ANY, ANY],
+        in_specs=[VMEM, ANY, ANY, ANY],
         out_specs=(VMEM,) * 2,
         scratch_shapes=[sems(4)],
         compiler_params=params,
         name="pick",
-    )(numbers, features, ends, side, goal_swap)
+    )(numbers, features, ends, side)
     outer, inner = send(outer_s, outer_way), send(inner_s, inner_way)
+    target_s, _ = lax.optimization_barrier((target, inner_s))
+    goal_swap = send(target_s, swap)
 
     shape = (nodes, rows, cols)
     patch, padded = bf(rows, line, width), bf(rows + 2, line + 2 * nodes, width)
@@ -600,10 +622,10 @@
             transcendentals=block * products,
         )
 
-    table, f_field, x_field, m_one, inner_s, outer_s, side_s = pl.pallas_call(
+    table, f_field, x_field, m_one, outer_s, inner_s, side_s = pl.pallas_call(
         functools.partial(first_edge_kernel, shape),
         out_shape=(jax.ShapeDtypeStruct((5 * step,), jnp.int32), padded, padded, patch) + edge_shapes,
-        in_specs=[ANY] * 7 + [VMEM] * 3,
+        in_specs=[ANY] * 8 + [VMEM] * 3,
         out_specs=(SMEM,) + (VMEM,) * 6,
         scratch_shapes=[
             pltpu.VMEM((3, TAIL, width), BF16),
@@ -614,33 +636,33 @@
         compiler_params=params,
         cost_estimate=cost(edge, edge),
         name="first_edge",
-    )(numbers, features, ends, middle, inner, outer, side, tiles, turned, w_first)
-
-    inner, outer, side = edges(inner_s, outer_s, side_s)
+    )(numbers, features, ends, middle, outer, inner, side, goal_swap, tiles, turned, w_first)
+
+    outer, inner, side = edges(outer_s, inner_s, side_s)
     x_field, m_one, m_two, gz_two, g_field, preds, goals, sums = pl.pallas_call(
         functools.partial(middle_compute_kernel, shape, scale),
         out_shape=(padded, patch, patch, patch, padded, goal_shape, goal_shape, sums_shape),
-        in_specs=[SMEM] + [VMEM] * 10,
+        in_specs=[SMEM] + [VMEM] * 12,
         out_specs=(VMEM,) * 8,
-        input_output_aliases={9: 0, 10: 1},
+        input_output_aliases={11: 0, 12: 1},
         compiler_params=params,
         cost_estimate=cost(2 * inside, 3 * inside),
         name="inner_forward",
-    )(table, f_field, tiles, turned, w_first, w_second, readout, target, goal_swap, x_field, m_one)
-
-    x_field, m_two, gz_two, g_field, preds, sums, inner_s, outer_s, side_s = pl.pallas_call(
+    )(table, f_field, tiles, turned, w_first, w_second, w_turned, readout, spread, target, goal_swap, x_field, m_one)
+
+    x_field, m_two, gz_two, g_field, preds, sums, outer_s, inner_s, side_s = pl.pallas_call(
         functools.partial(second_edge_kernel, shape, scale),
         out_shape=(padded, patch, patch, padded, goal_shape, sums_shape) + edge_shapes,
-        in_specs=[SMEM] + [ANY] * 3 + [VMEM] * 11,
+        in_specs=[SMEM] + [ANY] * 3 + [VMEM] * 13,
         out_specs=(VMEM,) * 9,
-        input_output_aliases={9 + i: i for i in range(6)},
+        input_output_aliases={11 + i: i for i in range(6)},
         scratch_shapes=[sems(2 + rows)],
         compiler_params=params,
         cost_estimate=cost(edge, 2 * edge),
         name="second_edge",
-    )(table, inner, outer, side, tiles, turned, w_second, readout, goals, x_field, m_two, gz_two, g_field, preds, sums)
-
-    inner, outer, side = edges(inner_s, outer_s, side_s)
+    )(table, outer, inner, side, tiles, turned, w_second, w_turned, readout, spread, goals, x_field, m_two, gz_two, g_field, preds, sums)
+
+    outer, inner, side = edges(outer_s, inner_s, side_s)
     preds_swap = send(preds, swap)
     gz_one, first, second = pl.pallas_call(
         functools.partial(back_inner_kernel, shape, scale),
@@ -663,7 +685,7 @@
         compiler_params=params,
         cost_estimate=cost(edge, 2 * edge),
         name="back_edge",
-    )(table, inner, outer, side, tiles, turned, w_first, readout, goals, preds, preds_swap, m_one, first, second, sums,
+    )(table, outer, inner, side, tiles, turned, w_first, readout, goals, preds, preds_swap, m_one, first, second, sums,
       g_field, gz_one)
     first, second, extra = sum_shares(outs, count, share, width, params)
     return pred_out, first, second, extra[0]

time: 107 us -> 97.3 us (0.909)
  starting transfers between devices: 51.1 us -> 39.3 us
  waiting for transfers between devices: 18.9 us -> 20.9 us
    ppermute x13, starting transfers between devices: 41.7 us -> 32.9 us  [send(): return lax.ppermute(value, AXES, way)]
    ppermute x6, starting transfers between devices: 9.37 us -> 6.4 us  [sum_shares(): lax.ppermute(outs[k], AXES, [(i, i ^ k * base) for i in range(count)])]
    ppermute x13, waiting for transfers between devices: 8.45 us -> 10.1 us  [send(): return lax.ppermute(value, AXES, way)]
  transfers between devices with their start and end apart: 19 -> 19, of which waited for: 6 -> 6; matrix products, arithmetic and copies ran while one was open for 0% -> 0% of each run, Pallas kernels for 13% -> 14%
where the time goes in v5:
time: 97.3 us; the launch traced here: 97 us
  starting transfers between devices  39.3 us (40%)
  Pallas kernels  33.2 us (34%)
  waiting for transfers between devices  20.9 us (21%)
  local copies, waits for them, and re-layouts  2.63 us (3%)
    ppermute x13, starting transfers between devices, send(): return lax.ppermute(value, AXES, way)  32.9 us
    ppermute x6, waiting for transfers between devices, sum_shares(): lax.ppermute(outs[k], AXES, [(i, i ^ k * base) for i in range(count)])  10.8 us
    ppermute x13, waiting for transfers between devices, send(): return lax.ppermute(value, AXES, way)  10.1 us
    pallas_call x1, Pallas kernels, per_device(): pl.pallas_call(functools.partial(second_edge_kernel, shape, scale), out_s...  8.2 us
    pallas_call x1, Pallas kernels, per_device(): pl.pallas_call(functools.partial(middle_compute_kernel, shape, scale), ou...  7.72 us
    pallas_call x1, Pallas kernels, per_device(): pl.pallas_call(functools.partial(first_edge_kernel, shape), out_shape=(ja...  6.61 us
    ppermute x6, starting transfers between devices, sum_shares(): lax.ppermute(outs[k], AXES, [(i, i ^ k * base) for i in range(count)])  6.4 us
    pallas_call x1, Pallas kernels, per_device(): pl.pallas_call(functools.partial(back_inner_kernel, shape, scale), out_sh...  4.04 us
  transfers between devices with their start and end apart: 19, of which 6 were waited for; matrix products, arithmetic and copies ran while one was open for 0% of the time, Pallas kernels for 14%

profile of v5, /device:TPU:0, one launch (start us, length us, event | category | flops | bytes accessed | tf_op | source)
XLA Modules:
  0.0 97.0 jit_solution(16768666949115353523)
XLA Ops:
  0.6 1.6 %copy-done = bf16[4,8,128,256]{3,2,1,0:T(8,128)(2,1)S(1)} copy-done((bf16[4,8,128,256]{3,2,1,0:T(8,128)(2,1)S(1)}, bf16[4,8,128,256]{3,2,1,0:T(8,128)(2,1)}, u32[]{:S(2)}) %copy-start) | copy-done | bytes 2097176
  2.2 0.7 copy-done.6
  3.4 0.9 collective-permute-start
  4.6 0.9 collective-permute-start.1
  5.5 6.9 %collective-permute-start.2 = (bf16[528,256]{1,0:T(8,128)(2,1)S(1)}, bf16[528,256]{1,0:T(8,128)(2,1)S(1)}, u32[]{:S(2)}, u32[]{:S(2)}) collective-permute-start(bf16[528,256]{1,0:T(8,128)(2,1)S(1)} %get-tuple-element.58.after), channel_id=1, source_target_pairs={{1,0},{3,1},{0,2},{2,3},{5,4},{7,5},{4,6},{6,7},{9,8},{11,9},{8,10... | collective-permute-start | bytes 811016 | tf_op jit(solution)/shard_map/ppermute | solution.py:550
  12.4 6.9 %collective-permute-done.2.after.side = bf16[528,256]{1,0:T(8,128)(2,1)S(1)} collective-permute-done((bf16[528,256]{1,0:T(8,128)(2,1)S(1)}, bf16[528,256]{1,0:T(8,128)(2,1)S(1)}, u32[]{:S(2)}, u32[]{:S(2)}) %collective-permute-start.2) | collective-permute-done | bytes 270368 | tf_op jit(solution)/shard_map/ppermute | solution.py:550
  19.5 0.7 collective-permute-start.3
  20.2 6.0 %collective-permute-start.4 = (bf16[1040,256]{1,0:T(8,128)(2,1)S(1)}, bf16[1040,256]{1,0:T(8,128)(2,1)S(1)}, u32[]{:S(2)}, u32[]{:S(2)}) collective-permute-start(bf16[1040,256]{1,0:T(8,128)(2,1)S(1)} %get-tuple-element.60), channel_id=1, source_target_pairs={{1,0},{0,1},{3,2},{2,3},{5,4},{4,5},{7,6},{6,7},{9,8},{8,9},{11,10... | collective-permute-start | bytes 1597448 | tf_op jit(solution)/shard_map/ppermute | solution.py:550
  26.1 0.7 collective-permute-start.5
  26.8 1.6 %prepare.1 = (bf16[16,128,128]{2,1,0:T(8,128)(2,1)S(1)}, bf16[16,128,128]{2,1,0:T(8,128)(2,1)S(1)}, bf16[256,256]{1,0:T(8,128)(2,1)S(1)}, bf16[256,256]{1,0:T(8,128)(2,1)S(1)}, bf16[256,256]{1,0:T(8,128)(2,1)S(1)}) custom-call(bf16[16,128,128]{2,1,0:T(8,128)(2,1)S(1)} %copy-done.2, bf16[256,256]{1,0:T(8,128)(2,1)S(1)} %copy-done.3, ...), custom_call_target="tpu_custom_call" | custom-call | tf_op jit(solution)/shard_map/prepare/pallas_call | solution.py:584
  28.5 6.6 %first_edge.1 = (s32[160]{0:T(256)S(1)}, bf16[6,1280,256]{2,1,0:T(8,128)(2,1)S(1)}, bf16[6,1280,256]{2,1,0:T(8,128)(2,1)S(1)}, bf16[4,1024,256]{2,1,0:T(8,128)(2...) custom-call(bf16[16,256]{1,0:T(8,128)(2,1)S(1)} %get-tuple-element.56.numbers, ...), custom_call_target="tpu_custom_call" | custom-call | flops 1207959552 | bytes 4718592 | tf_op jit(solution)/shard_map/first_edge/pallas_call | solution.py:625
  35.1 0.7 collective-permute-start.6
  35.8 8.2 %collective-permute-start.7 = (bf16[1024,256]{1,0:T(8,128)(2,1)S(1)}, bf16[1024,256]{1,0:T(8,128)(2,1)S(1)}, u32[]{:S(2)}, u32[]{:S(2)}) collective-permute-start(bf16[1024,256]{1,0:T(8,128)(2,1)S(1)} %get-tuple-element.70), channel_id=1, source_target_pairs={{1,0},{0,1},{3,2},{2,3},{5,4},{4,5},{7,6},{6,7},{9,8},{8,9},{11,10... | collective-permute-start | bytes 1572872 | tf_op jit(solution)/shard_map/ppermute | solution.py:550
  44.0 3.3 %collective-permute-start.8 = (bf16[512,256]{1,0:T(8,128)(2,1)S(1)}, bf16[512,256]{1,0:T(8,128)(2,1)S(1)}, u32[]{:S(2)}, u32[]{:S(2)}) collective-permute-start(bf16[512,256]{1,0:T(8,128)(2,1)S(1)} %get-tuple-element.71), channel_id=1, source_target_pairs={{2,0},{3,1},{0,2},{1,3},{6,4},{7,5},{4,6},{5,7},{10,8},{11,9},{8,1... | collective-permute-start | bytes 786440 | tf_op jit(solution)/shard_map/ppermute | solution.py:550
  47.4 7.7 %inner_forward.1 = (bf16[6,1280,256]{2,1,0:T(8,128)(2,1)S(1)}, bf16[4,1024,256]{2,1,0:T(8,128)(2,1)S(1)}, bf16[4,1024,256]{2,1,0:T(8,128)(2,1)S(1)}, bf16[4,1024...) custom-call(s32[160]{0:T(256)S(1)} %get-tuple-element.68.table, ...), custom_call_target="tpu_custom_call", output_to_operand_aliasing={{0}: (11, {}), {1}: (12, {})} | custom-call | flops 2113929216 | bytes 9175040 | tf_op jit(solution)/shard_map/inner_forward/pallas_call | solution.py:642
  55.2 8.2 %second_edge.1 = (bf16[6,1280,256]{2,1,0:T(8,128)(2,1)S(1)}, bf16[4,1024,256]{2,1,0:T(8,128)(2,1)S(1)}, bf16[4,1024,256]{2,1,0:T(8,128)(2,1)S(1)}, bf16[6,1280,2...) custom-call(s32[160]{0:T(256)S(1)} %get-tuple-element.68.table, ...), custom_call_target="tpu_custom_call", output_to_operand_aliasing={{0}: (11, {}), {1}: (12, {}), {2}: (13, {}), {3}: (14, {}),... | custom-call | flops 1509949440 | bytes 7077888 | tf_op jit(solution)/shard_map/second_edge/pallas_call | solution.py:653
  63.4 0.7 collective-permute-start.9
  64.1 3.0 %collective-permute-start.10 = (bf16[1024,256]{1,0:T(8,128)(2,1)S(1)}, bf16[1024,256]{1,0:T(8,128)(2,1)S(1)}, u32[]{:S(2)}, u32[]{:S(2)}) collective-permute-start(bf16[1024,256]{1,0:T(8,128)(2,1)S(1)} %get-tuple-element.85), channel_id=1, source_target_pairs={{1,0},{0,1},{3,2},{2,3},{5,4},{4,5},{7,6},{6,7},{9,8},{8,9},{11,10... | collective-permute-start | bytes 1572872 | tf_op jit(solution)/shard_map/ppermute | solution.py:550
  67.5 0.7 collective-permute-start.12
  68.2 4.0 %back_inner.1 = (bf16[4,1024,256]{2,1,0:T(8,128)(2,1)S(1)}, f32[256,256]{1,0:T(8,128)S(1)}, f32[256,256]{1,0:T(8,128)S(1)}) custom-call(s32[160]{0:T(256)S(1)} %get-tuple-element.68.table, bf16[6,1280,256]{2,1,0:T(8,128)(2,1)S(1)} %get-tuple-element.89.g_field.g_in, bf16[16,128,128]{2,1,0:T(8,128)(2,1)S(1)} %get-tuple-element.65.tiles, ...), custom_call_target="tpu_custom_call" | custom-call | flops 1711276032 | bytes 9699328 | tf_op jit(solution)/shard_map/back_inner/pallas_call | solution.py:667
  72.2 3.2 %collective-permute-done.11.side = bf16[512,256]{1,0:T(8,128)(2,1)S(1)} collective-permute-done((bf16[512,256]{1,0:T(8,128)(2,1)S(1)}, bf16[512,256]{1,0:T(8,128)(2,1)S(1)}, u32[]{:S(2)}, u32[]{:S(2)}) %collective-permute-start.11) | collective-permute-done | bytes 262176 | tf_op jit(solution)/shard_map/ppermute | solution.py:550
  75.4 3.7 %back_edge.1 = (bf16[6,1280,256]{2,1,0:T(8,128)(2,1)S(1)}, bf16[4,1024,256]{2,1,0:T(8,128)(2,1)S(1)}, f32[136,256]{1,0:T(8,128)S(1)}, f32[136,256]{1,0:T(8,128)S...) custom-call(s32[160]{0:T(256)S(1)} %get-tuple-element.68.table, ...), custom_call_target="tpu_custom_call", output_to_operand_aliasing={{0}: (15, {}), {1}: (16, {})} | custom-call | flops 1509949440 | bytes 7077888 | tf_op jit(solution)/shard_map/back_edge/pallas_call | solution.py:678
  79.3 0.5 collective-permute-start.14
  79.8 1.2 %collective-permute-start.15 = (f32[136,256]{1,0:T(8,128)S(1)}, f32[136,256]{1,0:T(8,128)S(1)}, u32[]{:S(2)}, u32[]{:S(2)}) collective-permute-start(f32[136,256]{1,0:T(8,128)S(1)} %get-tuple-element.100), channel_id=1, source_target_pairs={{0,3},{1,2},{2,1},{3,0},{4,7},{5,6},{6,5},{7,4},{8,11},{9,10},{10,... | collective-permute-start | bytes 417800 | tf_op jit(solution)/shard_map/ppermute | solution.py:514
  81.0 4.8 %collective-permute-done.14.two = f32[136,256]{1,0:T(8,128)S(1)} collective-permute-done((f32[136,256]{1,0:T(8,128)S(1)}, f32[136,256]{1,0:T(8,128)S(1)}, u32[]{:S(2)}, u32[]{:S(2)}) %collective-permute-start.14) | collective-permute-done | bytes 139296 | tf_op jit(solution)/shard_map/ppermute | solution.py:514
  85.8 1.9 %collective-permute-done.15.three = f32[136,256]{1,0:T(8,128)S(1)} collective-permute-done((f32[136,256]{1,0:T(8,128)S(1)}, f32[136,256]{1,0:T(8,128)S(1)}, u32[]{:S(2)}, u32[]{:S(2)}) %collective-permute-start.15) | collective-permute-done | bytes 139296 | tf_op jit(solution)/shard_map/ppermute | solution.py:514
  87.7 1.7 %collective-permute-start.16 = (f32[40,256]{1,0:T(8,128)S(1)}, f32[40,256]{1,0:T(8,128)S(1)}, u32[]{:S(2)}, u32[]{:S(2)}) collective-permute-start(f32[40,256]{1,0:T(8,128)S(1)} %get-tuple-element.102), channel_id=1, source_target_pairs={{0,4},{1,5},{2,6},{3,7},{4,0},{5,1},{6,2},{7,3},{8,12},{9,13},{10,... | collective-permute-start | bytes 122888 | tf_op jit(solution)/shard_map/ppermute | solution.py:514
  89.4 1.2 %collective-permute-start.17 = (f32[40,256]{1,0:T(8,128)S(1)}, f32[40,256]{1,0:T(8,128)S(1)}, u32[]{:S(2)}, u32[]{:S(2)}) collective-permute-start(f32[40,256]{1,0:T(8,128)S(1)} %get-tuple-element.103), channel_id=1, source_target_pairs={{0,8},{1,9},{2,10},{3,11},{4,12},{5,13},{6,14},{7,15},{8,0},{9,1},... | collective-permute-start | bytes 122888 | tf_op jit(solution)/shard_map/ppermute | solution.py:514
  90.5 1.6 %collective-permute-start.18 = (f32[40,256]{1,0:T(8,128)S(1)}, f32[40,256]{1,0:T(8,128)S(1)}, u32[]{:S(2)}, u32[]{:S(2)}) collective-permute-start(f32[40,256]{1,0:T(8,128)S(1)} %get-tuple-element.104), channel_id=1, source_target_pairs={{0,12},{1,13},{2,14},{3,15},{4,8},{5,9},{6,10},{7,11},{8,4},{9,5},... | collective-permute-start | bytes 122888 | tf_op jit(solution)/shard_map/ppermute | solution.py:514
  92.2 3.3 %collective-permute-done.17.two = f32[40,256]{1,0:T(8,128)S(1)} collective-permute-done((f32[40,256]{1,0:T(8,128)S(1)}, f32[40,256]{1,0:T(8,128)S(1)}, u32[]{:S(2)}, u32[]{:S(2)}) %collective-permute-start.17) | collective-permute-done | bytes 40992 | tf_op jit(solution)/shard_map/ppermute | solution.py:514
  95.5 0.9 collective-permute-done.18.three
  96.3 0.6 last_fold.1
  (35 shorter events, 1.7 us)
Async XLA Ops:
  0.6 1.6 %copy-start = (bf16[4,8,128,256]{3,2,1,0:T(8,128)(2,1)S(1)}, bf16[4,8,128,256]{3,2,1,0:T(8,128)(2,1)}, u32[]{:S(2)}) copy-start(bf16[4,8,128,256]{3,2,1,0:T(8,128)(2,1)} %param.7) | copy-start | bytes 6291460
  2.2 0.7 copy-start.6
  2.9 1.6 %copy-start.1 = (bf16[4,8,128,256]{3,2,1,0:T(8,128)(2,1)S(1)}, bf16[4,8,128,256]{3,2,1,0:T(8,128)(2,1)}, u32[]{:S(2)}) copy-start(bf16[4,8,128,256]{3,2,1,0:T(8,128)(2,1)} %param.7) | copy-start | bytes 6291460
  3.4 15.9 %collective-permute-start = (bf16[2064,256]{1,0:T(8,128)(2,1)S(1)}, bf16[2064,256]{1,0:T(8,128)(2,1)S(1)}, u32[]{:S(2)}, u32[]{:S(2)}) collective-permute-start(bf16[2064,256]{1,0:T(8,128)(2,1)S(1)} %get-tuple-element.57), channel_id=1, source_target_pairs={{2,1},{1,2},{6,5},{5,6},{10,9},{9,10},{14,13},{13,14},{18,17},{17,... | collective-permute-start | bytes 3170312 | tf_op jit(solution)/shard_map/ppermute | solution.py:550
  4.6 21.5 %copy-start.5 = (f32[4,8,128]{2,1,0:T(8,128)S(1)}, f32[4,8,128]{2,1,0:T(8,128)}, u32[]{:S(2)}) copy-start(f32[4,8,128]{2,1,0:T(8,128)} %target.1) | copy-start | bytes 49156
  4.6 22.2 %copy-start.2 = (bf16[16,128,128]{2,1,0:T(8,128)(2,1)S(1)}, bf16[16,128,128]{2,1,0:T(8,128)(2,1)}, u32[]{:S(2)}) copy-start(bf16[16,128,128]{2,1,0:T(8,128)(2,1)} %tiles) | copy-start | bytes 1572868
  4.6 22.2 %copy-start.3 = (bf16[256,256]{1,0:T(8,128)(2,1)S(1)}, bf16[256,256]{1,0:T(8,128)(2,1)}, u32[]{:S(2)}) copy-start(bf16[256,256]{1,0:T(8,128)(2,1)} %first) | copy-start | bytes 393220
  4.6 22.2 %copy-start.4 = (bf16[256,256]{1,0:T(8,128)(2,1)S(1)}, bf16[256,256]{1,0:T(8,128)(2,1)}, u32[]{:S(2)}) copy-start(bf16[256,256]{1,0:T(8,128)(2,1)} %second) | copy-start | bytes 393220
  4.6 23.8 %collective-permute-start.1 = (bf16[2,1024,256]{2,1,0:T(8,128)(2,1)S(1)}, bf16[2,1024,256]{2,1,0:T(8,128)(2,1)S(1)}, u32[]{:S(2)}, u32[]{:S(2)}) collective-permute-start(bf16[2,1024,256]{2,1,0:T(8,128)(2,1)S(1)} %pack_middle.1), channel_id=1, source_target_pairs={{2,1},{1,2},{6,5},{5,6},{10,9},{9,10},{14,13},{13,14},{18,17},{17,... | collective-permute-start | bytes 3145736 | tf_op jit(solution)/shard_map/ppermute | solution.py:550
  5.5 13.8 %collective-permute-start.2 = (bf16[528,256]{1,0:T(8,128)(2,1)S(1)}, bf16[528,256]{1,0:T(8,128)(2,1)S(1)}, u32[]{:S(2)}, u32[]{:S(2)}) collective-permute-start(bf16[528,256]{1,0:T(8,128)(2,1)S(1)} %get-tuple-element.58.after), channel_id=1, source_target_pairs={{1,0},{3,1},{0,2},{2,3},{5,4},{7,5},{4,6},{6,7},{9,8},{11,9},{8,10... | collective-permute-start | bytes 811016 | tf_op jit(solution)/shard_map/ppermute | solution.py:550
  19.5 9.0 %collective-permute-start.3 = (bf16[1040,256]{1,0:T(8,128)(2,1)S(1)}, bf16[1040,256]{1,0:T(8,128)(2,1)S(1)}, u32[]{:S(2)}, u32[]{:S(2)}) collective-permute-start(bf16[1040,256]{1,0:T(8,128)(2,1)S(1)} %get-tuple-element.59), channel_id=1, source_target_pairs={{1,4},{3,6},{5,8},{7,10},{9,12},{11,14},{4,1},{6,3},{8,5},{10,7},{... | collective-permute-start | bytes 1597448 | tf_op jit(solution)/shard_map/ppermute | solution.py:550
  20.2 8.3 %collective-permute-start.4 = (bf16[1040,256]{1,0:T(8,128)(2,1)S(1)}, bf16[1040,256]{1,0:T(8,128)(2,1)S(1)}, u32[]{:S(2)}, u32[]{:S(2)}) collective-permute-start(bf16[1040,256]{1,0:T(8,128)(2,1)S(1)} %get-tuple-element.60), channel_id=1, source_target_pairs={{1,0},{0,1},{3,2},{2,3},{5,4},{4,5},{7,6},{6,7},{9,8},{8,9},{11,10... | collective-permute-start | bytes 1597448 | tf_op jit(solution)/shard_map/ppermute | solution.py:550
  26.1 2.3 %collective-permute-start.5 = (f32[4,8,128]{2,1,0:T(8,128)S(1)}, f32[4,8,128]{2,1,0:T(8,128)S(1)}, u32[]{:S(2)}, u32[]{:S(2)}) collective-permute-start(f32[4,8,128]{2,1,0:T(8,128)S(1)} %copy-done.5), channel_id=1, source_target_pairs={{2,1},{1,2},{6,5},{5,6},{10,9},{9,10},{14,13},{13,14},{18,17},{17,... | collective-permute-start | bytes 49160 | tf_op jit(solution)/shard_map/ppermute | solution.py:550
  28.5 18.8 %copy-start.7 = (bf16[256]{0:T(256)(128)(2,1)S(1)}, bf16[256]{0:T(256)(128)(2,1)}, u32[]{:S(2)}) copy-start(bf16[256]{0:T(256)(128)(2,1)} %param.12) | copy-start | bytes 1540
  35.1 20.0 %collective-permute-start.6 = (bf16[1024,256]{1,0:T(8,128)(2,1)S(1)}, bf16[1024,256]{1,0:T(8,128)(2,1)S(1)}, u32[]{:S(2)}, u32[]{:S(2)}) collective-permute-start(bf16[1024,256]{1,0:T(8,128)(2,1)S(1)} %get-tuple-element.69), channel_id=1, source_target_pairs={{1,4},{3,6},{5,8},{7,10},{9,12},{11,14},{4,1},{6,3},{8,5},{10,7},{... | collective-permute-start | bytes 1572872 | tf_op jit(solution)/shard_map/ppermute | solution.py:550
  35.8 19.4 %collective-permute-start.7 = (bf16[1024,256]{1,0:T(8,128)(2,1)S(1)}, bf16[1024,256]{1,0:T(8,128)(2,1)S(1)}, u32[]{:S(2)}, u32[]{:S(2)}) collective-permute-start(bf16[1024,256]{1,0:T(8,128)(2,1)S(1)} %get-tuple-element.70), channel_id=1, source_target_pairs={{1,0},{0,1},{3,2},{2,3},{5,4},{4,5},{7,6},{6,7},{9,8},{8,9},{11,10... | collective-permute-start | bytes 1572872 | tf_op jit(solution)/shard_map/ppermute | solution.py:550
  44.0 11.1 %collective-permute-start.8 = (bf16[512,256]{1,0:T(8,128)(2,1)S(1)}, bf16[512,256]{1,0:T(8,128)(2,1)S(1)}, u32[]{:S(2)}, u32[]{:S(2)}) collective-permute-start(bf16[512,256]{1,0:T(8,128)(2,1)S(1)} %get-tuple-element.71), channel_id=1, source_target_pairs={{2,0},{3,1},{0,2},{1,3},{6,4},{7,5},{4,6},{5,7},{10,8},{11,9},{8,1... | collective-permute-start | bytes 786440 | tf_op jit(solution)/shard_map/ppermute | solution.py:550
  63.4 12.0 %collective-permute-start.9 = (bf16[1024,256]{1,0:T(8,128)(2,1)S(1)}, bf16[1024,256]{1,0:T(8,128)(2,1)S(1)}, u32[]{:S(2)}, u32[]{:S(2)}) collective-permute-start(bf16[1024,256]{1,0:T(8,128)(2,1)S(1)} %get-tuple-element.84), channel_id=1, source_target_pairs={{1,4},{3,6},{5,8},{7,10},{9,12},{11,14},{4,1},{6,3},{8,5},{10,7},{... | collective-permute-start | bytes 1572872 | tf_op jit(solution)/shard_map/ppermute | solution.py:550
  64.1 11.3 %collective-permute-start.10 = (bf16[1024,256]{1,0:T(8,128)(2,1)S(1)}, bf16[1024,256]{1,0:T(8,128)(2,1)S(1)}, u32[]{:S(2)}, u32[]{:S(2)}) collective-permute-start(bf16[1024,256]{1,0:T(8,128)(2,1)S(1)} %get-tuple-element.85), channel_id=1, source_target_pairs={{1,0},{0,1},{3,2},{2,3},{5,4},{4,5},{7,6},{6,7},{9,8},{8,9},{11,10... | collective-permute-start | bytes 1572872 | tf_op jit(solution)/shard_map/ppermute | solution.py:550
  67.1 8.3 %collective-permute-start.11 = (bf16[512,256]{1,0:T(8,128)(2,1)S(1)}, bf16[512,256]{1,0:T(8,128)(2,1)S(1)}, u32[]{:S(2)}, u32[]{:S(2)}) collective-permute-start(bf16[512,256]{1,0:T(8,128)(2,1)S(1)} %get-tuple-element.86), channel_id=1, source_target_pairs={{2,0},{3,1},{0,2},{1,3},{6,4},{7,5},{4,6},{5,7},{10,8},{11,9},{8,1... | collective-permute-start | bytes 786440 | tf_op jit(solution)/shard_map/ppermute | solution.py:550
  67.5 4.7 %collective-permute-start.12 = (f32[4,8,128]{2,1,0:T(8,128)S(1)}, f32[4,8,128]{2,1,0:T(8,128)S(1)}, u32[]{:S(2)}, u32[]{:S(2)}) collective-permute-start(f32[4,8,128]{2,1,0:T(8,128)S(1)} %get-tuple-element.87.preds), channel_id=1, source_target_pairs={{2,1},{1,2},{6,5},{5,6},{10,9},{9,10},{14,13},{13,14},{18,17},{17,... | collective-permute-start | bytes 49160 | tf_op jit(solution)/shard_map/ppermute | solution.py:550
  79.1 1.9 %collective-permute-start.13 = (f32[136,256]{1,0:T(8,128)S(1)}, f32[136,256]{1,0:T(8,128)S(1)}, u32[]{:S(2)}, u32[]{:S(2)}) collective-permute-start(f32[136,256]{1,0:T(8,128)S(1)} %get-tuple-element.98), channel_id=1, source_target_pairs={{0,1},{1,0},{2,3},{3,2},{4,5},{5,4},{6,7},{7,6},{8,9},{9,8},{10,11... | collective-permute-start | bytes 417800 | tf_op jit(solution)/shard_map/ppermute | solution.py:514
  79.3 6.5 %collective-permute-start.14 = (f32[136,256]{1,0:T(8,128)S(1)}, f32[136,256]{1,0:T(8,128)S(1)}, u32[]{:S(2)}, u32[]{:S(2)}) collective-permute-start(f32[136,256]{1,0:T(8,128)S(1)} %get-tuple-element.99), channel_id=1, source_target_pairs={{0,2},{1,3},{2,0},{3,1},{4,6},{5,7},{6,4},{7,5},{8,10},{9,11},{10,... | collective-permute-start | bytes 417800 | tf_op jit(solution)/shard_map/ppermute | solution.py:514
  79.8 7.8 %collective-permute-start.15 = (f32[136,256]{1,0:T(8,128)S(1)}, f32[136,256]{1,0:T(8,128)S(1)}, u32[]{:S(2)}, u32[]{:S(2)}) collective-permute-start(f32[136,256]{1,0:T(8,128)S(1)} %get-tuple-element.100), channel_id=1, source_target_pairs={{0,3},{1,2},{2,1},{3,0},{4,7},{5,6},{6,5},{7,4},{8,11},{9,10},{10,... | collective-permute-start | bytes 417800 | tf_op jit(solution)/shard_map/ppermute | solution.py:514
  87.7 4.5 %collective-permute-start.16 = (f32[40,256]{1,0:T(8,128)S(1)}, f32[40,256]{1,0:T(8,128)S(1)}, u32[]{:S(2)}, u32[]{:S(2)}) collective-permute-start(f32[40,256]{1,0:T(8,128)S(1)} %get-tuple-element.102), channel_id=1, source_target_pairs={{0,4},{1,5},{2,6},{3,7},{4,0},{5,1},{6,2},{7,3},{8,12},{9,13},{10,... | collective-permute-start | bytes 122888 | tf_op jit(solution)/shard_map/ppermute | solution.py:514
  89.4 6.1 %collective-permute-start.17 = (f32[40,256]{1,0:T(8,128)S(1)}, f32[40,256]{1,0:T(8,128)S(1)}, u32[]{:S(2)}, u32[]{:S(2)}) collective-permute-start(f32[40,256]{1,0:T(8,128)S(1)} %get-tuple-element.103), channel_id=1, source_target_pairs={{0,8},{1,9},{2,10},{3,11},{4,12},{5,13},{6,14},{7,15},{8,0},{9,1},... | collective-permute-start | bytes 122888 | tf_op jit(solution)/shard_map/ppermute | solution.py:514
  90.5 5.8 %collective-permute-start.18 = (f32[40,256]{1,0:T(8,128)S(1)}, f32[40,256]{1,0:T(8,128)S(1)}, u32[]{:S(2)}, u32[]{:S(2)}) collective-permute-start(f32[40,256]{1,0:T(8,128)S(1)} %get-tuple-element.104), channel_id=1, source_target_pairs={{0,12},{1,13},{2,14},{3,15},{4,8},{5,9},{6,10},{7,11},{8,4},{9,5},... | collective-permute-start | bytes 122888 | tf_op jit(solution)/shard_map/ppermute | solution.py:514

commit v6 on v5

--- a/solution.py
+++ b/solution.py
@@ -60,20 +60,21 @@
 
 def block_product(table, field, tiles, turned, row, col, shape):
     nodes, rows, cols = shape
-    at = row * cols + col
-    step = rows * cols
+
+    def number(kind):
+        return table[kind * rows + row, col]
 
     def block(r, c):
         return field[r, at_block(c, nodes)]
 
     lhs = jnp.concatenate(
         [
-            tiles[table[SELF * step + at]],
-            turned[table[SELF * step + at]],
-            tiles[table[EAST * step + at]],
-            turned[table[WEST * step + at]],
-            tiles[table[NORTH * step + at]],
-            turned[table[SOUTH * step + at]],
+            tiles[number(SELF)],
+            turned[number(SELF)],
+            tiles[number(EAST)],
+            turned[number(WEST)],
+            tiles[number(NORTH)],
+            turned[number(SOUTH)],
         ],
         axis=1,
     )
@@ -92,57 +93,45 @@
     return jnp.dot(lhs, rhs, preferred_element_type=F32)
 
 
-def edge_blocks(shape, body, after_row=None):
+def edge_blocks(shape):
     _, rows, cols = shape
     half, right, _ = place()
-
-    def one_row(i, carry):
-        for col in range(0, cols, 2):
-            body(jnp.where(half == i, 0, rows - 1), [col, col + 1])
-        if after_row is not None:
-            after_row(i)
-        return carry
-
-    lax.fori_loop(0, 2, one_row, 0)
-    for row in range(1, rows - 1):
-        body(row, [jnp.where(right == 0, cols - 1, 0)])
-
-
-def inner_blocks(shape, body):
+    outer, inner = jnp.where(half == 0, 0, rows - 1), jnp.where(half == 0, rows - 1, 0)
+    beside = jnp.where(right == 0, cols - 1, 0)
+    blocks = [(outer, col) for col in range(cols)] + [(inner, col) for col in range(cols)]
+    return blocks + [(row, beside) for row in range(1, rows - 1)]
+
+
+def inner_blocks(shape):
     _, rows, cols = shape
     _, right, _ = place()
-
-    def one_row(row, carry):
-        for col in range(0, cols - 1, 2):
-            body(row, [right + c for c in range(col, min(col + 2, cols - 1))])
-        return carry
-
-    lax.fori_loop(1, rows - 1, one_row, 0)
-
-
-def group(cols, nodes):
-    start = cols[0] * nodes
-    return pl.ds(start if isinstance(start, int) else pl.multiple_of(start, nodes), len(cols) * nodes)
-
-
-def group_in_field(cols, nodes):
-    return group([cols[0] + 1] + cols[1:], nodes)
-
-
-def messages(table, field, tiles, turned, row, cols, shape):
-    parts = [block_product(table, field, tiles, turned, row, col, shape).astype(BF16) for col in cols]
-    return jnp.concatenate(parts, axis=0) if len(parts) > 1 else parts[0]
+    return [(row, right + col) for row in range(1, rows - 1) for col in range(cols - 1)]
+
+
+def gather(read, blocks):
+    return jnp.concatenate([read(row, col) for row, col in blocks], axis=0)
+
+
+def scatter(ref, blocks, value, nodes, shift):
+    for k, (row, col) in enumerate(blocks):
+        ref[row + shift, at_block(col + shift, nodes)] = value[k * nodes : (k + 1) * nodes]
+
+
+def messages(table, field, tiles, turned, blocks, shape):
+    return gather(
+        lambda row, col: block_product(table, field, tiles, turned, row, col, shape).astype(BF16), blocks
+    )
 
 
 def forward_one(shape, table, field, tiles, turned, weight, x_field, m_all):
     nodes = shape[0]
 
-    def body(row, cols):
-        m = messages(table, field, tiles, turned, row, cols, shape)
-        m_all[row, group(cols, nodes)] = m
+    def body(blocks):
+        m = messages(table, field, tiles, turned, blocks, shape)
+        scatter(m_all, blocks, m, nodes, 0)
         z = jnp.dot(m, weight[...], preferred_element_type=F32)
-        inside = group_in_field(cols, nodes)
-        x_field[row + 1, inside] = (field[row + 1, inside].astype(F32) + jnp.tanh(z)).astype(BF16)
+        base = gather(lambda row, col: field[row + 1, at_block(col + 1, nodes)], blocks)
+        scatter(x_field, blocks, (base.astype(F32) + jnp.tanh(z)).astype(BF16), nodes, 1)
 
     return body
 
@@ -157,23 +146,24 @@
     nodes = shape[0]
     readf = readout[...].astype(F32)
 
-    def body(row, cols):
-        m = messages(table, field, tiles, turned, row, cols, shape)
-        here, inside = group(cols, nodes), group_in_field(cols, nodes)
-        m_all[row, here] = m
+    def body(blocks):
+        m = messages(table, field, tiles, turned, blocks, shape)
+        scatter(m_all, blocks, m, nodes, 0)
         t = jnp.tanh(jnp.dot(m, weight[...], preferred_element_type=F32))
-        x = (field[row + 1, inside].astype(F32) + t).astype(BF16)
+        base = gather(lambda row, col: field[row + 1, at_block(col + 1, nodes)], blocks)
+        x = (base.astype(F32) + t).astype(BF16)
         seen = jnp.dot(x, spread[...], preferred_element_type=F32)
         parts = []
-        for k, col in enumerate(cols):
+        for k, (row, col) in enumerate(blocks):
             one = seen[k * nodes : (k + 1) * nodes].T[0:1]
             preds[row, pl.ds(col, 1)] = one
             parts.append(residual_columns(one, goals[row, pl.ds(col, 1)], scale))
-        gp = jnp.concatenate(parts, axis=0) if len(parts) > 1 else parts[0]
+        gp = jnp.concatenate(parts, axis=0)
         sums[...] += (x.astype(F32) * gp).reshape(gp.shape[0] // 8, 8, gp.shape[1]).sum(axis=0)
         gz = (gp * readf * (1.0 - t * t)).astype(BF16)
-        gz_all[row, here] = gz
-        g_field[row + 1, inside] = jnp.dot(gz, weight_turned[...], preferred_element_type=F32).astype(BF16)
+        scatter(gz_all, blocks, gz, nodes, 0)
+        g = jnp.dot(gz, weight_turned[...], preferred_element_type=F32).astype(BF16)
+        scatter(g_field, blocks, g, nodes, 1)
 
     return body
 
@@ -182,14 +172,16 @@
     nodes = shape[0]
     readf = readout[...].astype(F32)
 
-    def body(row, cols):
-        here = group(cols, nodes)
-        t = jnp.tanh(jnp.dot(m_all[row, here], weight[...], preferred_element_type=F32))
-        for k, col in enumerate(cols):
-            gp = residual_columns(preds[row, pl.ds(col, 1)], goals[row, pl.ds(col, 1)], scale)
-            gx = gp * readf + block_product(table, field, tiles, turned, row, col, shape)
-            tk = t[k * nodes : (k + 1) * nodes]
-            gz_all[row, at_block(col, nodes)] = (gx * (1.0 - tk * tk)).astype(BF16)
+    def body(blocks):
+        m = gather(lambda row, col: m_all[row, at_block(col, nodes)], blocks)
+        t = jnp.tanh(jnp.dot(m, weight[...], preferred_element_type=F32))
+        gp = gather(
+            lambda row, col: residual_columns(preds[row, pl.ds(col, 1)], goals[row, pl.ds(col, 1)], scale), blocks
+        )
+        gx = gp * readf + gather(
+            lambda row, col: block_product(table, field, tiles, turned, row, col, shape), blocks
+        )
+        scatter(gz_all, blocks, (gx * (1.0 - t * t)).astype(BF16), nodes, 0)
 
     return body
 
@@ -207,48 +199,28 @@
             field[row, at_block(col, nodes)] = jnp.zeros((nodes, field.shape[2]), field.dtype)
 
 
-def send_edges(field, outer, inner, side, shape, sems, body):
+def take_edges(field, outer, inner, side, shape):
     nodes, rows, cols = shape
     half, right, _ = place()
     inside = pl.ds(nodes, cols * nodes)
-    lines = [
-        pltpu.make_async_copy(field.at[jnp.where(half == i, 1, rows), inside], line, sems.at[i])
-        for i, line in enumerate((outer, inner))
-    ]
-
-    def after_row(i):
-        @pl.when(i == 0)
-        def _():
-            lines[0].start()
-
-        @pl.when(i == 1)
-        def _():
-            lines[1].start()
-
-    edge_blocks(shape, body, after_row)
-    beside = [
-        (field.at[row + 1, at_block(jnp.where(right == 0, cols, 1), nodes)], side.at[at_block(row, nodes)])
-        for row in range(rows)
-    ]
-    wait_all(lines + start_all(beside, sems, 2))
-
-
-def rim_pairs(field, inner, outer, side, shape):
+    outer[...] = field[jnp.where(half == 0, 1, rows), inside]
+    inner[...] = field[jnp.where(half == 0, rows, 1), inside]
+    column = at_block(jnp.where(right == 0, cols, 1), nodes)
+    for row in range(rows):
+        side[at_block(row, nodes)] = field[row + 1, column]
+
+
+def fill_rim(field, outer, inner, side, shape):
     nodes, rows, cols = shape
     half, right, _ = place()
-    zero_col = pl.multiple_of(jnp.where(right == 0, 0, (cols + 1) * nodes), nodes)
-    side_col = pl.multiple_of(jnp.where(right == 0, (cols + 1) * nodes, 0), nodes)
     inside = pl.ds(nodes, cols * nodes)
     line = pl.ds(0, cols * nodes)
-    for row in range(1, rows + 1):
-        field[row, pl.ds(zero_col, nodes)] = jnp.zeros((nodes, field.shape[2]), field.dtype)
-    pairs = [
-        (inner.at[line], field.at[jnp.where(half == 0, rows + 1, 0), inside]),
-        (outer.at[line], field.at[jnp.where(half == 0, 0, rows + 1), inside]),
-    ]
+    field[jnp.where(half == 0, 0, rows + 1), inside] = outer[line]
+    field[jnp.where(half == 0, rows + 1, 0), inside] = inner[line]
+    empty, column = jnp.where(right == 0, 0, cols + 1), jnp.where(right == 0, cols + 1, 0)
     for row in range(rows):
-        pairs.append((side.at[pl.ds(row * nodes, nodes)], field.at[row + 1, pl.ds(side_col, nodes)]))
-    return pairs
+        field[row + 1, at_block(empty, nodes)] = jnp.zeros((nodes, field.shape[2]), field.dtype)
+        field[row + 1, at_block(column, nodes)] = side[at_block(row, nodes)]
 
 
 def pack_kernel(nodes, cols, ids, own, ends, side, numbers, ids_in, wide_ids, sems):
@@ -316,85 +288,57 @@
 
 
 def first_edge_kernel(shape, numbers, own, ends, middle, outer, inner, side, later, tiles, turned, weight,
-                      table, field, x_field, m_all, outer_out, inner_out, side_out, heads, heads_int, marks, sems):
+                      table, field, x_field, m_all, outer_out, inner_out, side_out, own_ids, above_ids, spots, sems):
     nodes, rows, cols = shape
     line = cols * nodes
-    step = rows * cols
-    half, _, moved = place()
+    half, right, moved = place()
     inside = pl.ds(nodes, line)
-
-    def main_pairs(flag):
-        if flag:
-            pairs = [
-                (ends.at[pl.ds(2 * line, TAIL)], heads.at[0]),
-                (ends.at[pl.ds(0, line)], field.at[1, inside]),
-                (ends.at[pl.ds(line, line)], field.at[rows, inside]),
-                (middle, field.at[pl.ds(2, rows - 2), inside]),
-            ]
-        else:
-            pairs = [(numbers, heads.at[0]), (own, field.at[pl.ds(1, rows), inside])]
-        return pairs
-
-    def above_pairs(flag):
-        return [((inner if flag else outer).at[pl.ds(line, TAIL)], heads.at[1])]
-
-    def either(flag, build, first):
-        @pl.when(flag)
-        def _():
-            start_all(build(True), sems, first)
-
-        @pl.when(jnp.logical_not(flag))
-        def _():
-            start_all(build(False), sems, first)
-
-    def either_wait(flag, build, first, low, high):
-        def some(value):
-            for i, (a, b) in list(enumerate(build(value)))[low:high]:
-                pltpu.make_async_copy(a, b, sems.at[first + i]).wait()
-
-        @pl.when(flag)
-        def _():
-            some(True)
-
-        @pl.when(jnp.logical_not(flag))
-        def _():
-            some(False)
-
-    either(moved, main_pairs, 0)
-    either(half == 1, above_pairs, 4)
-    left = start_all([(side.at[pl.ds(rows * nodes, TAIL)], heads.at[2])], sems, 5)
-    rest = start_all(
-        rim_pairs(field, inner, outer, side, shape),
-        sems,
-        6,
-    )
-    either_wait(moved, main_pairs, 0, 0, 1)
-    either_wait(half == 1, above_pairs, 4, 0, 1)
-    wait_all(left)
-    heads_int[...] = heads[:, :, 0:128].astype(F32).astype(jnp.int32)
-    wait_all(start_all([(heads_int, marks)], sems, 5))
-
-    def fill(at, carry):
-        row, col = at // cols, lax.rem(at, cols)
-        last = rows - 1
-        up = jnp.where(row == 0, marks[1, rows + last, col], marks[0, rows + jnp.maximum(row - 1, 0), col])
-        back = jnp.where(
-            col == 0, marks[2, 2 * rows + row, cols - 1], marks[0, 2 * rows + row, jnp.maximum(col - 1, 0)]
-        )
-        table[SELF * step + at] = marks[0, row, col]
-        table[EAST * step + at] = marks[0, rows + row, col]
-        table[WEST * step + at] = up
-        table[NORTH * step + at] = marks[0, 2 * rows + row, col]
-        table[SOUTH * step + at] = back
-        return carry
-
-    lax.fori_loop(0, step, fill, 0)
+    tail = pl.ds(line, TAIL)
+
+    @pl.when(moved)
+    def _():
+        own_ids[...] = ends[pl.ds(2 * line, TAIL)].astype(F32)
+
+    @pl.when(jnp.logical_not(moved))
+    def _():
+        own_ids[...] = numbers[...].astype(F32)
+
+    @pl.when(half == 1)
+    def _():
+        above_ids[...] = inner[tail].astype(F32)
+
+    @pl.when(half == 0)
+    def _():
+        above_ids[...] = outer[tail].astype(F32)
+
+    left = side[pl.ds(rows * nodes, TAIL)].astype(F32)[2 * rows : 3 * rows, 0:128]
+    north = own_ids[2 * rows : 3 * rows, 0:128]
+    lanes = lax.broadcasted_iota(jnp.int32, north.shape, 1)
+    last = jnp.broadcast_to(left[:, cols - 1 : cols], left.shape)
+    spots[0 : 2 * rows] = own_ids[0 : 2 * rows, 0:128].astype(jnp.int32)
+    spots[WEST * rows : WEST * rows + 1] = above_ids[2 * rows - 1 : 2 * rows, 0:128].astype(jnp.int32)
+    spots[WEST * rows + 1 : (WEST + 1) * rows] = own_ids[rows : 2 * rows - 1, 0:128].astype(jnp.int32)
+    spots[NORTH * rows : (NORTH + 1) * rows] = north.astype(jnp.int32)
+    spots[SOUTH * rows : (SOUTH + 1) * rows] = jnp.where(lanes == 0, last, pltpu.roll(north, 1, 1)).astype(jnp.int32)
+    copies = start_all([(spots, table)], sems)
+
+    @pl.when(moved)
+    def _():
+        field[1, inside] = ends[pl.ds(0, line)]
+        field[rows, inside] = ends[pl.ds(line, line)]
+        for row in range(2, rows):
+            field[row, inside] = middle[row - 2]
+
+    @pl.when(jnp.logical_not(moved))
+    def _():
+        for row in range(rows):
+            field[row + 1, inside] = own[row]
+
+    fill_rim(field, outer, inner, side, shape)
     zero_rim(x_field, shape)
-    wait_all(rest)
-    either_wait(moved, main_pairs, 0, 1, None)
-
-    body = forward_one(shape, table, field, tiles, turned, weight, x_field, m_all)
-    send_edges(x_field, outer_out, inner_out, side_out, shape, sems, body)
+    wait_all(copies)
+    forward_one(shape, table, field, tiles, turned, weight, x_field, m_all)(edge_blocks(shape))
+    take_edges(x_field, outer_out, inner_out, side_out, shape)
 
 
 def middle_compute_kernel(shape, scale, table, field, tiles, turned, weight_one, weight_two, two_turned, readout, spread, target,
@@ -411,28 +355,32 @@
 
     zero_rim(g_field, shape)
     sums[...] = jnp.zeros_like(sums)
-    inner_blocks(shape, forward_one(shape, table, field, tiles, turned, weight_one, x_field, m_one))
-    inner_blocks(shape, through_two(
-        shape, scale, table, x_field, tiles, turned, weight_two, two_turned, readout, spread, goals, m_two, gz_two, g_field, preds, sums
-    ))
+    blocks = inner_blocks(shape)
+    forward_one(shape, table, field, tiles, turned, weight_one, x_field, m_one)(blocks)
+    through_two(
+        shape, scale, table, x_field, tiles, turned, weight_two, two_turned, readout, spread, goals, m_two, gz_two,
+        g_field, preds, sums,
+    )(blocks)
 
 
 def second_edge_kernel(shape, scale, table, outer, inner, side, tiles, turned, weight, weight_turned, readout, spread, goals,
                        x_in, m_in, gz_in, g_in, preds_in, sums_in,
-                       x_field, m_two, gz_two, g_field, preds, sums, outer_out, inner_out, side_out, sems):
-    wait_all(start_all(rim_pairs(x_field, inner, outer, side, shape), sems))
-    body = through_two(
+                       x_field, m_two, gz_two, g_field, preds, sums, outer_out, inner_out, side_out):
+    fill_rim(x_field, outer, inner, side, shape)
+    through_two(
         shape, scale, table, x_field, tiles, turned, weight, weight_turned, readout, spread, goals, m_two, gz_two,
         g_field, preds, sums,
-    )
-    send_edges(g_field, outer_out, inner_out, side_out, shape, sems, body)
+    )(edge_blocks(shape))
+    take_edges(g_field, outer_out, inner_out, side_out, shape)
 
 
 def back_inner_kernel(shape, scale, table, g_field, tiles, turned, weight, readout, goals, preds, m_one, m_two, gz_two,
                       gz_one, first_out, second_out):
     nodes, rows, cols = shape
     _, right, _ = place()
-    inner_blocks(shape, back_one(shape, scale, table, g_field, tiles, turned, weight, readout, goals, preds, m_one, gz_one))
+    back_one(shape, scale, table, g_field, tiles, turned, weight, readout, goals, preds, m_one, gz_one)(
+        inner_blocks(shape)
+    )
     part = pl.ds(pl.multiple_of(right * nodes, nodes), (cols - 1) * nodes)
     first_out[...] = jnp.zeros_like(first_out)
     second_out[...] = jnp.zeros_like(second_out)
@@ -449,23 +397,15 @@
     lax.fori_loop(0, rows, each_row, 0)
 
 
-def back_edge_kernel(shape, scale, table, outer, inner, side, tiles, turned, weight, readout, goals, preds, preds_swap,
-                     m_one, first_in, second, sums, g_in, gz_in, g_field, gz_one, keep, one, two, three, pred_out,
-                     first_out, parts, sems):
+def back_edge_kernel(shape, scale, table, outer, inner, side, tiles, turned, weight, readout, goals, preds,
+                     m_one, first_in, second, sums, g_in, gz_in, g_field, gz_one, keep, one, two, three,
+                     first_out, parts):
     nodes, rows, cols = shape
-    _, right, moved = place()
-    copies = start_all(rim_pairs(g_field, inner, outer, side, shape), sems)
-
-    @pl.when(moved)
-    def _():
-        pred_out[...] = preds_swap[...]
-
-    @pl.when(jnp.logical_not(moved))
-    def _():
-        pred_out[...] = preds[...]
-
-    wait_all(copies)
-    edge_blocks(shape, back_one(shape, scale, table, g_field, tiles, turned, weight, readout, goals, preds, m_one, gz_one))
+    _, right, _ = place()
+    fill_rim(g_field, outer, inner, side, shape)
+    back_one(shape, scale, table, g_field, tiles, turned, weight, readout, goals, preds, m_one, gz_one)(
+        edge_blocks(shape)
+    )
     first_out[...] = first_in[...]
     for row in (0, rows - 1):
         first_out[...] += over_nodes(m_one[row], gz_one[row])
@@ -476,6 +416,7 @@
     parts[:, : size // 2] = first_out[...].reshape(count, size // 2, width)
     parts[:, size // 2 :] = second[...].reshape(count, size // 2, width)
     spread_shares(parts, sums[...], lax.rem(lax.axis_index(AXES), 4), (keep, one, two, three))
+    ride_preds(preds, three)
 
 
 def spread_shares(parts, extra, digit, outs):
@@ -483,16 +424,42 @@
     for k, out in enumerate(outs):
         for group in range(parts.shape[0] // 4):
             out[group * size : (group + 1) * size] = parts[4 * group + jnp.bitwise_xor(digit, k)]
-        out[out.shape[0] - 8 :] = extra
-
-
-def fold_kernel(base, keep, one, two, three, *refs):
+        out[parts.shape[0] // 4 * size : parts.shape[0] // 4 * size + 8] = extra
+
+
+def take_preds(preds, riding, pred_out):
+    _, _, moved = place()
+    start = riding.shape[0] - preds.shape[0] * preds.shape[1] // 2
+
+    @pl.when(moved)
+    def _():
+        for row in range(preds.shape[0]):
+            at = start + row // 2 * preds.shape[1]
+            lane = row % 2 * preds.shape[2]
+            pred_out[row] = riding[at : at + preds.shape[1], lane : lane + preds.shape[2]]
+
+    @pl.when(jnp.logical_not(moved))
+    def _():
+        pred_out[...] = preds[...]
+
+
+def ride_preds(preds, riding):
+    start = riding.shape[0] - preds.shape[0] * preds.shape[1] // 2
+    for row in range(preds.shape[0]):
+        at = start + row // 2 * preds.shape[1]
+        lane = row % 2 * preds.shape[2]
+        riding[at : at + preds.shape[1], lane : lane + preds.shape[2]] = preds[row]
+
+
+def fold_kernel(base, keep, one, two, three, preds, *refs):
     digit = lax.rem(lax.axis_index(AXES) // base, 4)
-    parts = refs[-1]
+    *outs, parts = refs
+    if base == 4:
+        take_preds(preds, three, outs.pop())
     count, size, width = parts.shape
-    total = keep[...] + one[...] + two[...] + three[...]
+    total = keep[...] + one[...] + two[...] + three[: keep.shape[0]]
     parts[...] = total[: count * size].reshape(count, size, width)
-    spread_shares(parts, total[count * size :], digit, refs[:-1])
+    spread_shares(parts, total[count * size :], digit, outs)
 
 
 def last_fold_kernel(keep, one, two, three, first, second, readout):
@@ -503,12 +470,13 @@
     readout[...] = total[2 * share :].sum(axis=0, keepdims=True)
 
 
-def shares_shape(groups, size, width):
-    return (jax.ShapeDtypeStruct((groups * size + 8, width), F32),) * 4
-
-
-def sum_shares(outs, count, share, width, params):
-    base, groups = 1, count // 4
+def shares_shape(groups, size, width, riding=0):
+    rows = (groups * size + 8,) * 3 + (groups * size + 8 + riding,)
+    return tuple(jax.ShapeDtypeStruct((number, width), F32) for number in rows)
+
+
+def sum_shares(outs, preds, count, share, width, params):
+    base, groups, pred_out = 1, count // 4, ()
     while True:
         got = [
             lax.ppermute(outs[k], AXES, [(i, i ^ (k * base)) for i in range(count)]) for k in (1, 2, 3)
@@ -516,18 +484,23 @@
         if groups == 1:
             break
         base *= 4
-        outs = pl.pallas_call(
+        more = (jax.ShapeDtypeStruct(preds.shape, F32),) if base == 4 else ()
+        *outs, last = pl.pallas_call(
             functools.partial(fold_kernel, base),
-            out_shape=shares_shape(groups // 4, 2 * share, width),
-            in_specs=[VMEM] * 4,
-            out_specs=(VMEM,) * 4,
+            out_shape=shares_shape(groups // 4, 2 * share, width) + more,
+            in_specs=[VMEM] * 5,
+            out_specs=(VMEM,) * (4 + len(more)),
             scratch_shapes=[pltpu.VMEM((groups, 2 * share, width), F32)],
             compiler_params=params,
             name="fold",
-        )(outs[0], *got)
+        )(outs[0], *got, preds)
+        if more:
+            pred_out = last
+        else:
+            outs.append(last)
         groups //= 4
     small = jax.ShapeDtypeStruct((share, width), F32)
-    return pl.pallas_call(
+    sums = pl.pallas_call(
         last_fold_kernel,
         out_shape=(small, small, jax.ShapeDtypeStruct((1, width), F32)),
         in_specs=[VMEM] * 4,
@@ -535,6 +508,7 @@
         compiler_params=params,
         name="last_fold",
     )(outs[0], *got)
+    return *sums, pred_out
 
 
 def per_device(features, tile_ids, tiles, w_first, w_second, readout, target):
@@ -624,14 +598,14 @@
 
     table, f_field, x_field, m_one, outer_s, inner_s, side_s = pl.pallas_call(
         functools.partial(first_edge_kernel, shape),
-        out_shape=(jax.ShapeDtypeStruct((5 * step,), jnp.int32), padded, padded, patch) + edge_shapes,
-        in_specs=[ANY] * 8 + [VMEM] * 3,
+        out_shape=(jax.ShapeDtypeStruct((5 * rows, 128), jnp.int32), padded, padded, patch) + edge_shapes,
+        in_specs=[VMEM] * 7 + [ANY] + [VMEM] * 3,
         out_specs=(SMEM,) + (VMEM,) * 6,
         scratch_shapes=[
-            pltpu.VMEM((3, TAIL, width), BF16),
-            pltpu.VMEM((3, TAIL, 128), jnp.int32),
-            pltpu.SMEM((3, TAIL, 128), jnp.int32),
-            sems(8 + rows),
+            pltpu.VMEM((TAIL, width), F32),
+            pltpu.VMEM((TAIL, width), F32),
+            pltpu.VMEM((5 * rows, 128), jnp.int32),
+            sems(1),
         ],
         compiler_params=params,
         cost_estimate=cost(edge, edge),
@@ -653,17 +627,15 @@
     x_field, m_two, gz_two, g_field, preds, sums, outer_s, inner_s, side_s = pl.pallas_call(
         functools.partial(second_edge_kernel, shape, scale),
         out_shape=(padded, patch, patch, padded, goal_shape, sums_shape) + edge_shapes,
-        in_specs=[SMEM] + [ANY] * 3 + [VMEM] * 13,
+        in_specs=[SMEM] + [VMEM] * 16,
         out_specs=(VMEM,) * 9,
         input_output_aliases={11 + i: i for i in range(6)},
-        scratch_shapes=[sems(2 + rows)],
         compiler_params=params,
         cost_estimate=cost(edge, 2 * edge),
         name="second_edge",
     )(table, outer, inner, side, tiles, turned, w_second, w_turned, readout, spread, goals, x_field, m_two, gz_two, g_field, preds, sums)
 
     outer, inner, side = edges(outer_s, inner_s, side_s)
-    preds_swap = send(preds, swap)
     gz_one, first, second = pl.pallas_call(
         functools.partial(back_inner_kernel, shape, scale),
         out_shape=(patch, square, square),
@@ -675,19 +647,19 @@
     )(table, g_field, tiles, turned, w_first, readout, goals, preds, m_one, m_two, gz_two)
 
     share = width // count
-    _, _, *outs, pred_out = pl.pallas_call(
+    _, _, *outs = pl.pallas_call(
         functools.partial(back_edge_kernel, shape, scale),
-        out_shape=(padded, patch) + shares_shape(count // 4, 2 * share, width) + (goal_shape,),
-        in_specs=[SMEM] + [ANY] * 3 + [VMEM] * 13,
-        out_specs=(VMEM,) * 7,
-        input_output_aliases={15: 0, 16: 1},
-        scratch_shapes=[pltpu.VMEM((width, width), F32), pltpu.VMEM((count, 2 * share, width), F32), sems(2 + rows)],
+        out_shape=(padded, patch) + shares_shape(count // 4, 2 * share, width, step * nodes // width),
+        in_specs=[SMEM] + [VMEM] * 15,
+        out_specs=(VMEM,) * 6,
+        input_output_aliases={14: 0, 15: 1},
+        scratch_shapes=[pltpu.VMEM((width, width), F32), pltpu.VMEM((count, 2 * share, width), F32)],
         compiler_params=params,
         cost_estimate=cost(edge, 2 * edge),
         name="back_edge",
-    )(table, outer, inner, side, tiles, turned, w_first, readout, goals, preds, preds_swap, m_one, first, second, sums,
+    )(table, outer, inner, side, tiles, turned, w_first, readout, goals, preds, m_one, first, second, sums,
       g_field, gz_one)
-    first, second, extra = sum_shares(outs, count, share, width, params)
+    first, second, extra, pred_out = sum_shares(outs, preds, count, share, width, params)
     return pred_out, first, second, extra[0]
 
 

time: 97.3 us -> 88.7 us (0.912)
  Pallas kernels: 33.2 us -> 22 us
  waiting for transfers between devices: 20.9 us -> 22.6 us
  starting transfers between devices: 39.3 us -> 40.3 us
    pallas_call x1, Pallas kernels: 8.2 us -> 3.76 us  [per_device(): pl.pallas_call(functools.partial(second_edge_kernel, shape, scale), out_s...]
    pallas_call x1, Pallas kernels: 6.61 us -> 2.74 us  [per_device(): pl.pallas_call(functools.partial(first_edge_kernel, shape), out_shape=(ja...]
    pallas_call x1, Pallas kernels: 7.72 us -> 4.31 us  [per_device(): pl.pallas_call(functools.partial(middle_compute_kernel, shape, scale), ou...]
    ppermute x13 -> x12, waiting for transfers between devices: 10.1 us -> 11.5 us  [send(): return lax.ppermute(value, AXES, way)]
    ppermute x13 -> x12, starting transfers between devices: 32.9 us -> 33.7 us  [send(): return lax.ppermute(value, AXES, way)]
  transfers between devices with their start and end apart: 19 -> 18, of which waited for: 6 -> 7; matrix products, arithmetic and copies ran while one was open for 0% -> 0% of each run, Pallas kernels for 14% -> 12%
where the time goes in v6:
time: 88.7 us; the launch traced here: 88.4 us
  starting transfers between devices  40.3 us (45%)
  waiting for transfers between devices  22.6 us (25%)
  Pallas kernels  22 us (25%)
  local copies, waits for them, and re-layouts  2.63 us (3%)
    ppermute x12, starting transfers between devices, send(): return lax.ppermute(value, AXES, way)  33.7 us
    ppermute x12, waiting for transfers between devices, send(): return lax.ppermute(value, AXES, way)  11.5 us
    ppermute x6, waiting for transfers between devices, sum_shares(): lax.ppermute(outs[k], AXES, [(i, i ^ k * base) for i in range(count)])  11.1 us
    ppermute x6, starting transfers between devices, sum_shares(): lax.ppermute(outs[k], AXES, [(i, i ^ k * base) for i in range(count)])  6.59 us
    pallas_call x1, Pallas kernels, per_device(): pl.pallas_call(functools.partial(middle_compute_kernel, shape, scale), ou...  4.31 us
    pallas_call x1, Pallas kernels, per_device(): pl.pallas_call(functools.partial(back_inner_kernel, shape, scale), out_sh...  4.12 us
    pallas_call x1, Pallas kernels, per_device(): pl.pallas_call(functools.partial(second_edge_kernel, shape, scale), out_s...  3.76 us
    pallas_call x1, Pallas kernels, per_device(): pl.pallas_call(functools.partial(back_edge_kernel, shape, scale), out_sha...  3.55 us
  transfers between devices with their start and end apart: 18, of which 7 were waited for; matrix products, arithmetic and copies ran while one was open for 0% of the time, Pallas kernels for 12%

profile of v6, /device:TPU:0, one launch (start us, length us, event | category | flops | bytes accessed | tf_op | source)
XLA Modules:
  0.0 88.4 jit_solution(12023295593441282319)
XLA Ops:
  0.6 1.6 %copy-done = bf16[4,8,128,256]{3,2,1,0:T(8,128)(2,1)S(1)} copy-done((bf16[4,8,128,256]{3,2,1,0:T(8,128)(2,1)S(1)}, bf16[4,8,128,256]{3,2,1,0:T(8,128)(2,1)}, u32[]{:S(2)}) %copy-start) | copy-done | bytes 2097176
  2.2 0.7 copy-done.6
  3.4 0.9 collective-permute-start
  4.6 0.9 collective-permute-start.1
  5.5 6.9 %collective-permute-start.2 = (bf16[528,256]{1,0:T(8,128)(2,1)S(1)}, bf16[528,256]{1,0:T(8,128)(2,1)S(1)}, u32[]{:S(2)}, u32[]{:S(2)}) collective-permute-start(bf16[528,256]{1,0:T(8,128)(2,1)S(1)} %get-tuple-element.58.after), channel_id=1, source_target_pairs={{1,0},{3,1},{0,2},{2,3},{5,4},{7,5},{4,6},{6,7},{9,8},{11,9},{8,10... | collective-permute-start | bytes 811016 | tf_op jit(solution)/shard_map/ppermute | solution.py:524
  12.4 6.9 %collective-permute-done.2.after.side = bf16[528,256]{1,0:T(8,128)(2,1)S(1)} collective-permute-done((bf16[528,256]{1,0:T(8,128)(2,1)S(1)}, bf16[528,256]{1,0:T(8,128)(2,1)S(1)}, u32[]{:S(2)}, u32[]{:S(2)}) %collective-permute-start.2) | collective-permute-done | bytes 270368 | tf_op jit(solution)/shard_map/ppermute | solution.py:524
  19.5 0.7 collective-permute-start.3
  20.2 6.0 %collective-permute-start.4 = (bf16[1040,256]{1,0:T(8,128)(2,1)S(1)}, bf16[1040,256]{1,0:T(8,128)(2,1)S(1)}, u32[]{:S(2)}, u32[]{:S(2)}) collective-permute-start(bf16[1040,256]{1,0:T(8,128)(2,1)S(1)} %get-tuple-element.60), channel_id=1, source_target_pairs={{1,0},{0,1},{3,2},{2,3},{5,4},{4,5},{7,6},{6,7},{9,8},{8,9},{11,10... | collective-permute-start | bytes 1597448 | tf_op jit(solution)/shard_map/ppermute | solution.py:524
  26.1 0.7 collective-permute-start.5
  26.8 1.6 %prepare.1 = (bf16[16,128,128]{2,1,0:T(8,128)(2,1)S(1)}, bf16[16,128,128]{2,1,0:T(8,128)(2,1)S(1)}, bf16[256,256]{1,0:T(8,128)(2,1)S(1)}, bf16[256,256]{1,0:T(8,128)(2,1)S(1)}, bf16[256,256]{1,0:T(8,128)(2,1)S(1)}) custom-call(bf16[16,128,128]{2,1,0:T(8,128)(2,1)S(1)} %copy-done.2, bf16[256,256]{1,0:T(8,128)(2,1)S(1)} %copy-done.3, ...), custom_call_target="tpu_custom_call" | custom-call | tf_op jit(solution)/shard_map/prepare/pallas_call | solution.py:558
  28.5 2.7 %first_edge.1 = (s32[20,128]{1,0:T(8,128)S(1)}, bf16[6,1280,256]{2,1,0:T(8,128)(2,1)S(1)}, bf16[6,1280,256]{2,1,0:T(8,128)(2,1)S(1)}, bf16[4,1024,256]{2,1,0:T(8...) custom-call(bf16[16,256]{1,0:T(8,128)(2,1)S(1)} %get-tuple-element.56.num, ...), custom_call_target="tpu_custom_call" | custom-call | flops 1207959552 | bytes 4718592 | tf_op jit(solution)/shard_map/first_edge/pallas_call | solution.py:599
  31.3 0.7 collective-permute-start.6
  32.0 8.2 %collective-permute-start.7 = (bf16[1024,256]{1,0:T(8,128)(2,1)S(1)}, bf16[1024,256]{1,0:T(8,128)(2,1)S(1)}, u32[]{:S(2)}, u32[]{:S(2)}) collective-permute-start(bf16[1024,256]{1,0:T(8,128)(2,1)S(1)} %get-tuple-element.70), channel_id=1, source_target_pairs={{1,0},{0,1},{3,2},{2,3},{5,4},{4,5},{7,6},{6,7},{9,8},{8,9},{11,10... | collective-permute-start | bytes 1572872 | tf_op jit(solution)/shard_map/ppermute | solution.py:524
  40.2 3.3 %collective-permute-start.8 = (bf16[512,256]{1,0:T(8,128)(2,1)S(1)}, bf16[512,256]{1,0:T(8,128)(2,1)S(1)}, u32[]{:S(2)}, u32[]{:S(2)}) collective-permute-start(bf16[512,256]{1,0:T(8,128)(2,1)S(1)} %get-tuple-element.71), channel_id=1, source_target_pairs={{2,0},{3,1},{0,2},{1,3},{6,4},{7,5},{4,6},{5,7},{10,8},{11,9},{8,1... | collective-permute-start | bytes 786440 | tf_op jit(solution)/shard_map/ppermute | solution.py:524
  43.6 4.3 %inner_forward.1 = (bf16[6,1280,256]{2,1,0:T(8,128)(2,1)S(1)}, bf16[4,1024,256]{2,1,0:T(8,128)(2,1)S(1)}, bf16[4,1024,256]{2,1,0:T(8,128)(2,1)S(1)}, bf16[4,1024...) custom-call(s32[20,128]{1,0:T(8,128)S(1)} %get-tuple-element.68.tabl, ...), custom_call_target="tpu_custom_call", output_to_operand_aliasing={{0}: (11, {}), {1}: (12, {})} | custom-call | flops 2113929216 | bytes 9175040 | tf_op jit(solution)/shard_map/inner_forward/pallas_call | solution.py:616
  47.9 2.1 %collective-permute-done.8.side = bf16[512,256]{1,0:T(8,128)(2,1)S(1)} collective-permute-done((bf16[512,256]{1,0:T(8,128)(2,1)S(1)}, bf16[512,256]{1,0:T(8,128)(2,1)S(1)}, u32[]{:S(2)}, u32[]{:S(2)}) %collective-permute-start.8) | collective-permute-done | bytes 262176 | tf_op jit(solution)/shard_map/ppermute | solution.py:524
  50.0 3.8 %second_edge.1 = (bf16[6,1280,256]{2,1,0:T(8,128)(2,1)S(1)}, bf16[4,1024,256]{2,1,0:T(8,128)(2,1)S(1)}, bf16[4,1024,256]{2,1,0:T(8,128)(2,1)S(1)}, bf16[6,1280,2...) custom-call(s32[20,128]{1,0:T(8,128)S(1)} %get-tuple-element.68.tabl, ...), custom_call_target="tpu_custom_call", output_to_operand_aliasing={{0}: (11, {}), {1}: (12, {}), {2}: (13, {}), {3}: (14, {}),... | custom-call | flops 1509949440 | bytes 7077888 | tf_op jit(solution)/shard_map/second_edge/pallas_call | solution.py:627
  53.8 0.9 collective-permute-start.9
  54.6 3.0 %collective-permute-start.10 = (bf16[1024,256]{1,0:T(8,128)(2,1)S(1)}, bf16[1024,256]{1,0:T(8,128)(2,1)S(1)}, u32[]{:S(2)}, u32[]{:S(2)}) collective-permute-start(bf16[1024,256]{1,0:T(8,128)(2,1)S(1)} %get-tuple-element.85), channel_id=1, source_target_pairs={{1,0},{0,1},{3,2},{2,3},{5,4},{4,5},{7,6},{6,7},{9,8},{8,9},{11,10... | collective-permute-start | bytes 1572872 | tf_op jit(solution)/shard_map/ppermute | solution.py:524
  57.6 1.7 %collective-permute-start.11 = (bf16[512,256]{1,0:T(8,128)(2,1)S(1)}, bf16[512,256]{1,0:T(8,128)(2,1)S(1)}, u32[]{:S(2)}, u32[]{:S(2)}) collective-permute-start(bf16[512,256]{1,0:T(8,128)(2,1)S(1)} %get-tuple-element.86), channel_id=1, source_target_pairs={{2,0},{3,1},{0,2},{1,3},{6,4},{7,5},{4,6},{5,7},{10,8},{11,9},{8,1... | collective-permute-start | bytes 786440 | tf_op jit(solution)/shard_map/ppermute | solution.py:524
  59.4 4.1 %back_inner.1 = (bf16[4,1024,256]{2,1,0:T(8,128)(2,1)S(1)}, f32[256,256]{1,0:T(8,128)S(1)}, f32[256,256]{1,0:T(8,128)S(1)}) custom-call(s32[20,128]{1,0:T(8,128)S(1)} %get-tuple-element.68.table, bf16[6,1280,256]{2,1,0:T(8,128)(2,1)S(1)} %get-tuple-element.89.g_field.g_in, bf16[16,128,128]{2,1,0:T(8,128)(2,1)S(1)} %get-tuple-element.65.tiles, ...), custom_call_target="tpu_custom_call" | custom-call | flops 1711276032 | bytes 9699328 | tf_op jit(solution)/shard_map/back_inner/pallas_call | solution.py:639
  63.5 2.4 %collective-permute-done.11.side = bf16[512,256]{1,0:T(8,128)(2,1)S(1)} collective-permute-done((bf16[512,256]{1,0:T(8,128)(2,1)S(1)}, bf16[512,256]{1,0:T(8,128)(2,1)S(1)}, u32[]{:S(2)}, u32[]{:S(2)}) %collective-permute-start.11) | collective-permute-done | bytes 262176 | tf_op jit(solution)/shard_map/ppermute | solution.py:524
  65.9 3.5 %back_edge.1 = (bf16[6,1280,256]{2,1,0:T(8,128)(2,1)S(1)}, bf16[4,1024,256]{2,1,0:T(8,128)(2,1)S(1)}, f32[136,256]{1,0:T(8,128)S(1)}, f32[136,256]{1,0:T(8,128)S...) custom-call(s32[20,128]{1,0:T(8,128)S(1)} %get-tuple-element.68.table, ...), custom_call_target="tpu_custom_call", output_to_operand_aliasing={{0}: (14, {}), {1}: (15, {})} | custom-call | flops 1509949440 | bytes 7077888 | tf_op jit(solution)/shard_map/back_edge/pallas_call | solution.py:650
  69.5 0.7 collective-permute-start.14
  70.2 1.2 %collective-permute-start.12 = (f32[136,256]{1,0:T(8,128)S(1)}, f32[136,256]{1,0:T(8,128)S(1)}, u32[]{:S(2)}, u32[]{:S(2)}) collective-permute-start(f32[136,256]{1,0:T(8,128)S(1)} %get-tuple-element.97), channel_id=1, source_target_pairs={{0,1},{1,0},{2,3},{3,2},{4,5},{5,4},{6,7},{7,6},{8,9},{9,8},{10,11... | collective-permute-start | bytes 417800 | tf_op jit(solution)/shard_map/ppermute | solution.py:482
  71.7 0.7 collective-permute-done.12.one
  72.4 6.5 %collective-permute-done.13.two = f32[136,256]{1,0:T(8,128)S(1)} collective-permute-done((f32[136,256]{1,0:T(8,128)S(1)}, f32[136,256]{1,0:T(8,128)S(1)}, u32[]{:S(2)}, u32[]{:S(2)}) %collective-permute-start.13) | collective-permute-done | bytes 139296 | tf_op jit(solution)/shard_map/ppermute | solution.py:482
  79.5 1.6 %collective-permute-start.15 = (f32[40,256]{1,0:T(8,128)S(1)}, f32[40,256]{1,0:T(8,128)S(1)}, u32[]{:S(2)}, u32[]{:S(2)}) collective-permute-start(f32[40,256]{1,0:T(8,128)S(1)} %get-tuple-element.102), channel_id=1, source_target_pairs={{0,4},{1,5},{2,6},{3,7},{4,0},{5,1},{6,2},{7,3},{8,12},{9,13},{10,... | collective-permute-start | bytes 122888 | tf_op jit(solution)/shard_map/ppermute | solution.py:482
  81.1 0.9 %collective-permute-start.16 = (f32[40,256]{1,0:T(8,128)S(1)}, f32[40,256]{1,0:T(8,128)S(1)}, u32[]{:S(2)}, u32[]{:S(2)}) collective-permute-start(f32[40,256]{1,0:T(8,128)S(1)} %get-tuple-element.103), channel_id=1, source_target_pairs={{0,8},{1,9},{2,10},{3,11},{4,12},{5,13},{6,14},{7,15},{8,0},{9,1},... | collective-permute-start | bytes 122888 | tf_op jit(solution)/shard_map/ppermute | solution.py:482
  82.0 1.9 %collective-permute-start.17 = (f32[40,256]{1,0:T(8,128)S(1)}, f32[40,256]{1,0:T(8,128)S(1)}, u32[]{:S(2)}, u32[]{:S(2)}) collective-permute-start(f32[40,256]{1,0:T(8,128)S(1)} %get-tuple-element.104), channel_id=1, source_target_pairs={{0,12},{1,13},{2,14},{3,15},{4,8},{5,9},{6,10},{7,11},{8,4},{9,5},... | collective-permute-start | bytes 122888 | tf_op jit(solution)/shard_map/ppermute | solution.py:482
  83.9 2.9 %collective-permute-done.16.two = f32[40,256]{1,0:T(8,128)S(1)} collective-permute-done((f32[40,256]{1,0:T(8,128)S(1)}, f32[40,256]{1,0:T(8,128)S(1)}, u32[]{:S(2)}, u32[]{:S(2)}) %collective-permute-start.16) | collective-permute-done | bytes 40992 | tf_op jit(solution)/shard_map/ppermute | solution.py:482
  86.7 1.0 %collective-permute-done.17.three = f32[40,256]{1,0:T(8,128)S(1)} collective-permute-done((f32[40,256]{1,0:T(8,128)S(1)}, f32[40,256]{1,0:T(8,128)S(1)}, u32[]{:S(2)}, u32[]{:S(2)}) %collective-permute-start.17) | collective-permute-done | bytes 40992 | tf_op jit(solution)/shard_map/ppermute | solution.py:482
  (33 shorter events, 2.6 us)
Async XLA Ops:
  0.6 1.6 %copy-start = (bf16[4,8,128,256]{3,2,1,0:T(8,128)(2,1)S(1)}, bf16[4,8,128,256]{3,2,1,0:T(8,128)(2,1)}, u32[]{:S(2)}) copy-start(bf16[4,8,128,256]{3,2,1,0:T(8,128)(2,1)} %param.7) | copy-start | bytes 6291460
  2.2 0.7 copy-start.6
  2.9 1.6 %copy-start.1 = (bf16[4,8,128,256]{3,2,1,0:T(8,128)(2,1)S(1)}, bf16[4,8,128,256]{3,2,1,0:T(8,128)(2,1)}, u32[]{:S(2)}) copy-start(bf16[4,8,128,256]{3,2,1,0:T(8,128)(2,1)} %param.7) | copy-start | bytes 6291460
  3.4 15.9 %collective-permute-start = (bf16[2064,256]{1,0:T(8,128)(2,1)S(1)}, bf16[2064,256]{1,0:T(8,128)(2,1)S(1)}, u32[]{:S(2)}, u32[]{:S(2)}) collective-permute-start(bf16[2064,256]{1,0:T(8,128)(2,1)S(1)} %get-tuple-element.57), channel_id=1, source_target_pairs={{2,1},{1,2},{6,5},{5,6},{10,9},{9,10},{14,13},{13,14},{18,17},{17,... | collective-permute-start | bytes 3170312 | tf_op jit(solution)/shard_map/ppermute | solution.py:524
  4.6 21.5 %copy-start.5 = (f32[4,8,128]{2,1,0:T(8,128)S(1)}, f32[4,8,128]{2,1,0:T(8,128)}, u32[]{:S(2)}) copy-start(f32[4,8,128]{2,1,0:T(8,128)} %target.1) | copy-start | bytes 49156
  4.6 22.2 %copy-start.2 = (bf16[16,128,128]{2,1,0:T(8,128)(2,1)S(1)}, bf16[16,128,128]{2,1,0:T(8,128)(2,1)}, u32[]{:S(2)}) copy-start(bf16[16,128,128]{2,1,0:T(8,128)(2,1)} %tiles) | copy-start | bytes 1572868
  4.6 22.2 %copy-start.3 = (bf16[256,256]{1,0:T(8,128)(2,1)S(1)}, bf16[256,256]{1,0:T(8,128)(2,1)}, u32[]{:S(2)}) copy-start(bf16[256,256]{1,0:T(8,128)(2,1)} %first) | copy-start | bytes 393220
  4.6 22.2 %copy-start.4 = (bf16[256,256]{1,0:T(8,128)(2,1)S(1)}, bf16[256,256]{1,0:T(8,128)(2,1)}, u32[]{:S(2)}) copy-start(bf16[256,256]{1,0:T(8,128)(2,1)} %second) | copy-start | bytes 393220
  4.6 23.8 %collective-permute-start.1 = (bf16[2,1024,256]{2,1,0:T(8,128)(2,1)S(1)}, bf16[2,1024,256]{2,1,0:T(8,128)(2,1)S(1)}, u32[]{:S(2)}, u32[]{:S(2)}) collective-permute-start(bf16[2,1024,256]{2,1,0:T(8,128)(2,1)S(1)} %pack_middle.1), channel_id=1, source_target_pairs={{2,1},{1,2},{6,5},{5,6},{10,9},{9,10},{14,13},{13,14},{18,17},{17,... | collective-permute-start | bytes 3145736 | tf_op jit(solution)/shard_map/ppermute | solution.py:524
  5.5 13.8 %collective-permute-start.2 = (bf16[528,256]{1,0:T(8,128)(2,1)S(1)}, bf16[528,256]{1,0:T(8,128)(2,1)S(1)}, u32[]{:S(2)}, u32[]{:S(2)}) collective-permute-start(bf16[528,256]{1,0:T(8,128)(2,1)S(1)} %get-tuple-element.58.after), channel_id=1, source_target_pairs={{1,0},{3,1},{0,2},{2,3},{5,4},{7,5},{4,6},{6,7},{9,8},{11,9},{8,10... | collective-permute-start | bytes 811016 | tf_op jit(solution)/shard_map/ppermute | solution.py:524
  19.5 9.0 %collective-permute-start.3 = (bf16[1040,256]{1,0:T(8,128)(2,1)S(1)}, bf16[1040,256]{1,0:T(8,128)(2,1)S(1)}, u32[]{:S(2)}, u32[]{:S(2)}) collective-permute-start(bf16[1040,256]{1,0:T(8,128)(2,1)S(1)} %get-tuple-element.59), channel_id=1, source_target_pairs={{1,4},{3,6},{5,8},{7,10},{9,12},{11,14},{4,1},{6,3},{8,5},{10,7},{... | collective-permute-start | bytes 1597448 | tf_op jit(solution)/shard_map/ppermute | solution.py:524
  20.2 8.3 %collective-permute-start.4 = (bf16[1040,256]{1,0:T(8,128)(2,1)S(1)}, bf16[1040,256]{1,0:T(8,128)(2,1)S(1)}, u32[]{:S(2)}, u32[]{:S(2)}) collective-permute-start(bf16[1040,256]{1,0:T(8,128)(2,1)S(1)} %get-tuple-element.60), channel_id=1, source_target_pairs={{1,0},{0,1},{3,2},{2,3},{5,4},{4,5},{7,6},{6,7},{9,8},{8,9},{11,10... | collective-permute-start | bytes 1597448 | tf_op jit(solution)/shard_map/ppermute | solution.py:524
  26.1 2.3 %collective-permute-start.5 = (f32[4,8,128]{2,1,0:T(8,128)S(1)}, f32[4,8,128]{2,1,0:T(8,128)S(1)}, u32[]{:S(2)}, u32[]{:S(2)}) collective-permute-start(f32[4,8,128]{2,1,0:T(8,128)S(1)} %copy-done.5), channel_id=1, source_target_pairs={{2,1},{1,2},{6,5},{5,6},{10,9},{9,10},{14,13},{13,14},{18,17},{17,... | collective-permute-start | bytes 49160 | tf_op jit(solution)/shard_map/ppermute | solution.py:524
  28.5 15.0 %copy-start.7 = (bf16[256]{0:T(256)(128)(2,1)S(1)}, bf16[256]{0:T(256)(128)(2,1)}, u32[]{:S(2)}) copy-start(bf16[256]{0:T(256)(128)(2,1)} %param.12) | copy-start | bytes 1540
  31.3 18.7 %collective-permute-start.6 = (bf16[1024,256]{1,0:T(8,128)(2,1)S(1)}, bf16[1024,256]{1,0:T(8,128)(2,1)S(1)}, u32[]{:S(2)}, u32[]{:S(2)}) collective-permute-start(bf16[1024,256]{1,0:T(8,128)(2,1)S(1)} %get-tuple-element.69), channel_id=1, source_target_pairs={{1,4},{3,6},{5,8},{7,10},{9,12},{11,14},{4,1},{6,3},{8,5},{10,7},{... | collective-permute-start | bytes 1572872 | tf_op jit(solution)/shard_map/ppermute | solution.py:524
  32.0 18.0 %collective-permute-start.7 = (bf16[1024,256]{1,0:T(8,128)(2,1)S(1)}, bf16[1024,256]{1,0:T(8,128)(2,1)S(1)}, u32[]{:S(2)}, u32[]{:S(2)}) collective-permute-start(bf16[1024,256]{1,0:T(8,128)(2,1)S(1)} %get-tuple-element.70), channel_id=1, source_target_pairs={{1,0},{0,1},{3,2},{2,3},{5,4},{4,5},{7,6},{6,7},{9,8},{8,9},{11,10... | collective-permute-start | bytes 1572872 | tf_op jit(solution)/shard_map/ppermute | solution.py:524
  40.2 9.9 %collective-permute-start.8 = (bf16[512,256]{1,0:T(8,128)(2,1)S(1)}, bf16[512,256]{1,0:T(8,128)(2,1)S(1)}, u32[]{:S(2)}, u32[]{:S(2)}) collective-permute-start(bf16[512,256]{1,0:T(8,128)(2,1)S(1)} %get-tuple-element.71), channel_id=1, source_target_pairs={{2,0},{3,1},{0,2},{1,3},{6,4},{7,5},{4,6},{5,7},{10,8},{11,9},{8,1... | collective-permute-start | bytes 786440 | tf_op jit(solution)/shard_map/ppermute | solution.py:524
  53.8 12.1 %collective-permute-start.9 = (bf16[1024,256]{1,0:T(8,128)(2,1)S(1)}, bf16[1024,256]{1,0:T(8,128)(2,1)S(1)}, u32[]{:S(2)}, u32[]{:S(2)}) collective-permute-start(bf16[1024,256]{1,0:T(8,128)(2,1)S(1)} %get-tuple-element.84), channel_id=1, source_target_pairs={{1,4},{3,6},{5,8},{7,10},{9,12},{11,14},{4,1},{6,3},{8,5},{10,7},{... | collective-permute-start | bytes 1572872 | tf_op jit(solution)/shard_map/ppermute | solution.py:524
  54.6 11.3 %collective-permute-start.10 = (bf16[1024,256]{1,0:T(8,128)(2,1)S(1)}, bf16[1024,256]{1,0:T(8,128)(2,1)S(1)}, u32[]{:S(2)}, u32[]{:S(2)}) collective-permute-start(bf16[1024,256]{1,0:T(8,128)(2,1)S(1)} %get-tuple-element.85), channel_id=1, source_target_pairs={{1,0},{0,1},{3,2},{2,3},{5,4},{4,5},{7,6},{6,7},{9,8},{8,9},{11,10... | collective-permute-start | bytes 1572872 | tf_op jit(solution)/shard_map/ppermute | solution.py:524
  57.6 8.3 %collective-permute-start.11 = (bf16[512,256]{1,0:T(8,128)(2,1)S(1)}, bf16[512,256]{1,0:T(8,128)(2,1)S(1)}, u32[]{:S(2)}, u32[]{:S(2)}) collective-permute-start(bf16[512,256]{1,0:T(8,128)(2,1)S(1)} %get-tuple-element.86), channel_id=1, source_target_pairs={{2,0},{3,1},{0,2},{1,3},{6,4},{7,5},{4,6},{5,7},{10,8},{11,9},{8,1... | collective-permute-start | bytes 786440 | tf_op jit(solution)/shard_map/ppermute | solution.py:524
  69.5 9.4 %collective-permute-start.14 = (f32[152,256]{1,0:T(8,128)S(1)}, f32[152,256]{1,0:T(8,128)S(1)}, u32[]{:S(2)}, u32[]{:S(2)}) collective-permute-start(f32[152,256]{1,0:T(8,128)S(1)} %get-tuple-element.99), channel_id=1, source_target_pairs={{0,3},{1,2},{2,1},{3,0},{4,7},{5,6},{6,5},{7,4},{8,11},{9,10},{10,... | collective-permute-start | bytes 466952 | tf_op jit(solution)/shard_map/ppermute | solution.py:482
  70.2 2.2 %collective-permute-start.12 = (f32[136,256]{1,0:T(8,128)S(1)}, f32[136,256]{1,0:T(8,128)S(1)}, u32[]{:S(2)}, u32[]{:S(2)}) collective-permute-start(f32[136,256]{1,0:T(8,128)S(1)} %get-tuple-element.97), channel_id=1, source_target_pairs={{0,1},{1,0},{2,3},{3,2},{4,5},{5,4},{6,7},{7,6},{8,9},{9,8},{10,11... | collective-permute-start | bytes 417800 | tf_op jit(solution)/shard_map/ppermute | solution.py:482
  71.4 7.5 %collective-permute-start.13 = (f32[136,256]{1,0:T(8,128)S(1)}, f32[136,256]{1,0:T(8,128)S(1)}, u32[]{:S(2)}, u32[]{:S(2)}) collective-permute-start(f32[136,256]{1,0:T(8,128)S(1)} %get-tuple-element.98), channel_id=1, source_target_pairs={{0,2},{1,3},{2,0},{3,1},{4,6},{5,7},{6,4},{7,5},{8,10},{9,11},{10,... | collective-permute-start | bytes 417800 | tf_op jit(solution)/shard_map/ppermute | solution.py:482
  79.5 4.4 %collective-permute-start.15 = (f32[40,256]{1,0:T(8,128)S(1)}, f32[40,256]{1,0:T(8,128)S(1)}, u32[]{:S(2)}, u32[]{:S(2)}) collective-permute-start(f32[40,256]{1,0:T(8,128)S(1)} %get-tuple-element.102), channel_id=1, source_target_pairs={{0,4},{1,5},{2,6},{3,7},{4,0},{5,1},{6,2},{7,3},{8,12},{9,13},{10,... | collective-permute-start | bytes 122888 | tf_op jit(solution)/shard_map/ppermute | solution.py:482
  81.1 5.7 %collective-permute-start.16 = (f32[40,256]{1,0:T(8,128)S(1)}, f32[40,256]{1,0:T(8,128)S(1)}, u32[]{:S(2)}, u32[]{:S(2)}) collective-permute-start(f32[40,256]{1,0:T(8,128)S(1)} %get-tuple-element.103), channel_id=1, source_target_pairs={{0,8},{1,9},{2,10},{3,11},{4,12},{5,13},{6,14},{7,15},{8,0},{9,1},... | collective-permute-start | bytes 122888 | tf_op jit(solution)/shard_map/ppermute | solution.py:482
  82.0 5.8 %collective-permute-start.17 = (f32[40,256]{1,0:T(8,128)S(1)}, f32[40,256]{1,0:T(8,128)S(1)}, u32[]{:S(2)}, u32[]{:S(2)}) collective-permute-start(f32[40,256]{1,0:T(8,128)S(1)} %get-tuple-element.104), channel_id=1, source_target_pairs={{0,12},{1,13},{2,14},{3,15},{4,8},{5,9},{6,10},{7,11},{8,4},{9,5},... | collective-permute-start | bytes 122888 | tf_op jit(solution)/shard_map/ppermute | solution.py:482

commit v7 on v6

--- a/solution.py
+++ b/solution.py
@@ -58,7 +58,7 @@
     return pl.ds(col * nodes if isinstance(col, int) else pl.multiple_of(col * nodes, nodes), nodes)
 
 
-def block_product(table, field, tiles, turned, row, col, shape):
+def block_product(table, field, tiles, row, col, shape):
     nodes, rows, cols = shape
 
     def number(kind):
@@ -67,14 +67,15 @@
     def block(r, c):
         return field[r, at_block(c, nodes)]
 
+    half = tiles.shape[0] // 2
     lhs = jnp.concatenate(
         [
             tiles[number(SELF)],
-            turned[number(SELF)],
+            tiles[half + number(SELF)],
             tiles[number(EAST)],
-            turned[number(WEST)],
+            tiles[half + number(WEST)],
             tiles[number(NORTH)],
-            turned[number(SOUTH)],
+            tiles[half + number(SOUTH)],
         ],
         axis=1,
     )
@@ -117,17 +118,46 @@
         ref[row + shift, at_block(col + shift, nodes)] = value[k * nodes : (k + 1) * nodes]
 
 
-def messages(table, field, tiles, turned, blocks, shape):
+def messages(table, field, tiles, blocks, shape):
     return gather(
-        lambda row, col: block_product(table, field, tiles, turned, row, col, shape).astype(BF16), blocks
+        lambda row, col: block_product(table, field, tiles, row, col, shape).astype(BF16), blocks
     )
 
 
-def forward_one(shape, table, field, tiles, turned, weight, x_field, m_all):
+def rim_terms(table, tiles, outer, inner, side, shape):
+    nodes, rows, cols = shape
+    half, right, _ = place()
+    turned = tiles.shape[0] // 2
+
+    def product(tile, block):
+        return jnp.dot(tiles[tile], block, preferred_element_type=F32)
+
+    def beside(row):
+        tile = jnp.where(right == 0, table[NORTH * rows + row, cols - 1], turned + table[SOUTH * rows + row, 0])
+        return product(tile, side[at_block(row, nodes)])
+
+    terms = []
+    first, last = jnp.where(half == 0, 0, rows - 1), jnp.where(half == 0, rows - 1, 0)
+    for line, row, upward in ((outer, first, half == 0), (inner, last, half == 1)):
+        corner = beside(row)
+        for col in range(cols):
+            tile = jnp.where(upward, turned + table[WEST * rows + row, col], table[EAST * rows + row, col])
+            term = product(tile, line[at_block(col, nodes)])
+            if col in (0, cols - 1):
+                term = term + jnp.where((right == 0) == (col > 0), corner, 0.0)
+            terms.append(term)
+    return jnp.concatenate(terms + [beside(row) for row in range(1, rows - 1)], axis=0)
+
+
+def products(table, field, tiles, blocks, shape):
+    return gather(lambda row, col: block_product(table, field, tiles, row, col, shape), blocks)
+
+
+def forward_one(shape, table, field, tiles, weight, x_field, m_all):
     nodes = shape[0]
 
     def body(blocks):
-        m = messages(table, field, tiles, turned, blocks, shape)
+        m = messages(table, field, tiles, blocks, shape)
         scatter(m_all, blocks, m, nodes, 0)
         z = jnp.dot(m, weight[...], preferred_element_type=F32)
         base = gather(lambda row, col: field[row + 1, at_block(col + 1, nodes)], blocks)
@@ -142,12 +172,11 @@
     return jnp.concatenate([column, column], axis=1)
 
 
-def through_two(shape, scale, table, field, tiles, turned, weight, weight_turned, readout, spread, goals, m_all, gz_all, g_field, preds, sums):
+def through_two(shape, scale, table, field, tiles, weight, weight_turned, readout, spread, goals, m_all, gz_all, g_field, preds, sums):
     nodes = shape[0]
     readf = readout[...].astype(F32)
 
-    def body(blocks):
-        m = messages(table, field, tiles, turned, blocks, shape)
+    def body(blocks, m):
         scatter(m_all, blocks, m, nodes, 0)
         t = jnp.tanh(jnp.dot(m, weight[...], preferred_element_type=F32))
         base = gather(lambda row, col: field[row + 1, at_block(col + 1, nodes)], blocks)
@@ -168,22 +197,13 @@
     return body
 
 
-def back_one(shape, scale, table, field, tiles, turned, weight, readout, goals, preds, m_all, gz_all):
-    nodes = shape[0]
-    readf = readout[...].astype(F32)
-
-    def body(blocks):
-        m = gather(lambda row, col: m_all[row, at_block(col, nodes)], blocks)
-        t = jnp.tanh(jnp.dot(m, weight[...], preferred_element_type=F32))
-        gp = gather(
-            lambda row, col: residual_columns(preds[row, pl.ds(col, 1)], goals[row, pl.ds(col, 1)], scale), blocks
-        )
-        gx = gp * readf + gather(
-            lambda row, col: block_product(table, field, tiles, turned, row, col, shape), blocks
-        )
-        scatter(gz_all, blocks, (gx * (1.0 - t * t)).astype(BF16), nodes, 0)
-
-    return body
+def back_terms(scale, weight, readout, goals, preds, m_all, blocks, nodes):
+    m = gather(lambda row, col: m_all[row, at_block(col, nodes)], blocks)
+    t = jnp.tanh(jnp.dot(m, weight[...], preferred_element_type=F32))
+    gp = gather(
+        lambda row, col: residual_columns(preds[row, pl.ds(col, 1)], goals[row, pl.ds(col, 1)], scale), blocks
+    )
+    return gp * readout[...].astype(F32), 1.0 - t * t
 
 
 def over_nodes(left, right):
@@ -247,16 +267,17 @@
     wait_all(start_all([(own.at[pl.ds(1, own.shape[0] - 2)], middle)], sems))
 
 
-def prepare_kernel(tiles, first, second, plain, turned, first_in, second_in, second_turned, sems):
-    wait_all(start_all([(tiles, plain), (first, first_in), (second, second_in)], sems))
+def prepare_kernel(tiles, first, second, both, first_in, second_in, second_turned, sems):
+    number = tiles.shape[0]
+    wait_all(start_all([(tiles, both.at[pl.ds(0, number)]), (first, first_in), (second, second_in)], sems))
 
     second_turned[...] = second_in[...].T
 
     def one_tile(tile, carry):
-        turned[tile] = plain[tile].T
+        both[number + tile] = both[tile].T
         return carry
 
-    lax.fori_loop(0, tiles.shape[0], one_tile, 0)
+    lax.fori_loop(0, number, one_tile, 0)
 
 
 def pick_kernel(numbers, own, ends, after, outer, inner, sems):
@@ -267,27 +288,23 @@
 
     @pl.when(moved)
     def _():
-        near = pl.multiple_of(jnp.where(half == 0, line, 0), line)
-        far = pl.multiple_of(jnp.where(half == 0, 0, line), line)
-        wait_all(start_all([
-            (ends.at[pl.ds(near, line)], inner.at[whole]),
-            (ends.at[pl.ds(far, line)], outer.at[whole]),
-            (ends.at[pl.ds(2 * line, TAIL)], inner.at[tail]),
-            (ends.at[pl.ds(2 * line, TAIL)], outer.at[tail]),
-        ], sems))
+        outer[tail] = ends[pl.ds(2 * line, TAIL)]
+        inner[tail] = ends[pl.ds(2 * line, TAIL)]
+        outer[whole] = ends[pl.ds(pl.multiple_of(half * line, line), line)]
+        inner[whole] = ends[pl.ds(pl.multiple_of((1 - half) * line, line), line)]
 
     @pl.when(jnp.logical_not(moved))
     def _():
         copies = start_all([
+            (own.at[jnp.where(half == 0, 0, rows - 1)], outer.at[whole]),
             (own.at[jnp.where(half == 0, rows - 1, 0)], inner.at[whole]),
-            (own.at[jnp.where(half == 0, 0, rows - 1)], outer.at[whole]),
         ], sems)
-        inner[line:] = numbers[...]
-        outer[line:] = numbers[...]
+        outer[tail] = numbers[...]
+        inner[tail] = numbers[...]
         wait_all(copies)
 
 
-def first_edge_kernel(shape, numbers, own, ends, middle, outer, inner, side, later, tiles, turned, weight,
+def first_edge_kernel(shape, numbers, own, ends, middle, outer, inner, side, later, tiles, weight,
                       table, field, x_field, m_all, outer_out, inner_out, side_out, own_ids, above_ids, spots, sems):
     nodes, rows, cols = shape
     line = cols * nodes
@@ -314,12 +331,12 @@
     left = side[pl.ds(rows * nodes, TAIL)].astype(F32)[2 * rows : 3 * rows, 0:128]
     north = own_ids[2 * rows : 3 * rows, 0:128]
     lanes = lax.broadcasted_iota(jnp.int32, north.shape, 1)
-    last = jnp.broadcast_to(left[:, cols - 1 : cols], left.shape)
+    beside = jnp.broadcast_to(left[:, cols - 1 : cols], left.shape)
     spots[0 : 2 * rows] = own_ids[0 : 2 * rows, 0:128].astype(jnp.int32)
     spots[WEST * rows : WEST * rows + 1] = above_ids[2 * rows - 1 : 2 * rows, 0:128].astype(jnp.int32)
     spots[WEST * rows + 1 : (WEST + 1) * rows] = own_ids[rows : 2 * rows - 1, 0:128].astype(jnp.int32)
     spots[NORTH * rows : (NORTH + 1) * rows] = north.astype(jnp.int32)
-    spots[SOUTH * rows : (SOUTH + 1) * rows] = jnp.where(lanes == 0, last, pltpu.roll(north, 1, 1)).astype(jnp.int32)
+    spots[SOUTH * rows : (SOUTH + 1) * rows] = jnp.where(lanes == 0, beside, pltpu.roll(north, 1, 1)).astype(jnp.int32)
     copies = start_all([(spots, table)], sems)
 
     @pl.when(moved)
@@ -335,85 +352,74 @@
             field[row + 1, inside] = own[row]
 
     fill_rim(field, outer, inner, side, shape)
+    wait_all(copies)
+    forward_one(shape, table, field, tiles, weight, x_field, m_all)(edge_blocks(shape))
+    take_edges(x_field, outer_out, inner_out, side_out, shape)
+
+
+def middle_compute_kernel(shape, scale, table, field, tiles, weight_one, weight_two, two_turned, readout, spread, target,
+                          target_swap, x_in, m_in, x_field, m_one, m_two, gz_two, g_field, preds, goals, sums, local):
+    _, _, moved = place()
+
+    @pl.when(moved)
+    def _():
+        goals[...] = target_swap[...]
+
+    @pl.when(jnp.logical_not(moved))
+    def _():
+        goals[...] = target[...]
+
     zero_rim(x_field, shape)
-    wait_all(copies)
-    forward_one(shape, table, field, tiles, turned, weight, x_field, m_all)(edge_blocks(shape))
-    take_edges(x_field, outer_out, inner_out, side_out, shape)
-
-
-def middle_compute_kernel(shape, scale, table, field, tiles, turned, weight_one, weight_two, two_turned, readout, spread, target,
-                          target_swap, x_in, m_in, x_field, m_one, m_two, gz_two, g_field, preds, goals, sums):
-    _, _, moved = place()
-
-    @pl.when(moved)
-    def _():
-        goals[...] = target_swap[...]
-
-    @pl.when(jnp.logical_not(moved))
-    def _():
-        goals[...] = target[...]
-
     zero_rim(g_field, shape)
     sums[...] = jnp.zeros_like(sums)
     blocks = inner_blocks(shape)
-    forward_one(shape, table, field, tiles, turned, weight_one, x_field, m_one)(blocks)
+    forward_one(shape, table, field, tiles, weight_one, x_field, m_one)(blocks)
     through_two(
-        shape, scale, table, x_field, tiles, turned, weight_two, two_turned, readout, spread, goals, m_two, gz_two,
+        shape, scale, table, x_field, tiles, weight_two, two_turned, readout, spread, goals, m_two, gz_two,
         g_field, preds, sums,
-    )(blocks)
-
-
-def second_edge_kernel(shape, scale, table, outer, inner, side, tiles, turned, weight, weight_turned, readout, spread, goals,
-                       x_in, m_in, gz_in, g_in, preds_in, sums_in,
-                       x_field, m_two, gz_two, g_field, preds, sums, outer_out, inner_out, side_out):
-    fill_rim(x_field, outer, inner, side, shape)
+    )(blocks, messages(table, x_field, tiles, blocks, shape))
+    local[...] = products(table, x_field, tiles, edge_blocks(shape), shape)
+
+
+def second_edge_kernel(shape, scale, table, outer, inner, side, tiles, weight, weight_turned, readout, spread, goals,
+                       x_field, local, m_in, gz_in, g_in, preds_in, sums_in,
+                       m_two, gz_two, g_field, preds, sums, outer_out, inner_out, side_out):
+    m = (local[...] + rim_terms(table, tiles, outer, inner, side, shape)).astype(BF16)
     through_two(
-        shape, scale, table, x_field, tiles, turned, weight, weight_turned, readout, spread, goals, m_two, gz_two,
+        shape, scale, table, x_field, tiles, weight, weight_turned, readout, spread, goals, m_two, gz_two,
         g_field, preds, sums,
-    )(edge_blocks(shape))
+    )(edge_blocks(shape), m)
     take_edges(g_field, outer_out, inner_out, side_out, shape)
 
 
-def back_inner_kernel(shape, scale, table, g_field, tiles, turned, weight, readout, goals, preds, m_one, m_two, gz_two,
-                      gz_one, first_out, second_out):
+def back_inner_kernel(shape, scale, table, g_field, tiles, weight, readout, goals, preds, m_one, m_two, gz_two,
+                      first_out, second_out, local, slopes):
     nodes, rows, cols = shape
-    _, right, _ = place()
-    back_one(shape, scale, table, g_field, tiles, turned, weight, readout, goals, preds, m_one, gz_one)(
-        inner_blocks(shape)
-    )
-    part = pl.ds(pl.multiple_of(right * nodes, nodes), (cols - 1) * nodes)
-    first_out[...] = jnp.zeros_like(first_out)
+    blocks = inner_blocks(shape)
+    gx, slope = back_terms(scale, weight, readout, goals, preds, m_one, blocks, nodes)
+    gz = ((gx + products(table, g_field, tiles, blocks, shape)) * slope).astype(BF16)
+    first_out[...] = over_nodes(gather(lambda row, col: m_one[row, at_block(col, nodes)], blocks), gz)
+    gx, slope = back_terms(scale, weight, readout, goals, preds, m_one, edge_blocks(shape), nodes)
+    local[...] = gx + products(table, g_field, tiles, edge_blocks(shape), shape)
+    slopes[...] = slope
     second_out[...] = jnp.zeros_like(second_out)
-
-    def one_row(row, carry):
-        first_out[...] += over_nodes(m_one[row, part], gz_one[row, part])
-        return carry
 
     def each_row(row, carry):
         second_out[...] += over_nodes(m_two[row], gz_two[row])
         return carry
 
-    lax.fori_loop(1, rows - 1, one_row, 0)
     lax.fori_loop(0, rows, each_row, 0)
 
 
-def back_edge_kernel(shape, scale, table, outer, inner, side, tiles, turned, weight, readout, goals, preds,
-                     m_one, first_in, second, sums, g_in, gz_in, g_field, gz_one, keep, one, two, three,
-                     first_out, parts):
-    nodes, rows, cols = shape
-    _, right, _ = place()
-    fill_rim(g_field, outer, inner, side, shape)
-    back_one(shape, scale, table, g_field, tiles, turned, weight, readout, goals, preds, m_one, gz_one)(
-        edge_blocks(shape)
-    )
-    first_out[...] = first_in[...]
-    for row in (0, rows - 1):
-        first_out[...] += over_nodes(m_one[row], gz_one[row])
-    beside = at_block(jnp.where(right == 0, cols - 1, 0), nodes)
-    for row in range(1, rows - 1):
-        first_out[...] += over_nodes(m_one[row, beside], gz_one[row, beside])
+def back_edge_kernel(shape, table, outer, inner, side, tiles, preds, m_one, first_in, second, sums, local, slopes,
+                     keep, one, two, three, parts):
+    nodes = shape[0]
+    gx = local[...] + rim_terms(table, tiles, outer, inner, side, shape)
+    gz = (gx * slopes[...]).astype(BF16)
+    m = gather(lambda row, col: m_one[row, at_block(col, nodes)], edge_blocks(shape))
+    first = first_in[...] + over_nodes(m, gz)
     count, size, width = parts.shape
-    parts[:, : size // 2] = first_out[...].reshape(count, size // 2, width)
+    parts[:, : size // 2] = first.reshape(count, size // 2, width)
     parts[:, size // 2 :] = second[...].reshape(count, size // 2, width)
     spread_shares(parts, sums[...], lax.rem(lax.axis_index(AXES), 4), (keep, one, two, three))
     ride_preds(preds, three)
@@ -555,11 +561,11 @@
     )(features, side_s)
     middle = send(middle_s, swap)
     tiles, w_first, w_second, _ = lax.optimization_barrier((tiles, w_first, w_second, middle_s))
-    tiles, turned, w_first, w_second, w_turned = pl.pallas_call(
+    tiles, w_first, w_second, w_turned = pl.pallas_call(
         prepare_kernel,
-        out_shape=(bf(*tiles.shape), bf(*tiles.shape)) + (bf(width, width),) * 3,
+        out_shape=(bf(2 * tiles.shape[0], nodes, nodes),) + (bf(width, width),) * 3,
         in_specs=[ANY] * 3,
-        out_specs=(VMEM,) * 5,
+        out_specs=(VMEM,) * 4,
         scratch_shapes=[sems(3)],
         compiler_params=params,
         name="prepare",
@@ -570,7 +576,7 @@
     outer_s, inner_s = pl.pallas_call(
         pick_kernel,
         out_shape=(bf(line + TAIL, width),) * 2,
-        in_specs=[VMEM, ANY, ANY, ANY],
+        in_specs=[VMEM, ANY, VMEM, ANY],
         out_specs=(VMEM,) * 2,
         scratch_shapes=[sems(4)],
         compiler_params=params,
@@ -599,7 +605,7 @@
     table, f_field, x_field, m_one, outer_s, inner_s, side_s = pl.pallas_call(
         functools.partial(first_edge_kernel, shape),
         out_shape=(jax.ShapeDtypeStruct((5 * rows, 128), jnp.int32), padded, padded, patch) + edge_shapes,
-        in_specs=[VMEM] * 7 + [ANY] + [VMEM] * 3,
+        in_specs=[VMEM] * 7 + [ANY] + [VMEM] * 2,
         out_specs=(SMEM,) + (VMEM,) * 6,
         scratch_shapes=[
             pltpu.VMEM((TAIL, width), F32),
@@ -610,55 +616,55 @@
         compiler_params=params,
         cost_estimate=cost(edge, edge),
         name="first_edge",
-    )(numbers, features, ends, middle, outer, inner, side, goal_swap, tiles, turned, w_first)
+    )(numbers, features, ends, middle, outer, inner, side, goal_swap, tiles, w_first)
 
     outer, inner, side = edges(outer_s, inner_s, side_s)
-    x_field, m_one, m_two, gz_two, g_field, preds, goals, sums = pl.pallas_call(
+    edge_terms = jax.ShapeDtypeStruct((edge * nodes, width), F32)
+    x_field, m_one, m_two, gz_two, g_field, preds, goals, sums, local = pl.pallas_call(
         functools.partial(middle_compute_kernel, shape, scale),
-        out_shape=(padded, patch, patch, patch, padded, goal_shape, goal_shape, sums_shape),
-        in_specs=[SMEM] + [VMEM] * 12,
+        out_shape=(padded, patch, patch, patch, padded, goal_shape, goal_shape, sums_shape, edge_terms),
+        in_specs=[SMEM] + [VMEM] * 11,
+        out_specs=(VMEM,) * 9,
+        input_output_aliases={10: 0, 11: 1},
+        compiler_params=params,
+        cost_estimate=cost(2 * inside + edge, 3 * inside),
+        name="inner_forward",
+    )(table, f_field, tiles, w_first, w_second, w_turned, readout, spread, target, goal_swap, x_field, m_one)
+
+    m_two, gz_two, g_field, preds, sums, outer_s, inner_s, side_s = pl.pallas_call(
+        functools.partial(second_edge_kernel, shape, scale),
+        out_shape=(patch, patch, padded, goal_shape, sums_shape) + edge_shapes,
+        in_specs=[SMEM] + [VMEM] * 16,
         out_specs=(VMEM,) * 8,
-        input_output_aliases={11: 0, 12: 1},
-        compiler_params=params,
-        cost_estimate=cost(2 * inside, 3 * inside),
-        name="inner_forward",
-    )(table, f_field, tiles, turned, w_first, w_second, w_turned, readout, spread, target, goal_swap, x_field, m_one)
-
-    x_field, m_two, gz_two, g_field, preds, sums, outer_s, inner_s, side_s = pl.pallas_call(
-        functools.partial(second_edge_kernel, shape, scale),
-        out_shape=(padded, patch, patch, padded, goal_shape, sums_shape) + edge_shapes,
-        in_specs=[SMEM] + [VMEM] * 16,
-        out_specs=(VMEM,) * 9,
-        input_output_aliases={11 + i: i for i in range(6)},
-        compiler_params=params,
-        cost_estimate=cost(edge, 2 * edge),
+        input_output_aliases={12 + i: i for i in range(5)},
+        compiler_params=params,
+        cost_estimate=cost(edge // 4, 2 * edge),
         name="second_edge",
-    )(table, outer, inner, side, tiles, turned, w_second, w_turned, readout, spread, goals, x_field, m_two, gz_two, g_field, preds, sums)
+    )(table, outer, inner, side, tiles, w_second, w_turned, readout, spread, goals, x_field, local,
+      m_two, gz_two, g_field, preds, sums)
 
     outer, inner, side = edges(outer_s, inner_s, side_s)
-    gz_one, first, second = pl.pallas_call(
+    first, second, local, slopes = pl.pallas_call(
         functools.partial(back_inner_kernel, shape, scale),
-        out_shape=(patch, square, square),
-        in_specs=[SMEM] + [VMEM] * 10,
-        out_specs=(VMEM,) * 3,
-        compiler_params=params,
-        cost_estimate=cost(inside, 2 * inside + rows * cols),
+        out_shape=(square, square, edge_terms, edge_terms),
+        in_specs=[SMEM] + [VMEM] * 9,
+        out_specs=(VMEM,) * 4,
+        compiler_params=params,
+        cost_estimate=cost(rows * cols, 3 * rows * cols),
         name="back_inner",
-    )(table, g_field, tiles, turned, w_first, readout, goals, preds, m_one, m_two, gz_two)
+    )(table, g_field, tiles, w_first, readout, goals, preds, m_one, m_two, gz_two)
 
     share = width // count
-    _, _, *outs = pl.pallas_call(
-        functools.partial(back_edge_kernel, shape, scale),
-        out_shape=(padded, patch) + shares_shape(count // 4, 2 * share, width, step * nodes // width),
-        in_specs=[SMEM] + [VMEM] * 15,
-        out_specs=(VMEM,) * 6,
-        input_output_aliases={14: 0, 15: 1},
-        scratch_shapes=[pltpu.VMEM((width, width), F32), pltpu.VMEM((count, 2 * share, width), F32)],
-        compiler_params=params,
-        cost_estimate=cost(edge, 2 * edge),
+    outs = pl.pallas_call(
+        functools.partial(back_edge_kernel, shape),
+        out_shape=shares_shape(count // 4, 2 * share, width, step * nodes // width),
+        in_specs=[SMEM] + [VMEM] * 11,
+        out_specs=(VMEM,) * 4,
+        scratch_shapes=[pltpu.VMEM((count, 2 * share, width), F32)],
+        compiler_params=params,
+        cost_estimate=cost(edge // 4, edge),
         name="back_edge",
-    )(table, outer, inner, side, tiles, turned, w_first, readout, goals, preds, m_one, first, second, sums,
-      g_field, gz_one)
+    )(table, outer, inner, side, tiles, preds, m_one, first, second, sums, local, slopes)
     first, second, extra, pred_out = sum_shares(outs, preds, count, share, width, params)
     return pred_out, first, second, extra[0]
 

time: 88.7 us -> 86.4 us (0.974)
  waiting for transfers between devices: 22.6 us -> 20.7 us
    ppermute x12, waiting for transfers between devices: 11.5 us -> 9.66 us  [send(): return lax.ppermute(value, AXES, way)]
    pallas_call x2, Pallas kernels: 5.17 us -> 3.55 us  [the longest x1 1.93 us: per_device(): pl.pallas_call(functools.partial(back_edge_kernel, shape), out_shape=shar...]
    pallas_call x1, Pallas kernels: 4.31 us -> 5.46 us  [per_device(): pl.pallas_call(functools.partial(middle_compute_kernel, shape, scale), ou...]
  transfers between devices with their start and end apart: 18 -> 18, of which waited for: 7 -> 7; matrix products, arithmetic and copies ran while one was open for 0% -> 0% of each run, Pallas kernels for 12% -> 14%
where the time goes in v7:
time: 86.4 us; the launch traced here: 86.1 us
  starting transfers between devices  40.3 us (47%)
  Pallas kernels  21.5 us (25%)
  waiting for transfers between devices  20.7 us (24%)
  local copies, waits for them, and re-layouts  2.63 us (3%)
  between operations  0.87 us (1%)
    ppermute x12, starting transfers between devices, send(): return lax.ppermute(value, AXES, way)  33.7 us
    ppermute x6, waiting for transfers between devices, sum_shares(): lax.ppermute(outs[k], AXES, [(i, i ^ k * base) for i in range(count)])  11.1 us
    ppermute x12, waiting for transfers between devices, send(): return lax.ppermute(value, AXES, way)  9.66 us
    ppermute x6, starting transfers between devices, sum_shares(): lax.ppermute(outs[k], AXES, [(i, i ^ k * base) for i in range(count)])  6.59 us
    pallas_call x1, Pallas kernels, per_device(): pl.pallas_call(functools.partial(middle_compute_kernel, shape, scale), ou...  5.46 us
    pallas_call x1, Pallas kernels, per_device(): pl.pallas_call(functools.partial(back_inner_kernel, shape, scale), out_sh...  4.84 us
    pallas_call x1, Pallas kernels, per_device(): pl.pallas_call(functools.partial(second_edge_kernel, shape, scale), out_s...  2.97 us
    pallas_call x1, Pallas kernels, per_device(): pl.pallas_call(functools.partial(first_edge_kernel, shape), out_shape=(ja...  2.78 us
  transfers between devices with their start and end apart: 18, of which 7 were waited for; matrix products, arithmetic and copies ran while one was open for 0% of the time, Pallas kernels for 14%

profile of v7, /device:TPU:0, one launch (start us, length us, event | category | flops | bytes accessed | tf_op | source)
XLA Modules:
  0.0 86.1 jit_solution(10857935438458437646)
XLA Ops:
  0.6 1.6 %copy-done = bf16[4,8,128,256]{3,2,1,0:T(8,128)(2,1)S(1)} copy-done((bf16[4,8,128,256]{3,2,1,0:T(8,128)(2,1)S(1)}, bf16[4,8,128,256]{3,2,1,0:T(8,128)(2,1)}, u32[]{:S(2)}) %copy-start) | copy-done | bytes 2097176
  2.2 0.7 copy-done.6
  3.4 0.9 collective-permute-start
  4.6 0.9 collective-permute-start.1
  5.5 6.9 %collective-permute-start.2 = (bf16[528,256]{1,0:T(8,128)(2,1)S(1)}, bf16[528,256]{1,0:T(8,128)(2,1)S(1)}, u32[]{:S(2)}, u32[]{:S(2)}) collective-permute-start(bf16[528,256]{1,0:T(8,128)(2,1)S(1)} %get-tuple-element.59.after), channel_id=1, source_target_pairs={{1,0},{3,1},{0,2},{2,3},{5,4},{7,5},{4,6},{6,7},{9,8},{11,9},{8,10... | collective-permute-start | bytes 811016 | tf_op jit(solution)/shard_map/ppermute | solution.py:530
  12.4 6.9 %collective-permute-done.2.after.side = bf16[528,256]{1,0:T(8,128)(2,1)S(1)} collective-permute-done((bf16[528,256]{1,0:T(8,128)(2,1)S(1)}, bf16[528,256]{1,0:T(8,128)(2,1)S(1)}, u32[]{:S(2)}, u32[]{:S(2)}) %collective-permute-start.2) | collective-permute-done | bytes 270368 | tf_op jit(solution)/shard_map/ppermute | solution.py:530
  19.5 0.7 collective-permute-start.3
  20.2 6.0 %collective-permute-start.4 = (bf16[1040,256]{1,0:T(8,128)(2,1)S(1)}, bf16[1040,256]{1,0:T(8,128)(2,1)S(1)}, u32[]{:S(2)}, u32[]{:S(2)}) collective-permute-start(bf16[1040,256]{1,0:T(8,128)(2,1)S(1)} %get-tuple-element.61), channel_id=1, source_target_pairs={{1,0},{0,1},{3,2},{2,3},{5,4},{4,5},{7,6},{6,7},{9,8},{8,9},{11,10... | collective-permute-start | bytes 1597448 | tf_op jit(solution)/shard_map/ppermute | solution.py:530
  26.1 0.7 collective-permute-start.5
  26.8 1.6 %prepare.1 = (bf16[32,128,128]{2,1,0:T(8,128)(2,1)S(1)}, bf16[256,256]{1,0:T(8,128)(2,1)S(1)}, bf16[256,256]{1,0:T(8,128)(2,1)S(1)}, bf16[256,256]{1,0:T(8,128)(2,1)S(1)}) custom-call(bf16[16,128,128]{2,1,0:T(8,128)(2,1)S(1)} %copy-done.2, bf16[256,256]{1,0:T(8,128)(2,1)S(1)} %copy-done.3, bf16[256,256]{1,0:T(8,128)(2,1)S(1)} %copy-done.4), custom_call_target="tpu_custom_call" | custom-call | tf_op jit(solution)/shard_map/prepare/pallas_call | solution.py:564
  28.5 2.8 %first_edge.1 = (s32[20,128]{1,0:T(8,128)S(1)}, bf16[6,1280,256]{2,1,0:T(8,128)(2,1)S(1)}, bf16[6,1280,256]{2,1,0:T(8,128)(2,1)S(1)}, bf16[4,1024,256]{2,1,0:T(8...) custom-call(bf16[16,256]{1,0:T(8,128)(2,1)S(1)} %get-tuple-element.57.num, ...), custom_call_target="tpu_custom_call" | custom-call | flops 1207959552 | bytes 4718592 | tf_op jit(solution)/shard_map/first_edge/pallas_call | solution.py:605
  31.3 0.7 collective-permute-start.6
  32.0 8.2 %collective-permute-start.7 = (bf16[1024,256]{1,0:T(8,128)(2,1)S(1)}, bf16[1024,256]{1,0:T(8,128)(2,1)S(1)}, u32[]{:S(2)}, u32[]{:S(2)}) collective-permute-start(bf16[1024,256]{1,0:T(8,128)(2,1)S(1)} %get-tuple-element.70), channel_id=1, source_target_pairs={{1,0},{0,1},{3,2},{2,3},{5,4},{4,5},{7,6},{6,7},{9,8},{8,9},{11,10... | collective-permute-start | bytes 1572872 | tf_op jit(solution)/shard_map/ppermute | solution.py:530
  40.2 3.3 %collective-permute-start.8 = (bf16[512,256]{1,0:T(8,128)(2,1)S(1)}, bf16[512,256]{1,0:T(8,128)(2,1)S(1)}, u32[]{:S(2)}, u32[]{:S(2)}) collective-permute-start(bf16[512,256]{1,0:T(8,128)(2,1)S(1)} %get-tuple-element.71), channel_id=1, source_target_pairs={{2,0},{3,1},{0,2},{1,3},{6,4},{7,5},{4,6},{5,7},{10,8},{11,9},{8,1... | collective-permute-start | bytes 786440 | tf_op jit(solution)/shard_map/ppermute | solution.py:530
  43.6 5.5 %inner_forward.1 = (bf16[6,1280,256]{2,1,0:T(8,128)(2,1)S(1)}, bf16[4,1024,256]{2,1,0:T(8,128)(2,1)S(1)}, bf16[4,1024,256]{2,1,0:T(8,128)(2,1)S(1)}, bf16[4,1024...) custom-call(s32[20,128]{1,0:T(8,128)S(1)} %get-tuple-element.68.tabl, ...), custom_call_target="tpu_custom_call", output_to_operand_aliasing={{0}: (10, {}), {1}: (11, {})} | custom-call | flops 3019898880 | bytes 11534336 | tf_op jit(solution)/shard_map/inner_forward/pallas_call | solution.py:623
  49.1 1.0 %collective-permute-done.8.side = bf16[512,256]{1,0:T(8,128)(2,1)S(1)} collective-permute-done((bf16[512,256]{1,0:T(8,128)(2,1)S(1)}, bf16[512,256]{1,0:T(8,128)(2,1)S(1)}, u32[]{:S(2)}, u32[]{:S(2)}) %collective-permute-start.8) | collective-permute-done | bytes 262176 | tf_op jit(solution)/shard_map/ppermute | solution.py:530
  50.1 3.0 %second_edge.1 = (bf16[4,1024,256]{2,1,0:T(8,128)(2,1)S(1)}, bf16[4,1024,256]{2,1,0:T(8,128)(2,1)S(1)}, bf16[6,1280,256]{2,1,0:T(8,128)(2,1)S(1)}, f32[4,8,128]{...) custom-call(s32[20,128]{1,0:T(8,128)S(1)} %get-tuple-element.68.tabl, ...), custom_call_target="tpu_custom_call", output_to_operand_aliasing={{0}: (12, {}), {1}: (13, {}), {2}: (14, {}), {3}: (15, {}),... | custom-call | flops 805306368 | bytes 5242880 | tf_op jit(solution)/shard_map/second_edge/pallas_call | solution.py:634
  53.0 0.9 %collective-permute-start.9 = (bf16[1024,256]{1,0:T(8,128)(2,1)S(1)}, bf16[1024,256]{1,0:T(8,128)(2,1)S(1)}, u32[]{:S(2)}, u32[]{:S(2)}) collective-permute-start(bf16[1024,256]{1,0:T(8,128)(2,1)S(1)} %get-tuple-element.85), channel_id=1, source_target_pairs={{1,4},{3,6},{5,8},{7,10},{9,12},{11,14},{4,1},{6,3},{8,5},{10,7},{... | collective-permute-start | bytes 1572872 | tf_op jit(solution)/shard_map/ppermute | solution.py:530
  53.9 3.0 %collective-permute-start.10 = (bf16[1024,256]{1,0:T(8,128)(2,1)S(1)}, bf16[1024,256]{1,0:T(8,128)(2,1)S(1)}, u32[]{:S(2)}, u32[]{:S(2)}) collective-permute-start(bf16[1024,256]{1,0:T(8,128)(2,1)S(1)} %get-tuple-element.86), channel_id=1, source_target_pairs={{1,0},{0,1},{3,2},{2,3},{5,4},{4,5},{7,6},{6,7},{9,8},{8,9},{11,10... | collective-permute-start | bytes 1572872 | tf_op jit(solution)/shard_map/ppermute | solution.py:530
  56.9 1.7 %collective-permute-start.11 = (bf16[512,256]{1,0:T(8,128)(2,1)S(1)}, bf16[512,256]{1,0:T(8,128)(2,1)S(1)}, u32[]{:S(2)}, u32[]{:S(2)}) collective-permute-start(bf16[512,256]{1,0:T(8,128)(2,1)S(1)} %get-tuple-element.87), channel_id=1, source_target_pairs={{2,0},{3,1},{0,2},{1,3},{6,4},{7,5},{4,6},{5,7},{10,8},{11,9},{8,1... | collective-permute-start | bytes 786440 | tf_op jit(solution)/shard_map/ppermute | solution.py:530
  58.6 4.8 %back_inner.1 = (f32[256,256]{1,0:T(8,128)S(1)}, f32[256,256]{1,0:T(8,128)S(1)}, f32[2304,256]{1,0:T(8,128)S(1)}, f32[2304,256]{1,0:T(8,128)S(1)}) custom-call(s32[20,128]{1,0:T(8,128)S(1)} %get-tuple-element.68.table, bf16[6,1280,256]{2,1,0:T(8,128)(2,1)S(1)} %get-tuple-element.90.g_field, bf16[32,128,128]{2,1,0:T(8,128)(2,1)S(1)} %get-tuple-element.66.tiles, ...), custom_call_target="tpu_custom_call" | custom-call | flops 3221225472 | bytes 16777216 | tf_op jit(solution)/shard_map/back_inner/pallas_call | solution.py:647
  63.5 1.7 %collective-permute-done.11.side = bf16[512,256]{1,0:T(8,128)(2,1)S(1)} collective-permute-done((bf16[512,256]{1,0:T(8,128)(2,1)S(1)}, bf16[512,256]{1,0:T(8,128)(2,1)S(1)}, u32[]{:S(2)}, u32[]{:S(2)}) %collective-permute-start.11) | collective-permute-done | bytes 262176 | tf_op jit(solution)/shard_map/ppermute | solution.py:530
  65.2 1.9 %back_edge.1 = (f32[136,256]{1,0:T(8,128)S(1)}, f32[136,256]{1,0:T(8,128)S(1)}, f32[136,256]{1,0:T(8,128)S(1)}, f32[152,256]{1,0:T(8,128)S(1)}) custom-call(s32[20,128]{1,0:T(8,128)S(1)} %get-tuple-element.68.table, bf16[1024,256]{1,0:T(8,128)(2,1)S(1)} %collective-permute-done.9.outer, bf16[1024,256]{1,0:T(8,128)(2,1)S(1)} %collective-permute-done.10.inner, ...), custom_call_target="tpu_custom_call" | custom-call | flops 503316480 | bytes 2883584 | tf_op jit(solution)/shard_map/back_edge/pallas_call | solution.py:658
  67.1 0.6 collective-permute-start.14
  67.8 1.3 %collective-permute-start.12 = (f32[136,256]{1,0:T(8,128)S(1)}, f32[136,256]{1,0:T(8,128)S(1)}, u32[]{:S(2)}, u32[]{:S(2)}) collective-permute-start(f32[136,256]{1,0:T(8,128)S(1)} %get-tuple-element.99), channel_id=1, source_target_pairs={{0,1},{1,0},{2,3},{3,2},{4,5},{5,4},{6,7},{7,6},{8,9},{9,8},{10,11... | collective-permute-start | bytes 417800 | tf_op jit(solution)/shard_map/ppermute | solution.py:488
  69.3 0.7 collective-permute-done.12.one
  70.0 6.5 %collective-permute-done.13.two = f32[136,256]{1,0:T(8,128)S(1)} collective-permute-done((f32[136,256]{1,0:T(8,128)S(1)}, f32[136,256]{1,0:T(8,128)S(1)}, u32[]{:S(2)}, u32[]{:S(2)}) %collective-permute-start.13) | collective-permute-done | bytes 139296 | tf_op jit(solution)/shard_map/ppermute | solution.py:488
  77.1 1.6 %collective-permute-start.15 = (f32[40,256]{1,0:T(8,128)S(1)}, f32[40,256]{1,0:T(8,128)S(1)}, u32[]{:S(2)}, u32[]{:S(2)}) collective-permute-start(f32[40,256]{1,0:T(8,128)S(1)} %get-tuple-element.104), channel_id=1, source_target_pairs={{0,4},{1,5},{2,6},{3,7},{4,0},{5,1},{6,2},{7,3},{8,12},{9,13},{10,... | collective-permute-start | bytes 122888 | tf_op jit(solution)/shard_map/ppermute | solution.py:488
  78.7 0.9 %collective-permute-start.16 = (f32[40,256]{1,0:T(8,128)S(1)}, f32[40,256]{1,0:T(8,128)S(1)}, u32[]{:S(2)}, u32[]{:S(2)}) collective-permute-start(f32[40,256]{1,0:T(8,128)S(1)} %get-tuple-element.105), channel_id=1, source_target_pairs={{0,8},{1,9},{2,10},{3,11},{4,12},{5,13},{6,14},{7,15},{8,0},{9,1},... | collective-permute-start | bytes 122888 | tf_op jit(solution)/shard_map/ppermute | solution.py:488
  79.6 1.9 %collective-permute-start.17 = (f32[40,256]{1,0:T(8,128)S(1)}, f32[40,256]{1,0:T(8,128)S(1)}, u32[]{:S(2)}, u32[]{:S(2)}) collective-permute-start(f32[40,256]{1,0:T(8,128)S(1)} %get-tuple-element.106), channel_id=1, source_target_pairs={{0,12},{1,13},{2,14},{3,15},{4,8},{5,9},{6,10},{7,11},{8,4},{9,5},... | collective-permute-start | bytes 122888 | tf_op jit(solution)/shard_map/ppermute | solution.py:488
  81.5 2.9 %collective-permute-done.16.two = f32[40,256]{1,0:T(8,128)S(1)} collective-permute-done((f32[40,256]{1,0:T(8,128)S(1)}, f32[40,256]{1,0:T(8,128)S(1)}, u32[]{:S(2)}, u32[]{:S(2)}) %collective-permute-start.16) | collective-permute-done | bytes 40992 | tf_op jit(solution)/shard_map/ppermute | solution.py:488
  84.4 1.1 %collective-permute-done.17.three = f32[40,256]{1,0:T(8,128)S(1)} collective-permute-done((f32[40,256]{1,0:T(8,128)S(1)}, f32[40,256]{1,0:T(8,128)S(1)}, u32[]{:S(2)}, u32[]{:S(2)}) %collective-permute-start.17) | collective-permute-done | bytes 40992 | tf_op jit(solution)/shard_map/ppermute | solution.py:488
  (33 shorter events, 2.6 us)
Async XLA Ops:
  0.6 1.6 %copy-start = (bf16[4,8,128,256]{3,2,1,0:T(8,128)(2,1)S(1)}, bf16[4,8,128,256]{3,2,1,0:T(8,128)(2,1)}, u32[]{:S(2)}) copy-start(bf16[4,8,128,256]{3,2,1,0:T(8,128)(2,1)} %param.7) | copy-start | bytes 6291460
  2.2 0.7 copy-start.6
  2.9 1.6 %copy-start.1 = (bf16[4,8,128,256]{3,2,1,0:T(8,128)(2,1)S(1)}, bf16[4,8,128,256]{3,2,1,0:T(8,128)(2,1)}, u32[]{:S(2)}) copy-start(bf16[4,8,128,256]{3,2,1,0:T(8,128)(2,1)} %param.7) | copy-start | bytes 6291460
  3.4 15.9 %collective-permute-start = (bf16[2064,256]{1,0:T(8,128)(2,1)S(1)}, bf16[2064,256]{1,0:T(8,128)(2,1)S(1)}, u32[]{:S(2)}, u32[]{:S(2)}) collective-permute-start(bf16[2064,256]{1,0:T(8,128)(2,1)S(1)} %get-tuple-element.58), channel_id=1, source_target_pairs={{2,1},{1,2},{6,5},{5,6},{10,9},{9,10},{14,13},{13,14},{18,17},{17,... | collective-permute-start | bytes 3170312 | tf_op jit(solution)/shard_map/ppermute | solution.py:530
  4.6 21.5 %copy-start.5 = (f32[4,8,128]{2,1,0:T(8,128)S(1)}, f32[4,8,128]{2,1,0:T(8,128)}, u32[]{:S(2)}) copy-start(f32[4,8,128]{2,1,0:T(8,128)} %target.1) | copy-start | bytes 49156
  4.6 22.2 %copy-start.2 = (bf16[16,128,128]{2,1,0:T(8,128)(2,1)S(1)}, bf16[16,128,128]{2,1,0:T(8,128)(2,1)}, u32[]{:S(2)}) copy-start(bf16[16,128,128]{2,1,0:T(8,128)(2,1)} %tiles) | copy-start | bytes 1572868
  4.6 22.2 %copy-start.3 = (bf16[256,256]{1,0:T(8,128)(2,1)S(1)}, bf16[256,256]{1,0:T(8,128)(2,1)}, u32[]{:S(2)}) copy-start(bf16[256,256]{1,0:T(8,128)(2,1)} %first) | copy-start | bytes 393220
  4.6 22.2 %copy-start.4 = (bf16[256,256]{1,0:T(8,128)(2,1)S(1)}, bf16[256,256]{1,0:T(8,128)(2,1)}, u32[]{:S(2)}) copy-start(bf16[256,256]{1,0:T(8,128)(2,1)} %second) | copy-start | bytes 393220
  4.6 23.8 %collective-permute-start.1 = (bf16[2,1024,256]{2,1,0:T(8,128)(2,1)S(1)}, bf16[2,1024,256]{2,1,0:T(8,128)(2,1)S(1)}, u32[]{:S(2)}, u32[]{:S(2)}) collective-permute-start(bf16[2,1024,256]{2,1,0:T(8,128)(2,1)S(1)} %pack_middle.1), channel_id=1, source_target_pairs={{2,1},{1,2},{6,5},{5,6},{10,9},{9,10},{14,13},{13,14},{18,17},{17,... | collective-permute-start | bytes 3145736 | tf_op jit(solution)/shard_map/ppermute | solution.py:530
  5.5 13.8 %collective-permute-start.2 = (bf16[528,256]{1,0:T(8,128)(2,1)S(1)}, bf16[528,256]{1,0:T(8,128)(2,1)S(1)}, u32[]{:S(2)}, u32[]{:S(2)}) collective-permute-start(bf16[528,256]{1,0:T(8,128)(2,1)S(1)} %get-tuple-element.59.after), channel_id=1, source_target_pairs={{1,0},{3,1},{0,2},{2,3},{5,4},{7,5},{4,6},{6,7},{9,8},{11,9},{8,10... | collective-permute-start | bytes 811016 | tf_op jit(solution)/shard_map/ppermute | solution.py:530
  19.5 9.0 %collective-permute-start.3 = (bf16[1040,256]{1,0:T(8,128)(2,1)S(1)}, bf16[1040,256]{1,0:T(8,128)(2,1)S(1)}, u32[]{:S(2)}, u32[]{:S(2)}) collective-permute-start(bf16[1040,256]{1,0:T(8,128)(2,1)S(1)} %get-tuple-element.60), channel_id=1, source_target_pairs={{1,4},{3,6},{5,8},{7,10},{9,12},{11,14},{4,1},{6,3},{8,5},{10,7},{... | collective-permute-start | bytes 1597448 | tf_op jit(solution)/shard_map/ppermute | solution.py:530
  20.2 8.3 %collective-permute-start.4 = (bf16[1040,256]{1,0:T(8,128)(2,1)S(1)}, bf16[1040,256]{1,0:T(8,128)(2,1)S(1)}, u32[]{:S(2)}, u32[]{:S(2)}) collective-permute-start(bf16[1040,256]{1,0:T(8,128)(2,1)S(1)} %get-tuple-element.61), channel_id=1, source_target_pairs={{1,0},{0,1},{3,2},{2,3},{5,4},{4,5},{7,6},{6,7},{9,8},{8,9},{11,10... | collective-permute-start | bytes 1597448 | tf_op jit(solution)/shard_map/ppermute | solution.py:530
  26.1 2.3 %collective-permute-start.5 = (f32[4,8,128]{2,1,0:T(8,128)S(1)}, f32[4,8,128]{2,1,0:T(8,128)S(1)}, u32[]{:S(2)}, u32[]{:S(2)}) collective-permute-start(f32[4,8,128]{2,1,0:T(8,128)S(1)} %copy-done.5), channel_id=1, source_target_pairs={{2,1},{1,2},{6,5},{5,6},{10,9},{9,10},{14,13},{13,14},{18,17},{17,... | collective-permute-start | bytes 49160 | tf_op jit(solution)/shard_map/ppermute | solution.py:530
  28.5 11.7 %copy-start.7 = (bf16[256]{0:T(256)(128)(2,1)S(1)}, bf16[256]{0:T(256)(128)(2,1)}, u32[]{:S(2)}) copy-start(bf16[256]{0:T(256)(128)(2,1)} %param.12) | copy-start | bytes 1540
  31.3 18.8 %collective-permute-start.6 = (bf16[1024,256]{1,0:T(8,128)(2,1)S(1)}, bf16[1024,256]{1,0:T(8,128)(2,1)S(1)}, u32[]{:S(2)}, u32[]{:S(2)}) collective-permute-start(bf16[1024,256]{1,0:T(8,128)(2,1)S(1)} %get-tuple-element.69), channel_id=1, source_target_pairs={{1,4},{3,6},{5,8},{7,10},{9,12},{11,14},{4,1},{6,3},{8,5},{10,7},{... | collective-permute-start | bytes 1572872 | tf_op jit(solution)/shard_map/ppermute | solution.py:530
  32.0 18.1 %collective-permute-start.7 = (bf16[1024,256]{1,0:T(8,128)(2,1)S(1)}, bf16[1024,256]{1,0:T(8,128)(2,1)S(1)}, u32[]{:S(2)}, u32[]{:S(2)}) collective-permute-start(bf16[1024,256]{1,0:T(8,128)(2,1)S(1)} %get-tuple-element.70), channel_id=1, source_target_pairs={{1,0},{0,1},{3,2},{2,3},{5,4},{4,5},{7,6},{6,7},{9,8},{8,9},{11,10... | collective-permute-start | bytes 1572872 | tf_op jit(solution)/shard_map/ppermute | solution.py:530
  40.2 9.9 %collective-permute-start.8 = (bf16[512,256]{1,0:T(8,128)(2,1)S(1)}, bf16[512,256]{1,0:T(8,128)(2,1)S(1)}, u32[]{:S(2)}, u32[]{:S(2)}) collective-permute-start(bf16[512,256]{1,0:T(8,128)(2,1)S(1)} %get-tuple-element.71), channel_id=1, source_target_pairs={{2,0},{3,1},{0,2},{1,3},{6,4},{7,5},{4,6},{5,7},{10,8},{11,9},{8,1... | collective-permute-start | bytes 786440 | tf_op jit(solution)/shard_map/ppermute | solution.py:530
  53.0 12.1 %collective-permute-start.9 = (bf16[1024,256]{1,0:T(8,128)(2,1)S(1)}, bf16[1024,256]{1,0:T(8,128)(2,1)S(1)}, u32[]{:S(2)}, u32[]{:S(2)}) collective-permute-start(bf16[1024,256]{1,0:T(8,128)(2,1)S(1)} %get-tuple-element.85), channel_id=1, source_target_pairs={{1,4},{3,6},{5,8},{7,10},{9,12},{11,14},{4,1},{6,3},{8,5},{10,7},{... | collective-permute-start | bytes 1572872 | tf_op jit(solution)/shard_map/ppermute | solution.py:530
  53.9 11.3 %collective-permute-start.10 = (bf16[1024,256]{1,0:T(8,128)(2,1)S(1)}, bf16[1024,256]{1,0:T(8,128)(2,1)S(1)}, u32[]{:S(2)}, u32[]{:S(2)}) collective-permute-start(bf16[1024,256]{1,0:T(8,128)(2,1)S(1)} %get-tuple-element.86), channel_id=1, source_target_pairs={{1,0},{0,1},{3,2},{2,3},{5,4},{4,5},{7,6},{6,7},{9,8},{8,9},{11,10... | collective-permute-start | bytes 1572872 | tf_op jit(solution)/shard_map/ppermute | solution.py:530
  56.9 8.3 %collective-permute-start.11 = (bf16[512,256]{1,0:T(8,128)(2,1)S(1)}, bf16[512,256]{1,0:T(8,128)(2,1)S(1)}, u32[]{:S(2)}, u32[]{:S(2)}) collective-permute-start(bf16[512,256]{1,0:T(8,128)(2,1)S(1)} %get-tuple-element.87), channel_id=1, source_target_pairs={{2,0},{3,1},{0,2},{1,3},{6,4},{7,5},{4,6},{5,7},{10,8},{11,9},{8,1... | collective-permute-start | bytes 786440 | tf_op jit(solution)/shard_map/ppermute | solution.py:530
  67.1 9.4 %collective-permute-start.14 = (f32[152,256]{1,0:T(8,128)S(1)}, f32[152,256]{1,0:T(8,128)S(1)}, u32[]{:S(2)}, u32[]{:S(2)}) collective-permute-start(f32[152,256]{1,0:T(8,128)S(1)} %get-tuple-element.101), channel_id=1, source_target_pairs={{0,3},{1,2},{2,1},{3,0},{4,7},{5,6},{6,5},{7,4},{8,11},{9,10},{10,... | collective-permute-start | bytes 466952 | tf_op jit(solution)/shard_map/ppermute | solution.py:488
  67.8 2.3 %collective-permute-start.12 = (f32[136,256]{1,0:T(8,128)S(1)}, f32[136,256]{1,0:T(8,128)S(1)}, u32[]{:S(2)}, u32[]{:S(2)}) collective-permute-start(f32[136,256]{1,0:T(8,128)S(1)} %get-tuple-element.99), channel_id=1, source_target_pairs={{0,1},{1,0},{2,3},{3,2},{4,5},{5,4},{6,7},{7,6},{8,9},{9,8},{10,11... | collective-permute-start | bytes 417800 | tf_op jit(solution)/shard_map/ppermute | solution.py:488
  69.0 7.4 %collective-permute-start.13 = (f32[136,256]{1,0:T(8,128)S(1)}, f32[136,256]{1,0:T(8,128)S(1)}, u32[]{:S(2)}, u32[]{:S(2)}) collective-permute-start(f32[136,256]{1,0:T(8,128)S(1)} %get-tuple-element.100), channel_id=1, source_target_pairs={{0,2},{1,3},{2,0},{3,1},{4,6},{5,7},{6,4},{7,5},{8,10},{9,11},{10,... | collective-permute-start | bytes 417800 | tf_op jit(solution)/shard_map/ppermute | solution.py:488
  77.1 4.4 %collective-permute-start.15 = (f32[40,256]{1,0:T(8,128)S(1)}, f32[40,256]{1,0:T(8,128)S(1)}, u32[]{:S(2)}, u32[]{:S(2)}) collective-permute-start(f32[40,256]{1,0:T(8,128)S(1)} %get-tuple-element.104), channel_id=1, source_target_pairs={{0,4},{1,5},{2,6},{3,7},{4,0},{5,1},{6,2},{7,3},{8,12},{9,13},{10,... | collective-permute-start | bytes 122888 | tf_op jit(solution)/shard_map/ppermute | solution.py:488
  78.7 5.7 %collective-permute-start.16 = (f32[40,256]{1,0:T(8,128)S(1)}, f32[40,256]{1,0:T(8,128)S(1)}, u32[]{:S(2)}, u32[]{:S(2)}) collective-permute-start(f32[40,256]{1,0:T(8,128)S(1)} %get-tuple-element.105), channel_id=1, source_target_pairs={{0,8},{1,9},{2,10},{3,11},{4,12},{5,13},{6,14},{7,15},{8,0},{9,1},... | collective-permute-start | bytes 122888 | tf_op jit(solution)/shard_map/ppermute | solution.py:488
  79.6 5.8 %collective-permute-start.17 = (f32[40,256]{1,0:T(8,128)S(1)}, f32[40,256]{1,0:T(8,128)S(1)}, u32[]{:S(2)}, u32[]{:S(2)}) collective-permute-start(f32[40,256]{1,0:T(8,128)S(1)} %get-tuple-element.106), channel_id=1, source_target_pairs={{0,12},{1,13},{2,14},{3,15},{4,8},{5,9},{6,10},{7,11},{8,4},{9,5},... | collective-permute-start | bytes 122888 | tf_op jit(solution)/shard_map/ppermute | solution.py:488

commit v8 on v7

--- a/solution.py
+++ b/solution.py
@@ -412,7 +412,7 @@
 
 
 def back_edge_kernel(shape, table, outer, inner, side, tiles, preds, m_one, first_in, second, sums, local, slopes,
-                     keep, one, two, three, parts):
+                     keep, one, parts):
     nodes = shape[0]
     gx = local[...] + rim_terms(table, tiles, outer, inner, side, shape)
     gz = (gx * slopes[...]).astype(BF16)
@@ -421,16 +421,17 @@
     count, size, width = parts.shape
     parts[:, : size // 2] = first.reshape(count, size // 2, width)
     parts[:, size // 2 :] = second[...].reshape(count, size // 2, width)
-    spread_shares(parts, sums[...], lax.rem(lax.axis_index(AXES), 4), (keep, one, two, three))
-    ride_preds(preds, three)
+    spread_shares(parts, sums[...], lax.axis_index("narrow"), (keep, one))
+    ride_preds(preds, one)
 
 
 def spread_shares(parts, extra, digit, outs):
-    size = parts.shape[1]
+    size, radix = parts.shape[1], len(outs)
+    groups = parts.shape[0] // radix
     for k, out in enumerate(outs):
-        for group in range(parts.shape[0] // 4):
-            out[group * size : (group + 1) * size] = parts[4 * group + jnp.bitwise_xor(digit, k)]
-        out[parts.shape[0] // 4 * size : parts.shape[0] // 4 * size + 8] = extra
+        for group in range(groups):
+            out[group * size : (group + 1) * size] = parts[radix * group + jnp.bitwise_xor(digit, k)]
+        out[groups * size : groups * size + 8] = extra
 
 
 def take_preds(preds, riding, pred_out):
@@ -457,59 +458,73 @@
         riding[at : at + preds.shape[1], lane : lane + preds.shape[2]] = preds[row]
 
 
-def fold_kernel(base, keep, one, two, three, preds, *refs):
-    digit = lax.rem(lax.axis_index(AXES) // base, 4)
-    *outs, parts = refs
-    if base == 4:
-        take_preds(preds, three, outs.pop())
-    count, size, width = parts.shape
-    total = keep[...] + one[...] + two[...] + three[: keep.shape[0]]
-    parts[...] = total[: count * size].reshape(count, size, width)
-    spread_shares(parts, total[count * size :], digit, outs)
-
-
-def last_fold_kernel(keep, one, two, three, first, second, readout):
+def fold_kernel(base, step, radix, keep, *refs):
+    *got, preds = refs[: -1 - radix - (step == 2)]
+    outs, parts = list(refs[len(got) + 1 : -1]), refs[-1]
+    if step == 2:
+        take_preds(preds, got[0], outs.pop())
+    count, size, _ = parts.shape
+    total = keep[...]
+    for one in got:
+        total = total + one[: keep.shape[0]]
+    parts[...] = total[: count * size].reshape(parts.shape)
+    spread_shares(parts, total[count * size :], lax.rem(lax.axis_index(AXES) // base, radix), outs)
+    if step == 1:
+        riding = got[0].shape[0] - keep.shape[0]
+        outs[1][outs[1].shape[0] - riding :] = got[0][keep.shape[0] :]
+
+
+def last_fold_kernel(keep, *refs):
+    *got, first, second, readout = refs
     share = first.shape[0]
-    total = keep[...] + one[...] + two[...] + three[...]
+    total = keep[...]
+    for one in got:
+        total = total + one[...]
     first[...] = total[:share]
     second[...] = total[share : 2 * share]
     readout[...] = total[2 * share :].sum(axis=0, keepdims=True)
 
 
-def shares_shape(groups, size, width, riding=0):
-    rows = (groups * size + 8,) * 3 + (groups * size + 8 + riding,)
+def shares_shape(groups, size, width, radix, riding=0):
+    rows = [groups * size + 8] * radix
+    rows[1] += riding
     return tuple(jax.ShapeDtypeStruct((number, width), F32) for number in rows)
 
 
-def sum_shares(outs, preds, count, share, width, params):
-    base, groups, pred_out = 1, count // 4, ()
-    while True:
+def sum_shares(outs, preds, count, share, width, riding, params):
+    radices, left = [2, 2], count // 4
+    while left > 1:
+        radices.append(min(4, left))
+        left //= radices[-1]
+    base, groups, pred_out = 1, count // 2, None
+    for step, radix in enumerate(radices):
         got = [
-            lax.ppermute(outs[k], AXES, [(i, i ^ (k * base)) for i in range(count)]) for k in (1, 2, 3)
+            lax.ppermute(outs[k], AXES, [(i, i ^ (k * base)) for i in range(count)]) for k in range(1, radix)
         ]
-        if groups == 1:
+        if step == len(radices) - 1:
             break
-        base *= 4
-        more = (jax.ShapeDtypeStruct(preds.shape, F32),) if base == 4 else ()
-        *outs, last = pl.pallas_call(
-            functools.partial(fold_kernel, base),
-            out_shape=shares_shape(groups // 4, 2 * share, width) + more,
-            in_specs=[VMEM] * 5,
-            out_specs=(VMEM,) * (4 + len(more)),
+        base *= radix
+        radix = radices[step + 1]
+        more = (jax.ShapeDtypeStruct(preds.shape, F32),) if step == 1 else ()
+        shapes = shares_shape(groups // radix, 2 * share, width, radix, riding if step == 0 else 0) + more
+        folded = pl.pallas_call(
+            functools.partial(fold_kernel, base, step + 1, radix),
+            out_shape=shapes,
+            in_specs=[VMEM] * (2 + len(got)),
+            out_specs=(VMEM,) * len(shapes),
             scratch_shapes=[pltpu.VMEM((groups, 2 * share, width), F32)],
             compiler_params=params,
             name="fold",
         )(outs[0], *got, preds)
+        outs = folded[:radix]
         if more:
-            pred_out = last
-        else:
-            outs.append(last)
-        groups //= 4
+            pred_out = folded[-1]
+        groups //= radix
     small = jax.ShapeDtypeStruct((share, width), F32)
     sums = pl.pallas_call(
         last_fold_kernel,
         out_shape=(small, small, jax.ShapeDtypeStruct((1, width), F32)),
-        in_specs=[VMEM] * 4,
+        in_specs=[VMEM] * (1 + len(got)),
         out_specs=(VMEM,) * 3,
         compiler_params=params,
         name="last_fold",
@@ -654,18 +669,18 @@
         name="back_inner",
     )(table, g_field, tiles, w_first, readout, goals, preds, m_one, m_two, gz_two)
 
-    share = width // count
+    share, riding = width // count, step * nodes // width
     outs = pl.pallas_call(
         functools.partial(back_edge_kernel, shape),
-        out_shape=shares_shape(count // 4, 2 * share, width, step * nodes // width),
+        out_shape=shares_shape(count // 2, 2 * share, width, 2, riding),
         in_specs=[SMEM] + [VMEM] * 11,
-        out_specs=(VMEM,) * 4,
+        out_specs=(VMEM,) * 2,
         scratch_shapes=[pltpu.VMEM((count, 2 * share, width), F32)],
         compiler_params=params,
         cost_estimate=cost(edge // 4, edge),
         name="back_edge",
     )(table, outer, inner, side, tiles, preds, m_one, first, second, sums, local, slopes)
-    first, second, extra, pred_out = sum_shares(outs, preds, count, share, width, params)
+    first, second, extra, pred_out = sum_shares(outs, preds, count, share, width, riding, params)
     return pred_out, first, second, extra[0]
 
 

time: 86.4 us -> 84.9 us (0.983)
  waiting for transfers between devices: 20.7 us -> 19.5 us
    ppermute x6 -> x5, waiting for transfers between devices: 11.1 us -> 9.85 us  [sum_shares(): lax.ppermute(outs[k], AXES, [(i, i ^ k * base) for i in range(count)])]
    ppermute x6 -> x5, starting transfers between devices: 6.59 us -> 6.26 us  [sum_shares(): lax.ppermute(outs[k], AXES, [(i, i ^ k * base) for i in range(count)])]
  transfers between devices with their start and end apart: 18 -> 17, of which waited for: 7 -> 7; matrix products, arithmetic and copies ran while one was open for 0% -> 0% of each run, Pallas kernels for 14% -> 14%
where the time goes in v8:
time: 84.9 us; the launch traced here: 84.6 us
  starting transfers between devices  40 us (47%)
  Pallas kernels  21.6 us (25%)
  waiting for transfers between devices  19.5 us (23%)
  local copies, waits for them, and re-layouts  2.63 us (3%)
  between operations  0.88 us (1%)
    ppermute x12, starting transfers between devices, send(): return lax.ppermute(value, AXES, way)  33.7 us
    ppermute x5, waiting for transfers between devices, sum_shares(): lax.ppermute(outs[k], AXES, [(i, i ^ k * base) for i in range(count)])  9.85 us
    ppermute x12, waiting for transfers between devices, send(): return lax.ppermute(value, AXES, way)  9.66 us
    ppermute x5, starting transfers between devices, sum_shares(): lax.ppermute(outs[k], AXES, [(i, i ^ k * base) for i in range(count)])  6.26 us
    pallas_call x1, Pallas kernels, per_device(): pl.pallas_call(functools.partial(middle_compute_kernel, shape, scale), ou...  5.46 us
    pallas_call x1, Pallas kernels, per_device(): pl.pallas_call(functools.partial(back_inner_kernel, shape, scale), out_sh...  4.84 us
    pallas_call x1, Pallas kernels, per_device(): pl.pallas_call(functools.partial(second_edge_kernel, shape, scale), out_s...  2.96 us
    pallas_call x1, Pallas kernels, per_device(): pl.pallas_call(functools.partial(first_edge_kernel, shape), out_shape=(ja...  2.78 us
  transfers between devices with their start and end apart: 17, of which 7 were waited for; matrix products, arithmetic and copies ran while one was open for 0% of the time, Pallas kernels for 14%

profile of v8, /device:TPU:0, one launch (start us, length us, event | category | flops | bytes accessed | tf_op | source)
XLA Modules:
  0.0 84.6 jit_solution(12407137194066395235)
XLA Ops:
  0.6 1.6 %copy-done = bf16[4,8,128,256]{3,2,1,0:T(8,128)(2,1)S(1)} copy-done((bf16[4,8,128,256]{3,2,1,0:T(8,128)(2,1)S(1)}, bf16[4,8,128,256]{3,2,1,0:T(8,128)(2,1)}, u32[]{:S(2)}) %copy-start) | copy-done | bytes 2097176
  2.2 0.7 copy-done.6
  3.4 0.9 %collective-permute-start = (bf16[2064,256]{1,0:T(8,128)(2,1)S(1)}, bf16[2064,256]{1,0:T(8,128)(2,1)S(1)}, u32[]{:S(2)}, u32[]{:S(2)}) collective-permute-start(bf16[2064,256]{1,0:T(8,128)(2,1)S(1)} %get-tuple-element.58), channel_id=1, source_target_pairs={{2,1},{1,2},{6,5},{5,6},{10,9},{9,10},{14,13},{13,14},{18,17},{17,... | collective-permute-start | bytes 3170312 | tf_op jit(solution)/shard_map/ppermute | solution.py:545
  4.6 0.9 %collective-permute-start.1 = (bf16[2,1024,256]{2,1,0:T(8,128)(2,1)S(1)}, bf16[2,1024,256]{2,1,0:T(8,128)(2,1)S(1)}, u32[]{:S(2)}, u32[]{:S(2)}) collective-permute-start(bf16[2,1024,256]{2,1,0:T(8,128)(2,1)S(1)} %pack_middle.1), channel_id=1, source_target_pairs={{2,1},{1,2},{6,5},{5,6},{10,9},{9,10},{14,13},{13,14},{18,17},{17,... | collective-permute-start | bytes 3145736 | tf_op jit(solution)/shard_map/ppermute | solution.py:545
  5.5 6.9 %collective-permute-start.2 = (bf16[528,256]{1,0:T(8,128)(2,1)S(1)}, bf16[528,256]{1,0:T(8,128)(2,1)S(1)}, u32[]{:S(2)}, u32[]{:S(2)}) collective-permute-start(bf16[528,256]{1,0:T(8,128)(2,1)S(1)} %get-tuple-element.59.after), channel_id=1, source_target_pairs={{1,0},{3,1},{0,2},{2,3},{5,4},{7,5},{4,6},{6,7},{9,8},{11,9},{8,10... | collective-permute-start | bytes 811016 | tf_op jit(solution)/shard_map/ppermute | solution.py:545
  12.4 6.9 %collective-permute-done.2.after.side = bf16[528,256]{1,0:T(8,128)(2,1)S(1)} collective-permute-done((bf16[528,256]{1,0:T(8,128)(2,1)S(1)}, bf16[528,256]{1,0:T(8,128)(2,1)S(1)}, u32[]{:S(2)}, u32[]{:S(2)}) %collective-permute-start.2) | collective-permute-done | bytes 270368 | tf_op jit(solution)/shard_map/ppermute | solution.py:545
  19.5 0.7 collective-permute-start.3
  20.2 6.0 %collective-permute-start.4 = (bf16[1040,256]{1,0:T(8,128)(2,1)S(1)}, bf16[1040,256]{1,0:T(8,128)(2,1)S(1)}, u32[]{:S(2)}, u32[]{:S(2)}) collective-permute-start(bf16[1040,256]{1,0:T(8,128)(2,1)S(1)} %get-tuple-element.61), channel_id=1, source_target_pairs={{1,0},{0,1},{3,2},{2,3},{5,4},{4,5},{7,6},{6,7},{9,8},{8,9},{11,10... | collective-permute-start | bytes 1597448 | tf_op jit(solution)/shard_map/ppermute | solution.py:545
  26.1 0.7 collective-permute-start.5
  26.8 1.6 %prepare.1 = (bf16[32,128,128]{2,1,0:T(8,128)(2,1)S(1)}, bf16[256,256]{1,0:T(8,128)(2,1)S(1)}, bf16[256,256]{1,0:T(8,128)(2,1)S(1)}, bf16[256,256]{1,0:T(8,128)(2,1)S(1)}) custom-call(bf16[16,128,128]{2,1,0:T(8,128)(2,1)S(1)} %copy-done.2, bf16[256,256]{1,0:T(8,128)(2,1)S(1)} %copy-done.3, bf16[256,256]{1,0:T(8,128)(2,1)S(1)} %copy-done.4), custom_call_target="tpu_custom_call" | custom-call | tf_op jit(solution)/shard_map/prepare/pallas_call | solution.py:579
  28.5 2.8 %first_edge.1 = (s32[20,128]{1,0:T(8,128)S(1)}, bf16[6,1280,256]{2,1,0:T(8,128)(2,1)S(1)}, bf16[6,1280,256]{2,1,0:T(8,128)(2,1)S(1)}, bf16[4,1024,256]{2,1,0:T(8...) custom-call(bf16[16,256]{1,0:T(8,128)(2,1)S(1)} %get-tuple-element.57.num, ...), custom_call_target="tpu_custom_call" | custom-call | flops 1207959552 | bytes 4718592 | tf_op jit(solution)/shard_map/first_edge/pallas_call | solution.py:620
  31.3 0.7 collective-permute-start.6
  32.0 8.2 %collective-permute-start.7 = (bf16[1024,256]{1,0:T(8,128)(2,1)S(1)}, bf16[1024,256]{1,0:T(8,128)(2,1)S(1)}, u32[]{:S(2)}, u32[]{:S(2)}) collective-permute-start(bf16[1024,256]{1,0:T(8,128)(2,1)S(1)} %get-tuple-element.70), channel_id=1, source_target_pairs={{1,0},{0,1},{3,2},{2,3},{5,4},{4,5},{7,6},{6,7},{9,8},{8,9},{11,10... | collective-permute-start | bytes 1572872 | tf_op jit(solution)/shard_map/ppermute | solution.py:545
  40.2 3.3 %collective-permute-start.8 = (bf16[512,256]{1,0:T(8,128)(2,1)S(1)}, bf16[512,256]{1,0:T(8,128)(2,1)S(1)}, u32[]{:S(2)}, u32[]{:S(2)}) collective-permute-start(bf16[512,256]{1,0:T(8,128)(2,1)S(1)} %get-tuple-element.71), channel_id=1, source_target_pairs={{2,0},{3,1},{0,2},{1,3},{6,4},{7,5},{4,6},{5,7},{10,8},{11,9},{8,1... | collective-permute-start | bytes 786440 | tf_op jit(solution)/shard_map/ppermute | solution.py:545
  43.6 5.5 %inner_forward.1 = (bf16[6,1280,256]{2,1,0:T(8,128)(2,1)S(1)}, bf16[4,1024,256]{2,1,0:T(8,128)(2,1)S(1)}, bf16[4,1024,256]{2,1,0:T(8,128)(2,1)S(1)}, bf16[4,1024...) custom-call(s32[20,128]{1,0:T(8,128)S(1)} %get-tuple-element.68.tabl, ...), custom_call_target="tpu_custom_call", output_to_operand_aliasing={{0}: (10, {}), {1}: (11, {})} | custom-call | flops 3019898880 | bytes 11534336 | tf_op jit(solution)/shard_map/inner_forward/pallas_call | solution.py:638
  49.1 1.0 %collective-permute-done.8.side = bf16[512,256]{1,0:T(8,128)(2,1)S(1)} collective-permute-done((bf16[512,256]{1,0:T(8,128)(2,1)S(1)}, bf16[512,256]{1,0:T(8,128)(2,1)S(1)}, u32[]{:S(2)}, u32[]{:S(2)}) %collective-permute-start.8) | collective-permute-done | bytes 262176 | tf_op jit(solution)/shard_map/ppermute | solution.py:545
  50.1 3.0 %second_edge.1 = (bf16[4,1024,256]{2,1,0:T(8,128)(2,1)S(1)}, bf16[4,1024,256]{2,1,0:T(8,128)(2,1)S(1)}, bf16[6,1280,256]{2,1,0:T(8,128)(2,1)S(1)}, f32[4,8,128]{...) custom-call(s32[20,128]{1,0:T(8,128)S(1)} %get-tuple-element.68.tabl, ...), custom_call_target="tpu_custom_call", output_to_operand_aliasing={{0}: (12, {}), {1}: (13, {}), {2}: (14, {}), {3}: (15, {}),... | custom-call | flops 805306368 | bytes 5242880 | tf_op jit(solution)/shard_map/second_edge/pallas_call | solution.py:649
  53.0 0.9 %collective-permute-start.9 = (bf16[1024,256]{1,0:T(8,128)(2,1)S(1)}, bf16[1024,256]{1,0:T(8,128)(2,1)S(1)}, u32[]{:S(2)}, u32[]{:S(2)}) collective-permute-start(bf16[1024,256]{1,0:T(8,128)(2,1)S(1)} %get-tuple-element.85), channel_id=1, source_target_pairs={{1,4},{3,6},{5,8},{7,10},{9,12},{11,14},{4,1},{6,3},{8,5},{10,7},{... | collective-permute-start | bytes 1572872 | tf_op jit(solution)/shard_map/ppermute | solution.py:545
  53.9 3.0 %collective-permute-start.10 = (bf16[1024,256]{1,0:T(8,128)(2,1)S(1)}, bf16[1024,256]{1,0:T(8,128)(2,1)S(1)}, u32[]{:S(2)}, u32[]{:S(2)}) collective-permute-start(bf16[1024,256]{1,0:T(8,128)(2,1)S(1)} %get-tuple-element.86), channel_id=1, source_target_pairs={{1,0},{0,1},{3,2},{2,3},{5,4},{4,5},{7,6},{6,7},{9,8},{8,9},{11,10... | collective-permute-start | bytes 1572872 | tf_op jit(solution)/shard_map/ppermute | solution.py:545
  56.9 1.7 %collective-permute-start.11 = (bf16[512,256]{1,0:T(8,128)(2,1)S(1)}, bf16[512,256]{1,0:T(8,128)(2,1)S(1)}, u32[]{:S(2)}, u32[]{:S(2)}) collective-permute-start(bf16[512,256]{1,0:T(8,128)(2,1)S(1)} %get-tuple-element.87), channel_id=1, source_target_pairs={{2,0},{3,1},{0,2},{1,3},{6,4},{7,5},{4,6},{5,7},{10,8},{11,9},{8,1... | collective-permute-start | bytes 786440 | tf_op jit(solution)/shard_map/ppermute | solution.py:545
  58.6 4.8 %back_inner.1 = (f32[256,256]{1,0:T(8,128)S(1)}, f32[256,256]{1,0:T(8,128)S(1)}, f32[2304,256]{1,0:T(8,128)S(1)}, f32[2304,256]{1,0:T(8,128)S(1)}) custom-call(s32[20,128]{1,0:T(8,128)S(1)} %get-tuple-element.68.table, bf16[6,1280,256]{2,1,0:T(8,128)(2,1)S(1)} %get-tuple-element.90.g_field, bf16[32,128,128]{2,1,0:T(8,128)(2,1)S(1)} %get-tuple-element.66.tiles, ...), custom_call_target="tpu_custom_call" | custom-call | flops 3221225472 | bytes 16777216 | tf_op jit(solution)/shard_map/back_inner/pallas_call | solution.py:662
  63.5 1.7 %collective-permute-done.11.side = bf16[512,256]{1,0:T(8,128)(2,1)S(1)} collective-permute-done((bf16[512,256]{1,0:T(8,128)(2,1)S(1)}, bf16[512,256]{1,0:T(8,128)(2,1)S(1)}, u32[]{:S(2)}, u32[]{:S(2)}) %collective-permute-start.11) | collective-permute-done | bytes 262176 | tf_op jit(solution)/shard_map/ppermute | solution.py:545
  65.2 1.9 %back_edge.1 = (f32[264,256]{1,0:T(8,128)S(1)}, f32[280,256]{1,0:T(8,128)S(1)}) custom-call(s32[20,128]{1,0:T(8,128)S(1)} %get-tuple-element.68.table, bf16[1024,256]{1,0:T(8,128)(2,1)S(1)} %collective-permute-done.9.outer, bf16[1024,256]{1,0:T(8,128)(2,1)S(1)} %collective-permute-done.10.inner, bf16[512,256]{1,0:T(8,128)(2,1)S(1)} %collective-permute-done.11.side, ...), custom_call_target="tpu_custom_call" | custom-call | flops 503316480 | bytes 2883584 | tf_op jit(solution)/shard_map/back_edge/pallas_call | solution.py:673
  67.2 1.6 %collective-permute-done.12.refs_0_ = f32[280,256]{1,0:T(8,128)S(1)} collective-permute-done((f32[280,256]{1,0:T(8,128)S(1)}, f32[280,256]{1,0:T(8,128)S(1)}, u32[]{:S(2)}, u32[]{:S(2)}) %collective-permute-start.12) | collective-permute-done | bytes 286752 | tf_op jit(solution)/shard_map/ppermute | solution.py:502
  68.8 1.8 %collective-permute-start.13 = (f32[152,256]{1,0:T(8,128)S(1)}, f32[152,256]{1,0:T(8,128)S(1)}, u32[]{:S(2)}, u32[]{:S(2)}) collective-permute-start(f32[152,256]{1,0:T(8,128)S(1)} %get-tuple-element.101), channel_id=1, source_target_pairs={{0,2},{1,3},{2,0},{3,1},{4,6},{5,7},{6,4},{7,5},{8,10},{9,11},{10,... | collective-permute-start | bytes 466952 | tf_op jit(solution)/shard_map/ppermute | solution.py:502
  70.6 4.3 %collective-permute-done.13.refs_0_ = f32[152,256]{1,0:T(8,128)S(1)} collective-permute-done((f32[152,256]{1,0:T(8,128)S(1)}, f32[152,256]{1,0:T(8,128)S(1)}, u32[]{:S(2)}, u32[]{:S(2)}) %collective-permute-start.13) | collective-permute-done | bytes 155680 | tf_op jit(solution)/shard_map/ppermute | solution.py:502
  75.6 1.6 %collective-permute-start.14 = (f32[40,256]{1,0:T(8,128)S(1)}, f32[40,256]{1,0:T(8,128)S(1)}, u32[]{:S(2)}, u32[]{:S(2)}) collective-permute-start(f32[40,256]{1,0:T(8,128)S(1)} %get-tuple-element.104), channel_id=1, source_target_pairs={{0,4},{1,5},{2,6},{3,7},{4,0},{5,1},{6,2},{7,3},{8,12},{9,13},{10,... | collective-permute-start | bytes 122888 | tf_op jit(solution)/shard_map/ppermute | solution.py:502
  77.2 1.0 %collective-permute-start.15 = (f32[40,256]{1,0:T(8,128)S(1)}, f32[40,256]{1,0:T(8,128)S(1)}, u32[]{:S(2)}, u32[]{:S(2)}) collective-permute-start(f32[40,256]{1,0:T(8,128)S(1)} %get-tuple-element.105), channel_id=1, source_target_pairs={{0,8},{1,9},{2,10},{3,11},{4,12},{5,13},{6,14},{7,15},{8,0},{9,1},... | collective-permute-start | bytes 122888 | tf_op jit(solution)/shard_map/ppermute | solution.py:502
  78.1 1.8 %collective-permute-start.16 = (f32[40,256]{1,0:T(8,128)S(1)}, f32[40,256]{1,0:T(8,128)S(1)}, u32[]{:S(2)}, u32[]{:S(2)}) collective-permute-start(f32[40,256]{1,0:T(8,128)S(1)} %get-tuple-element.106), channel_id=1, source_target_pairs={{0,12},{1,13},{2,14},{3,15},{4,8},{5,9},{6,10},{7,11},{8,4},{9,5},... | collective-permute-start | bytes 122888 | tf_op jit(solution)/shard_map/ppermute | solution.py:502
  80.0 2.6 %collective-permute-done.15.refs_1_ = f32[40,256]{1,0:T(8,128)S(1)} collective-permute-done((f32[40,256]{1,0:T(8,128)S(1)}, f32[40,256]{1,0:T(8,128)S(1)}, u32[]{:S(2)}, u32[]{:S(2)}) %collective-permute-start.15) | collective-permute-done | bytes 40992 | tf_op jit(solution)/shard_map/ppermute | solution.py:502
  82.6 1.3 %collective-permute-done.16.refs_2_ = f32[40,256]{1,0:T(8,128)S(1)} collective-permute-done((f32[40,256]{1,0:T(8,128)S(1)}, f32[40,256]{1,0:T(8,128)S(1)}, u32[]{:S(2)}, u32[]{:S(2)}) %collective-permute-start.16) | collective-permute-done | bytes 40992 | tf_op jit(solution)/shard_map/ppermute | solution.py:502
  83.9 0.6 last_fold.1
  (32 shorter events, 1.8 us)
Async XLA Ops:
  0.6 1.6 %copy-start = (bf16[4,8,128,256]{3,2,1,0:T(8,128)(2,1)S(1)}, bf16[4,8,128,256]{3,2,1,0:T(8,128)(2,1)}, u32[]{:S(2)}) copy-start(bf16[4,8,128,256]{3,2,1,0:T(8,128)(2,1)} %param.7) | copy-start | bytes 6291460
  2.2 0.7 copy-start.6
  2.9 1.6 %copy-start.1 = (bf16[4,8,128,256]{3,2,1,0:T(8,128)(2,1)S(1)}, bf16[4,8,128,256]{3,2,1,0:T(8,128)(2,1)}, u32[]{:S(2)}) copy-start(bf16[4,8,128,256]{3,2,1,0:T(8,128)(2,1)} %param.7) | copy-start | bytes 6291460
  3.4 15.9 %collective-permute-start = (bf16[2064,256]{1,0:T(8,128)(2,1)S(1)}, bf16[2064,256]{1,0:T(8,128)(2,1)S(1)}, u32[]{:S(2)}, u32[]{:S(2)}) collective-permute-start(bf16[2064,256]{1,0:T(8,128)(2,1)S(1)} %get-tuple-element.58), channel_id=1, source_target_pairs={{2,1},{1,2},{6,5},{5,6},{10,9},{9,10},{14,13},{13,14},{18,17},{17,... | collective-permute-start | bytes 3170312 | tf_op jit(solution)/shard_map/ppermute | solution.py:545
  4.6 21.5 %copy-start.5 = (f32[4,8,128]{2,1,0:T(8,128)S(1)}, f32[4,8,128]{2,1,0:T(8,128)}, u32[]{:S(2)}) copy-start(f32[4,8,128]{2,1,0:T(8,128)} %target.1) | copy-start | bytes 49156
  4.6 22.2 %copy-start.2 = (bf16[16,128,128]{2,1,0:T(8,128)(2,1)S(1)}, bf16[16,128,128]{2,1,0:T(8,128)(2,1)}, u32[]{:S(2)}) copy-start(bf16[16,128,128]{2,1,0:T(8,128)(2,1)} %tiles) | copy-start | bytes 1572868
  4.6 22.2 %copy-start.3 = (bf16[256,256]{1,0:T(8,128)(2,1)S(1)}, bf16[256,256]{1,0:T(8,128)(2,1)}, u32[]{:S(2)}) copy-start(bf16[256,256]{1,0:T(8,128)(2,1)} %first) | copy-start | bytes 393220
  4.6 22.2 %copy-start.4 = (bf16[256,256]{1,0:T(8,128)(2,1)S(1)}, bf16[256,256]{1,0:T(8,128)(2,1)}, u32[]{:S(2)}) copy-start(bf16[256,256]{1,0:T(8,128)(2,1)} %second) | copy-start | bytes 393220
  4.6 23.8 %collective-permute-start.1 = (bf16[2,1024,256]{2,1,0:T(8,128)(2,1)S(1)}, bf16[2,1024,256]{2,1,0:T(8,128)(2,1)S(1)}, u32[]{:S(2)}, u32[]{:S(2)}) collective-permute-start(bf16[2,1024,256]{2,1,0:T(8,128)(2,1)S(1)} %pack_middle.1), channel_id=1, source_target_pairs={{2,1},{1,2},{6,5},{5,6},{10,9},{9,10},{14,13},{13,14},{18,17},{17,... | collective-permute-start | bytes 3145736 | tf_op jit(solution)/shard_map/ppermute | solution.py:545
  5.5 13.8 %collective-permute-start.2 = (bf16[528,256]{1,0:T(8,128)(2,1)S(1)}, bf16[528,256]{1,0:T(8,128)(2,1)S(1)}, u32[]{:S(2)}, u32[]{:S(2)}) collective-permute-start(bf16[528,256]{1,0:T(8,128)(2,1)S(1)} %get-tuple-element.59.after), channel_id=1, source_target_pairs={{1,0},{3,1},{0,2},{2,3},{5,4},{7,5},{4,6},{6,7},{9,8},{11,9},{8,10... | collective-permute-start | bytes 811016 | tf_op jit(solution)/shard_map/ppermute | solution.py:545
  19.5 9.0 %collective-permute-start.3 = (bf16[1040,256]{1,0:T(8,128)(2,1)S(1)}, bf16[1040,256]{1,0:T(8,128)(2,1)S(1)}, u32[]{:S(2)}, u32[]{:S(2)}) collective-permute-start(bf16[1040,256]{1,0:T(8,128)(2,1)S(1)} %get-tuple-element.60), channel_id=1, source_target_pairs={{1,4},{3,6},{5,8},{7,10},{9,12},{11,14},{4,1},{6,3},{8,5},{10,7},{... | collective-permute-start | bytes 1597448 | tf_op jit(solution)/shard_map/ppermute | solution.py:545
  20.2 8.3 %collective-permute-start.4 = (bf16[1040,256]{1,0:T(8,128)(2,1)S(1)}, bf16[1040,256]{1,0:T(8,128)(2,1)S(1)}, u32[]{:S(2)}, u32[]{:S(2)}) collective-permute-start(bf16[1040,256]{1,0:T(8,128)(2,1)S(1)} %get-tuple-element.61), channel_id=1, source_target_pairs={{1,0},{0,1},{3,2},{2,3},{5,4},{4,5},{7,6},{6,7},{9,8},{8,9},{11,10... | collective-permute-start | bytes 1597448 | tf_op jit(solution)/shard_map/ppermute | solution.py:545
  26.1 2.3 %collective-permute-start.5 = (f32[4,8,128]{2,1,0:T(8,128)S(1)}, f32[4,8,128]{2,1,0:T(8,128)S(1)}, u32[]{:S(2)}, u32[]{:S(2)}) collective-permute-start(f32[4,8,128]{2,1,0:T(8,128)S(1)} %copy-done.5), channel_id=1, source_target_pairs={{2,1},{1,2},{6,5},{5,6},{10,9},{9,10},{14,13},{13,14},{18,17},{17,... | collective-permute-start | bytes 49160 | tf_op jit(solution)/shard_map/ppermute | solution.py:545
  28.5 11.7 %copy-start.7 = (bf16[256]{0:T(256)(128)(2,1)S(1)}, bf16[256]{0:T(256)(128)(2,1)}, u32[]{:S(2)}) copy-start(bf16[256]{0:T(256)(128)(2,1)} %param.12) | copy-start | bytes 1540
  31.3 18.8 %collective-permute-start.6 = (bf16[1024,256]{1,0:T(8,128)(2,1)S(1)}, bf16[1024,256]{1,0:T(8,128)(2,1)S(1)}, u32[]{:S(2)}, u32[]{:S(2)}) collective-permute-start(bf16[1024,256]{1,0:T(8,128)(2,1)S(1)} %get-tuple-element.69), channel_id=1, source_target_pairs={{1,4},{3,6},{5,8},{7,10},{9,12},{11,14},{4,1},{6,3},{8,5},{10,7},{... | collective-permute-start | bytes 1572872 | tf_op jit(solution)/shard_map/ppermute | solution.py:545
  32.0 18.1 %collective-permute-start.7 = (bf16[1024,256]{1,0:T(8,128)(2,1)S(1)}, bf16[1024,256]{1,0:T(8,128)(2,1)S(1)}, u32[]{:S(2)}, u32[]{:S(2)}) collective-permute-start(bf16[1024,256]{1,0:T(8,128)(2,1)S(1)} %get-tuple-element.70), channel_id=1, source_target_pairs={{1,0},{0,1},{3,2},{2,3},{5,4},{4,5},{7,6},{6,7},{9,8},{8,9},{11,10... | collective-permute-start | bytes 1572872 | tf_op jit(solution)/shard_map/ppermute | solution.py:545
  40.2 9.9 %collective-permute-start.8 = (bf16[512,256]{1,0:T(8,128)(2,1)S(1)}, bf16[512,256]{1,0:T(8,128)(2,1)S(1)}, u32[]{:S(2)}, u32[]{:S(2)}) collective-permute-start(bf16[512,256]{1,0:T(8,128)(2,1)S(1)} %get-tuple-element.71), channel_id=1, source_target_pairs={{2,0},{3,1},{0,2},{1,3},{6,4},{7,5},{4,6},{5,7},{10,8},{11,9},{8,1... | collective-permute-start | bytes 786440 | tf_op jit(solution)/shard_map/ppermute | solution.py:545
  53.0 12.1 %collective-permute-start.9 = (bf16[1024,256]{1,0:T(8,128)(2,1)S(1)}, bf16[1024,256]{1,0:T(8,128)(2,1)S(1)}, u32[]{:S(2)}, u32[]{:S(2)}) collective-permute-start(bf16[1024,256]{1,0:T(8,128)(2,1)S(1)} %get-tuple-element.85), channel_id=1, source_target_pairs={{1,4},{3,6},{5,8},{7,10},{9,12},{11,14},{4,1},{6,3},{8,5},{10,7},{... | collective-permute-start | bytes 1572872 | tf_op jit(solution)/shard_map/ppermute | solution.py:545
  53.9 11.3 %collective-permute-start.10 = (bf16[1024,256]{1,0:T(8,128)(2,1)S(1)}, bf16[1024,256]{1,0:T(8,128)(2,1)S(1)}, u32[]{:S(2)}, u32[]{:S(2)}) collective-permute-start(bf16[1024,256]{1,0:T(8,128)(2,1)S(1)} %get-tuple-element.86), channel_id=1, source_target_pairs={{1,0},{0,1},{3,2},{2,3},{5,4},{4,5},{7,6},{6,7},{9,8},{8,9},{11,10... | collective-permute-start | bytes 1572872 | tf_op jit(solution)/shard_map/ppermute | solution.py:545
  56.9 8.3 %collective-permute-start.11 = (bf16[512,256]{1,0:T(8,128)(2,1)S(1)}, bf16[512,256]{1,0:T(8,128)(2,1)S(1)}, u32[]{:S(2)}, u32[]{:S(2)}) collective-permute-start(bf16[512,256]{1,0:T(8,128)(2,1)S(1)} %get-tuple-element.87), channel_id=1, source_target_pairs={{2,0},{3,1},{0,2},{1,3},{6,4},{7,5},{4,6},{5,7},{10,8},{11,9},{8,1... | collective-permute-start | bytes 786440 | tf_op jit(solution)/shard_map/ppermute | solution.py:545
  67.1 1.6 %collective-permute-start.12 = (f32[280,256]{1,0:T(8,128)S(1)}, f32[280,256]{1,0:T(8,128)S(1)}, u32[]{:S(2)}, u32[]{:S(2)}) collective-permute-start(f32[280,256]{1,0:T(8,128)S(1)} %get-tuple-element.99), channel_id=1, source_target_pairs={{0,1},{1,0},{2,3},{3,2},{4,5},{5,4},{6,7},{7,6},{8,9},{9,8},{10,11... | collective-permute-start | bytes 860168 | tf_op jit(solution)/shard_map/ppermute | solution.py:502
  68.8 6.1 %collective-permute-start.13 = (f32[152,256]{1,0:T(8,128)S(1)}, f32[152,256]{1,0:T(8,128)S(1)}, u32[]{:S(2)}, u32[]{:S(2)}) collective-permute-start(f32[152,256]{1,0:T(8,128)S(1)} %get-tuple-element.101), channel_id=1, source_target_pairs={{0,2},{1,3},{2,0},{3,1},{4,6},{5,7},{6,4},{7,5},{8,10},{9,11},{10,... | collective-permute-start | bytes 466952 | tf_op jit(solution)/shard_map/ppermute | solution.py:502
  75.6 4.4 %collective-permute-start.14 = (f32[40,256]{1,0:T(8,128)S(1)}, f32[40,256]{1,0:T(8,128)S(1)}, u32[]{:S(2)}, u32[]{:S(2)}) collective-permute-start(f32[40,256]{1,0:T(8,128)S(1)} %get-tuple-element.104), channel_id=1, source_target_pairs={{0,4},{1,5},{2,6},{3,7},{4,0},{5,1},{6,2},{7,3},{8,12},{9,13},{10,... | collective-permute-start | bytes 122888 | tf_op jit(solution)/shard_map/ppermute | solution.py:502
  77.2 5.4 %collective-permute-start.15 = (f32[40,256]{1,0:T(8,128)S(1)}, f32[40,256]{1,0:T(8,128)S(1)}, u32[]{:S(2)}, u32[]{:S(2)}) collective-permute-start(f32[40,256]{1,0:T(8,128)S(1)} %get-tuple-element.105), channel_id=1, source_target_pairs={{0,8},{1,9},{2,10},{3,11},{4,12},{5,13},{6,14},{7,15},{8,0},{9,1},... | collective-permute-start | bytes 122888 | tf_op jit(solution)/shard_map/ppermute | solution.py:502
  78.1 5.8 %collective-permute-start.16 = (f32[40,256]{1,0:T(8,128)S(1)}, f32[40,256]{1,0:T(8,128)S(1)}, u32[]{:S(2)}, u32[]{:S(2)}) collective-permute-start(f32[40,256]{1,0:T(8,128)S(1)} %get-tuple-element.106), channel_id=1, source_target_pairs={{0,12},{1,13},{2,14},{3,15},{4,8},{5,9},{6,10},{7,11},{8,4},{9,5},... | collective-permute-start | bytes 122888 | tf_op jit(solution)/shard_map/ppermute | solution.py:502

commit v9 on v8

--- a/solution.py
+++ b/solution.py
@@ -33,7 +33,9 @@
     outer = [(at(z - 1, y, 1), at(z, y, 0)) for z, y, c in every if c == 0 and z > 0]
     outer += [(at(z + 1, y, 0), at(z, y, 1)) for z, y, c in every if c == 1 and z + 1 < depth]
     side = [(at(z, 1 - y, c), at(z, y, c)) for z, y, c in every]
-    return swap, first_side, inner, outer, side
+    above = [(at(z, 0, y), at(z, y, 1)) for z, y, c in every if c == 1]
+    above += [(at(z - 1, 1, y), at(z, y, 0)) for z, y, c in every if c == 0 and z > 0]
+    return swap, first_side, inner, outer, side, above
 
 
 def place():
@@ -243,28 +245,27 @@
         field[row + 1, at_block(column, nodes)] = side[at_block(row, nodes)]
 
 
-def pack_kernel(nodes, cols, ids, own, ends, side, numbers, ids_in, wide_ids, sems):
-    rows, line = own.shape[0], own.shape[1]
-    ids_copy = start_all([(ids, ids_in)], sems, 2 + rows)
+def pack_kernel(nodes, cols, ids, own, after, side, numbers, wide_ids, sems):
+    rows = own.shape[0]
     half, _, _ = place()
     col = pl.multiple_of(jnp.where(half == 1, 0, (cols - 1) * nodes), nodes)
-    pairs = [(own.at[0], ends.at[pl.ds(0, line)]), (own.at[rows - 1], ends.at[pl.ds(line, line)])]
-    for row in range(rows):
-        pairs.append((own.at[row, pl.ds(col, nodes)], side.at[pl.ds(row * nodes, nodes)]))
-    copies = start_all(pairs, sems)
-    wait_all(ids_copy)
+    copies = start_all(
+        [(own.at[row, pl.ds(col, nodes)], side.at[pl.ds(row * nodes, nodes)]) for row in range(rows)], sems
+    )
     wide_ids[...] = jnp.zeros_like(wide_ids)
     for kind in range(3):
-        wide_ids[kind * rows : (kind + 1) * rows, 0:cols] = ids_in[kind].astype(F32)
+        wide_ids[kind * rows : (kind + 1) * rows, 0:cols] = ids[kind]
     tail = wide_ids[...].astype(BF16)
     numbers[...] = tail
-    ends[2 * line :] = tail
     side[rows * nodes :] = tail
     wait_all(copies)
 
 
-def middle_kernel(own, after, middle, sems):
-    wait_all(start_all([(own.at[pl.ds(1, own.shape[0] - 2)], middle)], sems))
+def middle_kernel(own, numbers, middle, sems):
+    rows, line = own.shape[0], own.shape[1]
+    copies = start_all([(own.at[row + 1], middle.at[pl.ds(row * line, line)]) for row in range(rows - 2)], sems)
+    middle[(rows - 2) * line :] = numbers[...]
+    wait_all(copies)
 
 
 def prepare_kernel(tiles, first, second, both, first_in, second_in, second_turned, sems):
@@ -280,54 +281,38 @@
     lax.fori_loop(0, number, one_tile, 0)
 
 
-def pick_kernel(numbers, own, ends, after, outer, inner, sems):
+def pick_kernel(own, ends, after, outer, inner, sems):
     rows, line = own.shape[0], own.shape[1]
     half, _, moved = place()
-    whole = pl.ds(0, line)
-    tail = pl.ds(line, TAIL)
 
     @pl.when(moved)
     def _():
-        outer[tail] = ends[pl.ds(2 * line, TAIL)]
-        inner[tail] = ends[pl.ds(2 * line, TAIL)]
-        outer[whole] = ends[pl.ds(pl.multiple_of(half * line, line), line)]
-        inner[whole] = ends[pl.ds(pl.multiple_of((1 - half) * line, line), line)]
+        outer[...] = ends[pl.ds(pl.multiple_of(half * line, line), line)]
+        inner[...] = ends[pl.ds(pl.multiple_of((1 - half) * line, line), line)]
 
     @pl.when(jnp.logical_not(moved))
     def _():
-        copies = start_all([
-            (own.at[jnp.where(half == 0, 0, rows - 1)], outer.at[whole]),
-            (own.at[jnp.where(half == 0, rows - 1, 0)], inner.at[whole]),
-        ], sems)
-        outer[tail] = numbers[...]
-        inner[tail] = numbers[...]
-        wait_all(copies)
-
-
-def first_edge_kernel(shape, numbers, own, ends, middle, outer, inner, side, later, tiles, weight,
+        wait_all(start_all([
+            (own.at[jnp.where(half == 0, 0, rows - 1)], outer),
+            (own.at[jnp.where(half == 0, rows - 1, 0)], inner),
+        ], sems))
+
+
+def first_edge_kernel(shape, numbers, above, own, ends, middle, outer, inner, side, later, tiles, weight,
                       table, field, x_field, m_all, outer_out, inner_out, side_out, own_ids, above_ids, spots, sems):
     nodes, rows, cols = shape
     line = cols * nodes
-    half, right, moved = place()
+    _, _, moved = place()
     inside = pl.ds(nodes, line)
-    tail = pl.ds(line, TAIL)
-
     @pl.when(moved)
     def _():
-        own_ids[...] = ends[pl.ds(2 * line, TAIL)].astype(F32)
+        own_ids[...] = middle[pl.ds((rows - 2) * line, TAIL)].astype(F32)
 
     @pl.when(jnp.logical_not(moved))
     def _():
         own_ids[...] = numbers[...].astype(F32)
 
-    @pl.when(half == 1)
-    def _():
-        above_ids[...] = inner[tail].astype(F32)
-
-    @pl.when(half == 0)
-    def _():
-        above_ids[...] = outer[tail].astype(F32)
-
+    above_ids[...] = above[...].astype(F32)
     left = side[pl.ds(rows * nodes, TAIL)].astype(F32)[2 * rows : 3 * rows, 0:128]
     north = own_ids[2 * rows : 3 * rows, 0:128]
     lanes = lax.broadcasted_iota(jnp.int32, north.shape, 1)
@@ -344,7 +329,7 @@
         field[1, inside] = ends[pl.ds(0, line)]
         field[rows, inside] = ends[pl.ds(line, line)]
         for row in range(2, rows):
-            field[row, inside] = middle[row - 2]
+            field[row, inside] = middle[pl.ds((row - 2) * line, line)]
 
     @pl.when(jnp.logical_not(moved))
     def _():
@@ -393,7 +378,7 @@
 
 
 def back_inner_kernel(shape, scale, table, g_field, tiles, weight, readout, goals, preds, m_one, m_two, gz_two,
-                      first_out, second_out, local, slopes):
+                      first_out, second_out, local, slopes, m_turned):
     nodes, rows, cols = shape
     blocks = inner_blocks(shape)
     gx, slope = back_terms(scale, weight, readout, goals, preds, m_one, blocks, nodes)
@@ -402,6 +387,7 @@
     gx, slope = back_terms(scale, weight, readout, goals, preds, m_one, edge_blocks(shape), nodes)
     local[...] = gx + products(table, g_field, tiles, edge_blocks(shape), shape)
     slopes[...] = slope
+    m_turned[...] = gather(lambda row, col: m_one[row, at_block(col, nodes)], edge_blocks(shape)).T
     second_out[...] = jnp.zeros_like(second_out)
 
     def each_row(row, carry):
@@ -411,14 +397,13 @@
     lax.fori_loop(0, rows, each_row, 0)
 
 
-def back_edge_kernel(shape, table, outer, inner, side, tiles, preds, m_one, first_in, second, sums, local, slopes,
+def back_edge_kernel(shape, table, outer, inner, side, tiles, preds, m_turned, first_in, second, sums, local, slopes,
                      keep, one, parts):
-    nodes = shape[0]
+    width = first_in.shape[1]
     gx = local[...] + rim_terms(table, tiles, outer, inner, side, shape)
     gz = (gx * slopes[...]).astype(BF16)
-    m = gather(lambda row, col: m_one[row, at_block(col, nodes)], edge_blocks(shape))
-    first = first_in[...] + over_nodes(m, gz)
-    count, size, width = parts.shape
+    first = first_in[...] + jnp.dot(m_turned[...], gz, preferred_element_type=F32)
+    count, size, _ = parts.shape
     parts[:, : size // 2] = first.reshape(count, size // 2, width)
     parts[:, size // 2 :] = second[...].reshape(count, size // 2, width)
     spread_shares(parts, sums[...], lax.axis_index("narrow"), (keep, one))
@@ -537,7 +522,7 @@
     wide, narrow = lax.axis_size("wide"), lax.axis_size("narrow")
     count = wide * narrow
     line, step = cols * nodes, rows * cols
-    swap, first_side, inner_way, outer_way, side_way = routes(wide)
+    swap, first_side, inner_way, outer_way, side_way, above_way = routes(wide)
     scale = float(np.sqrt(np.float32(width) / np.float32(rows * line * count)))
     params = pltpu.CompilerParams(vmem_limit_bytes=VMEM_LIMIT)
 
@@ -554,26 +539,27 @@
         return pltpu.SemaphoreType.DMA((number,))
 
     features = features.reshape(rows, line, width)
-    ends_s, side_s, numbers = pl.pallas_call(
+    ends_s = features[0 :: rows - 1].reshape(2 * line, width)
+    ends = send(ends_s, swap)
+    side_s, numbers = pl.pallas_call(
         functools.partial(pack_kernel, nodes, cols),
-        out_shape=(bf(2 * line + TAIL, width), bf(rows * nodes + TAIL, width), bf(TAIL, width)),
-        in_specs=[ANY, ANY],
-        out_specs=(VMEM,) * 3,
-        scratch_shapes=[pltpu.VMEM((3, rows, cols), jnp.int32), pltpu.VMEM((TAIL, width), F32), sems(3 + rows)],
+        out_shape=(bf(rows * nodes + TAIL, width), bf(TAIL, width)),
+        in_specs=[VMEM, ANY, ANY],
+        out_specs=(VMEM,) * 2,
+        scratch_shapes=[pltpu.VMEM((TAIL, width), F32), sems(rows)],
         compiler_params=params,
         name="pack",
-    )(jnp.transpose(tile_ids, (2, 0, 1)), features)
-    ends = send(ends_s, swap)
+    )(jnp.transpose(tile_ids, (2, 0, 1)).astype(F32), features, ends_s)
     side = send(side_s, first_side)
     middle_s = pl.pallas_call(
         middle_kernel,
-        out_shape=bf(rows - 2, line, width),
-        in_specs=[ANY, ANY],
+        out_shape=bf((rows - 2) * line + TAIL, width),
+        in_specs=[ANY, VMEM],
         out_specs=VMEM,
-        scratch_shapes=[sems(1)],
+        scratch_shapes=[sems(rows - 2)],
         compiler_params=params,
         name="pack_middle",
-    )(features, side_s)
+    )(features, numbers)
     middle = send(middle_s, swap)
     tiles, w_first, w_second, _ = lax.optimization_barrier((tiles, w_first, w_second, middle_s))
     tiles, w_first, w_second, w_turned = pl.pallas_call(
@@ -590,16 +576,17 @@
 
     outer_s, inner_s = pl.pallas_call(
         pick_kernel,
-        out_shape=(bf(line + TAIL, width),) * 2,
-        in_specs=[VMEM, ANY, VMEM, ANY],
+        out_shape=(bf(line, width),) * 2,
+        in_specs=[ANY, VMEM, ANY],
         out_specs=(VMEM,) * 2,
         scratch_shapes=[sems(4)],
         compiler_params=params,
         name="pick",
-    )(numbers, features, ends, side)
+    )(features, ends, side)
     outer, inner = send(outer_s, outer_way), send(inner_s, inner_way)
-    target_s, _ = lax.optimization_barrier((target, inner_s))
+    target_s, numbers_s, _ = lax.optimization_barrier((target, numbers, inner_s))
     goal_swap = send(target_s, swap)
+    above = send(numbers_s, above_way)
 
     shape = (nodes, rows, cols)
     patch, padded = bf(rows, line, width), bf(rows + 2, line + 2 * nodes, width)
@@ -620,7 +607,7 @@
     table, f_field, x_field, m_one, outer_s, inner_s, side_s = pl.pallas_call(
         functools.partial(first_edge_kernel, shape),
         out_shape=(jax.ShapeDtypeStruct((5 * rows, 128), jnp.int32), padded, padded, patch) + edge_shapes,
-        in_specs=[VMEM] * 7 + [ANY] + [VMEM] * 2,
+        in_specs=[VMEM] * 8 + [ANY] + [VMEM] * 2,
         out_specs=(SMEM,) + (VMEM,) * 6,
         scratch_shapes=[
             pltpu.VMEM((TAIL, width), F32),
@@ -631,7 +618,7 @@
         compiler_params=params,
         cost_estimate=cost(edge, edge),
         name="first_edge",
-    )(numbers, features, ends, middle, outer, inner, side, goal_swap, tiles, w_first)
+    )(numbers, above, features, ends, middle, outer, inner, side, goal_swap, tiles, w_first)
 
     outer, inner, side = edges(outer_s, inner_s, side_s)
     edge_terms = jax.ShapeDtypeStruct((edge * nodes, width), F32)
@@ -659,11 +646,11 @@
       m_two, gz_two, g_field, preds, sums)
 
     outer, inner, side = edges(outer_s, inner_s, side_s)
-    first, second, local, slopes = pl.pallas_call(
+    first, second, local, slopes, m_turned = pl.pallas_call(
         functools.partial(back_inner_kernel, shape, scale),
-        out_shape=(square, square, edge_terms, edge_terms),
+        out_shape=(square, square, edge_terms, edge_terms, bf(width, edge * nodes)),
         in_specs=[SMEM] + [VMEM] * 9,
-        out_specs=(VMEM,) * 4,
+        out_specs=(VMEM,) * 5,
         compiler_params=params,
         cost_estimate=cost(rows * cols, 3 * rows * cols),
         name="back_inner",
@@ -679,7 +666,7 @@
         compiler_params=params,
         cost_estimate=cost(edge // 4, edge),
         name="back_edge",
-    )(table, outer, inner, side, tiles, preds, m_one, first, second, sums, local, slopes)
+    )(table, outer, inner, side, tiles, preds, m_turned, first, second, sums, local, slopes)
     first, second, extra, pred_out = sum_shares(outs, preds, count, share, width, riding, params)
     return pred_out, first, second, extra[0]
 

time: 84.9 us -> 83.2 us (0.980)
  starting transfers between devices: 40 us -> 38.9 us
  local copies, waits for them, and re-layouts: 2.63 us -> 1.58 us
    unnamed x16 -> x12, local copies, waits for them, and re-layouts: 2.53 us -> 0.04 us
    slice x0 -> x1, local copies, waits for them, and re-layouts: none -> 1.45 us  [per_device(): ends_s = features[0::rows - 1].reshape(2 * line, width)]
    ppermute x12 -> x13, starting transfers between devices: 33.7 us -> 32.7 us  [send(): return lax.ppermute(value, AXES, way)]
    ppermute x12 -> x13, waiting for transfers between devices: 9.66 us -> 9.64 us  [send(): return lax.ppermute(value, AXES, way)]
  transfers between devices with their start and end apart: 17 -> 18, of which waited for: 7 -> 7; matrix products, arithmetic and copies ran while one was open for 0% -> 1% of each run, Pallas kernels for 14% -> 15%
where the time goes in v9:
time: 83.2 us; the launch traced here: 82.8 us
  starting transfers between devices  38.9 us (47%)
  Pallas kernels  21.3 us (26%)
  waiting for transfers between devices  19.5 us (23%)
  local copies, waits for them, and re-layouts  1.58 us (2%)
  between operations  0.89 us (1%)
    ppermute x13, starting transfers between devices, send(): return lax.ppermute(value, AXES, way)  32.7 us
    ppermute x5, waiting for transfers between devices, sum_shares(): lax.ppermute(outs[k], AXES, [(i, i ^ k * base) for i in range(count)])  9.84 us
    ppermute x13, waiting for transfers between devices, send(): return lax.ppermute(value, AXES, way)  9.64 us
    ppermute x5, starting transfers between devices, sum_shares(): lax.ppermute(outs[k], AXES, [(i, i ^ k * base) for i in range(count)])  6.26 us
    pallas_call x1, Pallas kernels, per_device(): pl.pallas_call(functools.partial(middle_compute_kernel, shape, scale), ou...  5.44 us
    pallas_call x1, Pallas kernels, per_device(): pl.pallas_call(functools.partial(back_inner_kernel, shape, scale), out_sh...  4.88 us
    pallas_call x1, Pallas kernels, per_device(): pl.pallas_call(functools.partial(second_edge_kernel, shape, scale), out_s...  2.96 us
    pallas_call x1, Pallas kernels, per_device(): pl.pallas_call(functools.partial(first_edge_kernel, shape), out_shape=(ja...  2.7 us
  transfers between devices with their start and end apart: 18, of which 7 were waited for; matrix products, arithmetic and copies ran while one was open for 1% of the time, Pallas kernels for 15%

profile of v9, /device:TPU:0, one launch (start us, length us, event | category | flops | bytes accessed | tf_op | source)
XLA Modules:
  0.0 82.8 jit_solution(7589723756980430919)
XLA Ops:
  0.6 1.4 %slice.3 = bf16[2,1024,256]{2,1,0:T(8,128)(2,1)S(1)} slice(bf16[4,1024,256]{2,1,0:T(8,128)(2,1)} %bitcast.5), slice={[0:4:3], [0:1024:1], [0:256:1]} | slice | bytes 2097152 | tf_op jit(solution)/shard_map/slice | solution.py:542
  2.1 0.7 collective-permute-start
  2.8 0.7 convert_bitcast_fusion.ids
  4.1 0.9 %collective-permute-start.3 = (bf16[2064,256]{1,0:T(8,128)(2,1)S(1)}, bf16[2064,256]{1,0:T(8,128)(2,1)S(1)}, u32[]{:S(2)}, u32[]{:S(2)}) collective-permute-start(bf16[2064,256]{1,0:T(8,128)(2,1)S(1)} %pack_middle.1), channel_id=1, source_target_pairs={{2,1},{1,2},{6,5},{5,6},{10,9},{9,10},{14,13},{13,14},{18,17},{17,... | collective-permute-start | bytes 3170312 | tf_op jit(solution)/shard_map/ppermute | solution.py:530
  4.9 7.1 %collective-permute-start.1 = (bf16[528,256]{1,0:T(8,128)(2,1)S(1)}, bf16[528,256]{1,0:T(8,128)(2,1)S(1)}, u32[]{:S(2)}, u32[]{:S(2)}) collective-permute-start(bf16[528,256]{1,0:T(8,128)(2,1)S(1)} %get-tuple-element.59), channel_id=1, source_target_pairs={{1,0},{3,1},{0,2},{2,3},{5,4},{7,5},{4,6},{6,7},{9,8},{11,9},{8,10... | collective-permute-start | bytes 811016 | tf_op jit(solution)/shard_map/ppermute | solution.py:530
  12.0 6.9 %collective-permute-done.1.after.side = bf16[528,256]{1,0:T(8,128)(2,1)S(1)} collective-permute-done((bf16[528,256]{1,0:T(8,128)(2,1)S(1)}, bf16[528,256]{1,0:T(8,128)(2,1)S(1)}, u32[]{:S(2)}, u32[]{:S(2)}) %collective-permute-start.1) | collective-permute-done | bytes 270368 | tf_op jit(solution)/shard_map/ppermute | solution.py:530
  19.1 0.7 collective-permute-start.4
  19.8 4.8 %collective-permute-start.5 = (bf16[1024,256]{1,0:T(8,128)(2,1)S(1)}, bf16[1024,256]{1,0:T(8,128)(2,1)S(1)}, u32[]{:S(2)}, u32[]{:S(2)}) collective-permute-start(bf16[1024,256]{1,0:T(8,128)(2,1)S(1)} %get-tuple-element.60), channel_id=1, source_target_pairs={{1,0},{0,1},{3,2},{2,3},{5,4},{4,5},{7,6},{6,7},{9,8},{8,9},{11,10... | collective-permute-start | bytes 1572872 | tf_op jit(solution)/shard_map/ppermute | solution.py:530
  24.6 0.7 collective-permute-start.6
  25.2 6.6 %collective-permute-start.2 = (bf16[16,256]{1,0:T(8,128)(2,1)S(1)}, bf16[16,256]{1,0:T(8,128)(2,1)S(1)}, u32[]{:S(2)}, u32[]{:S(2)}) collective-permute-start(bf16[16,256]{1,0:T(8,128)(2,1)S(1)} %get-tuple-element.61.numbers), channel_id=1, source_target_pairs={{0,1},{1,3},{4,5},{5,7},{8,9},{9,11},{12,13},{13,15},{2,4},{3,6},{... | collective-permute-start | bytes 24584 | tf_op jit(solution)/shard_map/ppermute | solution.py:530
  31.8 1.6 %prepare.1 = (bf16[32,128,128]{2,1,0:T(8,128)(2,1)S(1)}, bf16[256,256]{1,0:T(8,128)(2,1)S(1)}, bf16[256,256]{1,0:T(8,128)(2,1)S(1)}, bf16[256,256]{1,0:T(8,128)(2,1)S(1)}) custom-call(bf16[16,128,128]{2,1,0:T(8,128)(2,1)S(1)} %copy-done.1, bf16[256,256]{1,0:T(8,128)(2,1)S(1)} %copy-done.2, bf16[256,256]{1,0:T(8,128)(2,1)S(1)} %copy-done.3), custom_call_target="tpu_custom_call" | custom-call | tf_op jit(solution)/shard_map/prepare/pallas_call | solution.py:565
  33.5 2.7 %first_edge.1 = (s32[20,128]{1,0:T(8,128)S(1)}, bf16[6,1280,256]{2,1,0:T(8,128)(2,1)S(1)}, bf16[6,1280,256]{2,1,0:T(8,128)(2,1)S(1)}, bf16[4,1024,256]{2,1,0:T(8...) custom-call(bf16[16,256]{1,0:T(8,128)(2,1)S(1)} %get-tuple-element.61.num, ...), custom_call_target="tpu_custom_call" | custom-call | flops 1207959552 | bytes 4718592 | tf_op jit(solution)/shard_map/first_edge/pallas_call | solution.py:607
  36.2 0.7 collective-permute-start.7
  36.9 3.0 %collective-permute-start.8 = (bf16[1024,256]{1,0:T(8,128)(2,1)S(1)}, bf16[1024,256]{1,0:T(8,128)(2,1)S(1)}, u32[]{:S(2)}, u32[]{:S(2)}) collective-permute-start(bf16[1024,256]{1,0:T(8,128)(2,1)S(1)} %get-tuple-element.71), channel_id=1, source_target_pairs={{1,0},{0,1},{3,2},{2,3},{5,4},{4,5},{7,6},{6,7},{9,8},{8,9},{11,10... | collective-permute-start | bytes 1572872 | tf_op jit(solution)/shard_map/ppermute | solution.py:530
  39.9 2.1 %collective-permute-start.9 = (bf16[512,256]{1,0:T(8,128)(2,1)S(1)}, bf16[512,256]{1,0:T(8,128)(2,1)S(1)}, u32[]{:S(2)}, u32[]{:S(2)}) collective-permute-start(bf16[512,256]{1,0:T(8,128)(2,1)S(1)} %get-tuple-element.72), channel_id=1, source_target_pairs={{2,0},{3,1},{0,2},{1,3},{6,4},{7,5},{4,6},{5,7},{10,8},{11,9},{8,1... | collective-permute-start | bytes 786440 | tf_op jit(solution)/shard_map/ppermute | solution.py:530
  42.1 5.4 %inner_forward.1 = (bf16[6,1280,256]{2,1,0:T(8,128)(2,1)S(1)}, bf16[4,1024,256]{2,1,0:T(8,128)(2,1)S(1)}, bf16[4,1024,256]{2,1,0:T(8,128)(2,1)S(1)}, bf16[4,1024...) custom-call(s32[20,128]{1,0:T(8,128)S(1)} %get-tuple-element.69.tabl, ...), custom_call_target="tpu_custom_call", output_to_operand_aliasing={{0}: (10, {}), {1}: (11, {})} | custom-call | flops 3019898880 | bytes 11534336 | tf_op jit(solution)/shard_map/inner_forward/pallas_call | solution.py:625
  47.5 1.0 %collective-permute-done.9.side = bf16[512,256]{1,0:T(8,128)(2,1)S(1)} collective-permute-done((bf16[512,256]{1,0:T(8,128)(2,1)S(1)}, bf16[512,256]{1,0:T(8,128)(2,1)S(1)}, u32[]{:S(2)}, u32[]{:S(2)}) %collective-permute-start.9) | collective-permute-done | bytes 262176 | tf_op jit(solution)/shard_map/ppermute | solution.py:530
  48.5 3.0 %second_edge.1 = (bf16[4,1024,256]{2,1,0:T(8,128)(2,1)S(1)}, bf16[4,1024,256]{2,1,0:T(8,128)(2,1)S(1)}, bf16[6,1280,256]{2,1,0:T(8,128)(2,1)S(1)}, f32[4,8,128]{...) custom-call(s32[20,128]{1,0:T(8,128)S(1)} %get-tuple-element.69.tabl, ...), custom_call_target="tpu_custom_call", output_to_operand_aliasing={{0}: (12, {}), {1}: (13, {}), {2}: (14, {}), {3}: (15, {}),... | custom-call | flops 805306368 | bytes 5242880 | tf_op jit(solution)/shard_map/second_edge/pallas_call | solution.py:636
  51.5 0.9 %collective-permute-start.10 = (bf16[1024,256]{1,0:T(8,128)(2,1)S(1)}, bf16[1024,256]{1,0:T(8,128)(2,1)S(1)}, u32[]{:S(2)}, u32[]{:S(2)}) collective-permute-start(bf16[1024,256]{1,0:T(8,128)(2,1)S(1)} %get-tuple-element.86), channel_id=1, source_target_pairs={{1,4},{3,6},{5,8},{7,10},{9,12},{11,14},{4,1},{6,3},{8,5},{10,7},{... | collective-permute-start | bytes 1572872 | tf_op jit(solution)/shard_map/ppermute | solution.py:530
  52.4 3.0 %collective-permute-start.11 = (bf16[1024,256]{1,0:T(8,128)(2,1)S(1)}, bf16[1024,256]{1,0:T(8,128)(2,1)S(1)}, u32[]{:S(2)}, u32[]{:S(2)}) collective-permute-start(bf16[1024,256]{1,0:T(8,128)(2,1)S(1)} %get-tuple-element.87), channel_id=1, source_target_pairs={{1,0},{0,1},{3,2},{2,3},{5,4},{4,5},{7,6},{6,7},{9,8},{8,9},{11,10... | collective-permute-start | bytes 1572872 | tf_op jit(solution)/shard_map/ppermute | solution.py:530
  55.3 1.7 %collective-permute-start.12 = (bf16[512,256]{1,0:T(8,128)(2,1)S(1)}, bf16[512,256]{1,0:T(8,128)(2,1)S(1)}, u32[]{:S(2)}, u32[]{:S(2)}) collective-permute-start(bf16[512,256]{1,0:T(8,128)(2,1)S(1)} %get-tuple-element.88), channel_id=1, source_target_pairs={{2,0},{3,1},{0,2},{1,3},{6,4},{7,5},{4,6},{5,7},{10,8},{11,9},{8,1... | collective-permute-start | bytes 786440 | tf_op jit(solution)/shard_map/ppermute | solution.py:530
  57.1 4.9 %back_inner.1 = (f32[256,256]{1,0:T(8,128)S(1)}, f32[256,256]{1,0:T(8,128)S(1)}, f32[2304,256]{1,0:T(8,128)S(1)}, f32[2304,256]{1,0:T(8,128)S(1)}, bf16[256,2304]{1,0:T(8,128)(2,1)S(1)}) custom-call(s32[20,128]{1,0:T(8,128)S(1)} %get-tuple-element.69.table, bf16[6,1280,256]{2,1,0:T(8,128)(2,1)S(1)} %get-tuple-element.90.g_field, ...), custom_call_target="tpu_custom_call" | custom-call | flops 3221225472 | bytes 16777216 | tf_op jit(solution)/shard_map/back_inner/pallas_call | solution.py:649
  62.0 1.7 %collective-permute-done.12.side = bf16[512,256]{1,0:T(8,128)(2,1)S(1)} collective-permute-done((bf16[512,256]{1,0:T(8,128)(2,1)S(1)}, bf16[512,256]{1,0:T(8,128)(2,1)S(1)}, u32[]{:S(2)}, u32[]{:S(2)}) %collective-permute-start.12) | collective-permute-done | bytes 262176 | tf_op jit(solution)/shard_map/ppermute | solution.py:530
  63.6 1.8 %back_edge.1 = (f32[264,256]{1,0:T(8,128)S(1)}, f32[280,256]{1,0:T(8,128)S(1)}) custom-call(s32[20,128]{1,0:T(8,128)S(1)} %get-tuple-element.69.table, bf16[1024,256]{1,0:T(8,128)(2,1)S(1)} %collective-permute-done.10.outer, bf16[1024,256]{1,0:T(8,128)(2,1)S(1)} %collective-permute-done.11.inner, bf16[512,256]{1,0:T(8,128)(2,1)S(1)} %collective-permute-done.12.side, ...), custom_call_target="tpu_custom_call" | custom-call | flops 503316480 | bytes 2883584 | tf_op jit(solution)/shard_map/back_edge/pallas_call | solution.py:660
  65.5 1.6 %collective-permute-done.13.refs_0_ = f32[280,256]{1,0:T(8,128)S(1)} collective-permute-done((f32[280,256]{1,0:T(8,128)S(1)}, f32[280,256]{1,0:T(8,128)S(1)}, u32[]{:S(2)}, u32[]{:S(2)}) %collective-permute-start.13) | collective-permute-done | bytes 286752 | tf_op jit(solution)/shard_map/ppermute | solution.py:487
  67.1 1.8 %collective-permute-start.14 = (f32[152,256]{1,0:T(8,128)S(1)}, f32[152,256]{1,0:T(8,128)S(1)}, u32[]{:S(2)}, u32[]{:S(2)}) collective-permute-start(f32[152,256]{1,0:T(8,128)S(1)} %get-tuple-element.103), channel_id=1, source_target_pairs={{0,2},{1,3},{2,0},{3,1},{4,6},{5,7},{6,4},{7,5},{8,10},{9,11},{10,... | collective-permute-start | bytes 466952 | tf_op jit(solution)/shard_map/ppermute | solution.py:487
  68.9 4.3 %collective-permute-done.14.refs_0_ = f32[152,256]{1,0:T(8,128)S(1)} collective-permute-done((f32[152,256]{1,0:T(8,128)S(1)}, f32[152,256]{1,0:T(8,128)S(1)}, u32[]{:S(2)}, u32[]{:S(2)}) %collective-permute-start.14) | collective-permute-done | bytes 155680 | tf_op jit(solution)/shard_map/ppermute | solution.py:487
  73.9 1.6 %collective-permute-start.15 = (f32[40,256]{1,0:T(8,128)S(1)}, f32[40,256]{1,0:T(8,128)S(1)}, u32[]{:S(2)}, u32[]{:S(2)}) collective-permute-start(f32[40,256]{1,0:T(8,128)S(1)} %get-tuple-element.106), channel_id=1, source_target_pairs={{0,4},{1,5},{2,6},{3,7},{4,0},{5,1},{6,2},{7,3},{8,12},{9,13},{10,... | collective-permute-start | bytes 122888 | tf_op jit(solution)/shard_map/ppermute | solution.py:487
  75.4 1.0 %collective-permute-start.16 = (f32[40,256]{1,0:T(8,128)S(1)}, f32[40,256]{1,0:T(8,128)S(1)}, u32[]{:S(2)}, u32[]{:S(2)}) collective-permute-start(f32[40,256]{1,0:T(8,128)S(1)} %get-tuple-element.107), channel_id=1, source_target_pairs={{0,8},{1,9},{2,10},{3,11},{4,12},{5,13},{6,14},{7,15},{8,0},{9,1},... | collective-permute-start | bytes 122888 | tf_op jit(solution)/shard_map/ppermute | solution.py:487
  76.4 1.8 %collective-permute-start.17 = (f32[40,256]{1,0:T(8,128)S(1)}, f32[40,256]{1,0:T(8,128)S(1)}, u32[]{:S(2)}, u32[]{:S(2)}) collective-permute-start(f32[40,256]{1,0:T(8,128)S(1)} %get-tuple-element.108), channel_id=1, source_target_pairs={{0,12},{1,13},{2,14},{3,15},{4,8},{5,9},{6,10},{7,11},{8,4},{9,5},... | collective-permute-start | bytes 122888 | tf_op jit(solution)/shard_map/ppermute | solution.py:487
  78.3 2.6 %collective-permute-done.16.refs_1_ = f32[40,256]{1,0:T(8,128)S(1)} collective-permute-done((f32[40,256]{1,0:T(8,128)S(1)}, f32[40,256]{1,0:T(8,128)S(1)}, u32[]{:S(2)}, u32[]{:S(2)}) %collective-permute-start.16) | collective-permute-done | bytes 40992 | tf_op jit(solution)/shard_map/ppermute | solution.py:487
  80.9 1.3 %collective-permute-done.17.refs_2_ = f32[40,256]{1,0:T(8,128)S(1)} collective-permute-done((f32[40,256]{1,0:T(8,128)S(1)}, f32[40,256]{1,0:T(8,128)S(1)}, u32[]{:S(2)}, u32[]{:S(2)}) %collective-permute-start.17) | collective-permute-done | bytes 40992 | tf_op jit(solution)/shard_map/ppermute | solution.py:487
  (32 shorter events, 2.1 us)
Async XLA Ops:
  0.6 2.9 %copy-start = (bf16[4,8,128,256]{3,2,1,0:T(8,128)(2,1)S(1)}, bf16[4,8,128,256]{3,2,1,0:T(8,128)(2,1)}, u32[]{:S(2)}) copy-start(bf16[4,8,128,256]{3,2,1,0:T(8,128)(2,1)} %param.7) | copy-start | bytes 6291460
  2.1 16.9 %collective-permute-start = (bf16[2048,256]{1,0:T(8,128)(2,1)S(1)}, bf16[2048,256]{1,0:T(8,128)(2,1)S(1)}, u32[]{:S(2)}, u32[]{:S(2)}) collective-permute-start(bf16[2048,256]{1,0:T(8,128)(2,1)S(1)} %bitcast.10), channel_id=1, source_target_pairs={{2,1},{1,2},{6,5},{5,6},{10,9},{9,10},{14,13},{13,14},{18,17},{17,... | collective-permute-start | bytes 3145736 | tf_op jit(solution)/shard_map/ppermute | solution.py:530
  4.0 20.6 %copy-start.4 = (f32[4,8,128]{2,1,0:T(8,128)S(1)}, f32[4,8,128]{2,1,0:T(8,128)}, u32[]{:S(2)}) copy-start(f32[4,8,128]{2,1,0:T(8,128)} %target.1) | copy-start | bytes 49156
  4.0 27.8 %copy-start.1 = (bf16[16,128,128]{2,1,0:T(8,128)(2,1)S(1)}, bf16[16,128,128]{2,1,0:T(8,128)(2,1)}, u32[]{:S(2)}) copy-start(bf16[16,128,128]{2,1,0:T(8,128)(2,1)} %tiles) | copy-start | bytes 1572868
  4.0 27.8 %copy-start.2 = (bf16[256,256]{1,0:T(8,128)(2,1)S(1)}, bf16[256,256]{1,0:T(8,128)(2,1)}, u32[]{:S(2)}) copy-start(bf16[256,256]{1,0:T(8,128)(2,1)} %first) | copy-start | bytes 393220
  4.0 27.8 %copy-start.3 = (bf16[256,256]{1,0:T(8,128)(2,1)S(1)}, bf16[256,256]{1,0:T(8,128)(2,1)}, u32[]{:S(2)}) copy-start(bf16[256,256]{1,0:T(8,128)(2,1)} %second) | copy-start | bytes 393220
  4.1 29.4 %collective-permute-start.3 = (bf16[2064,256]{1,0:T(8,128)(2,1)S(1)}, bf16[2064,256]{1,0:T(8,128)(2,1)S(1)}, u32[]{:S(2)}, u32[]{:S(2)}) collective-permute-start(bf16[2064,256]{1,0:T(8,128)(2,1)S(1)} %pack_middle.1), channel_id=1, source_target_pairs={{2,1},{1,2},{6,5},{5,6},{10,9},{9,10},{14,13},{13,14},{18,17},{17,... | collective-permute-start | bytes 3170312 | tf_op jit(solution)/shard_map/ppermute | solution.py:530
  4.9 14.0 %collective-permute-start.1 = (bf16[528,256]{1,0:T(8,128)(2,1)S(1)}, bf16[528,256]{1,0:T(8,128)(2,1)S(1)}, u32[]{:S(2)}, u32[]{:S(2)}) collective-permute-start(bf16[528,256]{1,0:T(8,128)(2,1)S(1)} %get-tuple-element.59), channel_id=1, source_target_pairs={{1,0},{3,1},{0,2},{2,3},{5,4},{7,5},{4,6},{6,7},{9,8},{11,9},{8,10... | collective-permute-start | bytes 811016 | tf_op jit(solution)/shard_map/ppermute | solution.py:530
  19.1 14.4 %collective-permute-start.4 = (bf16[1024,256]{1,0:T(8,128)(2,1)S(1)}, bf16[1024,256]{1,0:T(8,128)(2,1)S(1)}, u32[]{:S(2)}, u32[]{:S(2)}) collective-permute-start(bf16[1024,256]{1,0:T(8,128)(2,1)S(1)} %get-tuple-element.62), channel_id=1, source_target_pairs={{1,4},{3,6},{5,8},{7,10},{9,12},{11,14},{4,1},{6,3},{8,5},{10,7},{... | collective-permute-start | bytes 1572872 | tf_op jit(solution)/shard_map/ppermute | solution.py:530
  19.8 13.7 %collective-permute-start.5 = (bf16[1024,256]{1,0:T(8,128)(2,1)S(1)}, bf16[1024,256]{1,0:T(8,128)(2,1)S(1)}, u32[]{:S(2)}, u32[]{:S(2)}) collective-permute-start(bf16[1024,256]{1,0:T(8,128)(2,1)S(1)} %get-tuple-element.60), channel_id=1, source_target_pairs={{1,0},{0,1},{3,2},{2,3},{5,4},{4,5},{7,6},{6,7},{9,8},{8,9},{11,10... | collective-permute-start | bytes 1572872 | tf_op jit(solution)/shard_map/ppermute | solution.py:530
  24.6 8.9 %collective-permute-start.6 = (f32[4,8,128]{2,1,0:T(8,128)S(1)}, f32[4,8,128]{2,1,0:T(8,128)S(1)}, u32[]{:S(2)}, u32[]{:S(2)}) collective-permute-start(f32[4,8,128]{2,1,0:T(8,128)S(1)} %copy-done.4), channel_id=1, source_target_pairs={{2,1},{1,2},{6,5},{5,6},{10,9},{9,10},{14,13},{13,14},{18,17},{17,... | collective-permute-start | bytes 49160 | tf_op jit(solution)/shard_map/ppermute | solution.py:530
  25.2 8.2 %collective-permute-start.2 = (bf16[16,256]{1,0:T(8,128)(2,1)S(1)}, bf16[16,256]{1,0:T(8,128)(2,1)S(1)}, u32[]{:S(2)}, u32[]{:S(2)}) collective-permute-start(bf16[16,256]{1,0:T(8,128)(2,1)S(1)} %get-tuple-element.61.numbers), channel_id=1, source_target_pairs={{0,1},{1,3},{4,5},{5,7},{8,9},{9,11},{12,13},{13,15},{2,4},{3,6},{... | collective-permute-start | bytes 24584 | tf_op jit(solution)/shard_map/ppermute | solution.py:530
  33.5 6.4 %copy-start.5 = (bf16[256]{0:T(256)(128)(2,1)S(1)}, bf16[256]{0:T(256)(128)(2,1)}, u32[]{:S(2)}) copy-start(bf16[256]{0:T(256)(128)(2,1)} %param.12) | copy-start | bytes 1540
  36.2 12.3 %collective-permute-start.7 = (bf16[1024,256]{1,0:T(8,128)(2,1)S(1)}, bf16[1024,256]{1,0:T(8,128)(2,1)S(1)}, u32[]{:S(2)}, u32[]{:S(2)}) collective-permute-start(bf16[1024,256]{1,0:T(8,128)(2,1)S(1)} %get-tuple-element.70), channel_id=1, source_target_pairs={{1,4},{3,6},{5,8},{7,10},{9,12},{11,14},{4,1},{6,3},{8,5},{10,7},{... | collective-permute-start | bytes 1572872 | tf_op jit(solution)/shard_map/ppermute | solution.py:530
  36.9 11.6 %collective-permute-start.8 = (bf16[1024,256]{1,0:T(8,128)(2,1)S(1)}, bf16[1024,256]{1,0:T(8,128)(2,1)S(1)}, u32[]{:S(2)}, u32[]{:S(2)}) collective-permute-start(bf16[1024,256]{1,0:T(8,128)(2,1)S(1)} %get-tuple-element.71), channel_id=1, source_target_pairs={{1,0},{0,1},{3,2},{2,3},{5,4},{4,5},{7,6},{6,7},{9,8},{8,9},{11,10... | collective-permute-start | bytes 1572872 | tf_op jit(solution)/shard_map/ppermute | solution.py:530
  39.9 8.6 %collective-permute-start.9 = (bf16[512,256]{1,0:T(8,128)(2,1)S(1)}, bf16[512,256]{1,0:T(8,128)(2,1)S(1)}, u32[]{:S(2)}, u32[]{:S(2)}) collective-permute-start(bf16[512,256]{1,0:T(8,128)(2,1)S(1)} %get-tuple-element.72), channel_id=1, source_target_pairs={{2,0},{3,1},{0,2},{1,3},{6,4},{7,5},{4,6},{5,7},{10,8},{11,9},{8,1... | collective-permute-start | bytes 786440 | tf_op jit(solution)/shard_map/ppermute | solution.py:530
  51.5 12.1 %collective-permute-start.10 = (bf16[1024,256]{1,0:T(8,128)(2,1)S(1)}, bf16[1024,256]{1,0:T(8,128)(2,1)S(1)}, u32[]{:S(2)}, u32[]{:S(2)}) collective-permute-start(bf16[1024,256]{1,0:T(8,128)(2,1)S(1)} %get-tuple-element.86), channel_id=1, source_target_pairs={{1,4},{3,6},{5,8},{7,10},{9,12},{11,14},{4,1},{6,3},{8,5},{10,7},{... | collective-permute-start | bytes 1572872 | tf_op jit(solution)/shard_map/ppermute | solution.py:530
  52.4 11.3 %collective-permute-start.11 = (bf16[1024,256]{1,0:T(8,128)(2,1)S(1)}, bf16[1024,256]{1,0:T(8,128)(2,1)S(1)}, u32[]{:S(2)}, u32[]{:S(2)}) collective-permute-start(bf16[1024,256]{1,0:T(8,128)(2,1)S(1)} %get-tuple-element.87), channel_id=1, source_target_pairs={{1,0},{0,1},{3,2},{2,3},{5,4},{4,5},{7,6},{6,7},{9,8},{8,9},{11,10... | collective-permute-start | bytes 1572872 | tf_op jit(solution)/shard_map/ppermute | solution.py:530
  55.3 8.3 %collective-permute-start.12 = (bf16[512,256]{1,0:T(8,128)(2,1)S(1)}, bf16[512,256]{1,0:T(8,128)(2,1)S(1)}, u32[]{:S(2)}, u32[]{:S(2)}) collective-permute-start(bf16[512,256]{1,0:T(8,128)(2,1)S(1)} %get-tuple-element.88), channel_id=1, source_target_pairs={{2,0},{3,1},{0,2},{1,3},{6,4},{7,5},{4,6},{5,7},{10,8},{11,9},{8,1... | collective-permute-start | bytes 786440 | tf_op jit(solution)/shard_map/ppermute | solution.py:530
  65.4 1.6 %collective-permute-start.13 = (f32[280,256]{1,0:T(8,128)S(1)}, f32[280,256]{1,0:T(8,128)S(1)}, u32[]{:S(2)}, u32[]{:S(2)}) collective-permute-start(f32[280,256]{1,0:T(8,128)S(1)} %get-tuple-element.101), channel_id=1, source_target_pairs={{0,1},{1,0},{2,3},{3,2},{4,5},{5,4},{6,7},{7,6},{8,9},{9,8},{10,11... | collective-permute-start | bytes 860168 | tf_op jit(solution)/shard_map/ppermute | solution.py:487
  67.1 6.1 %collective-permute-start.14 = (f32[152,256]{1,0:T(8,128)S(1)}, f32[152,256]{1,0:T(8,128)S(1)}, u32[]{:S(2)}, u32[]{:S(2)}) collective-permute-start(f32[152,256]{1,0:T(8,128)S(1)} %get-tuple-element.103), channel_id=1, source_target_pairs={{0,2},{1,3},{2,0},{3,1},{4,6},{5,7},{6,4},{7,5},{8,10},{9,11},{10,... | collective-permute-start | bytes 466952 | tf_op jit(solution)/shard_map/ppermute | solution.py:487
  73.9 4.4 %collective-permute-start.15 = (f32[40,256]{1,0:T(8,128)S(1)}, f32[40,256]{1,0:T(8,128)S(1)}, u32[]{:S(2)}, u32[]{:S(2)}) collective-permute-start(f32[40,256]{1,0:T(8,128)S(1)} %get-tuple-element.106), channel_id=1, source_target_pairs={{0,4},{1,5},{2,6},{3,7},{4,0},{5,1},{6,2},{7,3},{8,12},{9,13},{10,... | collective-permute-start | bytes 122888 | tf_op jit(solution)/shard_map/ppermute | solution.py:487
  75.4 5.4 %collective-permute-start.16 = (f32[40,256]{1,0:T(8,128)S(1)}, f32[40,256]{1,0:T(8,128)S(1)}, u32[]{:S(2)}, u32[]{:S(2)}) collective-permute-start(f32[40,256]{1,0:T(8,128)S(1)} %get-tuple-element.107), channel_id=1, source_target_pairs={{0,8},{1,9},{2,10},{3,11},{4,12},{5,13},{6,14},{7,15},{8,0},{9,1},... | collective-permute-start | bytes 122888 | tf_op jit(solution)/shard_map/ppermute | solution.py:487
  76.4 5.8 %collective-permute-start.17 = (f32[40,256]{1,0:T(8,128)S(1)}, f32[40,256]{1,0:T(8,128)S(1)}, u32[]{:S(2)}, u32[]{:S(2)}) collective-permute-start(f32[40,256]{1,0:T(8,128)S(1)} %get-tuple-element.108), channel_id=1, source_target_pairs={{0,12},{1,13},{2,14},{3,15},{4,8},{5,9},{6,10},{7,11},{8,4},{9,5},... | collective-permute-start | bytes 122888 | tf_op jit(solution)/shard_map/ppermute | solution.py:487

commit v10 on v9

--- a/solution.py
+++ b/solution.py
@@ -477,7 +477,7 @@
 
 
 def sum_shares(outs, preds, count, share, width, riding, params):
-    radices, left = [2, 2], count // 4
+    radices, left = [2, 4], count // 8
     while left > 1:
         radices.append(min(4, left))
         left //= radices[-1]

time: 83.2 us -> 82.5 us (level)
  starting transfers between devices: 38.9 us -> 37 us
  waiting for transfers between devices: 19.5 us -> 20.8 us
    ppermute x5, starting transfers between devices: 6.26 us -> 4.29 us  [sum_shares(): lax.ppermute(outs[k], AXES, [(i, i ^ k * base) for i in range(count)])]
    ppermute x5, waiting for transfers between devices: 9.84 us -> 11.2 us  [sum_shares(): lax.ppermute(outs[k], AXES, [(i, i ^ k * base) for i in range(count)])]
where the time goes in v10:
time: 82.5 us; the launch traced here: 82.2 us
  starting transfers between devices  37 us (45%)
  Pallas kernels  21.3 us (26%)
  waiting for transfers between devices  20.8 us (25%)
  local copies, waits for them, and re-layouts  1.58 us (2%)
  between operations  0.89 us (1%)
    ppermute x13, starting transfers between devices, send(): return lax.ppermute(value, AXES, way)  32.7 us
    ppermute x5, waiting for transfers between devices, sum_shares(): lax.ppermute(outs[k], AXES, [(i, i ^ k * base) for i in range(count)])  11.2 us
    ppermute x13, waiting for transfers between devices, send(): return lax.ppermute(value, AXES, way)  9.64 us
    pallas_call x1, Pallas kernels, per_device(): pl.pallas_call(functools.partial(middle_compute_kernel, shape, scale), ou...  5.44 us
    pallas_call x1, Pallas kernels, per_device(): pl.pallas_call(functools.partial(back_inner_kernel, shape, scale), out_sh...  4.88 us
    ppermute x5, starting transfers between devices, sum_shares(): lax.ppermute(outs[k], AXES, [(i, i ^ k * base) for i in range(count)])  4.29 us
    pallas_call x1, Pallas kernels, per_device(): pl.pallas_call(functools.partial(second_edge_kernel, shape, scale), out_s...  2.96 us
    pallas_call x1, Pallas kernels, per_device(): pl.pallas_call(functools.partial(first_edge_kernel, shape), out_shape=(ja...  2.7 us
  transfers between devices with their start and end apart: 18, of which 7 were waited for; matrix products, arithmetic and copies ran while one was open for 1% of the time, Pallas kernels for 15%

profile of v10, /device:TPU:0, one launch (start us, length us, event | category | flops | bytes accessed | tf_op | source)
XLA Modules:
  0.0 82.2 jit_solution(11156703769787827101)
XLA Ops:
  0.6 1.4 %slice.3 = bf16[2,1024,256]{2,1,0:T(8,128)(2,1)S(1)} slice(bf16[4,1024,256]{2,1,0:T(8,128)(2,1)} %bitcast.5), slice={[0:4:3], [0:1024:1], [0:256:1]} | slice | bytes 2097152 | tf_op jit(solution)/shard_map/slice | solution.py:542
  2.1 0.7 collective-permute-start
  2.8 0.7 convert_bitcast_fusion.ids
  4.1 0.9 %collective-permute-start.3 = (bf16[2064,256]{1,0:T(8,128)(2,1)S(1)}, bf16[2064,256]{1,0:T(8,128)(2,1)S(1)}, u32[]{:S(2)}, u32[]{:S(2)}) collective-permute-start(bf16[2064,256]{1,0:T(8,128)(2,1)S(1)} %pack_middle.1), channel_id=1, source_target_pairs={{2,1},{1,2},{6,5},{5,6},{10,9},{9,10},{14,13},{13,14},{18,17},{17,... | collective-permute-start | bytes 3170312 | tf_op jit(solution)/shard_map/ppermute | solution.py:530
  4.9 7.1 %collective-permute-start.1 = (bf16[528,256]{1,0:T(8,128)(2,1)S(1)}, bf16[528,256]{1,0:T(8,128)(2,1)S(1)}, u32[]{:S(2)}, u32[]{:S(2)}) collective-permute-start(bf16[528,256]{1,0:T(8,128)(2,1)S(1)} %get-tuple-element.59), channel_id=1, source_target_pairs={{1,0},{3,1},{0,2},{2,3},{5,4},{7,5},{4,6},{6,7},{9,8},{11,9},{8,10... | collective-permute-start | bytes 811016 | tf_op jit(solution)/shard_map/ppermute | solution.py:530
  12.0 6.9 %collective-permute-done.1.after.side = bf16[528,256]{1,0:T(8,128)(2,1)S(1)} collective-permute-done((bf16[528,256]{1,0:T(8,128)(2,1)S(1)}, bf16[528,256]{1,0:T(8,128)(2,1)S(1)}, u32[]{:S(2)}, u32[]{:S(2)}) %collective-permute-start.1) | collective-permute-done | bytes 270368 | tf_op jit(solution)/shard_map/ppermute | solution.py:530
  19.1 0.7 collective-permute-start.4
  19.8 4.8 %collective-permute-start.5 = (bf16[1024,256]{1,0:T(8,128)(2,1)S(1)}, bf16[1024,256]{1,0:T(8,128)(2,1)S(1)}, u32[]{:S(2)}, u32[]{:S(2)}) collective-permute-start(bf16[1024,256]{1,0:T(8,128)(2,1)S(1)} %get-tuple-element.60), channel_id=1, source_target_pairs={{1,0},{0,1},{3,2},{2,3},{5,4},{4,5},{7,6},{6,7},{9,8},{8,9},{11,10... | collective-permute-start | bytes 1572872 | tf_op jit(solution)/shard_map/ppermute | solution.py:530
  24.6 0.7 collective-permute-start.6
  25.2 6.6 %collective-permute-start.2 = (bf16[16,256]{1,0:T(8,128)(2,1)S(1)}, bf16[16,256]{1,0:T(8,128)(2,1)S(1)}, u32[]{:S(2)}, u32[]{:S(2)}) collective-permute-start(bf16[16,256]{1,0:T(8,128)(2,1)S(1)} %get-tuple-element.61.numbers), channel_id=1, source_target_pairs={{0,1},{1,3},{4,5},{5,7},{8,9},{9,11},{12,13},{13,15},{2,4},{3,6},{... | collective-permute-start | bytes 24584 | tf_op jit(solution)/shard_map/ppermute | solution.py:530
  31.8 1.6 %prepare.1 = (bf16[32,128,128]{2,1,0:T(8,128)(2,1)S(1)}, bf16[256,256]{1,0:T(8,128)(2,1)S(1)}, bf16[256,256]{1,0:T(8,128)(2,1)S(1)}, bf16[256,256]{1,0:T(8,128)(2,1)S(1)}) custom-call(bf16[16,128,128]{2,1,0:T(8,128)(2,1)S(1)} %copy-done.1, bf16[256,256]{1,0:T(8,128)(2,1)S(1)} %copy-done.2, bf16[256,256]{1,0:T(8,128)(2,1)S(1)} %copy-done.3), custom_call_target="tpu_custom_call" | custom-call | tf_op jit(solution)/shard_map/prepare/pallas_call | solution.py:565
  33.5 2.7 %first_edge.1 = (s32[20,128]{1,0:T(8,128)S(1)}, bf16[6,1280,256]{2,1,0:T(8,128)(2,1)S(1)}, bf16[6,1280,256]{2,1,0:T(8,128)(2,1)S(1)}, bf16[4,1024,256]{2,1,0:T(8...) custom-call(bf16[16,256]{1,0:T(8,128)(2,1)S(1)} %get-tuple-element.61.num, ...), custom_call_target="tpu_custom_call" | custom-call | flops 1207959552 | bytes 4718592 | tf_op jit(solution)/shard_map/first_edge/pallas_call | solution.py:607
  36.2 0.7 collective-permute-start.7
  36.9 3.0 %collective-permute-start.8 = (bf16[1024,256]{1,0:T(8,128)(2,1)S(1)}, bf16[1024,256]{1,0:T(8,128)(2,1)S(1)}, u32[]{:S(2)}, u32[]{:S(2)}) collective-permute-start(bf16[1024,256]{1,0:T(8,128)(2,1)S(1)} %get-tuple-element.71), channel_id=1, source_target_pairs={{1,0},{0,1},{3,2},{2,3},{5,4},{4,5},{7,6},{6,7},{9,8},{8,9},{11,10... | collective-permute-start | bytes 1572872 | tf_op jit(solution)/shard_map/ppermute | solution.py:530
  39.9 2.1 %collective-permute-start.9 = (bf16[512,256]{1,0:T(8,128)(2,1)S(1)}, bf16[512,256]{1,0:T(8,128)(2,1)S(1)}, u32[]{:S(2)}, u32[]{:S(2)}) collective-permute-start(bf16[512,256]{1,0:T(8,128)(2,1)S(1)} %get-tuple-element.72), channel_id=1, source_target_pairs={{2,0},{3,1},{0,2},{1,3},{6,4},{7,5},{4,6},{5,7},{10,8},{11,9},{8,1... | collective-permute-start | bytes 786440 | tf_op jit(solution)/shard_map/ppermute | solution.py:530
  42.1 5.4 %inner_forward.1 = (bf16[6,1280,256]{2,1,0:T(8,128)(2,1)S(1)}, bf16[4,1024,256]{2,1,0:T(8,128)(2,1)S(1)}, bf16[4,1024,256]{2,1,0:T(8,128)(2,1)S(1)}, bf16[4,1024...) custom-call(s32[20,128]{1,0:T(8,128)S(1)} %get-tuple-element.69.tabl, ...), custom_call_target="tpu_custom_call", output_to_operand_aliasing={{0}: (10, {}), {1}: (11, {})} | custom-call | flops 3019898880 | bytes 11534336 | tf_op jit(solution)/shard_map/inner_forward/pallas_call | solution.py:625
  47.5 1.0 %collective-permute-done.9.side = bf16[512,256]{1,0:T(8,128)(2,1)S(1)} collective-permute-done((bf16[512,256]{1,0:T(8,128)(2,1)S(1)}, bf16[512,256]{1,0:T(8,128)(2,1)S(1)}, u32[]{:S(2)}, u32[]{:S(2)}) %collective-permute-start.9) | collective-permute-done | bytes 262176 | tf_op jit(solution)/shard_map/ppermute | solution.py:530
  48.5 3.0 %second_edge.1 = (bf16[4,1024,256]{2,1,0:T(8,128)(2,1)S(1)}, bf16[4,1024,256]{2,1,0:T(8,128)(2,1)S(1)}, bf16[6,1280,256]{2,1,0:T(8,128)(2,1)S(1)}, f32[4,8,128]{...) custom-call(s32[20,128]{1,0:T(8,128)S(1)} %get-tuple-element.69.tabl, ...), custom_call_target="tpu_custom_call", output_to_operand_aliasing={{0}: (12, {}), {1}: (13, {}), {2}: (14, {}), {3}: (15, {}),... | custom-call | flops 805306368 | bytes 5242880 | tf_op jit(solution)/shard_map/second_edge/pallas_call | solution.py:636
  51.5 0.9 %collective-permute-start.10 = (bf16[1024,256]{1,0:T(8,128)(2,1)S(1)}, bf16[1024,256]{1,0:T(8,128)(2,1)S(1)}, u32[]{:S(2)}, u32[]{:S(2)}) collective-permute-start(bf16[1024,256]{1,0:T(8,128)(2,1)S(1)} %get-tuple-element.86), channel_id=1, source_target_pairs={{1,4},{3,6},{5,8},{7,10},{9,12},{11,14},{4,1},{6,3},{8,5},{10,7},{... | collective-permute-start | bytes 1572872 | tf_op jit(solution)/shard_map/ppermute | solution.py:530
  52.4 3.0 %collective-permute-start.11 = (bf16[1024,256]{1,0:T(8,128)(2,1)S(1)}, bf16[1024,256]{1,0:T(8,128)(2,1)S(1)}, u32[]{:S(2)}, u32[]{:S(2)}) collective-permute-start(bf16[1024,256]{1,0:T(8,128)(2,1)S(1)} %get-tuple-element.87), channel_id=1, source_target_pairs={{1,0},{0,1},{3,2},{2,3},{5,4},{4,5},{7,6},{6,7},{9,8},{8,9},{11,10... | collective-permute-start | bytes 1572872 | tf_op jit(solution)/shard_map/ppermute | solution.py:530
  55.3 1.7 %collective-permute-start.12 = (bf16[512,256]{1,0:T(8,128)(2,1)S(1)}, bf16[512,256]{1,0:T(8,128)(2,1)S(1)}, u32[]{:S(2)}, u32[]{:S(2)}) collective-permute-start(bf16[512,256]{1,0:T(8,128)(2,1)S(1)} %get-tuple-element.88), channel_id=1, source_target_pairs={{2,0},{3,1},{0,2},{1,3},{6,4},{7,5},{4,6},{5,7},{10,8},{11,9},{8,1... | collective-permute-start | bytes 786440 | tf_op jit(solution)/shard_map/ppermute | solution.py:530
  57.1 4.9 %back_inner.1 = (f32[256,256]{1,0:T(8,128)S(1)}, f32[256,256]{1,0:T(8,128)S(1)}, f32[2304,256]{1,0:T(8,128)S(1)}, f32[2304,256]{1,0:T(8,128)S(1)}, bf16[256,2304]{1,0:T(8,128)(2,1)S(1)}) custom-call(s32[20,128]{1,0:T(8,128)S(1)} %get-tuple-element.69.table, bf16[6,1280,256]{2,1,0:T(8,128)(2,1)S(1)} %get-tuple-element.90.g_field, ...), custom_call_target="tpu_custom_call" | custom-call | flops 3221225472 | bytes 16777216 | tf_op jit(solution)/shard_map/back_inner/pallas_call | solution.py:649
  62.0 1.7 %collective-permute-done.12.side = bf16[512,256]{1,0:T(8,128)(2,1)S(1)} collective-permute-done((bf16[512,256]{1,0:T(8,128)(2,1)S(1)}, bf16[512,256]{1,0:T(8,128)(2,1)S(1)}, u32[]{:S(2)}, u32[]{:S(2)}) %collective-permute-start.12) | collective-permute-done | bytes 262176 | tf_op jit(solution)/shard_map/ppermute | solution.py:530
  63.6 1.8 %back_edge.1 = (f32[264,256]{1,0:T(8,128)S(1)}, f32[280,256]{1,0:T(8,128)S(1)}) custom-call(s32[20,128]{1,0:T(8,128)S(1)} %get-tuple-element.69.table, bf16[1024,256]{1,0:T(8,128)(2,1)S(1)} %collective-permute-done.10.outer, bf16[1024,256]{1,0:T(8,128)(2,1)S(1)} %collective-permute-done.11.inner, bf16[512,256]{1,0:T(8,128)(2,1)S(1)} %collective-permute-done.12.side, ...), custom_call_target="tpu_custom_call" | custom-call | flops 503316480 | bytes 2883584 | tf_op jit(solution)/shard_map/back_edge/pallas_call | solution.py:660
  65.5 1.6 %collective-permute-done.13.refs_0_ = f32[280,256]{1,0:T(8,128)S(1)} collective-permute-done((f32[280,256]{1,0:T(8,128)S(1)}, f32[280,256]{1,0:T(8,128)S(1)}, u32[]{:S(2)}, u32[]{:S(2)}) %collective-permute-start.13) | collective-permute-done | bytes 286752 | tf_op jit(solution)/shard_map/ppermute | solution.py:487
  67.1 1.8 %collective-permute-start.14 = (f32[88,256]{1,0:T(8,128)S(1)}, f32[88,256]{1,0:T(8,128)S(1)}, u32[]{:S(2)}, u32[]{:S(2)}) collective-permute-start(f32[88,256]{1,0:T(8,128)S(1)} %get-tuple-element.103), channel_id=1, source_target_pairs={{0,2},{1,3},{2,0},{3,1},{4,6},{5,7},{6,4},{7,5},{8,10},{9,11},{10,... | collective-permute-start | bytes 270344 | tf_op jit(solution)/shard_map/ppermute | solution.py:487
  68.9 1.6 %collective-permute-start.15 = (f32[72,256]{1,0:T(8,128)S(1)}, f32[72,256]{1,0:T(8,128)S(1)}, u32[]{:S(2)}, u32[]{:S(2)}) collective-permute-start(f32[72,256]{1,0:T(8,128)S(1)} %get-tuple-element.104), channel_id=1, source_target_pairs={{0,4},{1,5},{2,6},{3,7},{4,0},{5,1},{6,2},{7,3},{8,12},{9,13},{10,... | collective-permute-start | bytes 221192 | tf_op jit(solution)/shard_map/ppermute | solution.py:487
  70.7 3.4 %collective-permute-done.15.refs_1_ = f32[72,256]{1,0:T(8,128)S(1)} collective-permute-done((f32[72,256]{1,0:T(8,128)S(1)}, f32[72,256]{1,0:T(8,128)S(1)}, u32[]{:S(2)}, u32[]{:S(2)}) %collective-permute-start.15) | collective-permute-done | bytes 73760 | tf_op jit(solution)/shard_map/ppermute | solution.py:487
  74.0 1.7 %collective-permute-done.16.refs_2_ = f32[72,256]{1,0:T(8,128)S(1)} collective-permute-done((f32[72,256]{1,0:T(8,128)S(1)}, f32[72,256]{1,0:T(8,128)S(1)}, u32[]{:S(2)}, u32[]{:S(2)}) %collective-permute-start.16) | collective-permute-done | bytes 73760 | tf_op jit(solution)/shard_map/ppermute | solution.py:487
  75.8 0.6 fold.3
  76.4 0.7 collective-permute-start.17
  77.0 4.6 %collective-permute-done.17.refs_0_ = f32[40,256]{1,0:T(8,128)S(1)} collective-permute-done((f32[40,256]{1,0:T(8,128)S(1)}, f32[40,256]{1,0:T(8,128)S(1)}, u32[]{:S(2)}, u32[]{:S(2)}) %collective-permute-start.17) | collective-permute-done | bytes 40992 | tf_op jit(solution)/shard_map/ppermute | solution.py:487
  (32 shorter events, 1.7 us)
Async XLA Ops:
  0.6 2.9 %copy-start = (bf16[4,8,128,256]{3,2,1,0:T(8,128)(2,1)S(1)}, bf16[4,8,128,256]{3,2,1,0:T(8,128)(2,1)}, u32[]{:S(2)}) copy-start(bf16[4,8,128,256]{3,2,1,0:T(8,128)(2,1)} %param.7) | copy-start | bytes 6291460
  2.1 16.9 %collective-permute-start = (bf16[2048,256]{1,0:T(8,128)(2,1)S(1)}, bf16[2048,256]{1,0:T(8,128)(2,1)S(1)}, u32[]{:S(2)}, u32[]{:S(2)}) collective-permute-start(bf16[2048,256]{1,0:T(8,128)(2,1)S(1)} %bitcast.10), channel_id=1, source_target_pairs={{2,1},{1,2},{6,5},{5,6},{10,9},{9,10},{14,13},{13,14},{18,17},{17,... | collective-permute-start | bytes 3145736 | tf_op jit(solution)/shard_map/ppermute | solution.py:530
  4.0 20.6 %copy-start.4 = (f32[4,8,128]{2,1,0:T(8,128)S(1)}, f32[4,8,128]{2,1,0:T(8,128)}, u32[]{:S(2)}) copy-start(f32[4,8,128]{2,1,0:T(8,128)} %target.1) | copy-start | bytes 49156
  4.0 27.8 %copy-start.1 = (bf16[16,128,128]{2,1,0:T(8,128)(2,1)S(1)}, bf16[16,128,128]{2,1,0:T(8,128)(2,1)}, u32[]{:S(2)}) copy-start(bf16[16,128,128]{2,1,0:T(8,128)(2,1)} %tiles) | copy-start | bytes 1572868
  4.0 27.8 %copy-start.2 = (bf16[256,256]{1,0:T(8,128)(2,1)S(1)}, bf16[256,256]{1,0:T(8,128)(2,1)}, u32[]{:S(2)}) copy-start(bf16[256,256]{1,0:T(8,128)(2,1)} %first) | copy-start | bytes 393220
  4.0 27.8 %copy-start.3 = (bf16[256,256]{1,0:T(8,128)(2,1)S(1)}, bf16[256,256]{1,0:T(8,128)(2,1)}, u32[]{:S(2)}) copy-start(bf16[256,256]{1,0:T(8,128)(2,1)} %second) | copy-start | bytes 393220
  4.1 29.4 %collective-permute-start.3 = (bf16[2064,256]{1,0:T(8,128)(2,1)S(1)}, bf16[2064,256]{1,0:T(8,128)(2,1)S(1)}, u32[]{:S(2)}, u32[]{:S(2)}) collective-permute-start(bf16[2064,256]{1,0:T(8,128)(2,1)S(1)} %pack_middle.1), channel_id=1, source_target_pairs={{2,1},{1,2},{6,5},{5,6},{10,9},{9,10},{14,13},{13,14},{18,17},{17,... | collective-permute-start | bytes 3170312 | tf_op jit(solution)/shard_map/ppermute | solution.py:530
  4.9 14.0 %collective-permute-start.1 = (bf16[528,256]{1,0:T(8,128)(2,1)S(1)}, bf16[528,256]{1,0:T(8,128)(2,1)S(1)}, u32[]{:S(2)}, u32[]{:S(2)}) collective-permute-start(bf16[528,256]{1,0:T(8,128)(2,1)S(1)} %get-tuple-element.59), channel_id=1, source_target_pairs={{1,0},{3,1},{0,2},{2,3},{5,4},{7,5},{4,6},{6,7},{9,8},{11,9},{8,10... | collective-permute-start | bytes 811016 | tf_op jit(solution)/shard_map/ppermute | solution.py:530
  19.1 14.4 %collective-permute-start.4 = (bf16[1024,256]{1,0:T(8,128)(2,1)S(1)}, bf16[1024,256]{1,0:T(8,128)(2,1)S(1)}, u32[]{:S(2)}, u32[]{:S(2)}) collective-permute-start(bf16[1024,256]{1,0:T(8,128)(2,1)S(1)} %get-tuple-element.62), channel_id=1, source_target_pairs={{1,4},{3,6},{5,8},{7,10},{9,12},{11,14},{4,1},{6,3},{8,5},{10,7},{... | collective-permute-start | bytes 1572872 | tf_op jit(solution)/shard_map/ppermute | solution.py:530
  19.8 13.7 %collective-permute-start.5 = (bf16[1024,256]{1,0:T(8,128)(2,1)S(1)}, bf16[1024,256]{1,0:T(8,128)(2,1)S(1)}, u32[]{:S(2)}, u32[]{:S(2)}) collective-permute-start(bf16[1024,256]{1,0:T(8,128)(2,1)S(1)} %get-tuple-element.60), channel_id=1, source_target_pairs={{1,0},{0,1},{3,2},{2,3},{5,4},{4,5},{7,6},{6,7},{9,8},{8,9},{11,10... | collective-permute-start | bytes 1572872 | tf_op jit(solution)/shard_map/ppermute | solution.py:530
  24.6 8.9 %collective-permute-start.6 = (f32[4,8,128]{2,1,0:T(8,128)S(1)}, f32[4,8,128]{2,1,0:T(8,128)S(1)}, u32[]{:S(2)}, u32[]{:S(2)}) collective-permute-start(f32[4,8,128]{2,1,0:T(8,128)S(1)} %copy-done.4), channel_id=1, source_target_pairs={{2,1},{1,2},{6,5},{5,6},{10,9},{9,10},{14,13},{13,14},{18,17},{17,... | collective-permute-start | bytes 49160 | tf_op jit(solution)/shard_map/ppermute | solution.py:530
  25.2 8.2 %collective-permute-start.2 = (bf16[16,256]{1,0:T(8,128)(2,1)S(1)}, bf16[16,256]{1,0:T(8,128)(2,1)S(1)}, u32[]{:S(2)}, u32[]{:S(2)}) collective-permute-start(bf16[16,256]{1,0:T(8,128)(2,1)S(1)} %get-tuple-element.61.numbers), channel_id=1, source_target_pairs={{0,1},{1,3},{4,5},{5,7},{8,9},{9,11},{12,13},{13,15},{2,4},{3,6},{... | collective-permute-start | bytes 24584 | tf_op jit(solution)/shard_map/ppermute | solution.py:530
  33.5 6.4 %copy-start.5 = (bf16[256]{0:T(256)(128)(2,1)S(1)}, bf16[256]{0:T(256)(128)(2,1)}, u32[]{:S(2)}) copy-start(bf16[256]{0:T(256)(128)(2,1)} %param.12) | copy-start | bytes 1540
  36.2 12.3 %collective-permute-start.7 = (bf16[1024,256]{1,0:T(8,128)(2,1)S(1)}, bf16[1024,256]{1,0:T(8,128)(2,1)S(1)}, u32[]{:S(2)}, u32[]{:S(2)}) collective-permute-start(bf16[1024,256]{1,0:T(8,128)(2,1)S(1)} %get-tuple-element.70), channel_id=1, source_target_pairs={{1,4},{3,6},{5,8},{7,10},{9,12},{11,14},{4,1},{6,3},{8,5},{10,7},{... | collective-permute-start | bytes 1572872 | tf_op jit(solution)/shard_map/ppermute | solution.py:530
  36.9 11.6 %collective-permute-start.8 = (bf16[1024,256]{1,0:T(8,128)(2,1)S(1)}, bf16[1024,256]{1,0:T(8,128)(2,1)S(1)}, u32[]{:S(2)}, u32[]{:S(2)}) collective-permute-start(bf16[1024,256]{1,0:T(8,128)(2,1)S(1)} %get-tuple-element.71), channel_id=1, source_target_pairs={{1,0},{0,1},{3,2},{2,3},{5,4},{4,5},{7,6},{6,7},{9,8},{8,9},{11,10... | collective-permute-start | bytes 1572872 | tf_op jit(solution)/shard_map/ppermute | solution.py:530
  39.9 8.6 %collective-permute-start.9 = (bf16[512,256]{1,0:T(8,128)(2,1)S(1)}, bf16[512,256]{1,0:T(8,128)(2,1)S(1)}, u32[]{:S(2)}, u32[]{:S(2)}) collective-permute-start(bf16[512,256]{1,0:T(8,128)(2,1)S(1)} %get-tuple-element.72), channel_id=1, source_target_pairs={{2,0},{3,1},{0,2},{1,3},{6,4},{7,5},{4,6},{5,7},{10,8},{11,9},{8,1... | collective-permute-start | bytes 786440 | tf_op jit(solution)/shard_map/ppermute | solution.py:530
  51.5 12.1 %collective-permute-start.10 = (bf16[1024,256]{1,0:T(8,128)(2,1)S(1)}, bf16[1024,256]{1,0:T(8,128)(2,1)S(1)}, u32[]{:S(2)}, u32[]{:S(2)}) collective-permute-start(bf16[1024,256]{1,0:T(8,128)(2,1)S(1)} %get-tuple-element.86), channel_id=1, source_target_pairs={{1,4},{3,6},{5,8},{7,10},{9,12},{11,14},{4,1},{6,3},{8,5},{10,7},{... | collective-permute-start | bytes 1572872 | tf_op jit(solution)/shard_map/ppermute | solution.py:530
  52.4 11.3 %collective-permute-start.11 = (bf16[1024,256]{1,0:T(8,128)(2,1)S(1)}, bf16[1024,256]{1,0:T(8,128)(2,1)S(1)}, u32[]{:S(2)}, u32[]{:S(2)}) collective-permute-start(bf16[1024,256]{1,0:T(8,128)(2,1)S(1)} %get-tuple-element.87), channel_id=1, source_target_pairs={{1,0},{0,1},{3,2},{2,3},{5,4},{4,5},{7,6},{6,7},{9,8},{8,9},{11,10... | collective-permute-start | bytes 1572872 | tf_op jit(solution)/shard_map/ppermute | solution.py:530
  55.3 8.3 %collective-permute-start.12 = (bf16[512,256]{1,0:T(8,128)(2,1)S(1)}, bf16[512,256]{1,0:T(8,128)(2,1)S(1)}, u32[]{:S(2)}, u32[]{:S(2)}) collective-permute-start(bf16[512,256]{1,0:T(8,128)(2,1)S(1)} %get-tuple-element.88), channel_id=1, source_target_pairs={{2,0},{3,1},{0,2},{1,3},{6,4},{7,5},{4,6},{5,7},{10,8},{11,9},{8,1... | collective-permute-start | bytes 786440 | tf_op jit(solution)/shard_map/ppermute | solution.py:530
  65.4 1.6 %collective-permute-start.13 = (f32[280,256]{1,0:T(8,128)S(1)}, f32[280,256]{1,0:T(8,128)S(1)}, u32[]{:S(2)}, u32[]{:S(2)}) collective-permute-start(f32[280,256]{1,0:T(8,128)S(1)} %get-tuple-element.101), channel_id=1, source_target_pairs={{0,1},{1,0},{2,3},{3,2},{4,5},{5,4},{6,7},{7,6},{8,9},{9,8},{10,11... | collective-permute-start | bytes 860168 | tf_op jit(solution)/shard_map/ppermute | solution.py:487
  67.1 8.6 %collective-permute-start.14 = (f32[88,256]{1,0:T(8,128)S(1)}, f32[88,256]{1,0:T(8,128)S(1)}, u32[]{:S(2)}, u32[]{:S(2)}) collective-permute-start(f32[88,256]{1,0:T(8,128)S(1)} %get-tuple-element.103), channel_id=1, source_target_pairs={{0,2},{1,3},{2,0},{3,1},{4,6},{5,7},{6,4},{7,5},{8,10},{9,11},{10,... | collective-permute-start | bytes 270344 | tf_op jit(solution)/shard_map/ppermute | solution.py:487
  68.9 5.1 %collective-permute-start.15 = (f32[72,256]{1,0:T(8,128)S(1)}, f32[72,256]{1,0:T(8,128)S(1)}, u32[]{:S(2)}, u32[]{:S(2)}) collective-permute-start(f32[72,256]{1,0:T(8,128)S(1)} %get-tuple-element.104), channel_id=1, source_target_pairs={{0,4},{1,5},{2,6},{3,7},{4,0},{5,1},{6,2},{7,3},{8,12},{9,13},{10,... | collective-permute-start | bytes 221192 | tf_op jit(solution)/shard_map/ppermute | solution.py:487
  70.5 5.3 %collective-permute-start.16 = (f32[72,256]{1,0:T(8,128)S(1)}, f32[72,256]{1,0:T(8,128)S(1)}, u32[]{:S(2)}, u32[]{:S(2)}) collective-permute-start(f32[72,256]{1,0:T(8,128)S(1)} %get-tuple-element.105), channel_id=1, source_target_pairs={{0,6},{1,7},{2,4},{3,5},{4,2},{5,3},{6,0},{7,1},{8,14},{9,15},{10,... | collective-permute-start | bytes 221192 | tf_op jit(solution)/shard_map/ppermute | solution.py:487
  76.4 5.2 %collective-permute-start.17 = (f32[40,256]{1,0:T(8,128)S(1)}, f32[40,256]{1,0:T(8,128)S(1)}, u32[]{:S(2)}, u32[]{:S(2)}) collective-permute-start(f32[40,256]{1,0:T(8,128)S(1)} %get-tuple-element.108), channel_id=1, source_target_pairs={{0,8},{1,9},{2,10},{3,11},{4,12},{5,13},{6,14},{7,15},{8,0},{9,1},... | collective-permute-start | bytes 122888 | tf_op jit(solution)/shard_map/ppermute | solution.py:487

commit v11 on v10

--- a/solution.py
+++ b/solution.py
@@ -174,22 +174,34 @@
     return jnp.concatenate([column, column], axis=1)
 
 
-def through_two(shape, scale, table, field, tiles, weight, weight_turned, readout, spread, goals, m_all, gz_all, g_field, preds, sums):
+def columns_of(goals, blocks):
+    rows = [goals[row, pl.ds(col, 1)] for row, col in blocks]
+    nodes = rows[0].shape[1]
+    turned = jnp.concatenate(rows + [jnp.zeros((nodes - len(rows), nodes), F32)], axis=0).T
+    return jnp.concatenate(
+        [jnp.broadcast_to(turned[:, k : k + 1], (nodes, nodes)) for k in range(len(rows))], axis=0
+    )
+
+
+def through_two(shape, scale, table, field, tiles, weight, weight_turned, readout, spread, m_all, gz_all, g_field, preds, sums):
     nodes = shape[0]
     readf = readout[...].astype(F32)
 
-    def body(blocks, m):
+    def body(blocks, m, goal_columns):
         scatter(m_all, blocks, m, nodes, 0)
         t = jnp.tanh(jnp.dot(m, weight[...], preferred_element_type=F32))
         base = gather(lambda row, col: field[row + 1, at_block(col + 1, nodes)], blocks)
         x = (base.astype(F32) + t).astype(BF16)
         seen = jnp.dot(x, spread[...], preferred_element_type=F32)
-        parts = []
+        lanes = lax.broadcasted_iota(jnp.int32, (nodes, 128), 1)
+        packed = jnp.zeros((nodes, 128), F32)
+        for k in range(len(blocks)):
+            packed = jnp.where(lanes == k, seen[k * nodes : (k + 1) * nodes], packed)
+        packed = packed.T
         for k, (row, col) in enumerate(blocks):
-            one = seen[k * nodes : (k + 1) * nodes].T[0:1]
-            preds[row, pl.ds(col, 1)] = one
-            parts.append(residual_columns(one, goals[row, pl.ds(col, 1)], scale))
-        gp = jnp.concatenate(parts, axis=0)
+            preds[row, pl.ds(col, 1)] = packed[k : k + 1]
+        gp = (seen - goal_columns) * scale
+        gp = jnp.concatenate([gp, gp], axis=1)
         sums[...] += (x.astype(F32) * gp).reshape(gp.shape[0] // 8, 8, gp.shape[1]).sum(axis=0)
         gz = (gp * readf * (1.0 - t * t)).astype(BF16)
         scatter(gz_all, blocks, gz, nodes, 0)
@@ -343,7 +355,7 @@
 
 
 def middle_compute_kernel(shape, scale, table, field, tiles, weight_one, weight_two, two_turned, readout, spread, target,
-                          target_swap, x_in, m_in, x_field, m_one, m_two, gz_two, g_field, preds, goals, sums, local):
+                          target_swap, x_in, m_in, x_field, m_one, m_two, gz_two, g_field, preds, goals, sums, local, goal_columns):
     _, _, moved = place()
 
     @pl.when(moved)
@@ -360,20 +372,21 @@
     blocks = inner_blocks(shape)
     forward_one(shape, table, field, tiles, weight_one, x_field, m_one)(blocks)
     through_two(
-        shape, scale, table, x_field, tiles, weight_two, two_turned, readout, spread, goals, m_two, gz_two,
+        shape, scale, table, x_field, tiles, weight_two, two_turned, readout, spread, m_two, gz_two,
         g_field, preds, sums,
-    )(blocks, messages(table, x_field, tiles, blocks, shape))
+    )(blocks, messages(table, x_field, tiles, blocks, shape), columns_of(goals, blocks))
+    goal_columns[...] = columns_of(goals, edge_blocks(shape))
     local[...] = products(table, x_field, tiles, edge_blocks(shape), shape)
 
 
-def second_edge_kernel(shape, scale, table, outer, inner, side, tiles, weight, weight_turned, readout, spread, goals,
+def second_edge_kernel(shape, scale, table, outer, inner, side, tiles, weight, weight_turned, readout, spread, goal_columns,
                        x_field, local, m_in, gz_in, g_in, preds_in, sums_in,
                        m_two, gz_two, g_field, preds, sums, outer_out, inner_out, side_out):
     m = (local[...] + rim_terms(table, tiles, outer, inner, side, shape)).astype(BF16)
     through_two(
-        shape, scale, table, x_field, tiles, weight, weight_turned, readout, spread, goals, m_two, gz_two,
+        shape, scale, table, x_field, tiles, weight, weight_turned, readout, spread, m_two, gz_two,
         g_field, preds, sums,
-    )(edge_blocks(shape), m)
+    )(edge_blocks(shape), m, goal_columns[...])
     take_edges(g_field, outer_out, inner_out, side_out, shape)
 
 
@@ -622,11 +635,12 @@
 
     outer, inner, side = edges(outer_s, inner_s, side_s)
     edge_terms = jax.ShapeDtypeStruct((edge * nodes, width), F32)
-    x_field, m_one, m_two, gz_two, g_field, preds, goals, sums, local = pl.pallas_call(
+    x_field, m_one, m_two, gz_two, g_field, preds, goals, sums, local, goal_columns = pl.pallas_call(
         functools.partial(middle_compute_kernel, shape, scale),
-        out_shape=(padded, patch, patch, patch, padded, goal_shape, goal_shape, sums_shape, edge_terms),
+        out_shape=(padded, patch, patch, patch, padded, goal_shape, goal_shape, sums_shape, edge_terms,
+                   jax.ShapeDtypeStruct((edge * nodes, 128), F32)),
         in_specs=[SMEM] + [VMEM] * 11,
-        out_specs=(VMEM,) * 9,
+        out_specs=(VMEM,) * 10,
         input_output_aliases={10: 0, 11: 1},
         compiler_params=params,
         cost_estimate=cost(2 * inside + edge, 3 * inside),
@@ -642,7 +656,7 @@
         compiler_params=params,
         cost_estimate=cost(edge // 4, 2 * edge),
         name="second_edge",
-    )(table, outer, inner, side, tiles, w_second, w_turned, readout, spread, goals, x_field, local,
+    )(table, outer, inner, side, tiles, w_second, w_turned, readout, spread, goal_columns, x_field, local,
       m_two, gz_two, g_field, preds, sums)
 
     outer, inner, side = edges(outer_s, inner_s, side_s)

time: 82.5 us -> 82.4 us (level)
  no operation moved by 1% of the time
where the time goes in v11:
time: 82.4 us; the launch traced here: 82.1 us
  starting transfers between devices  36.9 us (45%)
  Pallas kernels  21.2 us (26%)
  waiting for transfers between devices  20.7 us (25%)
  local copies, waits for them, and re-layouts  1.58 us (2%)
  between operations  0.89 us (1%)
    ppermute x13, starting transfers between devices, send(): return lax.ppermute(value, AXES, way)  32.7 us
    ppermute x5, waiting for transfers between devices, sum_shares(): lax.ppermute(outs[k], AXES, [(i, i ^ k * base) for i in range(count)])  11.2 us
    ppermute x13, waiting for transfers between devices, send(): return lax.ppermute(value, AXES, way)  9.53 us
    pallas_call x1, Pallas kernels, per_device(): pl.pallas_call(functools.partial(middle_compute_kernel, shape, scale), ou...  5.55 us
    pallas_call x1, Pallas kernels, per_device(): pl.pallas_call(functools.partial(back_inner_kernel, shape, scale), out_sh...  4.88 us
    ppermute x5, starting transfers between devices, sum_shares(): lax.ppermute(outs[k], AXES, [(i, i ^ k * base) for i in range(count)])  4.28 us
    pallas_call x1, Pallas kernels, per_device(): pl.pallas_call(functools.partial(second_edge_kernel, shape, scale), out_s...  2.81 us
    pallas_call x1, Pallas kernels, per_device(): pl.pallas_call(functools.partial(first_edge_kernel, shape), out_shape=(ja...  2.7 us
  transfers between devices with their start and end apart: 18, of which 7 were waited for; matrix products, arithmetic and copies ran while one was open for 1% of the time, Pallas kernels for 15%

profile of v11, /device:TPU:0, one launch (start us, length us, event | category | flops | bytes accessed | tf_op | source)
XLA Modules:
  0.0 82.1 jit_solution(10360333939014743421)
XLA Ops:
  0.6 1.4 %slice.3 = bf16[2,1024,256]{2,1,0:T(8,128)(2,1)S(1)} slice(bf16[4,1024,256]{2,1,0:T(8,128)(2,1)} %bitcast.5), slice={[0:4:3], [0:1024:1], [0:256:1]} | slice | bytes 2097152 | tf_op jit(solution)/shard_map/slice | solution.py:555
  2.1 0.7 collective-permute-start
  2.8 0.7 convert_bitcast_fusion.ids
  4.1 0.9 %collective-permute-start.3 = (bf16[2064,256]{1,0:T(8,128)(2,1)S(1)}, bf16[2064,256]{1,0:T(8,128)(2,1)S(1)}, u32[]{:S(2)}, u32[]{:S(2)}) collective-permute-start(bf16[2064,256]{1,0:T(8,128)(2,1)S(1)} %pack_middle.1), channel_id=1, source_target_pairs={{2,1},{1,2},{6,5},{5,6},{10,9},{9,10},{14,13},{13,14},{18,17},{17,... | collective-permute-start | bytes 3170312 | tf_op jit(solution)/shard_map/ppermute | solution.py:543
  4.9 7.1 %collective-permute-start.1 = (bf16[528,256]{1,0:T(8,128)(2,1)S(1)}, bf16[528,256]{1,0:T(8,128)(2,1)S(1)}, u32[]{:S(2)}, u32[]{:S(2)}) collective-permute-start(bf16[528,256]{1,0:T(8,128)(2,1)S(1)} %get-tuple-element.60), channel_id=1, source_target_pairs={{1,0},{3,1},{0,2},{2,3},{5,4},{7,5},{4,6},{6,7},{9,8},{11,9},{8,10... | collective-permute-start | bytes 811016 | tf_op jit(solution)/shard_map/ppermute | solution.py:543
  12.0 6.9 %collective-permute-done.1.after.side = bf16[528,256]{1,0:T(8,128)(2,1)S(1)} collective-permute-done((bf16[528,256]{1,0:T(8,128)(2,1)S(1)}, bf16[528,256]{1,0:T(8,128)(2,1)S(1)}, u32[]{:S(2)}, u32[]{:S(2)}) %collective-permute-start.1) | collective-permute-done | bytes 270368 | tf_op jit(solution)/shard_map/ppermute | solution.py:543
  19.1 0.7 collective-permute-start.4
  19.8 4.8 %collective-permute-start.5 = (bf16[1024,256]{1,0:T(8,128)(2,1)S(1)}, bf16[1024,256]{1,0:T(8,128)(2,1)S(1)}, u32[]{:S(2)}, u32[]{:S(2)}) collective-permute-start(bf16[1024,256]{1,0:T(8,128)(2,1)S(1)} %get-tuple-element.61), channel_id=1, source_target_pairs={{1,0},{0,1},{3,2},{2,3},{5,4},{4,5},{7,6},{6,7},{9,8},{8,9},{11,10... | collective-permute-start | bytes 1572872 | tf_op jit(solution)/shard_map/ppermute | solution.py:543
  24.6 0.7 collective-permute-start.6
  25.2 6.6 %collective-permute-start.2 = (bf16[16,256]{1,0:T(8,128)(2,1)S(1)}, bf16[16,256]{1,0:T(8,128)(2,1)S(1)}, u32[]{:S(2)}, u32[]{:S(2)}) collective-permute-start(bf16[16,256]{1,0:T(8,128)(2,1)S(1)} %get-tuple-element.62.numbers), channel_id=1, source_target_pairs={{0,1},{1,3},{4,5},{5,7},{8,9},{9,11},{12,13},{13,15},{2,4},{3,6},{... | collective-permute-start | bytes 24584 | tf_op jit(solution)/shard_map/ppermute | solution.py:543
  31.8 1.6 %prepare.1 = (bf16[32,128,128]{2,1,0:T(8,128)(2,1)S(1)}, bf16[256,256]{1,0:T(8,128)(2,1)S(1)}, bf16[256,256]{1,0:T(8,128)(2,1)S(1)}, bf16[256,256]{1,0:T(8,128)(2,1)S(1)}) custom-call(bf16[16,128,128]{2,1,0:T(8,128)(2,1)S(1)} %copy-done.1, bf16[256,256]{1,0:T(8,128)(2,1)S(1)} %copy-done.2, bf16[256,256]{1,0:T(8,128)(2,1)S(1)} %copy-done.3), custom_call_target="tpu_custom_call" | custom-call | tf_op jit(solution)/shard_map/prepare/pallas_call | solution.py:578
  33.5 2.7 %first_edge.1 = (s32[20,128]{1,0:T(8,128)S(1)}, bf16[6,1280,256]{2,1,0:T(8,128)(2,1)S(1)}, bf16[6,1280,256]{2,1,0:T(8,128)(2,1)S(1)}, bf16[4,1024,256]{2,1,0:T(8...) custom-call(bf16[16,256]{1,0:T(8,128)(2,1)S(1)} %get-tuple-element.62.num, ...), custom_call_target="tpu_custom_call" | custom-call | flops 1207959552 | bytes 4718592 | tf_op jit(solution)/shard_map/first_edge/pallas_call | solution.py:620
  36.2 0.7 collective-permute-start.7
  36.9 3.0 %collective-permute-start.8 = (bf16[1024,256]{1,0:T(8,128)(2,1)S(1)}, bf16[1024,256]{1,0:T(8,128)(2,1)S(1)}, u32[]{:S(2)}, u32[]{:S(2)}) collective-permute-start(bf16[1024,256]{1,0:T(8,128)(2,1)S(1)} %get-tuple-element.72), channel_id=1, source_target_pairs={{1,0},{0,1},{3,2},{2,3},{5,4},{4,5},{7,6},{6,7},{9,8},{8,9},{11,10... | collective-permute-start | bytes 1572872 | tf_op jit(solution)/shard_map/ppermute | solution.py:543
  39.9 2.1 %collective-permute-start.9 = (bf16[512,256]{1,0:T(8,128)(2,1)S(1)}, bf16[512,256]{1,0:T(8,128)(2,1)S(1)}, u32[]{:S(2)}, u32[]{:S(2)}) collective-permute-start(bf16[512,256]{1,0:T(8,128)(2,1)S(1)} %get-tuple-element.73), channel_id=1, source_target_pairs={{2,0},{3,1},{0,2},{1,3},{6,4},{7,5},{4,6},{5,7},{10,8},{11,9},{8,1... | collective-permute-start | bytes 786440 | tf_op jit(solution)/shard_map/ppermute | solution.py:543
  42.1 5.5 %inner_forward.1 = (bf16[6,1280,256]{2,1,0:T(8,128)(2,1)S(1)}, bf16[4,1024,256]{2,1,0:T(8,128)(2,1)S(1)}, bf16[4,1024,256]{2,1,0:T(8,128)(2,1)S(1)}, bf16[4,1024...) custom-call(s32[20,128]{1,0:T(8,128)S(1)} %get-tuple-element.70.tabl, ...), custom_call_target="tpu_custom_call", output_to_operand_aliasing={{0}: (10, {}), {1}: (11, {})} | custom-call | flops 3019898880 | bytes 11534336 | tf_op jit(solution)/shard_map/inner_forward/pallas_call | solution.py:638
  47.6 0.9 %collective-permute-done.9.side = bf16[512,256]{1,0:T(8,128)(2,1)S(1)} collective-permute-done((bf16[512,256]{1,0:T(8,128)(2,1)S(1)}, bf16[512,256]{1,0:T(8,128)(2,1)S(1)}, u32[]{:S(2)}, u32[]{:S(2)}) %collective-permute-start.9) | collective-permute-done | bytes 262176 | tf_op jit(solution)/shard_map/ppermute | solution.py:543
  48.5 2.8 %second_edge.1 = (bf16[4,1024,256]{2,1,0:T(8,128)(2,1)S(1)}, bf16[4,1024,256]{2,1,0:T(8,128)(2,1)S(1)}, bf16[6,1280,256]{2,1,0:T(8,128)(2,1)S(1)}, f32[4,8,128]{...) custom-call(s32[20,128]{1,0:T(8,128)S(1)} %get-tuple-element.70.tabl, ...), custom_call_target="tpu_custom_call", output_to_operand_aliasing={{0}: (12, {}), {1}: (13, {}), {2}: (14, {}), {3}: (15, {}),... | custom-call | flops 805306368 | bytes 5242880 | tf_op jit(solution)/shard_map/second_edge/pallas_call | solution.py:650
  51.3 0.9 %collective-permute-start.10 = (bf16[1024,256]{1,0:T(8,128)(2,1)S(1)}, bf16[1024,256]{1,0:T(8,128)(2,1)S(1)}, u32[]{:S(2)}, u32[]{:S(2)}) collective-permute-start(bf16[1024,256]{1,0:T(8,128)(2,1)S(1)} %get-tuple-element.87), channel_id=1, source_target_pairs={{1,4},{3,6},{5,8},{7,10},{9,12},{11,14},{4,1},{6,3},{8,5},{10,7},{... | collective-permute-start | bytes 1572872 | tf_op jit(solution)/shard_map/ppermute | solution.py:543
  52.2 3.0 %collective-permute-start.11 = (bf16[1024,256]{1,0:T(8,128)(2,1)S(1)}, bf16[1024,256]{1,0:T(8,128)(2,1)S(1)}, u32[]{:S(2)}, u32[]{:S(2)}) collective-permute-start(bf16[1024,256]{1,0:T(8,128)(2,1)S(1)} %get-tuple-element.88), channel_id=1, source_target_pairs={{1,0},{0,1},{3,2},{2,3},{5,4},{4,5},{7,6},{6,7},{9,8},{8,9},{11,10... | collective-permute-start | bytes 1572872 | tf_op jit(solution)/shard_map/ppermute | solution.py:543
  55.2 1.7 %collective-permute-start.12 = (bf16[512,256]{1,0:T(8,128)(2,1)S(1)}, bf16[512,256]{1,0:T(8,128)(2,1)S(1)}, u32[]{:S(2)}, u32[]{:S(2)}) collective-permute-start(bf16[512,256]{1,0:T(8,128)(2,1)S(1)} %get-tuple-element.89), channel_id=1, source_target_pairs={{2,0},{3,1},{0,2},{1,3},{6,4},{7,5},{4,6},{5,7},{10,8},{11,9},{8,1... | collective-permute-start | bytes 786440 | tf_op jit(solution)/shard_map/ppermute | solution.py:543
  56.9 4.9 %back_inner.1 = (f32[256,256]{1,0:T(8,128)S(1)}, f32[256,256]{1,0:T(8,128)S(1)}, f32[2304,256]{1,0:T(8,128)S(1)}, f32[2304,256]{1,0:T(8,128)S(1)}, bf16[256,2304]{1,0:T(8,128)(2,1)S(1)}) custom-call(s32[20,128]{1,0:T(8,128)S(1)} %get-tuple-element.70.table, bf16[6,1280,256]{2,1,0:T(8,128)(2,1)S(1)} %get-tuple-element.91.g_field, ...), custom_call_target="tpu_custom_call" | custom-call | flops 3221225472 | bytes 16777216 | tf_op jit(solution)/shard_map/back_inner/pallas_call | solution.py:663
  61.8 1.7 %collective-permute-done.12.side = bf16[512,256]{1,0:T(8,128)(2,1)S(1)} collective-permute-done((bf16[512,256]{1,0:T(8,128)(2,1)S(1)}, bf16[512,256]{1,0:T(8,128)(2,1)S(1)}, u32[]{:S(2)}, u32[]{:S(2)}) %collective-permute-start.12) | collective-permute-done | bytes 262176 | tf_op jit(solution)/shard_map/ppermute | solution.py:543
  63.5 1.8 %back_edge.1 = (f32[264,256]{1,0:T(8,128)S(1)}, f32[280,256]{1,0:T(8,128)S(1)}) custom-call(s32[20,128]{1,0:T(8,128)S(1)} %get-tuple-element.70.table, bf16[1024,256]{1,0:T(8,128)(2,1)S(1)} %collective-permute-done.10.outer, bf16[1024,256]{1,0:T(8,128)(2,1)S(1)} %collective-permute-done.11.inner, bf16[512,256]{1,0:T(8,128)(2,1)S(1)} %collective-permute-done.12.side, ...), custom_call_target="tpu_custom_call" | custom-call | flops 503316480 | bytes 2883584 | tf_op jit(solution)/shard_map/back_edge/pallas_call | solution.py:674
  65.4 1.6 %collective-permute-done.13.refs_0_ = f32[280,256]{1,0:T(8,128)S(1)} collective-permute-done((f32[280,256]{1,0:T(8,128)S(1)}, f32[280,256]{1,0:T(8,128)S(1)}, u32[]{:S(2)}, u32[]{:S(2)}) %collective-permute-start.13) | collective-permute-done | bytes 286752 | tf_op jit(solution)/shard_map/ppermute | solution.py:500
  67.0 1.8 %collective-permute-start.14 = (f32[88,256]{1,0:T(8,128)S(1)}, f32[88,256]{1,0:T(8,128)S(1)}, u32[]{:S(2)}, u32[]{:S(2)}) collective-permute-start(f32[88,256]{1,0:T(8,128)S(1)} %get-tuple-element.105), channel_id=1, source_target_pairs={{0,2},{1,3},{2,0},{3,1},{4,6},{5,7},{6,4},{7,5},{8,10},{9,11},{10,... | collective-permute-start | bytes 270344 | tf_op jit(solution)/shard_map/ppermute | solution.py:500
  68.8 1.6 %collective-permute-start.15 = (f32[72,256]{1,0:T(8,128)S(1)}, f32[72,256]{1,0:T(8,128)S(1)}, u32[]{:S(2)}, u32[]{:S(2)}) collective-permute-start(f32[72,256]{1,0:T(8,128)S(1)} %get-tuple-element.106), channel_id=1, source_target_pairs={{0,4},{1,5},{2,6},{3,7},{4,0},{5,1},{6,2},{7,3},{8,12},{9,13},{10,... | collective-permute-start | bytes 221192 | tf_op jit(solution)/shard_map/ppermute | solution.py:500
  70.5 3.4 %collective-permute-done.15.refs_1_ = f32[72,256]{1,0:T(8,128)S(1)} collective-permute-done((f32[72,256]{1,0:T(8,128)S(1)}, f32[72,256]{1,0:T(8,128)S(1)}, u32[]{:S(2)}, u32[]{:S(2)}) %collective-permute-start.15) | collective-permute-done | bytes 73760 | tf_op jit(solution)/shard_map/ppermute | solution.py:500
  73.9 1.7 %collective-permute-done.16.refs_2_ = f32[72,256]{1,0:T(8,128)S(1)} collective-permute-done((f32[72,256]{1,0:T(8,128)S(1)}, f32[72,256]{1,0:T(8,128)S(1)}, u32[]{:S(2)}, u32[]{:S(2)}) %collective-permute-start.16) | collective-permute-done | bytes 73760 | tf_op jit(solution)/shard_map/ppermute | solution.py:500
  75.6 0.6 fold.3
  76.2 0.7 collective-permute-start.17
  76.9 4.6 %collective-permute-done.17.refs_0_ = f32[40,256]{1,0:T(8,128)S(1)} collective-permute-done((f32[40,256]{1,0:T(8,128)S(1)}, f32[40,256]{1,0:T(8,128)S(1)}, u32[]{:S(2)}, u32[]{:S(2)}) %collective-permute-start.17) | collective-permute-done | bytes 40992 | tf_op jit(solution)/shard_map/ppermute | solution.py:500
  (32 shorter events, 1.7 us)
Async XLA Ops:
  0.6 2.9 %copy-start = (bf16[4,8,128,256]{3,2,1,0:T(8,128)(2,1)S(1)}, bf16[4,8,128,256]{3,2,1,0:T(8,128)(2,1)}, u32[]{:S(2)}) copy-start(bf16[4,8,128,256]{3,2,1,0:T(8,128)(2,1)} %param.7) | copy-start | bytes 6291460
  2.1 16.9 %collective-permute-start = (bf16[2048,256]{1,0:T(8,128)(2,1)S(1)}, bf16[2048,256]{1,0:T(8,128)(2,1)S(1)}, u32[]{:S(2)}, u32[]{:S(2)}) collective-permute-start(bf16[2048,256]{1,0:T(8,128)(2,1)S(1)} %bitcast.10), channel_id=1, source_target_pairs={{2,1},{1,2},{6,5},{5,6},{10,9},{9,10},{14,13},{13,14},{18,17},{17,... | collective-permute-start | bytes 3145736 | tf_op jit(solution)/shard_map/ppermute | solution.py:543
  4.0 20.6 %copy-start.4 = (f32[4,8,128]{2,1,0:T(8,128)S(1)}, f32[4,8,128]{2,1,0:T(8,128)}, u32[]{:S(2)}) copy-start(f32[4,8,128]{2,1,0:T(8,128)} %target.1) | copy-start | bytes 49156
  4.0 27.8 %copy-start.1 = (bf16[16,128,128]{2,1,0:T(8,128)(2,1)S(1)}, bf16[16,128,128]{2,1,0:T(8,128)(2,1)}, u32[]{:S(2)}) copy-start(bf16[16,128,128]{2,1,0:T(8,128)(2,1)} %tiles) | copy-start | bytes 1572868
  4.0 27.8 %copy-start.2 = (bf16[256,256]{1,0:T(8,128)(2,1)S(1)}, bf16[256,256]{1,0:T(8,128)(2,1)}, u32[]{:S(2)}) copy-start(bf16[256,256]{1,0:T(8,128)(2,1)} %first) | copy-start | bytes 393220
  4.0 27.8 %copy-start.3 = (bf16[256,256]{1,0:T(8,128)(2,1)S(1)}, bf16[256,256]{1,0:T(8,128)(2,1)}, u32[]{:S(2)}) copy-start(bf16[256,256]{1,0:T(8,128)(2,1)} %second) | copy-start | bytes 393220
  4.1 29.4 %collective-permute-start.3 = (bf16[2064,256]{1,0:T(8,128)(2,1)S(1)}, bf16[2064,256]{1,0:T(8,128)(2,1)S(1)}, u32[]{:S(2)}, u32[]{:S(2)}) collective-permute-start(bf16[2064,256]{1,0:T(8,128)(2,1)S(1)} %pack_middle.1), channel_id=1, source_target_pairs={{2,1},{1,2},{6,5},{5,6},{10,9},{9,10},{14,13},{13,14},{18,17},{17,... | collective-permute-start | bytes 3170312 | tf_op jit(solution)/shard_map/ppermute | solution.py:543
  4.9 14.0 %collective-permute-start.1 = (bf16[528,256]{1,0:T(8,128)(2,1)S(1)}, bf16[528,256]{1,0:T(8,128)(2,1)S(1)}, u32[]{:S(2)}, u32[]{:S(2)}) collective-permute-start(bf16[528,256]{1,0:T(8,128)(2,1)S(1)} %get-tuple-element.60), channel_id=1, source_target_pairs={{1,0},{3,1},{0,2},{2,3},{5,4},{7,5},{4,6},{6,7},{9,8},{11,9},{8,10... | collective-permute-start | bytes 811016 | tf_op jit(solution)/shard_map/ppermute | solution.py:543
  19.1 14.4 %collective-permute-start.4 = (bf16[1024,256]{1,0:T(8,128)(2,1)S(1)}, bf16[1024,256]{1,0:T(8,128)(2,1)S(1)}, u32[]{:S(2)}, u32[]{:S(2)}) collective-permute-start(bf16[1024,256]{1,0:T(8,128)(2,1)S(1)} %get-tuple-element.63), channel_id=1, source_target_pairs={{1,4},{3,6},{5,8},{7,10},{9,12},{11,14},{4,1},{6,3},{8,5},{10,7},{... | collective-permute-start | bytes 1572872 | tf_op jit(solution)/shard_map/ppermute | solution.py:543
  19.8 13.7 %collective-permute-start.5 = (bf16[1024,256]{1,0:T(8,128)(2,1)S(1)}, bf16[1024,256]{1,0:T(8,128)(2,1)S(1)}, u32[]{:S(2)}, u32[]{:S(2)}) collective-permute-start(bf16[1024,256]{1,0:T(8,128)(2,1)S(1)} %get-tuple-element.61), channel_id=1, source_target_pairs={{1,0},{0,1},{3,2},{2,3},{5,4},{4,5},{7,6},{6,7},{9,8},{8,9},{11,10... | collective-permute-start | bytes 1572872 | tf_op jit(solution)/shard_map/ppermute | solution.py:543
  24.6 8.9 %collective-permute-start.6 = (f32[4,8,128]{2,1,0:T(8,128)S(1)}, f32[4,8,128]{2,1,0:T(8,128)S(1)}, u32[]{:S(2)}, u32[]{:S(2)}) collective-permute-start(f32[4,8,128]{2,1,0:T(8,128)S(1)} %copy-done.4), channel_id=1, source_target_pairs={{2,1},{1,2},{6,5},{5,6},{10,9},{9,10},{14,13},{13,14},{18,17},{17,... | collective-permute-start | bytes 49160 | tf_op jit(solution)/shard_map/ppermute | solution.py:543
  25.2 8.2 %collective-permute-start.2 = (bf16[16,256]{1,0:T(8,128)(2,1)S(1)}, bf16[16,256]{1,0:T(8,128)(2,1)S(1)}, u32[]{:S(2)}, u32[]{:S(2)}) collective-permute-start(bf16[16,256]{1,0:T(8,128)(2,1)S(1)} %get-tuple-element.62.numbers), channel_id=1, source_target_pairs={{0,1},{1,3},{4,5},{5,7},{8,9},{9,11},{12,13},{13,15},{2,4},{3,6},{... | collective-permute-start | bytes 24584 | tf_op jit(solution)/shard_map/ppermute | solution.py:543
  33.5 6.4 %copy-start.5 = (bf16[256]{0:T(256)(128)(2,1)S(1)}, bf16[256]{0:T(256)(128)(2,1)}, u32[]{:S(2)}) copy-start(bf16[256]{0:T(256)(128)(2,1)} %param.12) | copy-start | bytes 1540
  36.2 12.3 %collective-permute-start.7 = (bf16[1024,256]{1,0:T(8,128)(2,1)S(1)}, bf16[1024,256]{1,0:T(8,128)(2,1)S(1)}, u32[]{:S(2)}, u32[]{:S(2)}) collective-permute-start(bf16[1024,256]{1,0:T(8,128)(2,1)S(1)} %get-tuple-element.71), channel_id=1, source_target_pairs={{1,4},{3,6},{5,8},{7,10},{9,12},{11,14},{4,1},{6,3},{8,5},{10,7},{... | collective-permute-start | bytes 1572872 | tf_op jit(solution)/shard_map/ppermute | solution.py:543
  36.9 11.6 %collective-permute-start.8 = (bf16[1024,256]{1,0:T(8,128)(2,1)S(1)}, bf16[1024,256]{1,0:T(8,128)(2,1)S(1)}, u32[]{:S(2)}, u32[]{:S(2)}) collective-permute-start(bf16[1024,256]{1,0:T(8,128)(2,1)S(1)} %get-tuple-element.72), channel_id=1, source_target_pairs={{1,0},{0,1},{3,2},{2,3},{5,4},{4,5},{7,6},{6,7},{9,8},{8,9},{11,10... | collective-permute-start | bytes 1572872 | tf_op jit(solution)/shard_map/ppermute | solution.py:543
  39.9 8.6 %collective-permute-start.9 = (bf16[512,256]{1,0:T(8,128)(2,1)S(1)}, bf16[512,256]{1,0:T(8,128)(2,1)S(1)}, u32[]{:S(2)}, u32[]{:S(2)}) collective-permute-start(bf16[512,256]{1,0:T(8,128)(2,1)S(1)} %get-tuple-element.73), channel_id=1, source_target_pairs={{2,0},{3,1},{0,2},{1,3},{6,4},{7,5},{4,6},{5,7},{10,8},{11,9},{8,1... | collective-permute-start | bytes 786440 | tf_op jit(solution)/shard_map/ppermute | solution.py:543
  51.3 12.1 %collective-permute-start.10 = (bf16[1024,256]{1,0:T(8,128)(2,1)S(1)}, bf16[1024,256]{1,0:T(8,128)(2,1)S(1)}, u32[]{:S(2)}, u32[]{:S(2)}) collective-permute-start(bf16[1024,256]{1,0:T(8,128)(2,1)S(1)} %get-tuple-element.87), channel_id=1, source_target_pairs={{1,4},{3,6},{5,8},{7,10},{9,12},{11,14},{4,1},{6,3},{8,5},{10,7},{... | collective-permute-start | bytes 1572872 | tf_op jit(solution)/shard_map/ppermute | solution.py:543
  52.2 11.3 %collective-permute-start.11 = (bf16[1024,256]{1,0:T(8,128)(2,1)S(1)}, bf16[1024,256]{1,0:T(8,128)(2,1)S(1)}, u32[]{:S(2)}, u32[]{:S(2)}) collective-permute-start(bf16[1024,256]{1,0:T(8,128)(2,1)S(1)} %get-tuple-element.88), channel_id=1, source_target_pairs={{1,0},{0,1},{3,2},{2,3},{5,4},{4,5},{7,6},{6,7},{9,8},{8,9},{11,10... | collective-permute-start | bytes 1572872 | tf_op jit(solution)/shard_map/ppermute | solution.py:543
  55.2 8.3 %collective-permute-start.12 = (bf16[512,256]{1,0:T(8,128)(2,1)S(1)}, bf16[512,256]{1,0:T(8,128)(2,1)S(1)}, u32[]{:S(2)}, u32[]{:S(2)}) collective-permute-start(bf16[512,256]{1,0:T(8,128)(2,1)S(1)} %get-tuple-element.89), channel_id=1, source_target_pairs={{2,0},{3,1},{0,2},{1,3},{6,4},{7,5},{4,6},{5,7},{10,8},{11,9},{8,1... | collective-permute-start | bytes 786440 | tf_op jit(solution)/shard_map/ppermute | solution.py:543
  65.3 1.6 %collective-permute-start.13 = (f32[280,256]{1,0:T(8,128)S(1)}, f32[280,256]{1,0:T(8,128)S(1)}, u32[]{:S(2)}, u32[]{:S(2)}) collective-permute-start(f32[280,256]{1,0:T(8,128)S(1)} %get-tuple-element.103), channel_id=1, source_target_pairs={{0,1},{1,0},{2,3},{3,2},{4,5},{5,4},{6,7},{7,6},{8,9},{9,8},{10,11... | collective-permute-start | bytes 860168 | tf_op jit(solution)/shard_map/ppermute | solution.py:500
  67.0 8.6 %collective-permute-start.14 = (f32[88,256]{1,0:T(8,128)S(1)}, f32[88,256]{1,0:T(8,128)S(1)}, u32[]{:S(2)}, u32[]{:S(2)}) collective-permute-start(f32[88,256]{1,0:T(8,128)S(1)} %get-tuple-element.105), channel_id=1, source_target_pairs={{0,2},{1,3},{2,0},{3,1},{4,6},{5,7},{6,4},{7,5},{8,10},{9,11},{10,... | collective-permute-start | bytes 270344 | tf_op jit(solution)/shard_map/ppermute | solution.py:500
  68.8 5.1 %collective-permute-start.15 = (f32[72,256]{1,0:T(8,128)S(1)}, f32[72,256]{1,0:T(8,128)S(1)}, u32[]{:S(2)}, u32[]{:S(2)}) collective-permute-start(f32[72,256]{1,0:T(8,128)S(1)} %get-tuple-element.106), channel_id=1, source_target_pairs={{0,4},{1,5},{2,6},{3,7},{4,0},{5,1},{6,2},{7,3},{8,12},{9,13},{10,... | collective-permute-start | bytes 221192 | tf_op jit(solution)/shard_map/ppermute | solution.py:500
  70.4 5.3 %collective-permute-start.16 = (f32[72,256]{1,0:T(8,128)S(1)}, f32[72,256]{1,0:T(8,128)S(1)}, u32[]{:S(2)}, u32[]{:S(2)}) collective-permute-start(f32[72,256]{1,0:T(8,128)S(1)} %get-tuple-element.107), channel_id=1, source_target_pairs={{0,6},{1,7},{2,4},{3,5},{4,2},{5,3},{6,0},{7,1},{8,14},{9,15},{10,... | collective-permute-start | bytes 221192 | tf_op jit(solution)/shard_map/ppermute | solution.py:500
  76.2 5.2 %collective-permute-start.17 = (f32[40,256]{1,0:T(8,128)S(1)}, f32[40,256]{1,0:T(8,128)S(1)}, u32[]{:S(2)}, u32[]{:S(2)}) collective-permute-start(f32[40,256]{1,0:T(8,128)S(1)} %get-tuple-element.110), channel_id=1, source_target_pairs={{0,8},{1,9},{2,10},{3,11},{4,12},{5,13},{6,14},{7,15},{8,0},{9,1},... | collective-permute-start | bytes 122888 | tf_op jit(solution)/shard_map/ppermute | solution.py:500

commit v12 on v11

--- a/solution.py
+++ b/solution.py
@@ -311,7 +311,7 @@
 
 
 def first_edge_kernel(shape, numbers, above, own, ends, middle, outer, inner, side, later, tiles, weight,
-                      table, field, x_field, m_all, outer_out, inner_out, side_out, own_ids, above_ids, spots, sems):
+                      spots, field, x_field, m_all, outer_out, inner_out, side_out, own_ids, above_ids, table, sems):
     nodes, rows, cols = shape
     line = cols * nodes
     _, _, moved = place()
@@ -621,11 +621,11 @@
         functools.partial(first_edge_kernel, shape),
         out_shape=(jax.ShapeDtypeStruct((5 * rows, 128), jnp.int32), padded, padded, patch) + edge_shapes,
         in_specs=[VMEM] * 8 + [ANY] + [VMEM] * 2,
-        out_specs=(SMEM,) + (VMEM,) * 6,
+        out_specs=(VMEM,) * 7,
         scratch_shapes=[
             pltpu.VMEM((TAIL, width), F32),
             pltpu.VMEM((TAIL, width), F32),
-            pltpu.VMEM((5 * rows, 128), jnp.int32),
+            pltpu.SMEM((5 * rows, 128), jnp.int32),
             sems(1),
         ],
         compiler_params=params,

time: 82.4 us -> 82.3 us (level)
  no operation moved by 1% of the time
where the time goes in v12:
time: 82.3 us; the launch traced here: 82 us
  starting transfers between devices  37 us (45%)
  Pallas kernels  21.1 us (26%)
  waiting for transfers between devices  20.7 us (25%)
  local copies, waits for them, and re-layouts  1.58 us (2%)
  between operations  0.89 us (1%)
    ppermute x13, starting transfers between devices, send(): return lax.ppermute(value, AXES, way)  32.7 us
    ppermute x5, waiting for transfers between devices, sum_shares(): lax.ppermute(outs[k], AXES, [(i, i ^ k * base) for i in range(count)])  11.2 us
    ppermute x13, waiting for transfers between devices, send(): return lax.ppermute(value, AXES, way)  9.53 us
    pallas_call x1, Pallas kernels, per_device(): pl.pallas_call(functools.partial(middle_compute_kernel, shape, scale), ou...  5.55 us
    pallas_call x1, Pallas kernels, per_device(): pl.pallas_call(functools.partial(back_inner_kernel, shape, scale), out_sh...  4.88 us
    ppermute x5, starting transfers between devices, sum_shares(): lax.ppermute(outs[k], AXES, [(i, i ^ k * base) for i in range(count)])  4.28 us
    pallas_call x1, Pallas kernels, per_device(): pl.pallas_call(functools.partial(second_edge_kernel, shape, scale), out_s...  2.81 us
    pallas_call x1, Pallas kernels, per_device(): pl.pallas_call(functools.partial(first_edge_kernel, shape), out_shape=(ja...  2.58 us
  transfers between devices with their start and end apart: 18, of which 7 were waited for; matrix products, arithmetic and copies ran while one was open for 1% of the time, Pallas kernels for 15%

profile of v12, /device:TPU:0, one launch (start us, length us, event | category | flops | bytes accessed | tf_op | source)
XLA Modules:
  0.0 82.0 jit_solution(3422746000523725365)
XLA Ops:
  0.6 1.4 %slice.3 = bf16[2,1024,256]{2,1,0:T(8,128)(2,1)S(1)} slice(bf16[4,1024,256]{2,1,0:T(8,128)(2,1)} %bitcast.5), slice={[0:4:3], [0:1024:1], [0:256:1]} | slice | bytes 2097152 | tf_op jit(solution)/shard_map/slice | solution.py:555
  2.1 0.7 collective-permute-start
  2.8 0.7 convert_bitcast_fusion.ids
  4.1 0.9 %collective-permute-start.3 = (bf16[2064,256]{1,0:T(8,128)(2,1)S(1)}, bf16[2064,256]{1,0:T(8,128)(2,1)S(1)}, u32[]{:S(2)}, u32[]{:S(2)}) collective-permute-start(bf16[2064,256]{1,0:T(8,128)(2,1)S(1)} %pack_middle.1), channel_id=1, source_target_pairs={{2,1},{1,2},{6,5},{5,6},{10,9},{9,10},{14,13},{13,14},{18,17},{17,... | collective-permute-start | bytes 3170312 | tf_op jit(solution)/shard_map/ppermute | solution.py:543
  4.9 7.1 %collective-permute-start.1 = (bf16[528,256]{1,0:T(8,128)(2,1)S(1)}, bf16[528,256]{1,0:T(8,128)(2,1)S(1)}, u32[]{:S(2)}, u32[]{:S(2)}) collective-permute-start(bf16[528,256]{1,0:T(8,128)(2,1)S(1)} %get-tuple-element.60), channel_id=1, source_target_pairs={{1,0},{3,1},{0,2},{2,3},{5,4},{7,5},{4,6},{6,7},{9,8},{11,9},{8,10... | collective-permute-start | bytes 811016 | tf_op jit(solution)/shard_map/ppermute | solution.py:543
  12.0 6.9 %collective-permute-done.1.after.side = bf16[528,256]{1,0:T(8,128)(2,1)S(1)} collective-permute-done((bf16[528,256]{1,0:T(8,128)(2,1)S(1)}, bf16[528,256]{1,0:T(8,128)(2,1)S(1)}, u32[]{:S(2)}, u32[]{:S(2)}) %collective-permute-start.1) | collective-permute-done | bytes 270368 | tf_op jit(solution)/shard_map/ppermute | solution.py:543
  19.1 0.7 collective-permute-start.4
  19.8 4.8 %collective-permute-start.5 = (bf16[1024,256]{1,0:T(8,128)(2,1)S(1)}, bf16[1024,256]{1,0:T(8,128)(2,1)S(1)}, u32[]{:S(2)}, u32[]{:S(2)}) collective-permute-start(bf16[1024,256]{1,0:T(8,128)(2,1)S(1)} %get-tuple-element.61), channel_id=1, source_target_pairs={{1,0},{0,1},{3,2},{2,3},{5,4},{4,5},{7,6},{6,7},{9,8},{8,9},{11,10... | collective-permute-start | bytes 1572872 | tf_op jit(solution)/shard_map/ppermute | solution.py:543
  24.6 0.7 collective-permute-start.6
  25.2 6.6 %collective-permute-start.2 = (bf16[16,256]{1,0:T(8,128)(2,1)S(1)}, bf16[16,256]{1,0:T(8,128)(2,1)S(1)}, u32[]{:S(2)}, u32[]{:S(2)}) collective-permute-start(bf16[16,256]{1,0:T(8,128)(2,1)S(1)} %get-tuple-element.62.numbers), channel_id=1, source_target_pairs={{0,1},{1,3},{4,5},{5,7},{8,9},{9,11},{12,13},{13,15},{2,4},{3,6},{... | collective-permute-start | bytes 24584 | tf_op jit(solution)/shard_map/ppermute | solution.py:543
  31.8 1.6 %prepare.1 = (bf16[32,128,128]{2,1,0:T(8,128)(2,1)S(1)}, bf16[256,256]{1,0:T(8,128)(2,1)S(1)}, bf16[256,256]{1,0:T(8,128)(2,1)S(1)}, bf16[256,256]{1,0:T(8,128)(2,1)S(1)}) custom-call(bf16[16,128,128]{2,1,0:T(8,128)(2,1)S(1)} %copy-done.1, bf16[256,256]{1,0:T(8,128)(2,1)S(1)} %copy-done.2, bf16[256,256]{1,0:T(8,128)(2,1)S(1)} %copy-done.3), custom_call_target="tpu_custom_call" | custom-call | tf_op jit(solution)/shard_map/prepare/pallas_call | solution.py:578
  33.5 2.6 %first_edge.1 = (s32[20,128]{1,0:T(8,128)S(1)}, bf16[6,1280,256]{2,1,0:T(8,128)(2,1)S(1)}, bf16[6,1280,256]{2,1,0:T(8,128)(2,1)S(1)}, bf16[4,1024,256]{2,1,0:T(8...) custom-call(bf16[16,256]{1,0:T(8,128)(2,1)S(1)} %get-tuple-element.62.num, ...), custom_call_target="tpu_custom_call" | custom-call | flops 1207959552 | bytes 4718592 | tf_op jit(solution)/shard_map/first_edge/pallas_call | solution.py:620
  36.1 0.7 collective-permute-start.7
  36.8 3.0 %collective-permute-start.8 = (bf16[1024,256]{1,0:T(8,128)(2,1)S(1)}, bf16[1024,256]{1,0:T(8,128)(2,1)S(1)}, u32[]{:S(2)}, u32[]{:S(2)}) collective-permute-start(bf16[1024,256]{1,0:T(8,128)(2,1)S(1)} %get-tuple-element.72), channel_id=1, source_target_pairs={{1,0},{0,1},{3,2},{2,3},{5,4},{4,5},{7,6},{6,7},{9,8},{8,9},{11,10... | collective-permute-start | bytes 1572872 | tf_op jit(solution)/shard_map/ppermute | solution.py:543
  39.8 2.1 %collective-permute-start.9 = (bf16[512,256]{1,0:T(8,128)(2,1)S(1)}, bf16[512,256]{1,0:T(8,128)(2,1)S(1)}, u32[]{:S(2)}, u32[]{:S(2)}) collective-permute-start(bf16[512,256]{1,0:T(8,128)(2,1)S(1)} %get-tuple-element.73), channel_id=1, source_target_pairs={{2,0},{3,1},{0,2},{1,3},{6,4},{7,5},{4,6},{5,7},{10,8},{11,9},{8,1... | collective-permute-start | bytes 786440 | tf_op jit(solution)/shard_map/ppermute | solution.py:543
  42.0 5.5 %inner_forward.1 = (bf16[6,1280,256]{2,1,0:T(8,128)(2,1)S(1)}, bf16[4,1024,256]{2,1,0:T(8,128)(2,1)S(1)}, bf16[4,1024,256]{2,1,0:T(8,128)(2,1)S(1)}, bf16[4,1024...) custom-call(s32[20,128]{1,0:T(8,128)S(1)} %get-tuple-element.70.tabl, ...), custom_call_target="tpu_custom_call", output_to_operand_aliasing={{0}: (10, {}), {1}: (11, {})} | custom-call | flops 3019898880 | bytes 11534336 | tf_op jit(solution)/shard_map/inner_forward/pallas_call | solution.py:638
  47.5 0.9 %collective-permute-done.9.side = bf16[512,256]{1,0:T(8,128)(2,1)S(1)} collective-permute-done((bf16[512,256]{1,0:T(8,128)(2,1)S(1)}, bf16[512,256]{1,0:T(8,128)(2,1)S(1)}, u32[]{:S(2)}, u32[]{:S(2)}) %collective-permute-start.9) | collective-permute-done | bytes 262176 | tf_op jit(solution)/shard_map/ppermute | solution.py:543
  48.4 2.8 %second_edge.1 = (bf16[4,1024,256]{2,1,0:T(8,128)(2,1)S(1)}, bf16[4,1024,256]{2,1,0:T(8,128)(2,1)S(1)}, bf16[6,1280,256]{2,1,0:T(8,128)(2,1)S(1)}, f32[4,8,128]{...) custom-call(s32[20,128]{1,0:T(8,128)S(1)} %get-tuple-element.70.tabl, ...), custom_call_target="tpu_custom_call", output_to_operand_aliasing={{0}: (12, {}), {1}: (13, {}), {2}: (14, {}), {3}: (15, {}),... | custom-call | flops 805306368 | bytes 5242880 | tf_op jit(solution)/shard_map/second_edge/pallas_call | solution.py:650
  51.2 0.9 %collective-permute-start.10 = (bf16[1024,256]{1,0:T(8,128)(2,1)S(1)}, bf16[1024,256]{1,0:T(8,128)(2,1)S(1)}, u32[]{:S(2)}, u32[]{:S(2)}) collective-permute-start(bf16[1024,256]{1,0:T(8,128)(2,1)S(1)} %get-tuple-element.87), channel_id=1, source_target_pairs={{1,4},{3,6},{5,8},{7,10},{9,12},{11,14},{4,1},{6,3},{8,5},{10,7},{... | collective-permute-start | bytes 1572872 | tf_op jit(solution)/shard_map/ppermute | solution.py:543
  52.1 3.0 %collective-permute-start.11 = (bf16[1024,256]{1,0:T(8,128)(2,1)S(1)}, bf16[1024,256]{1,0:T(8,128)(2,1)S(1)}, u32[]{:S(2)}, u32[]{:S(2)}) collective-permute-start(bf16[1024,256]{1,0:T(8,128)(2,1)S(1)} %get-tuple-element.88), channel_id=1, source_target_pairs={{1,0},{0,1},{3,2},{2,3},{5,4},{4,5},{7,6},{6,7},{9,8},{8,9},{11,10... | collective-permute-start | bytes 1572872 | tf_op jit(solution)/shard_map/ppermute | solution.py:543
  55.1 1.7 %collective-permute-start.12 = (bf16[512,256]{1,0:T(8,128)(2,1)S(1)}, bf16[512,256]{1,0:T(8,128)(2,1)S(1)}, u32[]{:S(2)}, u32[]{:S(2)}) collective-permute-start(bf16[512,256]{1,0:T(8,128)(2,1)S(1)} %get-tuple-element.89), channel_id=1, source_target_pairs={{2,0},{3,1},{0,2},{1,3},{6,4},{7,5},{4,6},{5,7},{10,8},{11,9},{8,1... | collective-permute-start | bytes 786440 | tf_op jit(solution)/shard_map/ppermute | solution.py:543
  56.8 4.9 %back_inner.1 = (f32[256,256]{1,0:T(8,128)S(1)}, f32[256,256]{1,0:T(8,128)S(1)}, f32[2304,256]{1,0:T(8,128)S(1)}, f32[2304,256]{1,0:T(8,128)S(1)}, bf16[256,2304]{1,0:T(8,128)(2,1)S(1)}) custom-call(s32[20,128]{1,0:T(8,128)S(1)} %get-tuple-element.70.table, bf16[6,1280,256]{2,1,0:T(8,128)(2,1)S(1)} %get-tuple-element.91.g_field, ...), custom_call_target="tpu_custom_call" | custom-call | flops 3221225472 | bytes 16777216 | tf_op jit(solution)/shard_map/back_inner/pallas_call | solution.py:663
  61.7 1.7 %collective-permute-done.12.side = bf16[512,256]{1,0:T(8,128)(2,1)S(1)} collective-permute-done((bf16[512,256]{1,0:T(8,128)(2,1)S(1)}, bf16[512,256]{1,0:T(8,128)(2,1)S(1)}, u32[]{:S(2)}, u32[]{:S(2)}) %collective-permute-start.12) | collective-permute-done | bytes 262176 | tf_op jit(solution)/shard_map/ppermute | solution.py:543
  63.4 1.8 %back_edge.1 = (f32[264,256]{1,0:T(8,128)S(1)}, f32[280,256]{1,0:T(8,128)S(1)}) custom-call(s32[20,128]{1,0:T(8,128)S(1)} %get-tuple-element.70.table, bf16[1024,256]{1,0:T(8,128)(2,1)S(1)} %collective-permute-done.10.outer, bf16[1024,256]{1,0:T(8,128)(2,1)S(1)} %collective-permute-done.11.inner, bf16[512,256]{1,0:T(8,128)(2,1)S(1)} %collective-permute-done.12.side, ...), custom_call_target="tpu_custom_call" | custom-call | flops 503316480 | bytes 2883584 | tf_op jit(solution)/shard_map/back_edge/pallas_call | solution.py:674
  65.2 1.6 %collective-permute-done.13.refs_0_ = f32[280,256]{1,0:T(8,128)S(1)} collective-permute-done((f32[280,256]{1,0:T(8,128)S(1)}, f32[280,256]{1,0:T(8,128)S(1)}, u32[]{:S(2)}, u32[]{:S(2)}) %collective-permute-start.13) | collective-permute-done | bytes 286752 | tf_op jit(solution)/shard_map/ppermute | solution.py:500
  66.9 1.8 %collective-permute-start.14 = (f32[88,256]{1,0:T(8,128)S(1)}, f32[88,256]{1,0:T(8,128)S(1)}, u32[]{:S(2)}, u32[]{:S(2)}) collective-permute-start(f32[88,256]{1,0:T(8,128)S(1)} %get-tuple-element.105), channel_id=1, source_target_pairs={{0,2},{1,3},{2,0},{3,1},{4,6},{5,7},{6,4},{7,5},{8,10},{9,11},{10,... | collective-permute-start | bytes 270344 | tf_op jit(solution)/shard_map/ppermute | solution.py:500
  68.7 1.6 %collective-permute-start.15 = (f32[72,256]{1,0:T(8,128)S(1)}, f32[72,256]{1,0:T(8,128)S(1)}, u32[]{:S(2)}, u32[]{:S(2)}) collective-permute-start(f32[72,256]{1,0:T(8,128)S(1)} %get-tuple-element.106), channel_id=1, source_target_pairs={{0,4},{1,5},{2,6},{3,7},{4,0},{5,1},{6,2},{7,3},{8,12},{9,13},{10,... | collective-permute-start | bytes 221192 | tf_op jit(solution)/shard_map/ppermute | solution.py:500
  70.4 3.4 %collective-permute-done.15.refs_1_ = f32[72,256]{1,0:T(8,128)S(1)} collective-permute-done((f32[72,256]{1,0:T(8,128)S(1)}, f32[72,256]{1,0:T(8,128)S(1)}, u32[]{:S(2)}, u32[]{:S(2)}) %collective-permute-start.15) | collective-permute-done | bytes 73760 | tf_op jit(solution)/shard_map/ppermute | solution.py:500
  73.8 1.7 %collective-permute-done.16.refs_2_ = f32[72,256]{1,0:T(8,128)S(1)} collective-permute-done((f32[72,256]{1,0:T(8,128)S(1)}, f32[72,256]{1,0:T(8,128)S(1)}, u32[]{:S(2)}, u32[]{:S(2)}) %collective-permute-start.16) | collective-permute-done | bytes 73760 | tf_op jit(solution)/shard_map/ppermute | solution.py:500
  75.5 0.6 fold.3
  76.1 0.7 collective-permute-start.17
  76.8 4.6 %collective-permute-done.17.refs_0_ = f32[40,256]{1,0:T(8,128)S(1)} collective-permute-done((f32[40,256]{1,0:T(8,128)S(1)}, f32[40,256]{1,0:T(8,128)S(1)}, u32[]{:S(2)}, u32[]{:S(2)}) %collective-permute-start.17) | collective-permute-done | bytes 40992 | tf_op jit(solution)/shard_map/ppermute | solution.py:500
  (32 shorter events, 1.7 us)
Async XLA Ops:
  0.6 2.9 %copy-start = (bf16[4,8,128,256]{3,2,1,0:T(8,128)(2,1)S(1)}, bf16[4,8,128,256]{3,2,1,0:T(8,128)(2,1)}, u32[]{:S(2)}) copy-start(bf16[4,8,128,256]{3,2,1,0:T(8,128)(2,1)} %param.7) | copy-start | bytes 6291460
  2.1 16.9 %collective-permute-start = (bf16[2048,256]{1,0:T(8,128)(2,1)S(1)}, bf16[2048,256]{1,0:T(8,128)(2,1)S(1)}, u32[]{:S(2)}, u32[]{:S(2)}) collective-permute-start(bf16[2048,256]{1,0:T(8,128)(2,1)S(1)} %bitcast.10), channel_id=1, source_target_pairs={{2,1},{1,2},{6,5},{5,6},{10,9},{9,10},{14,13},{13,14},{18,17},{17,... | collective-permute-start | bytes 3145736 | tf_op jit(solution)/shard_map/ppermute | solution.py:543
  4.0 20.6 %copy-start.4 = (f32[4,8,128]{2,1,0:T(8,128)S(1)}, f32[4,8,128]{2,1,0:T(8,128)}, u32[]{:S(2)}) copy-start(f32[4,8,128]{2,1,0:T(8,128)} %target.1) | copy-start | bytes 49156
  4.0 27.8 %copy-start.1 = (bf16[16,128,128]{2,1,0:T(8,128)(2,1)S(1)}, bf16[16,128,128]{2,1,0:T(8,128)(2,1)}, u32[]{:S(2)}) copy-start(bf16[16,128,128]{2,1,0:T(8,128)(2,1)} %tiles) | copy-start | bytes 1572868
  4.0 27.8 %copy-start.2 = (bf16[256,256]{1,0:T(8,128)(2,1)S(1)}, bf16[256,256]{1,0:T(8,128)(2,1)}, u32[]{:S(2)}) copy-start(bf16[256,256]{1,0:T(8,128)(2,1)} %first) | copy-start | bytes 393220
  4.0 27.8 %copy-start.3 = (bf16[256,256]{1,0:T(8,128)(2,1)S(1)}, bf16[256,256]{1,0:T(8,128)(2,1)}, u32[]{:S(2)}) copy-start(bf16[256,256]{1,0:T(8,128)(2,1)} %second) | copy-start | bytes 393220
  4.1 29.4 %collective-permute-start.3 = (bf16[2064,256]{1,0:T(8,128)(2,1)S(1)}, bf16[2064,256]{1,0:T(8,128)(2,1)S(1)}, u32[]{:S(2)}, u32[]{:S(2)}) collective-permute-start(bf16[2064,256]{1,0:T(8,128)(2,1)S(1)} %pack_middle.1), channel_id=1, source_target_pairs={{2,1},{1,2},{6,5},{5,6},{10,9},{9,10},{14,13},{13,14},{18,17},{17,... | collective-permute-start | bytes 3170312 | tf_op jit(solution)/shard_map/ppermute | solution.py:543
  4.9 14.0 %collective-permute-start.1 = (bf16[528,256]{1,0:T(8,128)(2,1)S(1)}, bf16[528,256]{1,0:T(8,128)(2,1)S(1)}, u32[]{:S(2)}, u32[]{:S(2)}) collective-permute-start(bf16[528,256]{1,0:T(8,128)(2,1)S(1)} %get-tuple-element.60), channel_id=1, source_target_pairs={{1,0},{3,1},{0,2},{2,3},{5,4},{7,5},{4,6},{6,7},{9,8},{11,9},{8,10... | collective-permute-start | bytes 811016 | tf_op jit(solution)/shard_map/ppermute | solution.py:543
  19.1 14.4 %collective-permute-start.4 = (bf16[1024,256]{1,0:T(8,128)(2,1)S(1)}, bf16[1024,256]{1,0:T(8,128)(2,1)S(1)}, u32[]{:S(2)}, u32[]{:S(2)}) collective-permute-start(bf16[1024,256]{1,0:T(8,128)(2,1)S(1)} %get-tuple-element.63), channel_id=1, source_target_pairs={{1,4},{3,6},{5,8},{7,10},{9,12},{11,14},{4,1},{6,3},{8,5},{10,7},{... | collective-permute-start | bytes 1572872 | tf_op jit(solution)/shard_map/ppermute | solution.py:543
  19.8 13.7 %collective-permute-start.5 = (bf16[1024,256]{1,0:T(8,128)(2,1)S(1)}, bf16[1024,256]{1,0:T(8,128)(2,1)S(1)}, u32[]{:S(2)}, u32[]{:S(2)}) collective-permute-start(bf16[1024,256]{1,0:T(8,128)(2,1)S(1)} %get-tuple-element.61), channel_id=1, source_target_pairs={{1,0},{0,1},{3,2},{2,3},{5,4},{4,5},{7,6},{6,7},{9,8},{8,9},{11,10... | collective-permute-start | bytes 1572872 | tf_op jit(solution)/shard_map/ppermute | solution.py:543
  24.6 8.9 %collective-permute-start.6 = (f32[4,8,128]{2,1,0:T(8,128)S(1)}, f32[4,8,128]{2,1,0:T(8,128)S(1)}, u32[]{:S(2)}, u32[]{:S(2)}) collective-permute-start(f32[4,8,128]{2,1,0:T(8,128)S(1)} %copy-done.4), channel_id=1, source_target_pairs={{2,1},{1,2},{6,5},{5,6},{10,9},{9,10},{14,13},{13,14},{18,17},{17,... | collective-permute-start | bytes 49160 | tf_op jit(solution)/shard_map/ppermute | solution.py:543
  25.2 8.2 %collective-permute-start.2 = (bf16[16,256]{1,0:T(8,128)(2,1)S(1)}, bf16[16,256]{1,0:T(8,128)(2,1)S(1)}, u32[]{:S(2)}, u32[]{:S(2)}) collective-permute-start(bf16[16,256]{1,0:T(8,128)(2,1)S(1)} %get-tuple-element.62.numbers), channel_id=1, source_target_pairs={{0,1},{1,3},{4,5},{5,7},{8,9},{9,11},{12,13},{13,15},{2,4},{3,6},{... | collective-permute-start | bytes 24584 | tf_op jit(solution)/shard_map/ppermute | solution.py:543
  33.5 6.3 %copy-start.5 = (bf16[256]{0:T(256)(128)(2,1)S(1)}, bf16[256]{0:T(256)(128)(2,1)}, u32[]{:S(2)}) copy-start(bf16[256]{0:T(256)(128)(2,1)} %param.12) | copy-start | bytes 1540
  36.1 12.3 %collective-permute-start.7 = (bf16[1024,256]{1,0:T(8,128)(2,1)S(1)}, bf16[1024,256]{1,0:T(8,128)(2,1)S(1)}, u32[]{:S(2)}, u32[]{:S(2)}) collective-permute-start(bf16[1024,256]{1,0:T(8,128)(2,1)S(1)} %get-tuple-element.71), channel_id=1, source_target_pairs={{1,4},{3,6},{5,8},{7,10},{9,12},{11,14},{4,1},{6,3},{8,5},{10,7},{... | collective-permute-start | bytes 1572872 | tf_op jit(solution)/shard_map/ppermute | solution.py:543
  36.8 11.6 %collective-permute-start.8 = (bf16[1024,256]{1,0:T(8,128)(2,1)S(1)}, bf16[1024,256]{1,0:T(8,128)(2,1)S(1)}, u32[]{:S(2)}, u32[]{:S(2)}) collective-permute-start(bf16[1024,256]{1,0:T(8,128)(2,1)S(1)} %get-tuple-element.72), channel_id=1, source_target_pairs={{1,0},{0,1},{3,2},{2,3},{5,4},{4,5},{7,6},{6,7},{9,8},{8,9},{11,10... | collective-permute-start | bytes 1572872 | tf_op jit(solution)/shard_map/ppermute | solution.py:543
  39.8 8.6 %collective-permute-start.9 = (bf16[512,256]{1,0:T(8,128)(2,1)S(1)}, bf16[512,256]{1,0:T(8,128)(2,1)S(1)}, u32[]{:S(2)}, u32[]{:S(2)}) collective-permute-start(bf16[512,256]{1,0:T(8,128)(2,1)S(1)} %get-tuple-element.73), channel_id=1, source_target_pairs={{2,0},{3,1},{0,2},{1,3},{6,4},{7,5},{4,6},{5,7},{10,8},{11,9},{8,1... | collective-permute-start | bytes 786440 | tf_op jit(solution)/shard_map/ppermute | solution.py:543
  51.2 12.1 %collective-permute-start.10 = (bf16[1024,256]{1,0:T(8,128)(2,1)S(1)}, bf16[1024,256]{1,0:T(8,128)(2,1)S(1)}, u32[]{:S(2)}, u32[]{:S(2)}) collective-permute-start(bf16[1024,256]{1,0:T(8,128)(2,1)S(1)} %get-tuple-element.87), channel_id=1, source_target_pairs={{1,4},{3,6},{5,8},{7,10},{9,12},{11,14},{4,1},{6,3},{8,5},{10,7},{... | collective-permute-start | bytes 1572872 | tf_op jit(solution)/shard_map/ppermute | solution.py:543
  52.1 11.3 %collective-permute-start.11 = (bf16[1024,256]{1,0:T(8,128)(2,1)S(1)}, bf16[1024,256]{1,0:T(8,128)(2,1)S(1)}, u32[]{:S(2)}, u32[]{:S(2)}) collective-permute-start(bf16[1024,256]{1,0:T(8,128)(2,1)S(1)} %get-tuple-element.88), channel_id=1, source_target_pairs={{1,0},{0,1},{3,2},{2,3},{5,4},{4,5},{7,6},{6,7},{9,8},{8,9},{11,10... | collective-permute-start | bytes 1572872 | tf_op jit(solution)/shard_map/ppermute | solution.py:543
  55.1 8.3 %collective-permute-start.12 = (bf16[512,256]{1,0:T(8,128)(2,1)S(1)}, bf16[512,256]{1,0:T(8,128)(2,1)S(1)}, u32[]{:S(2)}, u32[]{:S(2)}) collective-permute-start(bf16[512,256]{1,0:T(8,128)(2,1)S(1)} %get-tuple-element.89), channel_id=1, source_target_pairs={{2,0},{3,1},{0,2},{1,3},{6,4},{7,5},{4,6},{5,7},{10,8},{11,9},{8,1... | collective-permute-start | bytes 786440 | tf_op jit(solution)/shard_map/ppermute | solution.py:543
  65.2 1.6 %collective-permute-start.13 = (f32[280,256]{1,0:T(8,128)S(1)}, f32[280,256]{1,0:T(8,128)S(1)}, u32[]{:S(2)}, u32[]{:S(2)}) collective-permute-start(f32[280,256]{1,0:T(8,128)S(1)} %get-tuple-element.103), channel_id=1, source_target_pairs={{0,1},{1,0},{2,3},{3,2},{4,5},{5,4},{6,7},{7,6},{8,9},{9,8},{10,11... | collective-permute-start | bytes 860168 | tf_op jit(solution)/shard_map/ppermute | solution.py:500
  66.9 8.6 %collective-permute-start.14 = (f32[88,256]{1,0:T(8,128)S(1)}, f32[88,256]{1,0:T(8,128)S(1)}, u32[]{:S(2)}, u32[]{:S(2)}) collective-permute-start(f32[88,256]{1,0:T(8,128)S(1)} %get-tuple-element.105), channel_id=1, source_target_pairs={{0,2},{1,3},{2,0},{3,1},{4,6},{5,7},{6,4},{7,5},{8,10},{9,11},{10,... | collective-permute-start | bytes 270344 | tf_op jit(solution)/shard_map/ppermute | solution.py:500
  68.7 5.1 %collective-permute-start.15 = (f32[72,256]{1,0:T(8,128)S(1)}, f32[72,256]{1,0:T(8,128)S(1)}, u32[]{:S(2)}, u32[]{:S(2)}) collective-permute-start(f32[72,256]{1,0:T(8,128)S(1)} %get-tuple-element.106), channel_id=1, source_target_pairs={{0,4},{1,5},{2,6},{3,7},{4,0},{5,1},{6,2},{7,3},{8,12},{9,13},{10,... | collective-permute-start | bytes 221192 | tf_op jit(solution)/shard_map/ppermute | solution.py:500
  70.2 5.3 %collective-permute-start.16 = (f32[72,256]{1,0:T(8,128)S(1)}, f32[72,256]{1,0:T(8,128)S(1)}, u32[]{:S(2)}, u32[]{:S(2)}) collective-permute-start(f32[72,256]{1,0:T(8,128)S(1)} %get-tuple-element.107), channel_id=1, source_target_pairs={{0,6},{1,7},{2,4},{3,5},{4,2},{5,3},{6,0},{7,1},{8,14},{9,15},{10,... | collective-permute-start | bytes 221192 | tf_op jit(solution)/shard_map/ppermute | solution.py:500
  76.1 5.2 %collective-permute-start.17 = (f32[40,256]{1,0:T(8,128)S(1)}, f32[40,256]{1,0:T(8,128)S(1)}, u32[]{:S(2)}, u32[]{:S(2)}) collective-permute-start(f32[40,256]{1,0:T(8,128)S(1)} %get-tuple-element.110), channel_id=1, source_target_pairs={{0,8},{1,9},{2,10},{3,11},{4,12},{5,13},{6,14},{7,15},{8,0},{9,1},... | collective-permute-start | bytes 122888 | tf_op jit(solution)/shard_map/ppermute | solution.py:500
